TPU v7x, 256 devices: a whole 4x4x8 slice. The times are simulated.
256 devices in a mesh: req: 16 (over z_hi, y, core), tp: 16 (over z_lo, x).
Axes of the slice: x: 4, y: 4, z: 8 (z_hi: 2, z_lo: 4; z = z_hi * 4 + z_lo), core: 2. Of those that a mesh axis runs over, the one named last changes fastest.
Arguments:
- queries: bfloat16 [64, 32, 4096], P('req'), may hold values from -128 to 128
- cache_keys: bfloat16 [64, 4096, 512], P('req', 'tp'), may hold values from -4 to 4
- cache_values: bfloat16 [64, 4096, 512], P('req', 'tp'), may hold values from -5 to 5
- tree_keys: bfloat16 [64, 32, 512], P('req', 'tp'), may hold values from -5 to 5
- tree_values: bfloat16 [64, 32, 512], P('req', 'tp'), may hold values from -5 to 5
- parents: int32 [64, 32], P('req'), may hold values from -1 to 30, as said below
- lengths: int32 [64], P('req'), may hold values from 2 to 4096
- accepted_leaf: int32 [64], P('req'), may hold values from 0 to 31
- residual: bfloat16 [64, 32, 8192], P('req', None, 'tp'), may hold values from -12 to 12
- norm_gain: float32 [8192], replicated, may hold values from 0.5 to 4
- out_weight: bfloat16 [4096, 8192], P('tp'), may hold values from -0.09375 to 0.09375
- prev_feature: bfloat16 [64, 8192], P('req'), may hold values from -5 to 5
- draft_weight: bfloat16 [8192, 8192], P('req', 'tp'), may hold values from -0.0625 to 0.0625
- first_moment: float32 [8192, 8192], P('req', 'tp'), may hold values from -5 to 5
- second_moment: float32 [8192, 8192], P('req', 'tp'), may hold values from 0.25 to 4
Outputs:
- features: bfloat16 [64, 32, 8192], P('req', None, 'tp')
- new_weight: bfloat16 [8192, 8192], P('req', 'tp')
- new_first: float32 [8192, 8192], P('req', 'tp')
- new_second: float32 [8192, 8192], P('req', 'tp')
- draft_loss: float32 [], replicated
Inputs may be any that keep to these rules, and one draw needn't show every extreme that they name: parents[r, 0] = -1; for i of 1 or more, parents[r, i] lies in 0 to i - 1; node 31 is a child of node 30.
All inputs are finite; a program needn't handle non-finite values.
Results may differ from a plain program's by a relative error of at most 0.014.
Values may be sent and summed in bfloat16 or wider, within the bound.
No kernel may reach another device: no remote copies, remote signals or barrier semaphores. Data moves between devices by JAX's collectives and lax.ppermute only.
A program may use at most 128 MiB of HBM per device.

v0:
```python
import math

import jax
import jax.numpy as jnp
from jax import lax
from jax.sharding import PartitionSpec as P

HEADS = 32
KV_HEADS = 4
HEAD = 128
NODES = 32
CACHE = 4096


NEG_FILL = -1e30
NORM_EPSILON = 1e-06
BETA_ONE = 0.9
BETA_TWO = 0.95
CORRECT_ONE = 1.0 - 0.9**10
CORRECT_TWO = 1.0 - 0.95**10
LEARN_RATE = 0.001


def closure(parents):
    node_count = parents.shape[-1]
    onehot = (parents[:, :, None] == jnp.arange(node_count, dtype=jnp.int32)[None, None, :]).astype(
        jnp.float32
    )
    reach_map = jnp.eye(node_count, dtype=jnp.float32)[None] + onehot
    for repeat in range(node_count.bit_length()):
        reach_map = jnp.minimum(
            jnp.einsum("rij,rjk->rik", reach_map, reach_map, precision=lax.Precision.HIGHEST), 1.0
        )
    return reach_map


def body(
    queries,
    cache_keys,
    cache_values,
    tree_keys,
    tree_values,
    parents,
    lengths,
    accepted_leaf,
    residual,
    norm_gain,
    out_weight,
    prev_feature,
    draft_weight,
    first_moment,
    second_moment,
):
    full_residual = lax.all_gather(residual, "tp", axis=2, tiled=True)
    requests = queries.shape[0]
    row_count = requests * NODES
    groups = HEADS // KV_HEADS
    score_scale = 1.0 / math.sqrt(HEAD)
    tp_rank = lax.axis_index("tp")
    cache_span = cache_keys.shape[1]
    tree_span = tree_keys.shape[1]
    reach_map = closure(parents)
    query_view = queries.reshape(requests, NODES, KV_HEADS, groups, HEAD)
    cache_view = cache_keys.reshape(requests, cache_span, KV_HEADS, HEAD)
    tree_view = tree_keys.reshape(requests, tree_span, KV_HEADS, HEAD)
    cache_scores = (
        jnp.einsum("rnkgd,rckd->rkgnc", query_view, cache_view, preferred_element_type=jnp.float32)
        * score_scale
    )
    tree_scores = (
        jnp.einsum("rnkgd,rjkd->rkgnj", query_view, tree_view, preferred_element_type=jnp.float32)
        * score_scale
    )
    positions = tp_rank * cache_span + jnp.arange(cache_span, dtype=jnp.int32)
    cache_live = (positions[None, :] < lengths[:, None])[:, None, None, None, :]
    visible = lax.dynamic_slice_in_dim(reach_map, tp_rank * tree_span, tree_span, 2)
    tree_live = (visible > 0.5)[:, None, None, :, :]
    cache_scores = jnp.where(cache_live, cache_scores, NEG_FILL)
    tree_scores = jnp.where(tree_live, tree_scores, NEG_FILL)
    local_top = jnp.maximum(jnp.max(cache_scores, axis=-1), jnp.max(tree_scores, axis=-1))
    row_top = lax.pmax(local_top, "tp")
    cache_probs = jnp.where(cache_live, jnp.exp(cache_scores - row_top[..., None]), 0.0).astype(
        jnp.bfloat16
    )
    tree_probs = jnp.where(tree_live, jnp.exp(tree_scores - row_top[..., None]), 0.0).astype(
        jnp.bfloat16
    )
    totals = jnp.sum(cache_probs, axis=-1, dtype=jnp.float32) + jnp.sum(
        tree_probs, axis=-1, dtype=jnp.float32
    )
    value_view = cache_values.reshape(requests, cache_span, KV_HEADS, HEAD)
    tree_value_view = tree_values.reshape(requests, tree_span, KV_HEADS, HEAD)
    weighted = jnp.einsum(
        "rkgnc,rckd->rnkgd", cache_probs, value_view, preferred_element_type=jnp.float32
    )
    weighted = weighted + jnp.einsum(
        "rkgnj,rjkd->rnkgd", tree_probs, tree_value_view, preferred_element_type=jnp.float32
    )
    weighted = weighted.reshape(row_count, HEADS * HEAD)
    totals = jnp.transpose(totals, (0, 3, 1, 2)).reshape(row_count, HEADS)
    head_sums, head_totals = (
        lax.psum_scatter(weighted, "tp", scatter_dimension=1, tiled=True),
        lax.psum_scatter(totals, "tp", scatter_dimension=1, tiled=True),
    )
    own_heads = head_totals.shape[1]
    attended = (head_sums.reshape(row_count, own_heads, HEAD) / head_totals[:, :, None]).astype(
        jnp.bfloat16
    )
    partial_value = jnp.dot(
        attended.reshape(row_count, own_heads * HEAD),
        out_weight,
        preferred_element_type=jnp.float32,
    )
    partial_value = lax.optimization_barrier(partial_value.astype(jnp.bfloat16)).astype(jnp.float32)
    model_width = partial_value.shape[1]
    block_width = model_width // lax.axis_size("tp")
    summed = lax.psum(partial_value.astype(jnp.bfloat16), "tp").astype(jnp.float32)
    mixed = full_residual.reshape(row_count, model_width).astype(jnp.float32) + summed
    mean_sq = jnp.mean(mixed * mixed, axis=1, keepdims=True)
    features = (mixed * lax.rsqrt(mean_sq + NORM_EPSILON) * norm_gain[None, :]).astype(jnp.bfloat16)
    own_block = lax.dynamic_slice_in_dim(features, tp_rank * block_width, block_width, 1)
    feature_table = jnp.concatenate(
        [prev_feature[:, None, :], features.reshape(requests, NODES, model_width)], axis=1
    )
    inputs = jnp.take_along_axis(feature_table, (parents + 1)[:, :, None], axis=1).reshape(
        row_count, model_width
    )
    leaf_hot = (accepted_leaf[:, None] == jnp.arange(NODES, dtype=jnp.int32)[None, :]).astype(
        jnp.float32
    )
    accepted = jnp.einsum("rn,rnj->rj", leaf_hot, reach_map, precision=lax.Precision.HIGHEST)
    fill_share = 0.5 + lengths.astype(jnp.float32) / CACHE
    weights = ((1.0 + 3.0 * accepted) * fill_share[:, None]).reshape(row_count, 1)
    columns = inputs
    predicted = jnp.dot(
        columns,
        lax.all_gather(draft_weight, "req", axis=0, tiled=True),
        preferred_element_type=jnp.float32,
    )
    pred_error = predicted - own_block.astype(jnp.float32)
    scaled_err = (weights * pred_error).astype(jnp.bfloat16)
    columns = inputs
    gradient = lax.psum_scatter(
        lax.dot_general(
            columns, scaled_err, (((0,), (0,)), ((), ())), preferred_element_type=jnp.float32
        ),
        "req",
        scatter_dimension=0,
        tiled=True,
    )
    square_total, error_total = lax.psum(
        (jnp.sum(gradient * gradient), jnp.sum(weights * pred_error * pred_error)), ("req", "tp")
    )
    draft_loss = 0.5 * error_total / (row_count * lax.axis_size("req") * model_width)
    grad_norm = jnp.sqrt(square_total) + 1e-06
    clip_factor = jnp.minimum(1.0, model_width / grad_norm)
    clipped = gradient * clip_factor
    new_first = BETA_ONE * first_moment + (1.0 - BETA_ONE) * clipped
    new_second = BETA_TWO * second_moment + (1.0 - BETA_TWO) * clipped * clipped
    direction = new_first / CORRECT_ONE / (jnp.sqrt(new_second / CORRECT_TWO) + 1e-08)
    new_weight = (draft_weight.astype(jnp.float32) - LEARN_RATE * direction).astype(jnp.bfloat16)
    return (
        own_block.reshape(requests, NODES, block_width),
        new_weight,
        new_first,
        new_second,
        draft_loss,
    )


def solution(mesh):
    placed = (
        P("req", None, None),
        P("req", "tp", None),
        P("req", "tp", None),
        P("req", "tp", None),
        P("req", "tp", None),
        P("req", None),
        P("req"),
        P("req"),
        P("req", None, "tp"),
        P(),
        P("tp", None),
        P("req", None),
        P("req", "tp"),
        P("req", "tp"),
        P("req", "tp"),
    )
    return jax.shard_map(
        body,
        mesh=mesh,
        in_specs=placed,
        out_specs=(P("req", None, "tp"), P("req", "tp"), P("req", "tp"), P("req", "tp"), P()),
        check_vma=False,
    )
```

profile of v0, /device:TPU:1, one launch (start us, length us, event | category | flops | bytes accessed | tf_op | source)
XLA Modules:
  0.0 868.4 jit_solution(2874297902461404456)
XLA Ops:
  7.2 0.0 copy-start
  7.2 0.0 reduce-scatter.3.cloned.1.call-start
  7.3 1.1 convolution_minimum_fusion.4
  8.4 0.1 copy.91
  8.5 0.3 convolution_minimum_fusion.3
  8.8 0.1 copy.92
  8.9 0.3 convolution_minimum_fusion.2
  9.2 0.1 copy.93
  9.3 0.3 convolution_minimum_fusion.1
  9.6 0.1 copy.94
  9.7 0.3 convolution_minimum_fusion
  10.0 0.1 copy.95
  10.1 0.2 fusion.19
  10.3 0.1 copy_minimum_fusion
  10.4 1.4 copy.89
  11.8 1.1 reshape.107
  13.0 0.3 reshape.110
  13.2 0.1 broadcast_compare_fusion
  13.3 1.5 fusion.38
  14.8 4.1 bitcast_reduce_fusion
  19.0 67.8 %pmax.7 = f32[4,4,8,32]{3,2,1,0:T(8,128)S(1)} all-reduce(f32[4,4,8,32]{3,2,1,0:T(8,128)S(1)} %max.5), channel_id=1, replica_groups=mesh['req'=16,'tp'=16] {'tp'}, use_global_device_ids=true, to_apply=%region_2.3 | all-reduce | flops 4096 | bytes 32768 | tf_op jit(solution)/shard_map/pmax | solution.py:81
  86.7 0.3 convert_reduce_fusion.1
  87.0 3.0 fusion.6
  90.0 0.5 add_bitcast_fusion
  90.5 1.2 copy.74
  91.7 1.5 reshape.112
  93.2 0.0 reduce-scatter.3.cloned.1.call-update
  93.3 0.0 all-gather.3.cloned.1.call-start
  93.3 0.7 all-gather.3.cloned.1.call-update
  94.0 0.0 all-reduce.4.cloned.1.call-start
  94.1 3.1 convert_reduce_fusion
  97.3 0.1 reshape.113
  97.4 0.6 dynamic-slice
  98.6 61.0 %all-reduce = f32[128,32]{0,1:T(8,128)S(1)} all-reduce(f32[128,32]{0,1:T(8,128)S(1)} %reshape.113), channel_id=3, replica_groups=mesh['req'=16,'tp'=16] {'tp'}, use_global_device_ids=true, to_apply=%region_6.7.clone | all-reduce | flops 4096 | bytes 32768
  159.6 0.1 copy.76
  159.7 23.9 %reduce-scatter.3.cloned.1.call-done = f32[128,256]{1,0:T(8,128)} async-done(((f32[128,4096]{1,0:T(8,128)}), f32[128,256]{1,0:T(8,128)}) %reduce-scatter.3.cloned.1.call-update) | async-done | bytes 131088 | tf_op jit(solution)/shard_map/reduce_scatter | solution.py:102
  183.7 0.2 div.41
  183.9 4.3 convolution_convert_fusion
  188.2 0.0 all-reduce.4.cloned.1.call-update
  188.2 0.0 all-gather.5.cloned.1.call-start
  188.3 0.5 all-gather.5.cloned.1.call-update
  188.8 0.2 reduce-scatter.5.cloned.1.call-start
  189.1 0.1 broadcast_in_dim.74
  189.2 0.1 reshape.117
  189.3 0.1 fusion.33
  189.3 0.2 fusion.17
  189.5 0.1 add_multiply_fusion
  189.6 0.1 mul.137
  189.7 75.2 %all-gather.3.cloned.1.call-done = bf16[4,32,8192]{2,1,0:T(8,128)(2,1)} async-done(((bf16[4,32,512]{2,1,0:T(8,128)(2,1)}), bf16[4,32,8192]{2,1,0:T(8,128)(2,1)}) %all-gather.3.cloned.1.call-update) | async-done | bytes 2097168 | tf_op jit(solution)/shard_map/all_gather | solution.py:54
  264.8 168.2 %all-reduce.4.cloned.1.call-done = bf16[128,8192]{1,0:T(8,128)(2,1)} async-done(((bf16[128,8192]{1,0:T(8,128)(2,1)}), bf16[128,8192]{1,0:T(8,128)(2,1)}) %all-reduce.4.cloned.1.call-update) | async-done | bytes 2097168 | tf_op jit(solution)/shard_map/psum | solution.py:117
  433.0 3.1 multiply_reduce_fusion
  436.2 1.0 multiply_convert_fusion
  437.2 1.6 copy.77
  438.9 1.4 pad_maximum_fusion
  440.3 8.3 gather_fusion
  448.5 0.9 constant_dynamic-slice_fusion.1
  449.5 103.7 %all-gather.5.cloned.1.call-done = bf16[8192,512]{1,0:T(8,128)(2,1)} async-done(((bf16[512,512]{1,0:T(8,128)(2,1)}), bf16[8192,512]{1,0:T(8,128)(2,1)}) %all-gather.5.cloned.1.call-update) | async-done | bytes 8388624 | tf_op jit(solution)/shard_map/all_gather | solution.py:137
  553.2 6.2 fusion.13
  559.4 8.2 fusion.12
  567.6 0.0 reduce-scatter.5.cloned.1.call-update
  567.6 210.0 %reduce-scatter.5.cloned.1.call-done = f32[512,512]{1,0:T(8,128)} async-done(((f32[8192,512]{1,0:T(8,128)}), f32[512,512]{1,0:T(8,128)}) %reduce-scatter.5.cloned.1.call-update) | async-done | bytes 1048592 | tf_op jit(solution)/shard_map/reduce_scatter | solution.py:143
  777.6 2.1 multiply_reduce_fusion.1
  779.7 76.2 %all-reduce.1 = (f32[]{:T(128)}, f32[]{:T(128)}) all-reduce(f32[]{:T(128)} %multiply_reduce_fusion.1, f32[]{:T(128)} %get-tuple-element.16), channel_id=1, replica_groups=mesh['req'=16,'tp'=16] {'req','tp'}, use_global_device_ids=true, to_apply=%region_11.12 | all-reduce | flops 2 | bytes 16 | tf_op jit(solution)/shard_map/psum | solution.py:151
  857.3 3.4 subtract_convert_fusion
  (49 shorter events, 0.2 us)
Async XLA Ops:
  7.2 82.8 %copy-start = (bf16[4,2,512]{2,1,0:T(2,128)(2,1)S(1)}, bf16[4,2,512]{2,1,0:T(2,128)(2,1)}, u32[]{:S(2)}) copy-start(bf16[4,2,512]{2,1,0:T(2,128)(2,1)} %param.19) | copy-start | bytes 24580
  7.2 4.7 copy-start.9
  7.2 5.8 copy-start.10
  7.2 6.0 copy-start.15
  7.2 6.1 copy-start.16
  7.2 176.4 %reduce-scatter.3.cloned.1.call-start = ((), (), s32[]{:S(2)}) async-start(), calls=%async_computation.3 | async-start | bytes 2228224 | tf_op jit(solution)/shard_map/reduce_scatter | solution.py:102
  93.2 4.2 copy-start.18
  93.3 171.5 %all-gather.3.cloned.1.call-start = ((), (), s32[]{:S(2)}) async-start(), calls=%async_computation.2 | async-start | bytes 2228224 | tf_op jit(solution)/shard_map/all_gather | solution.py:54
  94.0 338.9 %all-reduce.4.cloned.1.call-start = ((), (), s32[]{:S(2)}) async-start(), calls=%async_computation.4 | async-start | bytes 4194304 | tf_op jit(solution)/shard_map/psum | solution.py:117
  183.9 5.2 copy-start.14
  183.9 5.4 copy-start.17
  188.2 247.9 %copy-start.13 = (f32[8192]{0:T(1024)S(1)}, f32[8192]{0:T(1024)}, u32[]{:S(2)}) copy-start(f32[8192]{0:T(1024)} %param.24) | copy-start | bytes 98308
  188.2 365.0 %all-gather.5.cloned.1.call-start = ((), (), s32[]{:S(2)}) async-start(), calls=%async_computation.5 | async-start | bytes 8912896 | tf_op jit(solution)/shard_map/all_gather | solution.py:137
  188.8 588.8 %reduce-scatter.5.cloned.1.call-start = ((), (), s32[]{:S(2)}) async-start(), calls=%async_computation.6 | async-start | bytes 17825792 | tf_op jit(solution)/shard_map/reduce_scatter | solution.py:143
  264.8 171.3 %copy-start.4 = (bf16[4,32,8192]{2,1,0:T(8,128)(2,1)S(1)}, bf16[4,32,8192]{2,1,0:T(8,128)(2,1)}, u32[]{:S(2)}) copy-start(bf16[4,32,8192]{2,1,0:T(8,128)(2,1)} %all-gather.3.cloned.1.call-done) | copy-start | bytes 6291460
  433.0 3.2 copy-start.5
  436.1 2.7 copy-start.12
  437.2 1.6 copy-start.3
  449.5 109.9 %copy-start.11 = (bf16[128,512]{1,0:T(8,128)(2,1)}, bf16[128,512]{1,0:T(8,128)(2,1)S(1)}, u32[]{:S(2)}) copy-start(bf16[128,512]{1,0:T(8,128)(2,1)S(1)} %constant_dynamic-slice_fusion.1) | copy-start | bytes 393220
  449.5 109.9 %copy-start.2 = (bf16[128,8192]{1,0:T(8,128)(2,1)S(1)}, bf16[128,8192]{1,0:T(8,128)(2,1)}, u32[]{:S(2)}) copy-start(bf16[128,8192]{1,0:T(8,128)(2,1)} %gather_fusion) | copy-start | bytes 6291460
  567.6 289.7 %copy-start.6 = (bf16[512,512]{1,0:T(8,128)(2,1)S(1)}, bf16[512,512]{1,0:T(8,128)(2,1)}, u32[]{:S(2)}) copy-start(bf16[512,512]{1,0:T(8,128)(2,1)} %param.27) | copy-start | bytes 1572868
  567.6 289.7 %copy-start.7 = (f32[512,512]{1,0:T(8,128)S(1)}, f32[512,512]{1,0:T(8,128)}, u32[]{:S(2)}) copy-start(f32[512,512]{1,0:T(8,128)} %param.28) | copy-start | bytes 3145732
  567.6 289.7 %copy-start.8 = (f32[512,512]{1,0:T(8,128)S(1)}, f32[512,512]{1,0:T(8,128)}, u32[]{:S(2)}) copy-start(f32[512,512]{1,0:T(8,128)} %param.29) | copy-start | bytes 3145732
  567.6 293.1 %copy-start.1 = (bf16[4,2,512]{2,1,0:T(2,128)(2,1)S(1)}, bf16[4,2,512]{2,1,0:T(2,128)(2,1)}, u32[]{:S(2)}) copy-start(bf16[4,2,512]{2,1,0:T(2,128)(2,1)} %param.19) | copy-start | bytes 24580
Sparse Core Ops, SparseCore 0:
  93.4 90.2 reduce-scatter.2
  185.5 79.3 all-gather.2
  267.5 165.4 all-reduce.3
  435.6 117.5 all-gather.4
  567.7 209.8 reduce-scatter.4
where the time goes:
time: 869 us; the launch traced here: 868 us
  waiting for transfers between devices  582 us (67%)
  blocking collectives  205 us (24%)
  matrix products  30.4 us (3%)
  local copies, waits for them, and re-layouts  18.2 us (2%)
  between operations  17.4 us (2%)
  other arithmetic  14.8 us (2%)
    reduce_scatter x1, waiting for transfers between devices, body(): lax.psum_scatter(lax.dot_general(columns, scaled_err, (((0,), (0,)), ((),...  210 us
    psum x1, waiting for transfers between devices, body(): lax.psum(partial_value.astype(jnp.bfloat16), 'tp').astype(jnp.float32)  168 us
    all_gather x1, waiting for transfers between devices, body(): lax.all_gather(draft_weight, 'req', axis=0, tiled=True)  104 us
    psum x1, blocking collectives, body(): lax.psum((jnp.sum(gradient * gradient), jnp.sum(weights * pred_error * pr...  76.2 us
    all_gather x1, waiting for transfers between devices, body(): full_residual = lax.all_gather(residual, 'tp', axis=2, tiled=True)  75.2 us
    pmax x1, blocking collectives, body(): row_top = lax.pmax(local_top, 'tp')  67.8 us
    unnamed x1, blocking collectives  61 us
    reduce_scatter x1, waiting for transfers between devices, body(): lax.psum_scatter(weighted, 'tp', scatter_dimension=1, tiled=True)  23.9 us
  transfers between devices with their start and end apart: 5, of which 5 were waited for; matrix products, arithmetic and copies ran while one was open for 3% of the time, Pallas kernels for 0%

commit v1 on v0

v1 whole, which is shorter than its diff:
```python
import math

import jax
import jax.numpy as jnp
from jax import lax
from jax.sharding import Mesh
from jax.sharding import PartitionSpec as P

HEADS = 32
KV_HEADS = 4
HEAD = 128
NODES = 32
CACHE = 4096
D = 8192
N_TP = 16
N_REQ = 16

NEG_FILL = -1e30
NORM_EPSILON = 1e-06
BETA_ONE = 0.9
BETA_TWO = 0.95
CORRECT_ONE = 1.0 - 0.9**10
CORRECT_TWO = 1.0 - 0.95**10
LEARN_RATE = 0.001

REQ = ("zh", "y", "c")
TP = ("zl", "x")
F32 = jnp.float32
BF16 = jnp.bfloat16


def exchange(value, axis):
    return lax.all_to_all(value, axis, 0, 0, tiled=True)


def spread(value, axis, count):
    wide = jnp.broadcast_to(value[None], (count, *value.shape))
    return exchange(wide.reshape(count * value.shape[0], *value.shape[1:]), axis)


def gather(value, axis):
    return lax.all_gather(value, axis, axis=0, tiled=True)


def closure(parents):
    onehot = (parents[:, :, None] == jnp.arange(NODES, dtype=jnp.int32)[None, None, :]).astype(BF16)
    reach_map = jnp.eye(NODES, dtype=BF16)[None] + onehot
    for repeat in range((NODES - 1).bit_length()):
        squared = jnp.einsum("rij,rjk->rik", reach_map, reach_map, preferred_element_type=F32)
        reach_map = jnp.minimum(squared, 1.0).astype(BF16)
    return reach_map


def pieces(value):
    high = value.astype(BF16)
    return high, (value - high.astype(F32)).astype(BF16)


def body(
    queries,
    cache_keys,
    cache_values,
    tree_keys,
    tree_values,
    parents,
    lengths,
    accepted_leaf,
    residual,
    norm_gain,
    out_weight,
    prev_feature,
    draft_weight,
    first_moment,
    second_moment,
):
    requests = queries.shape[0]
    rows = requests * NODES
    groups = HEADS // KV_HEADS
    score_scale = 1.0 / math.sqrt(HEAD)
    tp_rank = lax.axis_index(TP)
    cache_span = cache_keys.shape[1]
    tree_span = tree_keys.shape[1]
    block = residual.shape[2]

    all_weight = gather(gather(gather(draft_weight[None], "zh"), "y"), "c")
    all_weight = jnp.transpose(
        all_weight.reshape(2, 4, 2, *draft_weight.shape), (2, 1, 0, 3, 4)
    ).reshape(D, block)

    reach_map = closure(parents)
    query_view = queries.reshape(requests, NODES, KV_HEADS, groups, HEAD)
    cache_view = cache_keys.reshape(requests, cache_span, KV_HEADS, HEAD)
    tree_view = tree_keys.reshape(requests, tree_span, KV_HEADS, HEAD)
    cache_scores = (
        jnp.einsum("rnkgd,rckd->rkgnc", query_view, cache_view, preferred_element_type=F32)
        * score_scale
    )
    tree_scores = (
        jnp.einsum("rnkgd,rjkd->rkgnj", query_view, tree_view, preferred_element_type=F32)
        * score_scale
    )
    positions = tp_rank * cache_span + jnp.arange(cache_span, dtype=jnp.int32)
    cache_live = (positions[None, :] < lengths[:, None])[:, None, None, None, :]
    visible = lax.dynamic_slice_in_dim(reach_map, tp_rank * tree_span, tree_span, 2)
    tree_live = (visible > 0.5)[:, None, None, :, :]
    cache_scores = jnp.where(cache_live, cache_scores, NEG_FILL)
    tree_scores = jnp.where(tree_live, tree_scores, NEG_FILL)
    local_top = jnp.maximum(jnp.max(cache_scores, axis=-1), jnp.max(tree_scores, axis=-1)).astype(BF16)
    shift = local_top.astype(F32)[..., None]
    cache_probs = jnp.where(cache_live, jnp.exp(cache_scores - shift), 0.0).astype(BF16)
    tree_probs = jnp.where(tree_live, jnp.exp(tree_scores - shift), 0.0).astype(BF16)
    totals = jnp.sum(cache_probs, axis=-1, dtype=F32) + jnp.sum(tree_probs, axis=-1, dtype=F32)
    value_view = cache_values.reshape(requests, cache_span, KV_HEADS, HEAD)
    tree_value_view = tree_values.reshape(requests, tree_span, KV_HEADS, HEAD)
    weighted = jnp.einsum("rkgnc,rckd->rkgnd", cache_probs, value_view, preferred_element_type=F32)
    weighted = weighted + jnp.einsum(
        "rkgnj,rjkd->rkgnd", tree_probs, tree_value_view, preferred_element_type=F32
    )
    weighted = weighted.astype(BF16).reshape(requests, N_TP, 2, NODES, HEAD)
    weighted = jnp.transpose(weighted, (1, 0, 3, 2, 4)).reshape(N_TP, rows, 2 * HEAD)
    total_high, total_low = pieces(totals)
    stats = jnp.stack([local_top, total_high, total_low]).reshape(3, requests, N_TP, 2, NODES)
    stats = jnp.transpose(stats, (2, 0, 3, 1, 4)).reshape(N_TP, 3, 2 * rows)
    stats = jnp.pad(stats, ((0, 0), (0, 13), (0, 0)))
    parcel = jnp.concatenate([weighted, stats], axis=1).reshape(N_TP * (rows + 16), 2 * HEAD)
    parcel = exchange(parcel, TP).reshape(N_TP, rows + 16, 2 * HEAD)
    sums = parcel[:, :rows].reshape(N_TP, rows, 2, HEAD).astype(F32)
    stats = parcel[:, rows : rows + 3].astype(F32).reshape(N_TP, 3, 2, rows)
    tops = stats[:, 0]
    factor = jnp.exp(tops - jnp.max(tops, axis=0, keepdims=True))
    share = factor / jnp.sum(factor * (stats[:, 1] + stats[:, 2]), axis=0, keepdims=True)
    share = jnp.transpose(share, (0, 2, 1))[..., None]
    attended = jnp.sum(sums * share, axis=0).astype(BF16).reshape(rows, 2 * HEAD)

    partial_value = jnp.dot(attended, out_weight, preferred_element_type=F32).astype(BF16)
    partial_value = jnp.transpose(partial_value.reshape(rows, 4, 4, block), (2, 1, 0, 3))
    along_x = exchange(partial_value.reshape(16 * rows, block), "x").reshape(4, 4 * rows, block)
    along_x = jnp.sum(along_x.astype(F32), axis=0).astype(BF16)
    along_z = exchange(along_x, "zl").reshape(4, rows, block)
    projected = jnp.sum(along_z.astype(F32), axis=0)
    mixed = residual.reshape(rows, block).astype(F32) + projected

    near = gather(mixed.astype(BF16)[None], "zl")
    far = spread(near, "x", 4).reshape(4, 4, rows, block)
    table = jnp.transpose(far, (1, 0, 2, 3)).reshape(N_TP, rows, block).astype(F32)
    mean_sq = jnp.mean(table * table, axis=(0, 2))[:, None]
    scale = lax.rsqrt(mean_sq + NORM_EPSILON)
    own_gain = lax.dynamic_slice_in_dim(norm_gain, tp_rank * block, block, 0)
    own_features = (mixed * scale * own_gain[None, :]).astype(BF16)
    table = (table * scale[None] * norm_gain.reshape(N_TP, 1, block)).astype(BF16)
    prev = jnp.transpose(prev_feature.reshape(requests, N_TP, block), (1, 0, 2))[:, :, None, :]
    last = (jnp.arange(NODES) == NODES - 1)[None, None, :, None]
    table = jnp.where(last, prev, table.reshape(N_TP, requests, NODES, block))
    table = table.reshape(N_TP, rows, block)
    pick = jnp.where(parents < 0, NODES - 1, parents)
    pick = (pick[:, :, None] == jnp.arange(NODES, dtype=jnp.int32)[None, None, :]).astype(F32)

    columns = exchange(table.reshape(N_TP * rows, block), REQ)

    leaf_hot = (accepted_leaf[:, None] == jnp.arange(NODES, dtype=jnp.int32)[None, :]).astype(BF16)
    accepted = jnp.einsum("rn,rnj->rj", leaf_hot, reach_map, preferred_element_type=F32)
    fill_share = 0.5 + lengths.astype(F32) / CACHE
    weights = ((1.0 + 3.0 * accepted) * fill_share[:, None]).reshape(rows, 1)

    ahead = jnp.dot(
        jnp.transpose(table, (1, 0, 2)).reshape(rows, D), all_weight, preferred_element_type=F32
    )
    predicted = jnp.einsum(
        "rij,rjd->rid", pick, ahead.reshape(requests, NODES, block), precision=lax.Precision.HIGHEST
    ).reshape(rows, block)
    pred_error = predicted - own_features.astype(F32)
    weighted_err = weights * pred_error
    scaled_err = jnp.einsum(
        "rij,rid->rjd",
        pick,
        weighted_err.reshape(requests, NODES, block),
        precision=lax.Precision.HIGHEST,
    ).astype(BF16)
    all_err = gather(scaled_err.reshape(1, rows, block), "zh")
    all_err = spread(spread(all_err, "y", 4), "c", 2)
    all_err = jnp.transpose(all_err.reshape(2, 4, 2, rows, block), (2, 1, 0, 3, 4))
    gradient = lax.dot_general(
        columns,
        all_err.reshape(N_REQ * rows, block),
        (((0,), (0,)), ((), ())),
        preferred_element_type=F32,
    )
    square = jnp.sum(gradient * gradient)
    error = jnp.sum(weighted_err * pred_error)
    lane = jnp.arange(128)[None, :]
    pair = jnp.where(lane == 0, square, jnp.where(lane == 1, error, 0.0))
    pair = jnp.sum(spread(pair, REQ + TP, N_REQ * N_TP), axis=0)
    square_total, error_total = pair[0], pair[1]
    draft_loss = 0.5 * error_total / (rows * N_REQ * D)
    grad_norm = jnp.sqrt(square_total) + 1e-06
    clip_factor = jnp.minimum(1.0, D / grad_norm)
    clipped = gradient * clip_factor
    new_first = BETA_ONE * first_moment + (1.0 - BETA_ONE) * clipped
    new_second = BETA_TWO * second_moment + (1.0 - BETA_TWO) * clipped * clipped
    direction = new_first / CORRECT_ONE / (jnp.sqrt(new_second / CORRECT_TWO) + 1e-08)
    new_weight = (draft_weight.astype(F32) - LEARN_RATE * direction).astype(BF16)
    return (
        own_features.reshape(requests, NODES, block),
        new_weight,
        new_first,
        new_second,
        draft_loss,
    )


def solution(mesh):
    fine = Mesh(mesh.devices.reshape(2, 4, 2, 4, 4), REQ + TP)
    placed = (
        P(REQ, None, None),
        P(REQ, TP, None),
        P(REQ, TP, None),
        P(REQ, TP, None),
        P(REQ, TP, None),
        P(REQ, None),
        P(REQ),
        P(REQ),
        P(REQ, None, TP),
        P(),
        P(TP, None),
        P(REQ, None),
        P(REQ, TP),
        P(REQ, TP),
        P(REQ, TP),
    )
    return jax.shard_map(
        body,
        mesh=fine,
        in_specs=placed,
        out_specs=(P(REQ, None, TP), P(REQ, TP), P(REQ, TP), P(REQ, TP), P()),
        check_vma=False,
    )
```

time: 869 us -> 368 us (0.42)
  waiting for transfers between devices: 582 us -> 153 us
  blocking collectives: 205 us -> 101 us
  starting transfers between devices: 0.38 us -> 21 us
  local copies, waits for them, and re-layouts: 18.2 us -> 37 us
    reduce_scatter x2 -> x0, waiting for transfers between devices: 234 us -> none  [the longest x1 210 us: body(): lax.psum_scatter(lax.dot_general(columns, scaled_err, (((0,), (0,)), ((),...]
    psum x1 -> x0, waiting for transfers between devices: 168 us -> none  [body(): lax.psum(partial_value.astype(jnp.bfloat16), 'tp').astype(jnp.float32)]
    all_gather x2 -> x3, waiting for transfers between devices: 179 us -> 73.2 us  [gather(): return lax.all_gather(value, axis, axis=0, tiled=True)]
    all_to_all x0 -> x4, waiting for transfers between devices: none -> 78.8 us  [exchange(): return lax.all_to_all(value, axis, 0, 0, tiled=True)]
    all_to_all x0 -> x4, blocking collectives: none -> 76.9 us  [exchange(): return lax.all_to_all(value, axis, 0, 0, tiled=True)]
    psum x1 -> x0, blocking collectives: 76.2 us -> none  [body(): lax.psum((jnp.sum(gradient * gradient), jnp.sum(weights * pred_error * pr...]
    pmax x1 -> x0, blocking collectives: 67.8 us -> none  [body(): row_top = lax.pmax(local_top, 'tp')]
    unnamed x1 -> x0, blocking collectives: 61 us -> none
  transfers between devices with their start and end apart: 5 -> 7, of which waited for: 5 -> 5; matrix products, arithmetic and copies ran while one was open for 3% -> 14% of each run, Pallas kernels for 0% -> 0%
where the time goes in v1:
time: 368 us; the launch traced here: 367 us
  waiting for transfers between devices  153 us (42%)
  blocking collectives  101 us (27%)
  local copies, waits for them, and re-layouts  37 us (10%)
  matrix products  23 us (6%)
  starting transfers between devices  21 us (6%)
  between operations  16.8 us (5%)
  other arithmetic  14.8 us (4%)
    all_to_all x4, waiting for transfers between devices, exchange(): return lax.all_to_all(value, axis, 0, 0, tiled=True)  78.8 us
    all_to_all x4, blocking collectives, exchange(): return lax.all_to_all(value, axis, 0, 0, tiled=True)  76.9 us
    all_gather x3, waiting for transfers between devices, gather(): return lax.all_gather(value, axis, axis=0, tiled=True)  73.2 us
    all_gather x2, blocking collectives, gather(): return lax.all_gather(value, axis, axis=0, tiled=True)  24.5 us
    all_to_all x4, starting transfers between devices, exchange(): return lax.all_to_all(value, axis, 0, 0, tiled=True)  20.8 us
    transpose x1, local copies, waits for them, and re-layouts, body(): jnp.transpose(all_weight.reshape(2, 4, 2, *draft_weight.shape), (2, 1, 0,...  7.37 us
  transfers between devices with their start and end apart: 7, of which 5 were waited for; matrix products, arithmetic and copies ran while one was open for 14% of the time, Pallas kernels for 0%

profile of v1, /device:TPU:1, one launch (start us, length us, event | category | flops | bytes accessed | tf_op | source)
XLA Modules:
  0.0 366.7 jit_solution(16399183638599829381)
XLA Ops:
  7.2 0.7 all-gather.9.cloned.1.call-update
  8.0 47.4 %all-gather.9.cloned.1.call-done = bf16[1024,512]{1,0:T(8,128)(2,1)} async-done(((bf16[512,512]{1,0:T(8,128)(2,1)}), bf16[1024,512]{1,0:T(8,128)(2,1)}) %all-gather.9.cloned.1.call-update) | async-done | bytes 1048592 | tf_op jit(solution)/shard_map/all_gather | solution.py:42
  55.4 1.0 fusion.10
  56.4 0.1 copy.222
  56.5 0.2 fusion.11
  56.7 0.1 copy.223
  56.8 0.2 fusion.12
  57.0 0.1 copy.224
  57.1 0.2 fusion.13
  57.3 0.1 copy.225
  57.4 0.1 fusion.32
  57.6 1.2 copy.220
  58.8 1.1 reshape.390
  59.9 0.3 reshape.393
  60.3 2.7 fusion.54
  63.1 2.3 bitcast_reduce_fusion
  65.4 0.3 convert_reduce_fusion.2
  65.7 1.6 fusion.15
  67.3 0.5 add_convert_fusion
  67.8 1.1 copy.263
  68.9 0.7 reshape.396
  69.7 3.1 convert_reduce_fusion
  73.0 0.1 reshape.397
  73.2 1.2 fusion.7
  74.4 4.1 %all-to-all-start = ((bf16[16,144,256]{2,1,0:T(8,128)(2,1)}), bf16[16,144,256]{2,1,0:T(8,128)(2,1)S(1)}, u32[]{:S(2)}, u32[]{:S(2)}) async-start(bf16[16,144,256]{2,1,0:T(8,128)(2,1)} %fusion.7), calls=%async_computation | async-start | bytes 2359296 | tf_op jit(solution)/shard_map/all_to_all | solution.py:33
  78.6 25.8 %all-gather.5.cloned.1.call-done = bf16[8,512,512]{2,1,0:T(8,128)(2,1)} async-done(((bf16[2,512,512]{2,1,0:T(8,128)(2,1)}), bf16[8,512,512]{2,1,0:T(8,128)(2,1)}) %all-gather.5.cloned.1.call-update) | async-done | bytes 4194320 | tf_op jit(solution)/shard_map/all_gather | solution.py:42
  104.5 0.4 copy.198
  104.9 3.5 mul.176
  108.4 2.9 mul.177
  111.3 0.2 multiply_reduce_fusion.1
  111.5 2.9 convolution_convert_fusion
  114.4 2.8 reshape.400
  117.2 3.1 copy.199
  120.3 27.8 %all_to_all.54 = bf16[4,512,512]{2,1,0:T(8,128)(2,1)S(1)} all-to-all(bf16[4,512,512]{2,1,0:T(8,128)(2,1)S(1)} %bitcast.135), channel_id=1, replica_groups=mesh['zh'=2,'y'=4,'c'=2,'zl'=4,'x'=4] {'x'}, dimensions={0} | all-to-all | bytes 4194304 | tf_op jit(solution)/shard_map/all_to_all | solution.py:33
  148.1 1.2 reduce_sum.101
  149.3 5.4 %all-to-all-start.2 = ((bf16[4,128,512]{2,1,0:T(8,128)(2,1)}), bf16[4,128,512]{2,1,0:T(8,128)(2,1)S(1)}, u32[]{:S(2)}, u32[]{:S(2)}) async-start(bf16[4,128,512]{2,1,0:T(8,128)(2,1)} %bitcast.20), calls=%async_computation.2 | async-start | bytes 1048576 | tf_op jit(solution)/shard_map/all_to_all | solution.py:33
  154.7 11.5 %all-to-all-done.2 = bf16[4,128,512]{2,1,0:T(8,128)(2,1)S(1)} async-done(((bf16[4,128,512]{2,1,0:T(8,128)(2,1)}), bf16[4,128,512]{2,1,0:T(8,128)(2,1)S(1)}, u32[]{:S(2)}, u32[]{:S(2)}) %all-to-all-start.2) | async-done | bytes 524320 | tf_op jit(solution)/shard_map/all_to_all | solution.py:33
  166.3 14.1 %all_gather.15 = bf16[4,128,512]{2,1,0:T(8,128)(2,1)S(1)} all-gather(bf16[1,128,512]{2,1,0:T(8,128)(2,1)S(1)} %fusion.23), channel_id=1, replica_groups=mesh['zh'=2,'y'=4,'c'=2,'zl'=4,'x'=4] {'zl'}, dimensions={0}, use_global_device_ids=true | all-gather | bytes 655360 | tf_op jit(solution)/shard_map/all_gather | solution.py:42
  180.4 1.5 broadcast_in_dim.131
  181.9 3.8 %all-to-all-start.3 = ((bf16[16,128,512]{2,1,0:T(8,128)(2,1)}), bf16[16,128,512]{2,1,0:T(8,128)(2,1)S(1)}, u32[]{:S(2)}, u32[]{:S(2)}) async-start(bf16[16,128,512]{2,1,0:T(8,128)(2,1)} %bitcast.132), calls=%async_computation.3 | async-start | bytes 4194304 | tf_op jit(solution)/shard_map/all_to_all | solution.py:33
  186.1 0.1 fusion.30
  186.3 20.0 %all-to-all-done.3 = bf16[16,128,512]{2,1,0:T(8,128)(2,1)S(1)} async-done(((bf16[16,128,512]{2,1,0:T(8,128)(2,1)}), bf16[16,128,512]{2,1,0:T(8,128)(2,1)S(1)}, u32[]{:S(2)}, u32[]{:S(2)}) %all-to-all-start.3) | async-done | bytes 2097184 | tf_op jit(solution)/shard_map/all_to_all | solution.py:33
  206.3 0.5 multiply_reduce_fusion
  206.9 0.6 convert_element_type.229
  207.4 0.6 copy.201
  208.0 2.2 fusion.6
  210.2 4.1 %copy.202 = bf16[128,16,512]{2,1,0:T(8,128)(2,1)} copy(bf16[128,16,512]{2,0,1:T(8,128)(2,1)} %bitcast.34) | data formatting | bytes 4194304 | tf_op jit(solution)/shard_map/transpose | solution.py:166
  214.3 2.9 dot_general.58
  217.4 7.4 %copy.203 = bf16[2,4,2,512,512]{4,3,2,1,0:T(8,128)(2,1)} copy(bf16[2,4,2,512,512]{4,3,0,1,2:T(8,128)(2,1)} %bitcast.133) | data formatting | bytes 16777216 | tf_op jit(solution)/shard_map/transpose | solution.py:86
  224.7 4.6 %fusion.55 = f32[4,32,512]{2,1,0:T(8,128)S(1)} fusion(bf16[4,32,8192]{2,1,0:T(8,128)(2,1)S(1)} %dot_general.58, bf16[8192,512,1]{1,0,2:T(8,128)(2,1)} %bitcast.130), kind=kOutput, calls=%fused_computation.105 | convolution fusion | flops 1073741824 | bytes 10747904 | tf_op jit(solution)/shard_map/dot_general | solution.py:165
  229.4 1.0 fusion.22
  230.3 0.3 convolution_convert_fusion.1
  230.7 10.4 %all_gather.19 = bf16[2,128,512]{2,1,0:T(8,128)(2,1)S(1)} all-gather(bf16[1,128,512]{2,1,0:T(8,128)(2,1)S(1)} %bitcast.151), channel_id=1, replica_groups=mesh['zh'=2,'y'=4,'c'=2,'zl'=4,'x'=4] {'zh'}, dimensions={0}, use_global_device_ids=true | all-gather | bytes 393216 | tf_op jit(solution)/shard_map/all_gather | solution.py:42
  241.2 12.2 %all_to_all.55 = bf16[8,128,512]{2,1,0:T(8,128)(2,1)S(1)} all-to-all(bf16[8,128,512]{2,1,0:T(8,128)(2,1)S(1)} %bitcast.138), channel_id=1, replica_groups=mesh['zh'=2,'y'=4,'c'=2,'zl'=4,'x'=4] {'y'}, dimensions={0} | all-to-all | bytes 2097152 | tf_op jit(solution)/shard_map/all_to_all | solution.py:33
  253.4 0.2 broadcast_in_dim.140
  253.6 13.7 %all_to_all.56 = bf16[16,128,512]{2,1,0:T(8,128)(2,1)S(1)} all-to-all(bf16[16,128,512]{2,1,0:T(8,128)(2,1)S(1)} %bitcast.136), channel_id=1, replica_groups=mesh['zh'=2,'y'=4,'c'=2,'zl'=4,'x'=4] {'c'}, dimensions={0} | all-to-all | bytes 4194304 | tf_op jit(solution)/shard_map/all_to_all | solution.py:33
  267.3 7.6 %all-to-all-start.4 = ((bf16[16,128,512]{2,1,0:T(8,128)(2,1)}), bf16[16,128,512]{2,1,0:T(8,128)(2,1)}, u32[]{:S(2)}, u32[]{:S(2)}) async-start(bf16[16,128,512]{2,1,0:T(8,128)(2,1)} %fusion.6), calls=%async_computation.4 | async-start | bytes 4194304 | tf_op jit(solution)/shard_map/all_to_all | solution.py:33
  274.9 1.5 copy.205
  276.4 47.4 %all-to-all-done.4 = bf16[16,128,512]{2,1,0:T(8,128)(2,1)} async-done(((bf16[16,128,512]{2,1,0:T(8,128)(2,1)}), bf16[16,128,512]{2,1,0:T(8,128)(2,1)}, u32[]{:S(2)}, u32[]{:S(2)}) %all-to-all-start.4) | async-done | bytes 2097184 | tf_op jit(solution)/shard_map/all_to_all | solution.py:33
  323.8 5.2 %multiply_reduce_fusion.2 = (f32[]{:T(128)}, f32[512,512]{1,0:T(8,128)}) fusion(bf16[2048,512]{1,0:T(8,128)(2,1)} %bitcast.30, bf16[2048,512]{1,0:T(8,128)(2,1)} %bitcast.141), kind=kOutput, calls=%fused_computation.40 | convolution fusion | flops 1074266112 | bytes 5242884 | tf_op jit(solution)/shard_map/dot_general | solution.py:182
  329.0 1.3 compare_select_fusion.2
  330.4 23.3 %all_to_all.57 = f32[256,1,128]{2,1,0:T(1,128)S(1)} all-to-all(f32[256,1,128]{2,1,0:T(1,128)S(1)} %reshape.410), channel_id=1, replica_groups=mesh['zh'=2,'y'=4,'c'=2,'zl'=4,'x'=4] {'zh','y','c','zl','x'}, dimensions={0} | all-to-all | bytes 262144 | tf_op jit(solution)/shard_map/all_to_all | solution.py:33
  353.7 0.6 fusion.53
  355.7 3.4 subtract_convert_fusion
  (82 shorter events, 1.7 us)
Async XLA Ops:
  7.2 60.2 %copy-start = (bf16[4,2,512]{2,1,0:T(2,128)(2,1)S(1)}, bf16[4,2,512]{2,1,0:T(2,128)(2,1)}, u32[]{:S(2)}) copy-start(bf16[4,2,512]{2,1,0:T(2,128)(2,1)} %param.19) | copy-start | bytes 24580
  7.2 50.4 %copy-start.6 = (bf16[4,32,4096]{2,1,0:T(8,128)(2,1)S(1)}, bf16[4,32,4096]{2,1,0:T(8,128)(2,1)}, u32[]{:S(2)}) copy-start(bf16[4,32,4096]{2,1,0:T(8,128)(2,1)} %param.15) | copy-start | bytes 3145732
  7.2 51.6 %copy-start.7 = (bf16[4,256,512]{2,1,0:T(8,128)(2,1)S(1)}, bf16[4,256,512]{2,1,0:T(8,128)(2,1)}, u32[]{:S(2)}) copy-start(bf16[4,256,512]{2,1,0:T(8,128)(2,1)} %param.16) | copy-start | bytes 3145732
  7.2 48.2 %all-gather.9.cloned.1.call-start = ((), (), s32[]{:S(2)}) async-start(), calls=%async_computation.10 | async-start | bytes 1572864 | tf_op jit(solution)/shard_map/all_gather | solution.py:42
  7.9 96.4 %all-gather.5.cloned.1.call-start = ((), (), s32[]{:S(2)}) async-start(), calls=%async_computation.8 | async-start | bytes 5242880 | tf_op jit(solution)/shard_map/all_gather | solution.py:42
  56.5 3.4 copy-start.8
  58.8 1.4 copy-start.15
  58.8 1.5 copy-start.16
  59.9 3.1 copy-start.9
  65.4 2.0 copy-start.2
  74.4 30.0 %all-to-all-start = ((bf16[16,144,256]{2,1,0:T(8,128)(2,1)}), bf16[16,144,256]{2,1,0:T(8,128)(2,1)S(1)}, u32[]{:S(2)}, u32[]{:S(2)}) async-start(bf16[16,144,256]{2,1,0:T(8,128)(2,1)} %fusion.7), calls=%async_computation | async-start | bytes 2359296 | tf_op jit(solution)/shard_map/all_to_all | solution.py:33
  78.5 138.8 %all-gather.7.cloned.1.call-start = ((), (), s32[]{:S(2)}) async-start(), calls=%async_computation.9 | async-start | bytes 12582912 | tf_op jit(solution)/shard_map/all_gather | solution.py:42
  148.1 6.6 %copy-start.10 = (bf16[4,32,512]{2,1,0:T(8,128)(2,1)S(1)}, bf16[4,32,512]{2,1,0:T(8,128)(2,1)}, u32[]{:S(2)}) copy-start(bf16[4,32,512]{2,1,0:T(8,128)(2,1)} %param.23) | copy-start | bytes 393220
  149.3 16.8 %all-to-all-start.2 = ((bf16[4,128,512]{2,1,0:T(8,128)(2,1)}), bf16[4,128,512]{2,1,0:T(8,128)(2,1)S(1)}, u32[]{:S(2)}, u32[]{:S(2)}) async-start(bf16[4,128,512]{2,1,0:T(8,128)(2,1)} %bitcast.20), calls=%async_computation.2 | async-start | bytes 1048576 | tf_op jit(solution)/shard_map/all_to_all | solution.py:33
  181.9 3.9 %copy-start.13 = (f32[8192]{0:T(1024)S(1)}, f32[8192]{0:T(1024)}, u32[]{:S(2)}) copy-start(f32[8192]{0:T(1024)} %param.24) | copy-start | bytes 98308
  181.9 4.0 %copy-start.12 = (bf16[4,8192]{1,0:T(4,128)(2,1)S(1)}, bf16[4,8192]{1,0:T(4,128)(2,1)}, u32[]{:S(2)}) copy-start(bf16[4,8192]{1,0:T(4,128)(2,1)} %param.26) | copy-start | bytes 196612
  181.9 4.1 %copy-start.17 = (s32[4]{0:T(128)S(1)}, s32[4]{0:T(128)}, u32[]{:S(2)}) copy-start(s32[4]{0:T(128)} %param.22) | copy-start | bytes 52
  181.9 4.1 %copy-start.14 = (s32[4,32]{1,0:T(4,128)S(1)}, s32[4,32]{1,0:T(4,128)}, u32[]{:S(2)}) copy-start(s32[4,32]{1,0:T(4,128)} %param.20) | copy-start | bytes 1540
  181.9 24.3 %all-to-all-start.3 = ((bf16[16,128,512]{2,1,0:T(8,128)(2,1)}), bf16[16,128,512]{2,1,0:T(8,128)(2,1)S(1)}, u32[]{:S(2)}, u32[]{:S(2)}) async-start(bf16[16,128,512]{2,1,0:T(8,128)(2,1)} %bitcast.132), calls=%async_computation.3 | async-start | bytes 4194304 | tf_op jit(solution)/shard_map/all_to_all | solution.py:33
  217.3 12.1 %copy-start.11 = (bf16[4,32,512]{2,1,0:T(8,128)(2,1)}, bf16[4,32,512]{2,1,0:T(8,128)(2,1)S(1)}, u32[]{:S(2)}) copy-start(bf16[4,32,512]{2,1,0:T(8,128)(2,1)S(1)} %multiply_convert_fusion) | copy-start | bytes 393220
  267.3 56.5 %all-to-all-start.4 = ((bf16[16,128,512]{2,1,0:T(8,128)(2,1)}), bf16[16,128,512]{2,1,0:T(8,128)(2,1)}, u32[]{:S(2)}, u32[]{:S(2)}) async-start(bf16[16,128,512]{2,1,0:T(8,128)(2,1)} %fusion.6), calls=%async_computation.4 | async-start | bytes 4194304 | tf_op jit(solution)/shard_map/all_to_all | solution.py:33
  323.8 31.9 %copy-start.3 = (bf16[512,512]{1,0:T(8,128)(2,1)S(1)}, bf16[512,512]{1,0:T(8,128)(2,1)}, u32[]{:S(2)}) copy-start(bf16[512,512]{1,0:T(8,128)(2,1)} %param.27) | copy-start | bytes 1572868
  323.8 31.9 %copy-start.4 = (f32[512,512]{1,0:T(8,128)S(1)}, f32[512,512]{1,0:T(8,128)}, u32[]{:S(2)}) copy-start(f32[512,512]{1,0:T(8,128)} %param.28) | copy-start | bytes 3145732
  323.8 31.9 %copy-start.5 = (f32[512,512]{1,0:T(8,128)S(1)}, f32[512,512]{1,0:T(8,128)}, u32[]{:S(2)}) copy-start(f32[512,512]{1,0:T(8,128)} %param.29) | copy-start | bytes 3145732
  355.6 3.4 copy-start.1
Sparse Core Ops, SparseCore 0:
  9.8 45.5 all-gather.8
  57.2 47.0 all-gather.4
  106.1 26.4 all-gather.6

commit v2 on v1

v2 whole, which is shorter than its diff:
```python
import math

import jax
import jax.numpy as jnp
from jax import lax
from jax.experimental import pallas as pl
from jax.experimental.pallas import tpu as pltpu
from jax.sharding import Mesh
from jax.sharding import PartitionSpec as P

KV_HEADS = 4
HEAD = 128
NODES = 32
CACHE = 4096
D = 8192
N_TP = 16
N_REQ = 16

NEG_FILL = -1e30
NORM_EPSILON = 1e-06
BETA_ONE = 0.9
BETA_TWO = 0.95
CORRECT_ONE = 1.0 - 0.9**10
CORRECT_TWO = 1.0 - 0.95**10
LEARN_RATE = 0.001

REQ = ("zh", "y", "c")
TP = ("zl", "x")
F32 = jnp.float32
BF16 = jnp.bfloat16


def exchange(value, axis):
    return lax.all_to_all(value, axis, 0, 0, tiled=True)


def spread(value, axis, count):
    wide = jnp.broadcast_to(value[None], (count, *value.shape))
    return exchange(wide.reshape(count * value.shape[0], *value.shape[1:]), axis)


def turn(count, step):
    return [(i, (i + step) % count) for i in range(count)]


def gather(value, axis):
    return lax.all_gather(value, axis, axis=0, tiled=True)


def dot(left, right, dims, **kwargs):
    return lax.dot_general(left, right, (dims, ((), ())), preferred_element_type=F32, **kwargs)


def same_request(width=128):
    row = lax.broadcasted_iota(jnp.int32, (128, width), 0)
    lane = lax.broadcasted_iota(jnp.int32, (128, width), 1)
    return row, lane


def attend_kernel(rank_ref, len_ref, par_ref, q_ref, ck_ref, cv_ref, tk_ref, tv_ref, out_ref, reach_ref, stat_ref):
    rank = rank_ref[0]
    row, lane = same_request()
    base = (row // NODES) * NODES
    up = jnp.where(par_ref[...] + base == lane, jnp.where(par_ref[...] >= 0, 1.0, 0.0), 0.0)
    reach = (jnp.where(row == lane, 1.0, 0.0) + up).astype(BF16)
    for _ in range((NODES - 1).bit_length()):
        reach = jnp.minimum(dot(reach, reach, ((1,), (0,))), 1.0).astype(BF16)
    reach_ref[...] = reach
    pick = jnp.where(row % NODES == 2 * rank + lane, jnp.where(lane < 2, 1.0, 0.0), 0.0)
    visible = dot(reach, pick.astype(BF16), ((1,), (0,)))
    scale = 1.0 / math.sqrt(HEAD)
    span = ck_ref.shape[1]
    slot = lax.broadcasted_iota(jnp.int32, (256, span), 1) + rank * span
    wide_lane = lax.broadcasted_iota(jnp.int32, (NODES, 128), 1)
    for r in range(q_ref.shape[0]):
        live = slot < len_ref[r]
        seen = visible[r * NODES : (r + 1) * NODES, :8]
        seen = jnp.concatenate([seen] * 8, axis=0) > 0.5
        stats = jnp.zeros((NODES, 128), F32)
        for k in range(KV_HEADS):
            head = slice(k * HEAD, (k + 1) * HEAD)
            query = jnp.concatenate(
                [q_ref[r, :, (k * 8 + g) * HEAD : (k * 8 + g + 1) * HEAD] for g in range(8)], axis=0
            )
            scores = dot(query, ck_ref[r, :, head], ((1,), (1,))) * scale
            tree = dot(query, tk_ref[r, :, head], ((1,), (1,))) * scale
            scores = jnp.where(live, scores, NEG_FILL)
            tree = jnp.where(seen, tree, NEG_FILL)
            top = jnp.maximum(
                jnp.max(scores, axis=1, keepdims=True), jnp.max(tree, axis=1, keepdims=True)
            )
            top = top.astype(BF16).astype(F32)
            probs = jnp.where(live, jnp.exp(scores - top), 0.0).astype(BF16)
            tree = jnp.where(seen, jnp.exp(tree - top), 0.0).astype(BF16)
            total = jnp.sum(probs.astype(F32), axis=1, keepdims=True) + jnp.sum(
                tree.astype(F32), axis=1, keepdims=True
            )
            high = total.astype(BF16).astype(F32)
            low = total - high
            value = dot(probs, cv_ref[r, :, head], ((1,), (0,))) + dot(
                tree, tv_ref[r, :, head], ((1,), (0,))
            )
            value = value.astype(BF16)
            for g in range(8):
                h = k * 8 + g
                part = slice(g * NODES, (g + 1) * NODES)
                out_ref[h // 2, r * NODES : (r + 1) * NODES, (h % 2) * HEAD : (h % 2 + 1) * HEAD] = value[part]
                for at, column in enumerate((top, high, low)):
                    stats = jnp.where(wide_lane == h * 4 + at, column[part], stats)
        stat_ref[r * NODES : (r + 1) * NODES, :] = stats
    turned = jnp.transpose(stat_ref[...])
    empty = jnp.zeros((8, 128), F32)
    blank = jnp.zeros((16, 128), BF16)
    for owner in range(N_TP):
        block = jnp.concatenate([turned[owner * 8 : (owner + 1) * 8], empty], axis=0)
        out_ref[owner, 128:144, 0:128] = block.astype(BF16)
        out_ref[owner, 128:144, 128:256] = blank


def project_kernel(parcel_ref, weight_ref, out_ref, att_ref):
    @pl.when(pl.program_id(0) == 0)
    def join():
        stats = jnp.concatenate(
            [parcel_ref[src, 128:144, 0:128].astype(F32)[0:8] for src in range(N_TP)], axis=0
        )
        total = pltpu.roll(stats, 127, 0) + pltpu.roll(stats, 126, 0)
        stats = stats.reshape(N_TP, 8, 128)
        factor = jnp.exp(stats - jnp.max(stats, axis=0, keepdims=True))
        share = factor / jnp.sum(factor * total.reshape(N_TP, 8, 128), axis=0, keepdims=True)
        share = jnp.transpose(share.reshape(128, 128))
        for side in range(2):
            cols = slice(side * HEAD, (side + 1) * HEAD)
            joined = jnp.zeros((128, HEAD), F32)
            for src in range(N_TP):
                at = src * 8 + side * 4
                joined = joined + parcel_ref[src, 0:128, cols].astype(F32) * share[:, at : at + 1]
            att_ref[:, cols] = joined.astype(BF16)

    out_ref[0, 0] = dot(att_ref[...], weight_ref[...], ((1,), (0,))).astype(BF16)


def predict_kernel(
    far_ref, mixed_ref, gain_ref, own_gain_ref, prev_ref, par_ref, scale_w_ref, weight_ref,
    table_ref, own_ref, err_ref, loss_ref, scale_ref, ahead_ref,
):
    p = pl.program_id(0)

    @pl.when(p == 0)
    def start():
        square = jnp.zeros((128, 1), F32)
        for zl in range(4):
            for x in range(4):
                part = far_ref[x, zl].astype(F32)
                square = square + jnp.sum(part * part, axis=1, keepdims=True)
        scale = lax.rsqrt(square / D + NORM_EPSILON)
        scale_ref[...] = jnp.broadcast_to(scale, (128, 128))
        own_ref[...] = (mixed_ref[...] * scale * own_gain_ref[...]).astype(BF16)
        ahead_ref[...] = jnp.zeros_like(ahead_ref)

    block = far_ref[lax.rem(p, 4), p // 4].astype(F32) * scale_ref[:, 0:1] * gain_ref[0]
    node = lax.broadcasted_iota(jnp.int32, (NODES, 1), 0)
    prev = prev_ref[...].astype(F32)
    block = jnp.concatenate(
        [
            jnp.where(node == NODES - 1, prev[r : r + 1], block[r * NODES : (r + 1) * NODES])
            for r in range(4)
        ],
        axis=0,
    ).astype(BF16)
    table_ref[0] = block
    ahead_ref[...] += dot(block, weight_ref[0], ((1,), (0,)))

    @pl.when(p == N_TP - 1)
    def finish():
        row, lane = same_request()
        parent = jnp.where(par_ref[...] < 0, NODES - 1, par_ref[...])
        pick = jnp.where(parent + (row // NODES) * NODES == lane, 1.0, 0.0)
        predicted = dot(pick, ahead_ref[...], ((1,), (0,)), precision=lax.Precision.HIGHEST)
        error = predicted - own_ref[...].astype(F32)
        weighted = scale_w_ref[...] * error
        err_ref[...] = dot(pick, weighted, ((0,), (0,)), precision=lax.Precision.HIGHEST).astype(BF16)
        loss = jnp.sum(jnp.sum(weighted * error, axis=0, keepdims=True), axis=1, keepdims=True)
        loss_ref[...] = jnp.broadcast_to(loss, (8, 128))


def differentiate_kernel(source_ref, column_ref, near_ref, other_ref, loss_ref, grad_ref, pair_ref):
    for part in range(4):
        left = jnp.concatenate([column_ref[source_ref[part * 4 + i]] for i in range(4)], axis=0)
        err_ref = near_ref if part < 2 else other_ref
        right = jnp.concatenate(
            [err_ref[(part % 2) * 2 + i // 2, i % 2] for i in range(4)], axis=0
        )
        term = dot(left, right, ((0,), (0,)))
        if part == 0:
            grad_ref[...] = term
        else:
            grad_ref[...] += term
    value = grad_ref[...]
    square = jnp.sum(jnp.sum(value * value, axis=0, keepdims=True), axis=1, keepdims=True)
    lane = lax.broadcasted_iota(jnp.int32, (8, 128), 1)
    pair = jnp.where(lane == 0, square, jnp.where(lane == 1, loss_ref[...], 0.0))
    for i in range(32):
        pair_ref[i * 8 : (i + 1) * 8] = pair


def in_vmem():
    return pl.BlockSpec(memory_space=pltpu.VMEM)


def in_smem():
    return pl.BlockSpec(memory_space=pltpu.SMEM)


def attend(rank, lengths, parent_column, queries, cache_keys, cache_values, tree_keys, tree_values):
    return pl.pallas_call(
        attend_kernel,
        out_shape=(
            jax.ShapeDtypeStruct((N_TP, 144, 2 * HEAD), BF16),
            jax.ShapeDtypeStruct((128, 128), BF16),
        ),
        in_specs=[in_smem(), in_smem()] + [in_vmem()] * 6,
        out_specs=(in_vmem(), in_vmem()),
        scratch_shapes=[pltpu.VMEM((128, 128), F32)],
        cost_estimate=pl.CostEstimate(
            flops=2 * 2 * 16 * 256 * 256 * 128, bytes_accessed=4 << 20, transcendentals=16 * 256 * 256
        ),
        name="attend",
    )(rank, lengths, parent_column, queries, cache_keys, cache_values, tree_keys, tree_values)


def project(parcel, out_weight):
    return pl.pallas_call(
        project_kernel,
        grid=(N_TP,),
        out_shape=jax.ShapeDtypeStruct((4, 4, 128, 512), BF16),
        in_specs=[
            pl.BlockSpec((N_TP, 144, 2 * HEAD), lambda p: (0, 0, 0)),
            pl.BlockSpec((2 * HEAD, 512), lambda p: (0, p)),
        ],
        out_specs=pl.BlockSpec((1, 1, 128, 512), lambda p: (lax.rem(p, 4), p // 4, 0, 0)),
        scratch_shapes=[pltpu.VMEM((128, 2 * HEAD), BF16)],
        cost_estimate=pl.CostEstimate(
            flops=2 * 128 * 256 * 8192, bytes_accessed=7 << 20, transcendentals=0
        ),
        name="project",
    )(parcel, out_weight)


def differentiate(source, columns, near_err, other_err, loss):
    return pl.pallas_call(
        differentiate_kernel,
        out_shape=(
            jax.ShapeDtypeStruct((512, 512), F32),
            jax.ShapeDtypeStruct((N_REQ * N_TP, 128), F32),
        ),
        in_specs=[in_smem()] + [in_vmem()] * 4,
        out_specs=(in_vmem(), in_vmem()),
        cost_estimate=pl.CostEstimate(
            flops=2 * 2048 * 512 * 512, bytes_accessed=5 << 20, transcendentals=0
        ),
        name="differentiate",
    )(source, columns, near_err, other_err, loss)


def predict(far, mixed, gain, own_gain, prev, parent_column, weights, all_weight):
    return pl.pallas_call(
        predict_kernel,
        grid=(N_TP,),
        out_shape=(
            jax.ShapeDtypeStruct((N_TP, 128, 512), BF16),
            jax.ShapeDtypeStruct((128, 512), BF16),
            jax.ShapeDtypeStruct((128, 512), BF16),
            jax.ShapeDtypeStruct((8, 128), F32),
        ),
        in_specs=[
            pl.BlockSpec((4, 4, 128, 512), lambda p: (0, 0, 0, 0)),
            pl.BlockSpec((128, 512), lambda p: (0, 0)),
            pl.BlockSpec((1, 1, 512), lambda p: (p, 0, 0)),
            pl.BlockSpec((1, 512), lambda p: (0, 0)),
            pl.BlockSpec((4, 512), lambda p: (0, p)),
            pl.BlockSpec((128, 1), lambda p: (0, 0)),
            pl.BlockSpec((128, 1), lambda p: (0, 0)),
            pl.BlockSpec(
                (1, 512, 512),
                lambda p: (lax.rem(p, 2) * 8 + lax.rem(p // 2, 4) * 2 + p // 8, 0, 0),
            ),
        ],
        out_specs=(
            pl.BlockSpec((1, 128, 512), lambda p: (p, 0, 0)),
            pl.BlockSpec((128, 512), lambda p: (0, 0)),
            pl.BlockSpec((128, 512), lambda p: (0, 0)),
            pl.BlockSpec((8, 128), lambda p: (0, 0)),
        ),
        scratch_shapes=[pltpu.VMEM((128, 128), F32), pltpu.VMEM((128, 512), F32)],
        cost_estimate=pl.CostEstimate(
            flops=2 * 128 * 8192 * 512, bytes_accessed=13 << 20, transcendentals=0
        ),
        name="predict",
    )(far, mixed, gain, own_gain, prev, parent_column, weights, all_weight)


def body(
    queries,
    cache_keys,
    cache_values,
    tree_keys,
    tree_values,
    parents,
    lengths,
    accepted_leaf,
    residual,
    norm_gain,
    out_weight,
    prev_feature,
    draft_weight,
    first_moment,
    second_moment,
):
    requests = queries.shape[0]
    rows = requests * NODES
    tp_rank = lax.axis_index(TP)
    block = residual.shape[2]
    parent_column = parents.reshape(rows, 1)

    wide_weight = gather(draft_weight[None], "zh")

    pad = ((0, 0), (0, 6), (0, 0))
    parcel, reach = attend(
        tp_rank.reshape(1),
        lengths,
        parent_column,
        queries,
        cache_keys,
        cache_values,
        jnp.pad(tree_keys, pad),
        jnp.pad(tree_values, pad),
    )
    parcel = exchange(parcel, TP)
    parcel, wide_weight = lax.optimization_barrier((parcel, wide_weight))
    wide_weight = gather(wide_weight, "y")

    leaf = jnp.arange(requests, dtype=jnp.int32) * NODES + accepted_leaf
    leaf_hot = (leaf[:, None] == jnp.arange(rows, dtype=jnp.int32)[None, :]).astype(BF16)
    accepted = jnp.dot(jnp.sum(leaf_hot, axis=0, keepdims=True), reach, preferred_element_type=F32)
    fill_share = jnp.repeat(0.5 + lengths.astype(F32) / CACHE, NODES)
    weights = ((1.0 + 3.0 * accepted.reshape(rows)) * fill_share).reshape(rows, 1)
    own_gain = lax.dynamic_slice_in_dim(norm_gain, tp_rank * block, block, 0).reshape(1, block)

    partial_value = project(parcel, out_weight)
    along_x = exchange(partial_value, "x")
    along_x = jnp.sum(along_x.astype(F32), axis=0).astype(BF16)
    along_x, wide_weight = lax.optimization_barrier((along_x, wide_weight))
    all_weight = gather(wide_weight, "c")
    along_z = exchange(along_x, "zl")
    projected = jnp.sum(along_z.astype(F32), axis=0)
    mixed = residual.reshape(rows, block).astype(F32) + projected

    near = gather(mixed.astype(BF16)[None], "zl")
    far = spread(near, "x", 4).reshape(4, 4, rows, block)
    table, own_features, scaled_err, loss = predict(
        far,
        mixed,
        norm_gain.reshape(N_TP, 1, block),
        own_gain,
        prev_feature,
        parent_column,
        weights,
        all_weight,
    )
    columns = exchange(table, REQ)
    near_err = jnp.stack([scaled_err, lax.ppermute(scaled_err, "zh", turn(2, 1))])
    near_err = jnp.stack(
        [near_err] + [lax.ppermute(near_err, "y", turn(4, step)) for step in (1, 2, 3)]
    )
    other_err = lax.ppermute(near_err, "c", turn(2, 1))
    zh, y, c = lax.axis_index("zh"), lax.axis_index("y"), lax.axis_index("c")
    piece = jnp.arange(N_REQ, dtype=jnp.int32)
    source = (
        ((zh + piece % 2) % 2) * 8 + ((y + 4 - (piece // 2) % 4) % 4) * 2 + (c + piece // 8) % 2
    )
    gradient, pair = differentiate(source, columns, near_err, other_err, loss)
    pair = jnp.sum(exchange(pair, REQ + TP), axis=0)
    square_total, error_total = pair[0], pair[1]
    draft_loss = 0.5 * error_total / (rows * N_REQ * D)
    grad_norm = jnp.sqrt(square_total) + 1e-06
    clip_factor = jnp.minimum(1.0, D / grad_norm)
    clipped = gradient * clip_factor
    new_first = BETA_ONE * first_moment + (1.0 - BETA_ONE) * clipped
    new_second = BETA_TWO * second_moment + (1.0 - BETA_TWO) * clipped * clipped
    direction = new_first / CORRECT_ONE / (jnp.sqrt(new_second / CORRECT_TWO) + 1e-08)
    new_weight = (draft_weight.astype(F32) - LEARN_RATE * direction).astype(BF16)
    return (
        own_features.reshape(requests, NODES, block),
        new_weight,
        new_first,
        new_second,
        draft_loss,
    )


def solution(mesh):
    fine = Mesh(mesh.devices.reshape(2, 4, 2, 4, 4), REQ + TP)
    placed = (
        P(REQ, None, None),
        P(REQ, TP, None),
        P(REQ, TP, None),
        P(REQ, TP, None),
        P(REQ, TP, None),
        P(REQ, None),
        P(REQ),
        P(REQ),
        P(REQ, None, TP),
        P(),
        P(TP, None),
        P(REQ, None),
        P(REQ, TP),
        P(REQ, TP),
        P(REQ, TP),
    )

    return jax.shard_map(
        body,
        mesh=fine,
        in_specs=placed,
        out_specs=(P(REQ, None, TP), P(REQ, TP), P(REQ, TP), P(REQ, TP), P()),
        check_vma=False,
    )
```

time: 368 us -> 335 us (0.910)
  Pallas kernels: 0 us -> 40.8 us
  blocking collectives: 101 us -> 68.9 us
  starting transfers between devices: 21 us -> 52.4 us
  local copies, waits for them, and re-layouts: 37 us -> 12 us
  matrix products: 23 us -> 0.13 us
  waiting for transfers between devices: 153 us -> 136 us
  other arithmetic: 14.8 us -> 7.29 us
    ppermute x0 -> x5, waiting for transfers between devices: none -> 52.4 us  [the longest x1 40.8 us: body(): lax.ppermute(scaled_err, 'zh', turn(2, 1))]
    all_to_all x4, waiting for transfers between devices: 78.8 us -> 32.4 us  [exchange(): return lax.all_to_all(value, axis, 0, 0, tiled=True)]
    pallas_call x0 -> x4, Pallas kernels: none -> 40.8 us  [the longest x1 15.1 us: predict(): pl.pallas_call(predict_kernel, grid=(N_TP,), out_shape=(jax.ShapeDtypeStr...]
    dot_general x15 -> x1, matrix products: 23 us -> 0.13 us  [body(): jnp.dot(jnp.sum(leaf_hot, axis=0, keepdims=True), reach, preferred_elemen...]
    all_gather x3, waiting for transfers between devices: 73.2 us -> 50.5 us  [gather(): return lax.all_gather(value, axis, axis=0, tiled=True)]
    ppermute x0 -> x5, starting transfers between devices: none -> 21.3 us  [the longest x3 15.4 us: body(): lax.ppermute(near_err, 'y', turn(4, step))]
    all_to_all x4 -> x2, blocking collectives: 76.9 us -> 56.1 us  [exchange(): return lax.all_to_all(value, axis, 0, 0, tiled=True)]
    transpose x5 -> x0, local copies, waits for them, and re-layouts: 13.4 us -> none  [the longest x1 7.37 us: body(): jnp.transpose(all_weight.reshape(2, 4, 2, *draft_weight.shape), (2, 1, 0,...]
  transfers between devices with their start and end apart: 7 -> 12, of which waited for: 5 -> 8; matrix products, arithmetic and copies ran while one was open for 14% -> 2% of each run, Pallas kernels for 0% -> 4%
where the time goes in v2:
time: 335 us; the launch traced here: 334 us
  waiting for transfers between devices  136 us (41%)
  blocking collectives  68.9 us (21%)
  starting transfers between devices  52.4 us (16%)
  Pallas kernels  40.8 us (12%)
  between operations  16.3 us (5%)
  local copies, waits for them, and re-layouts  12 us (4%)
  other arithmetic  7.29 us (2%)
    all_to_all x2, blocking collectives, exchange(): return lax.all_to_all(value, axis, 0, 0, tiled=True)  56.1 us
    all_gather x3, waiting for transfers between devices, gather(): return lax.all_gather(value, axis, axis=0, tiled=True)  50.5 us
    ppermute x1, waiting for transfers between devices, body(): lax.ppermute(scaled_err, 'zh', turn(2, 1))  40.8 us
    all_to_all x4, waiting for transfers between devices, exchange(): return lax.all_to_all(value, axis, 0, 0, tiled=True)  32.4 us
    all_to_all x4, starting transfers between devices, exchange(): return lax.all_to_all(value, axis, 0, 0, tiled=True)  31 us
    ppermute x3, starting transfers between devices, body(): lax.ppermute(near_err, 'y', turn(4, step))  15.4 us
    pallas_call x1, Pallas kernels, predict(): pl.pallas_call(predict_kernel, grid=(N_TP,), out_shape=(jax.ShapeDtypeStr...  15.1 us
    all_gather x1, blocking collectives, gather(): return lax.all_gather(value, axis, axis=0, tiled=True)  12.8 us
  transfers between devices with their start and end apart: 12, of which 8 were waited for; matrix products, arithmetic and copies ran while one was open for 2% of the time, Pallas kernels for 4%

profile of v2, /device:TPU:1, one launch (start us, length us, event | category | flops | bytes accessed | tf_op | source)
XLA Modules:
  0.0 334.0 jit_solution(16753021744849839630)
XLA Ops:
  7.2 1.3 pad.7.tk_ref
  8.5 1.3 pad.8.tv_ref
  9.8 1.4 reshape.98.par_ref
  11.2 9.1 %attend.1 = (bf16[16,144,256]{2,1,0:T(8,128)(2,1)}, bf16[128,128]{1,0:T(8,128)(2,1)}) custom-call(s32[1]{0:T(128)} %bitcast.1.rank_ref, s32[4]{0:T(128)} %len_ref.1, s32[128,1]{1,0:T(8,128)} %reshape.98.par_ref, bf16[4,32,4096]{2,1,0:T(8,128)(2,1)} %q_ref.1, bf16[4,256,512]{2,1,0:T(8,128)(2,1)} %ck_ref.1, bf16[4,256,512]{2,1,0:T(8,128)(2,1)} %cv_ref.1, ...), custom_call_target="tpu_custom_call" | custom-call | flops 536870912 | bytes 4194304 | tf_op jit(solution)/shard_map/attend/pallas_call | solution.py:215
  20.3 9.0 %all-to-all-start = ((bf16[16,144,256]{2,1,0:T(8,128)(2,1)}), bf16[16,144,256]{2,1,0:T(8,128)(2,1)S(1)}, u32[]{:S(2)}, u32[]{:S(2)}) async-start(bf16[16,144,256]{2,1,0:T(8,128)(2,1)} %get-tuple-element.17), calls=%async_computation | async-start | bytes 2359296 | tf_op jit(solution)/shard_map/all_to_all | solution.py:34
  29.3 0.0 all-gather.9.cloned.1.call-start
  29.4 0.7 all-gather.9.cloned.1.call-update
  30.0 0.0 all-gather.5.cloned.1.call-start
  30.1 38.7 %all-gather.9.cloned.1.call-done = bf16[1024,512]{1,0:T(8,128)(2,1)} async-done(((bf16[512,512]{1,0:T(8,128)(2,1)}), bf16[1024,512]{1,0:T(8,128)(2,1)}) %all-gather.9.cloned.1.call-update) | async-done | bytes 1048592 | tf_op jit(solution)/shard_map/all_gather | solution.py:47
  68.8 0.0 all-to-all-done.parcel_ref
  68.8 0.0 copy-start.2
  68.8 0.0 all-gather.5.cloned.1.call-update
  68.8 0.0 all-gather.7.cloned.1.call-start
  68.8 1.0 copy-done.2
  69.8 12.2 %project.1 = bf16[4,4,128,512]{3,2,1,0:T(8,128)(2,1)} custom-call(bf16[16,144,256]{2,1,0:T(8,128)(2,1)} %copy-done.2, bf16[256,8192]{1,0:T(8,128)(2,1)} %weight_ref.1), custom_call_target="tpu_custom_call" | custom-call | flops 536870912 | bytes 7340032 | tf_op jit(solution)/shard_map/project/pallas_call | solution.py:232
  82.0 36.2 %all_to_all.34 = bf16[4,4,128,512]{3,2,1,0:T(8,128)(2,1)S(1)} all-to-all(bf16[4,4,128,512]{3,2,1,0:T(8,128)(2,1)} %project.1), channel_id=1, replica_groups=mesh['zh'=2,'y'=4,'c'=2,'zl'=4,'x'=4] {'x'}, dimensions={0} | all-to-all | bytes 4194304 | tf_op jit(solution)/shard_map/all_to_all | solution.py:34
  118.2 1.3 reduce_sum.44
  119.4 11.8 %all-gather.5.cloned.1.call-done = bf16[8,512,512]{2,1,0:T(8,128)(2,1)} async-done(((bf16[2,512,512]{2,1,0:T(8,128)(2,1)}), bf16[8,512,512]{2,1,0:T(8,128)(2,1)}) %all-gather.5.cloned.1.call-update) | async-done | bytes 4194320 | tf_op jit(solution)/shard_map/all_gather | solution.py:47
  131.3 0.0 copy-start.4
  131.3 0.0 all-gather.7.cloned.1.call-update
  131.3 4.7 %all-to-all-start.2 = ((bf16[4,128,512]{2,1,0:T(8,128)(2,1)}), bf16[4,128,512]{2,1,0:T(8,128)(2,1)S(1)}, u32[]{:S(2)}, u32[]{:S(2)}) async-start(bf16[4,128,512]{2,1,0:T(8,128)(2,1)} %reduce_sum.44), calls=%async_computation.2 | async-start | bytes 1048576 | tf_op jit(solution)/shard_map/all_to_all | solution.py:34
  136.0 0.0 copy-done.4
  136.0 14.0 %all-to-all-done.2 = bf16[4,128,512]{2,1,0:T(8,128)(2,1)S(1)} async-done(((bf16[4,128,512]{2,1,0:T(8,128)(2,1)}), bf16[4,128,512]{2,1,0:T(8,128)(2,1)S(1)}, u32[]{:S(2)}, u32[]{:S(2)}) %all-to-all-start.2) | async-done | bytes 524320 | tf_op jit(solution)/shard_map/all_to_all | solution.py:34
  150.0 0.1 convert_reduce_fusion
  150.1 12.8 %all_gather.14 = bf16[4,128,512]{2,1,0:T(8,128)(2,1)S(1)} all-gather(bf16[1,128,512]{2,1,0:T(8,128)(2,1)S(1)} %fusion.5), channel_id=1, replica_groups=mesh['zh'=2,'y'=4,'c'=2,'zl'=4,'x'=4] {'zl'}, dimensions={0}, use_global_device_ids=true | all-gather | bytes 655360 | tf_op jit(solution)/shard_map/all_gather | solution.py:47
  162.9 1.5 broadcast_in_dim.7
  164.4 4.1 %all-to-all-start.3 = ((bf16[16,128,512]{2,1,0:T(8,128)(2,1)}), bf16[16,128,512]{2,1,0:T(8,128)(2,1)S(1)}, u32[]{:S(2)}, u32[]{:S(2)}) async-start(bf16[16,128,512]{2,1,0:T(8,128)(2,1)} %bitcast.4), calls=%async_computation.3 | async-start | bytes 4194304 | tf_op jit(solution)/shard_map/all_to_all | solution.py:34
  168.5 0.0 copy-done.6
  168.6 0.1 broadcast_in_dim.8
  168.6 0.1 reshape.91
  168.7 0.0 copy-done.8
  168.7 0.1 fusion.7
  168.8 0.0 copy-done.7
  168.8 0.1 fusion.3
  168.9 0.7 copy.29.scale_w_ref
  169.7 1.4 dynamic_slice.3
  171.0 0.7 bitcast_add_fusion.mixed_ref
  171.8 18.4 %all-to-all-done.3 = bf16[16,128,512]{2,1,0:T(8,128)(2,1)S(1)} async-done(((bf16[16,128,512]{2,1,0:T(8,128)(2,1)}), bf16[16,128,512]{2,1,0:T(8,128)(2,1)S(1)}, u32[]{:S(2)}, u32[]{:S(2)}) %all-to-all-start.3) | async-done | bytes 2097184 | tf_op jit(solution)/shard_map/all_to_all | solution.py:34
  190.2 1.3 copy-done.1
  191.5 15.1 %predict.1 = (bf16[16,128,512]{2,1,0:T(8,128)(2,1)}, bf16[128,512]{1,0:T(8,128)(2,1)}, bf16[128,512]{1,0:T(8,128)(2,1)}, f32[8,128]{1,0:T(8,128)}) custom-call(bf16[4,4,128,512]{3,2,1,0:T(8,128)(2,1)} %bitcast.44, f32[128,512]{1,0:T(8,128)} %bitcast_add_fusion.mixed_ref, f32[16,1,512]{2,1,0:T(1,128)} %bitcast.53, f32[1,512]{1,0:T(1,128)} %bitcast.54, ...), custom_call_target="tpu_custom_call" | custom-call | flops 1073741824 | bytes 13631488 | tf_op jit(solution)/shard_map/predict/pallas_call | solution.py:266
  206.6 0.0 copy-start.5
  206.6 13.3 %all-to-all-start.4 = ((bf16[16,128,512]{2,1,0:T(8,128)(2,1)}), bf16[16,128,512]{2,1,0:T(8,128)(2,1)S(1)}, u32[]{:S(2)}, u32[]{:S(2)}) async-start(bf16[16,128,512]{2,1,0:T(8,128)(2,1)} %get-tuple-element.24), calls=%async_computation.4 | async-start | bytes 4194304 | tf_op jit(solution)/shard_map/all_to_all | solution.py:34
  219.9 0.0 copy-done.5
  219.9 5.3 %collective-permute-start = (bf16[128,512]{1,0:T(8,128)(2,1)S(1)}, bf16[128,512]{1,0:T(8,128)(2,1)S(1)}, u32[]{:S(2)}, u32[]{:S(2)}) collective-permute-start(bf16[128,512]{1,0:T(8,128)(2,1)S(1)} %copy-done.5), channel_id=1, source_target_pairs={{0,128},{128,0},{1,129},{129,1},{2,130},{130,2},{3,131},{131,3},{4... | collective-permute-start | bytes 393224 | tf_op jit(solution)/shard_map/ppermute | solution.py:371
  225.2 40.8 %collective-permute-done = bf16[128,512]{1,0:T(8,128)(2,1)S(1)} collective-permute-done((bf16[128,512]{1,0:T(8,128)(2,1)S(1)}, bf16[128,512]{1,0:T(8,128)(2,1)S(1)}, u32[]{:S(2)}, u32[]{:S(2)}) %collective-permute-start) | collective-permute-done | bytes 131104 | tf_op jit(solution)/shard_map/ppermute | solution.py:371
  266.0 12.7 %collective-permute-start.2 = (bf16[2,128,512]{2,1,0:T(8,128)(2,1)S(1)}, bf16[2,128,512]{2,1,0:T(8,128)(2,1)S(1)}, u32[]{:S(2)}, u32[]{:S(2)}) collective-permute-start(bf16[2,128,512]{2,1,0:T(8,128)(2,1)S(1)} %get-tuple-element.33), channel_id=1, source_target_pairs={{0,64},{32,96},{64,0},{96,32},{1,65},{33,97},{65,1},{97,33},{2,66}... | collective-permute-start | bytes 786440 | tf_op jit(solution)/shard_map/ppermute | solution.py:373
  278.7 0.0 collective-permute-start.1
  278.7 2.7 collective-permute-start.3
  281.4 3.1 collective-permute-done.2
  284.5 6.6 %collective-permute-done.1 = bf16[2,128,512]{2,1,0:T(8,128)(2,1)S(1)} collective-permute-done((bf16[2,128,512]{2,1,0:T(8,128)(2,1)S(1)}, bf16[2,128,512]{2,1,0:T(8,128)(2,1)S(1)}, u32[]{:S(2)}, u32[]{:S(2)}) %collective-permute-start.1) | collective-permute-done | bytes 262176 | tf_op jit(solution)/shard_map/ppermute | solution.py:373
  291.1 0.0 collective-permute-done.3
  291.1 0.1 pad_maximum_fusion.near_ref
  291.2 0.0 copy-start.3
  291.2 0.6 collective-permute-start.4
  291.8 0.5 fusion.8.source_ref
  292.4 1.9 collective-permute-done.4.other_ref
  294.2 0.0 all-to-all-done.4.column_ref
  294.3 0.0 copy-done.3
  294.3 1.3 copy-done
  295.6 4.5 %differentiate.1 = (f32[512,512]{1,0:T(8,128)}, f32[256,128]{1,0:T(8,128)}) custom-call(s32[16]{0:T(128)} %fusion.8.source_ref, bf16[16,128,512]{2,1,0:T(8,128)(2,1)} %copy-done, bf16[4,2,128,512]{3,2,1,0:T(8,128)(2,1)} %copy-done.3, bf16[4,2,128,512]{3,2,1,0:T(8,128)(2,1)} %collective-permute-done.4.other_ref, f32[8,128]{1,0:T(8,128)} %get-tuple-element.26.loss_ref), custom_call_target="tpu_custom_call" | custom-call | flops 1073741824 | bytes 5242880 | tf_op jit(solution)/shard_map/differentiate/pallas_call | solution.py:250
  300.0 19.9 %all_to_all.35 = f32[256,1,128]{2,1,0:T(1,128)S(1)} all-to-all(f32[256,1,128]{2,1,0:T(1,128)} %bitcast.50), channel_id=1, replica_groups=mesh['zh'=2,'y'=4,'c'=2,'zl'=4,'x'=4] {'zh','y','c','zl','x'}, dimensions={0} | all-to-all | bytes 262144 | tf_op jit(solution)/shard_map/all_to_all | solution.py:34
  319.9 0.3 reduce_sum.48
  320.2 0.6 fusion.22
  322.2 4.1 %subtract_convert_fusion = (bf16[512,512]{1,0:T(8,128)(2,1)}, f32[512,512]{1,0:T(8,128)}, f32[512,512]{1,0:T(8,128)}) fusion(bf16[512,512]{1,0:T(8,128)(2,1)} %param.27, f32[512,512]{1,0:T(8,128)} %get-tuple-element.27, f32[]{:T(128)} %bitcast.21, f32[512,512]{1,0:T(8,128)} %param.28, f32[512,512]{1,0:T(8,128)} %param.29), kind=kLoop, calls=%fused_computation.8 | loop fusion | flops 4194304 | bytes 6291460 | tf_op jit(solution)/shard_map/convert_element_type | solution.py:391
  (11 shorter events, 0.1 us)
Async XLA Ops:
  20.3 48.5 %all-to-all-start = ((bf16[16,144,256]{2,1,0:T(8,128)(2,1)}), bf16[16,144,256]{2,1,0:T(8,128)(2,1)S(1)}, u32[]{:S(2)}, u32[]{:S(2)}) async-start(bf16[16,144,256]{2,1,0:T(8,128)(2,1)} %get-tuple-element.17), calls=%async_computation | async-start | bytes 2359296 | tf_op jit(solution)/shard_map/all_to_all | solution.py:34
  29.3 39.5 %all-gather.9.cloned.1.call-start = ((), (), s32[]{:S(2)}) async-start(), calls=%async_computation.8 | async-start | bytes 1572864 | tf_op jit(solution)/shard_map/all_gather | solution.py:47
  30.0 101.2 %all-gather.5.cloned.1.call-start = ((), (), s32[]{:S(2)}) async-start(), calls=%async_computation.6 | async-start | bytes 5242880 | tf_op jit(solution)/shard_map/all_gather | solution.py:47
  68.8 1.0 copy-start.2
  68.8 121.3 %all-gather.7.cloned.1.call-start = ((), (), s32[]{:S(2)}) async-start(), calls=%async_computation.7 | async-start | bytes 12582912 | tf_op jit(solution)/shard_map/all_gather | solution.py:47
  131.3 4.7 %copy-start.4 = (bf16[4,32,512]{2,1,0:T(8,128)(2,1)S(1)}, bf16[4,32,512]{2,1,0:T(8,128)(2,1)}, u32[]{:S(2)}) copy-start(bf16[4,32,512]{2,1,0:T(8,128)(2,1)} %param.23) | copy-start | bytes 393220
  131.3 18.7 %all-to-all-start.2 = ((bf16[4,128,512]{2,1,0:T(8,128)(2,1)}), bf16[4,128,512]{2,1,0:T(8,128)(2,1)S(1)}, u32[]{:S(2)}, u32[]{:S(2)}) async-start(bf16[4,128,512]{2,1,0:T(8,128)(2,1)} %reduce_sum.44), calls=%async_computation.2 | async-start | bytes 1048576 | tf_op jit(solution)/shard_map/all_to_all | solution.py:34
  164.4 4.1 %copy-start.6 = (s32[4]{0:T(128)S(1)}, s32[4]{0:T(128)}, u32[]{:S(2)}) copy-start(s32[4]{0:T(128)} %len_ref.1) | copy-start | bytes 52
  164.4 4.3 %copy-start.8 = (s32[4]{0:T(128)S(1)}, s32[4]{0:T(128)}, u32[]{:S(2)}) copy-start(s32[4]{0:T(128)} %param.22) | copy-start | bytes 52
  164.4 4.4 %copy-start.7 = (bf16[128,128]{1,0:T(8,128)(2,1)S(1)}, bf16[128,128]{1,0:T(8,128)(2,1)}, u32[]{:S(2)}) copy-start(bf16[128,128]{1,0:T(8,128)(2,1)} %get-tuple-element.21) | copy-start | bytes 98308
  164.4 25.7 %all-to-all-start.3 = ((bf16[16,128,512]{2,1,0:T(8,128)(2,1)}), bf16[16,128,512]{2,1,0:T(8,128)(2,1)S(1)}, u32[]{:S(2)}, u32[]{:S(2)}) async-start(bf16[16,128,512]{2,1,0:T(8,128)(2,1)} %bitcast.4), calls=%async_computation.3 | async-start | bytes 4194304 | tf_op jit(solution)/shard_map/all_to_all | solution.py:34
  190.1 1.3 copy-start.1
  206.6 13.3 %copy-start.5 = (bf16[128,512]{1,0:T(8,128)(2,1)S(1)}, bf16[128,512]{1,0:T(8,128)(2,1)}, u32[]{:S(2)}) copy-start(bf16[128,512]{1,0:T(8,128)(2,1)} %get-tuple-element.25) | copy-start | bytes 393220
  206.6 87.7 %all-to-all-start.4 = ((bf16[16,128,512]{2,1,0:T(8,128)(2,1)}), bf16[16,128,512]{2,1,0:T(8,128)(2,1)S(1)}, u32[]{:S(2)}, u32[]{:S(2)}) async-start(bf16[16,128,512]{2,1,0:T(8,128)(2,1)} %get-tuple-element.24), calls=%async_computation.4 | async-start | bytes 4194304 | tf_op jit(solution)/shard_map/all_to_all | solution.py:34
  219.9 46.1 %collective-permute-start = (bf16[128,512]{1,0:T(8,128)(2,1)S(1)}, bf16[128,512]{1,0:T(8,128)(2,1)S(1)}, u32[]{:S(2)}, u32[]{:S(2)}) collective-permute-start(bf16[128,512]{1,0:T(8,128)(2,1)S(1)} %copy-done.5), channel_id=1, source_target_pairs={{0,128},{128,0},{1,129},{129,1},{2,130},{130,2},{3,131},{131,3},{4... | collective-permute-start | bytes 393224 | tf_op jit(solution)/shard_map/ppermute | solution.py:371
  266.0 18.4 %collective-permute-start.2 = (bf16[2,128,512]{2,1,0:T(8,128)(2,1)S(1)}, bf16[2,128,512]{2,1,0:T(8,128)(2,1)S(1)}, u32[]{:S(2)}, u32[]{:S(2)}) collective-permute-start(bf16[2,128,512]{2,1,0:T(8,128)(2,1)S(1)} %get-tuple-element.33), channel_id=1, source_target_pairs={{0,64},{32,96},{64,0},{96,32},{1,65},{33,97},{65,1},{97,33},{2,66}... | collective-permute-start | bytes 786440 | tf_op jit(solution)/shard_map/ppermute | solution.py:373
  278.7 12.4 %collective-permute-start.1 = (bf16[2,128,512]{2,1,0:T(8,128)(2,1)S(1)}, bf16[2,128,512]{2,1,0:T(8,128)(2,1)S(1)}, u32[]{:S(2)}, u32[]{:S(2)}) collective-permute-start(bf16[2,128,512]{2,1,0:T(8,128)(2,1)S(1)} %get-tuple-element.33), channel_id=1, source_target_pairs={{0,32},{32,64},{64,96},{96,0},{1,33},{33,65},{65,97},{97,1},{2,34}... | collective-permute-start | bytes 786440 | tf_op jit(solution)/shard_map/ppermute | solution.py:373
  278.7 12.4 %collective-permute-start.3 = (bf16[2,128,512]{2,1,0:T(8,128)(2,1)S(1)}, bf16[2,128,512]{2,1,0:T(8,128)(2,1)S(1)}, u32[]{:S(2)}, u32[]{:S(2)}) collective-permute-start(bf16[2,128,512]{2,1,0:T(8,128)(2,1)S(1)} %get-tuple-element.33), channel_id=1, source_target_pairs={{0,96},{32,0},{64,32},{96,64},{1,97},{33,1},{65,33},{97,65},{2,98}... | collective-permute-start | bytes 786440 | tf_op jit(solution)/shard_map/ppermute | solution.py:373
  291.2 3.0 copy-start.3
  291.2 3.0 collective-permute-start.4
  294.2 1.3 copy-start
Sparse Core Ops, SparseCore 0:
  31.9 36.8 all-gather.8
  70.6 60.6 all-gather.4
  133.1 26.4 all-gather.6

commit v3 on v2

--- a/solution.py
+++ b/solution.py
@@ -24,6 +24,7 @@
 CORRECT_TWO = 1.0 - 0.95**10
 LEARN_RATE = 0.001
 
+
 REQ = ("zh", "y", "c")
 TP = ("zl", "x")
 F32 = jnp.float32
@@ -43,6 +44,12 @@
     return [(i, (i + step) % count) for i in range(count)]
 
 
+def turns(value, axis, count):
+    return jnp.stack(
+        [value] + [lax.ppermute(value, axis, turn(count, step)) for step in range(1, count)]
+    )
+
+
 def gather(value, axis):
     return lax.all_gather(value, axis, axis=0, tiled=True)
 
@@ -57,24 +64,41 @@
     return row, lane
 
 
-def attend_kernel(rank_ref, len_ref, par_ref, q_ref, ck_ref, cv_ref, tk_ref, tv_ref, out_ref, reach_ref, stat_ref):
+def attend_kernel(
+    rank_ref, len_ref, par_ref, q_ref, ck_ref, cv_ref, tk_ref, tv_ref,
+    out_ref, reach_ref, pick_ref, stat_ref,
+):
     rank = rank_ref[0]
     row, lane = same_request()
-    base = (row // NODES) * NODES
-    up = jnp.where(par_ref[...] + base == lane, jnp.where(par_ref[...] >= 0, 1.0, 0.0), 0.0)
+    base = (lane // NODES) * NODES
+    tile = jnp.where(
+        lax.broadcasted_iota(jnp.int32, (NODES, 128), 0)
+        == lax.broadcasted_iota(jnp.int32, (NODES, 128), 1) % NODES,
+        1.0,
+        0.0,
+    )
+    wide = dot(par_ref[...].astype(F32).astype(BF16), tile.astype(BF16), ((1,), (0,)))
+    lane_request = lax.broadcasted_iota(jnp.int32, (1, 128), 1) // NODES
+    parent = wide[0:1]
+    for r in range(1, 4):
+        parent = jnp.where(lane_request == r, wide[r : r + 1], parent)
+    parent = parent.astype(jnp.int32)
+    rooted = jnp.where(parent < 0, NODES - 1, parent)
+    pick_ref[...] = jnp.where(row == base + rooted, 1.0, 0.0).astype(BF16)
+    up = jnp.where(row == base + parent, jnp.where(parent >= 0, 1.0, 0.0), 0.0)
     reach = (jnp.where(row == lane, 1.0, 0.0) + up).astype(BF16)
     for _ in range((NODES - 1).bit_length()):
         reach = jnp.minimum(dot(reach, reach, ((1,), (0,))), 1.0).astype(BF16)
     reach_ref[...] = reach
-    pick = jnp.where(row % NODES == 2 * rank + lane, jnp.where(lane < 2, 1.0, 0.0), 0.0)
-    visible = dot(reach, pick.astype(BF16), ((1,), (0,)))
+    own = jnp.where(row % NODES == 2 * rank + lane, jnp.where(lane < 2, 1.0, 0.0), 0.0)
+    visible = dot(reach, own.astype(BF16), ((0,), (0,)))
     scale = 1.0 / math.sqrt(HEAD)
     span = ck_ref.shape[1]
     slot = lax.broadcasted_iota(jnp.int32, (256, span), 1) + rank * span
     wide_lane = lax.broadcasted_iota(jnp.int32, (NODES, 128), 1)
     for r in range(q_ref.shape[0]):
         live = slot < len_ref[r]
-        seen = visible[r * NODES : (r + 1) * NODES, :8]
+        seen = visible[r * NODES : (r + 1) * NODES, : tk_ref.shape[1]]
         seen = jnp.concatenate([seen] * 8, axis=0) > 0.5
         stats = jnp.zeros((NODES, 128), F32)
         for k in range(KV_HEADS):
@@ -136,49 +160,94 @@
                 joined = joined + parcel_ref[src, 0:128, cols].astype(F32) * share[:, at : at + 1]
             att_ref[:, cols] = joined.astype(BF16)
 
-    out_ref[0, 0] = dot(att_ref[...], weight_ref[...], ((1,), (0,))).astype(BF16)
+    for x in range(4):
+        cols = slice(x * 512, (x + 1) * 512)
+        out_ref[x, 0] = dot(att_ref[...], weight_ref[:, cols], ((1,), (0,))).astype(BF16)
+
+
+def settle_kernel(rank_ref, along_ref, residual_ref, gain_ref, prev_ref, mixed_ref, near_ref, table_ref):
+    mixed = residual_ref[...].astype(F32)
+    total = along_ref[0].astype(F32)
+    for term in range(1, 4):
+        total = total + along_ref[term].astype(F32)
+    mixed = mixed + total
+    mixed_ref[...] = mixed
+    near_ref[...] = mixed.astype(BF16)
+    scaled = mixed * gain_ref[0]
+    node = lax.broadcasted_iota(jnp.int32, (NODES, 1), 0)
+    prev = prev_ref[...].astype(F32)
+    for r in range(4):
+        part = slice(r * NODES, (r + 1) * NODES)
+        table_ref[part] = jnp.where(node == NODES - 1, prev[r : r + 1], scaled[part]).astype(BF16)
 
 
 def predict_kernel(
-    far_ref, mixed_ref, gain_ref, own_gain_ref, prev_ref, par_ref, scale_w_ref, weight_ref,
-    table_ref, own_ref, err_ref, loss_ref, scale_ref, ahead_ref,
+    source_ref, rank_ref, len_ref, leaf_ref, far_ref, mixed_ref, gain_ref, prev_ref, reach_ref,
+    pick_ref, near_ref, other_ref, own_ref, err_ref, loss_ref, scale_ref, ahead_ref,
 ):
-    p = pl.program_id(0)
-
-    @pl.when(p == 0)
+    step = pl.program_id(0)
+
+    @pl.when(step == 0)
     def start():
-        square = jnp.zeros((128, 1), F32)
+        square = jnp.zeros((128, 128), F32)
         for zl in range(4):
             for x in range(4):
                 part = far_ref[x, zl].astype(F32)
-                square = square + jnp.sum(part * part, axis=1, keepdims=True)
+                part = part * part
+                for i in range(4):
+                    square = square + part[:, i * 128 : (i + 1) * 128]
+        square = jnp.sum(square, axis=1, keepdims=True)
         scale = lax.rsqrt(square / D + NORM_EPSILON)
         scale_ref[...] = jnp.broadcast_to(scale, (128, 128))
-        own_ref[...] = (mixed_ref[...] * scale * own_gain_ref[...]).astype(BF16)
-        ahead_ref[...] = jnp.zeros_like(ahead_ref)
-
-    block = far_ref[lax.rem(p, 4), p // 4].astype(F32) * scale_ref[:, 0:1] * gain_ref[0]
+        own_ref[...] = (mixed_ref[...] * scale * gain_ref[rank_ref[0]]).astype(BF16)
+
     node = lax.broadcasted_iota(jnp.int32, (NODES, 1), 0)
-    prev = prev_ref[...].astype(F32)
-    block = jnp.concatenate(
-        [
-            jnp.where(node == NODES - 1, prev[r : r + 1], block[r * NODES : (r + 1) * NODES])
-            for r in range(4)
-        ],
-        axis=0,
-    ).astype(BF16)
-    table_ref[0] = block
-    ahead_ref[...] += dot(block, weight_ref[0], ((1,), (0,)))
-
-    @pl.when(p == N_TP - 1)
+
+    def multiply(weight_ref):
+        total = jnp.zeros((128, 512), F32)
+        for i in range(4):
+            p = source_ref[step * 4 + i]
+            block = far_ref[lax.rem(p, 4), p // 4].astype(F32) * scale_ref[:, 0:1] * gain_ref[p]
+            prev = prev_ref[:, pl.ds(pl.multiple_of(p * 512, 512), 512)].astype(F32)
+            block = jnp.concatenate(
+                [
+                    jnp.where(node == NODES - 1, prev[r : r + 1], block[r * NODES : (r + 1) * NODES])
+                    for r in range(4)
+                ],
+                axis=0,
+            ).astype(BF16)
+            total = total + dot(block, weight_ref[i], ((1,), (0,)))
+        return total
+
+    @pl.when(step == 0)
+    def first():
+        ahead_ref[...] = multiply(near_ref)
+
+    @pl.when(step == 1)
+    def second():
+        ahead_ref[...] += multiply(near_ref)
+
+    @pl.when(step >= 2)
+    def rest():
+        ahead_ref[...] += multiply(other_ref)
+
+    @pl.when(step == 3)
     def finish():
         row, lane = same_request()
-        parent = jnp.where(par_ref[...] < 0, NODES - 1, par_ref[...])
-        pick = jnp.where(parent + (row // NODES) * NODES == lane, 1.0, 0.0)
-        predicted = dot(pick, ahead_ref[...], ((1,), (0,)), precision=lax.Precision.HIGHEST)
+        accepted = []
+        for r in range(4):
+            part = slice(r * NODES, (r + 1) * NODES)
+            path = jnp.where(lane[part] == leaf_ref[r] + r * NODES, reach_ref[part].astype(F32), 0.0)
+            path = jnp.sum(path, axis=1, keepdims=True)
+            accepted.append((1.0 + 3.0 * path) * (0.5 + len_ref[r].astype(F32) / CACHE))
+        weights = jnp.concatenate(accepted, axis=0)
+        pick = pick_ref[...].astype(F32)
+        predicted = dot(pick, ahead_ref[...], ((0,), (0,)), precision=lax.Precision.HIGHEST)
         error = predicted - own_ref[...].astype(F32)
-        weighted = scale_w_ref[...] * error
-        err_ref[...] = dot(pick, weighted, ((0,), (0,)), precision=lax.Precision.HIGHEST).astype(BF16)
+        weighted = weights * error
+        joined = dot(pick, weighted, ((1,), (0,)), precision=lax.Precision.HIGHEST)
+        scale = jnp.where(row[:, 0:1] % NODES == NODES - 1, 1.0, scale_ref[:, 0:1])
+        err_ref[...] = (joined * scale).astype(BF16)
         loss = jnp.sum(jnp.sum(weighted * error, axis=0, keepdims=True), axis=1, keepdims=True)
         loss_ref[...] = jnp.broadcast_to(loss, (8, 128))
 
@@ -211,39 +280,99 @@
     return pl.BlockSpec(memory_space=pltpu.SMEM)
 
 
-def attend(rank, lengths, parent_column, queries, cache_keys, cache_values, tree_keys, tree_values):
+def attend(rank, lengths, parents, queries, cache_keys, cache_values, tree_keys, tree_values):
     return pl.pallas_call(
         attend_kernel,
         out_shape=(
             jax.ShapeDtypeStruct((N_TP, 144, 2 * HEAD), BF16),
             jax.ShapeDtypeStruct((128, 128), BF16),
+            jax.ShapeDtypeStruct((128, 128), BF16),
         ),
         in_specs=[in_smem(), in_smem()] + [in_vmem()] * 6,
-        out_specs=(in_vmem(), in_vmem()),
+        out_specs=(in_vmem(), in_vmem(), in_vmem()),
         scratch_shapes=[pltpu.VMEM((128, 128), F32)],
         cost_estimate=pl.CostEstimate(
             flops=2 * 2 * 16 * 256 * 256 * 128, bytes_accessed=4 << 20, transcendentals=16 * 256 * 256
         ),
         name="attend",
-    )(rank, lengths, parent_column, queries, cache_keys, cache_values, tree_keys, tree_values)
+    )(rank, lengths, parents, queries, cache_keys, cache_values, tree_keys, tree_values)
 
 
 def project(parcel, out_weight):
     return pl.pallas_call(
         project_kernel,
-        grid=(N_TP,),
+        grid=(4,),
         out_shape=jax.ShapeDtypeStruct((4, 4, 128, 512), BF16),
         in_specs=[
             pl.BlockSpec((N_TP, 144, 2 * HEAD), lambda p: (0, 0, 0)),
-            pl.BlockSpec((2 * HEAD, 512), lambda p: (0, p)),
+            pl.BlockSpec((2 * HEAD, 2048), lambda p: (0, p)),
         ],
-        out_specs=pl.BlockSpec((1, 1, 128, 512), lambda p: (lax.rem(p, 4), p // 4, 0, 0)),
+        out_specs=pl.BlockSpec((4, 1, 128, 512), lambda p: (0, p, 0, 0)),
         scratch_shapes=[pltpu.VMEM((128, 2 * HEAD), BF16)],
         cost_estimate=pl.CostEstimate(
             flops=2 * 128 * 256 * 8192, bytes_accessed=7 << 20, transcendentals=0
         ),
         name="project",
     )(parcel, out_weight)
+
+
+def settle(rank, along, residual, gain, prev):
+    return pl.pallas_call(
+        settle_kernel,
+        grid_spec=pltpu.PrefetchScalarGridSpec(
+            num_scalar_prefetch=1,
+            grid=(1,),
+            in_specs=[
+                pl.BlockSpec((4, 128, 512), lambda p, at: (0, 0, 0)),
+                pl.BlockSpec((128, 512), lambda p, at: (0, 0)),
+                pl.BlockSpec((1, 1, 512), lambda p, at: (at[0], 0, 0)),
+                pl.BlockSpec((4, 512), lambda p, at: (0, at[0])),
+            ],
+            out_specs=[pl.BlockSpec((128, 512), lambda p, at: (0, 0))] * 3,
+        ),
+        out_shape=(
+            jax.ShapeDtypeStruct((128, 512), F32),
+            jax.ShapeDtypeStruct((128, 512), BF16),
+            jax.ShapeDtypeStruct((128, 512), BF16),
+        ),
+        cost_estimate=pl.CostEstimate(
+            flops=128 * 512 * 8, bytes_accessed=2 << 20, transcendentals=0
+        ),
+        name="settle",
+    )(rank, along, residual, gain, prev)
+
+
+def predict(source, rank, lengths, leaf, far, mixed, gain, prev, reach, pick, near, other):
+    return pl.pallas_call(
+        predict_kernel,
+        grid=(4,),
+        out_shape=(
+            jax.ShapeDtypeStruct((128, 512), BF16),
+            jax.ShapeDtypeStruct((128, 512), BF16),
+            jax.ShapeDtypeStruct((8, 128), F32),
+        ),
+        in_specs=[in_smem()] * 4
+        + [
+            pl.BlockSpec((4, 4, 128, 512), lambda p: (0, 0, 0, 0)),
+            pl.BlockSpec((128, 512), lambda p: (0, 0)),
+            pl.BlockSpec((N_TP, 1, 512), lambda p: (0, 0, 0)),
+            pl.BlockSpec((4, D), lambda p: (0, 0)),
+            pl.BlockSpec((128, 128), lambda p: (0, 0)),
+            pl.BlockSpec((128, 128), lambda p: (0, 0)),
+            pl.BlockSpec((4, 512, 512), lambda p: (jnp.minimum(p, 1), 0, 0)),
+            pl.BlockSpec((4, 512, 512), lambda p: (jnp.maximum(p - 2, 0), 0, 0)),
+        ],
+        out_specs=(
+            pl.BlockSpec((128, 512), lambda p: (0, 0)),
+            pl.BlockSpec((128, 512), lambda p: (0, 0)),
+            pl.BlockSpec((8, 128), lambda p: (0, 0)),
+        ),
+        scratch_shapes=[pltpu.VMEM((128, 128), F32), pltpu.VMEM((128, 512), F32)],
+        cost_estimate=pl.CostEstimate(
+            flops=2 * 128 * 8192 * 512, bytes_accessed=13 << 20, transcendentals=0
+        ),
+        name="predict",
+    )(source, rank, lengths, leaf, far, mixed, gain, prev, reach, pick, near, other)
 
 
 def differentiate(source, columns, near_err, other_err, loss):
@@ -260,43 +389,6 @@
         ),
         name="differentiate",
     )(source, columns, near_err, other_err, loss)
-
-
-def predict(far, mixed, gain, own_gain, prev, parent_column, weights, all_weight):
-    return pl.pallas_call(
-        predict_kernel,
-        grid=(N_TP,),
-        out_shape=(
-            jax.ShapeDtypeStruct((N_TP, 128, 512), BF16),
-            jax.ShapeDtypeStruct((128, 512), BF16),
-            jax.ShapeDtypeStruct((128, 512), BF16),
-            jax.ShapeDtypeStruct((8, 128), F32),
-        ),
-        in_specs=[
-            pl.BlockSpec((4, 4, 128, 512), lambda p: (0, 0, 0, 0)),
-            pl.BlockSpec((128, 512), lambda p: (0, 0)),
-            pl.BlockSpec((1, 1, 512), lambda p: (p, 0, 0)),
-            pl.BlockSpec((1, 512), lambda p: (0, 0)),
-            pl.BlockSpec((4, 512), lambda p: (0, p)),
-            pl.BlockSpec((128, 1), lambda p: (0, 0)),
-            pl.BlockSpec((128, 1), lambda p: (0, 0)),
-            pl.BlockSpec(
-                (1, 512, 512),
-                lambda p: (lax.rem(p, 2) * 8 + lax.rem(p // 2, 4) * 2 + p // 8, 0, 0),
-            ),
-        ],
-        out_specs=(
-            pl.BlockSpec((1, 128, 512), lambda p: (p, 0, 0)),
-            pl.BlockSpec((128, 512), lambda p: (0, 0)),
-            pl.BlockSpec((128, 512), lambda p: (0, 0)),
-            pl.BlockSpec((8, 128), lambda p: (0, 0)),
-        ),
-        scratch_shapes=[pltpu.VMEM((128, 128), F32), pltpu.VMEM((128, 512), F32)],
-        cost_estimate=pl.CostEstimate(
-            flops=2 * 128 * 8192 * 512, bytes_accessed=13 << 20, transcendentals=0
-        ),
-        name="predict",
-    )(far, mixed, gain, own_gain, prev, parent_column, weights, all_weight)
 
 
 def body(
@@ -319,66 +411,59 @@
     requests = queries.shape[0]
     rows = requests * NODES
     tp_rank = lax.axis_index(TP)
+    rank = tp_rank.reshape(1)
     block = residual.shape[2]
-    parent_column = parents.reshape(rows, 1)
-
-    wide_weight = gather(draft_weight[None], "zh")
-
-    pad = ((0, 0), (0, 6), (0, 0))
-    parcel, reach = attend(
-        tp_rank.reshape(1),
-        lengths,
-        parent_column,
-        queries,
-        cache_keys,
-        cache_values,
-        jnp.pad(tree_keys, pad),
-        jnp.pad(tree_values, pad),
+    gain = norm_gain.reshape(N_TP, 1, block)
+    zh, y, c = lax.axis_index("zh"), lax.axis_index("y"), lax.axis_index("c")
+    piece = jnp.arange(N_REQ, dtype=jnp.int32)
+    source = (
+        ((zh + piece % 2) % 2) * 8 + ((y + 4 - (piece // 2) % 4) % 4) * 2 + (c + piece // 8) % 2
+    )
+    place = (source % 4) * 4 + (lax.axis_index("zl") + 4 - source // 4) % 4
+
+    wide_weight = turns(draft_weight, "zh", 2)
+    parcel, reach, pick = attend(
+        rank, lengths, parents, queries, cache_keys, cache_values, tree_keys, tree_values
     )
     parcel = exchange(parcel, TP)
     parcel, wide_weight = lax.optimization_barrier((parcel, wide_weight))
-    wide_weight = gather(wide_weight, "y")
-
-    leaf = jnp.arange(requests, dtype=jnp.int32) * NODES + accepted_leaf
-    leaf_hot = (leaf[:, None] == jnp.arange(rows, dtype=jnp.int32)[None, :]).astype(BF16)
-    accepted = jnp.dot(jnp.sum(leaf_hot, axis=0, keepdims=True), reach, preferred_element_type=F32)
-    fill_share = jnp.repeat(0.5 + lengths.astype(F32) / CACHE, NODES)
-    weights = ((1.0 + 3.0 * accepted.reshape(rows)) * fill_share).reshape(rows, 1)
-    own_gain = lax.dynamic_slice_in_dim(norm_gain, tp_rank * block, block, 0).reshape(1, block)
+    wide_weight = turns(wide_weight, "y", 4)
 
     partial_value = project(parcel, out_weight)
     along_x = exchange(partial_value, "x")
     along_x = jnp.sum(along_x.astype(F32), axis=0).astype(BF16)
     along_x, wide_weight = lax.optimization_barrier((along_x, wide_weight))
-    all_weight = gather(wide_weight, "c")
+    other_weight = lax.ppermute(wide_weight, "c", turn(2, 1))
     along_z = exchange(along_x, "zl")
-    projected = jnp.sum(along_z.astype(F32), axis=0)
-    mixed = residual.reshape(rows, block).astype(F32) + projected
-
-    near = gather(mixed.astype(BF16)[None], "zl")
-    far = spread(near, "x", 4).reshape(4, 4, rows, block)
-    table, own_features, scaled_err, loss = predict(
+    mixed, near, table = settle(rank, along_z, residual.reshape(rows, block), gain, prev_feature)
+
+    swapped = lax.ppermute(
+        table, REQ + TP, [(i * N_TP + j, j * N_TP + i) for i in range(16) for j in range(16)]
+    )
+    far = gather(near[None], "zl")
+    far = spread(far, "x", 4).reshape(4, 4, rows, block)
+    swapped, far = lax.optimization_barrier((swapped, far))
+    columns = turns(swapped, "zl", 4)
+    own_features, scaled_err, loss = predict(
+        source,
+        rank,
+        lengths,
+        accepted_leaf,
         far,
         mixed,
-        norm_gain.reshape(N_TP, 1, block),
-        own_gain,
+        gain,
         prev_feature,
-        parent_column,
-        weights,
-        all_weight,
-    )
-    columns = exchange(table, REQ)
-    near_err = jnp.stack([scaled_err, lax.ppermute(scaled_err, "zh", turn(2, 1))])
-    near_err = jnp.stack(
-        [near_err] + [lax.ppermute(near_err, "y", turn(4, step)) for step in (1, 2, 3)]
-    )
+        reach,
+        pick,
+        wide_weight.reshape(8, block, block),
+        other_weight.reshape(8, block, block),
+    )
+    columns, scaled_err = lax.optimization_barrier((columns, scaled_err))
+    columns = spread(columns, "x", 4).reshape(N_REQ, rows, block)
+    near_err = turns(scaled_err, "zh", 2)
+    near_err = turns(near_err, "y", 4)
     other_err = lax.ppermute(near_err, "c", turn(2, 1))
-    zh, y, c = lax.axis_index("zh"), lax.axis_index("y"), lax.axis_index("c")
-    piece = jnp.arange(N_REQ, dtype=jnp.int32)
-    source = (
-        ((zh + piece % 2) % 2) * 8 + ((y + 4 - (piece // 2) % 4) % 4) * 2 + (c + piece // 8) % 2
-    )
-    gradient, pair = differentiate(source, columns, near_err, other_err, loss)
+    gradient, pair = differentiate(place, columns, near_err, other_err, loss)
     pair = jnp.sum(exchange(pair, REQ + TP), axis=0)
     square_total, error_total = pair[0], pair[1]
     draft_loss = 0.5 * error_total / (rows * N_REQ * D)

time: 335 us -> 295 us (0.88)
  between operations: 16.3 us -> 3.3 us
  blocking collectives: 68.9 us -> 58 us
  Pallas kernels: 40.8 us -> 29.9 us
  local copies, waits for them, and re-layouts: 12 us -> 6.1 us
  starting transfers between devices: 52.4 us -> 55.9 us
    ppermute x4 -> x13, waiting for transfers between devices: 50.5 us -> 130 us  [the longest x11 110 us: turns(): lax.ppermute(value, axis, turn(count, step))]
    all_gather x3 -> x0, waiting for transfers between devices: 50.5 us -> none  [gather(): return lax.all_gather(value, axis, axis=0, tiled=True)]
    all_to_all x4, waiting for transfers between devices: 32.4 us -> 0.72 us  [exchange(): return lax.all_to_all(value, axis, 0, 0, tiled=True)]
    pallas_call x2 -> x3, Pallas kernels: 27.3 us -> 16.3 us  [the longest x1 8.28 us: predict(): pl.pallas_call(predict_kernel, grid=(4,), out_shape=(jax.ShapeDtypeStruct...]
    all_to_all x2, blocking collectives: 56.1 us -> 45.2 us  [exchange(): return lax.all_to_all(value, axis, 0, 0, tiled=True)]
    ppermute x4 -> x13, starting transfers between devices: 20.7 us -> 28.2 us  [the longest x11 19.6 us: turns(): lax.ppermute(value, axis, turn(count, step))]
    all_to_all x4, starting transfers between devices: 31 us -> 27.2 us  [exchange(): return lax.all_to_all(value, axis, 0, 0, tiled=True)]
  transfers between devices with their start and end apart: 12 -> 18, of which waited for: 8 -> 12; matrix products, arithmetic and copies ran while one was open for 2% -> 2% of each run, Pallas kernels for 4% -> 1%
where the time goes in v3:
time: 295 us; the launch traced here: 294 us
  waiting for transfers between devices  133 us (45%)
  blocking collectives  58 us (20%)
  starting transfers between devices  55.9 us (19%)
  Pallas kernels  29.9 us (10%)
  other arithmetic  8.12 us (3%)
  local copies, waits for them, and re-layouts  6.1 us (2%)
  between operations  3.3 us (1%)
    ppermute x11, waiting for transfers between devices, turns(): lax.ppermute(value, axis, turn(count, step))  110 us
    all_to_all x2, blocking collectives, exchange(): return lax.all_to_all(value, axis, 0, 0, tiled=True)  45.2 us
    all_to_all x4, starting transfers between devices, exchange(): return lax.all_to_all(value, axis, 0, 0, tiled=True)  27.2 us
    ppermute x1, waiting for transfers between devices, body(): lax.ppermute(table, REQ + TP, [(i * N_TP + j, j * N_TP + i) for i in rang...  20.2 us
    ppermute x11, starting transfers between devices, turns(): lax.ppermute(value, axis, turn(count, step))  19.6 us
    all_gather x1, blocking collectives, gather(): return lax.all_gather(value, axis, axis=0, tiled=True)  12.8 us
    pallas_call x1, Pallas kernels, attend(): pl.pallas_call(attend_kernel, out_shape=(jax.ShapeDtypeStruct((N_TP, 144,...  9.21 us
    pallas_call x1, Pallas kernels, predict(): pl.pallas_call(predict_kernel, grid=(4,), out_shape=(jax.ShapeDtypeStruct...  8.28 us
  transfers between devices with their start and end apart: 18, of which 12 were waited for; matrix products, arithmetic and copies ran while one was open for 2% of the time, Pallas kernels for 1%

profile of v3, /device:TPU:1, one launch (start us, length us, event | category | flops | bytes accessed | tf_op | source)
XLA Modules:
  0.0 294.4 jit_solution(14987992997641756161)
XLA Ops:
  0.6 0.0 copy-start.4
  0.7 9.2 %attend.1 = (bf16[16,144,256]{2,1,0:T(8,128)(2,1)}, bf16[128,128]{1,0:T(8,128)(2,1)}, bf16[128,128]{1,0:T(8,128)(2,1)}) custom-call(s32[1]{0:T(128)} %bitcast.rank_ref, s32[4]{0:T(128)} %len_ref.3, s32[4,32]{1,0:T(4,128)} %par_ref.1, bf16[4,32,4096]{2,1,0:T(8,128)(2,1)} %q_ref.1, bf16[4,256,512]{2,1,0:T(8,128)(2,1)} %ck_ref.1, bf16[4,256,512]{2,1,0:T(8,128)(2,1)} %cv_ref.1, ...), custom_call_target="tpu_custom_call" | custom-call | flops 536870912 | bytes 4194304 | tf_op jit(solution)/shard_map/attend/pallas_call | solution.py:284
  9.9 9.0 %all-to-all-start = ((bf16[16,144,256]{2,1,0:T(8,128)(2,1)}), bf16[16,144,256]{2,1,0:T(8,128)(2,1)S(1)}, u32[]{:S(2)}, u32[]{:S(2)}) async-start(bf16[16,144,256]{2,1,0:T(8,128)(2,1)} %get-tuple-element.24), calls=%async_computation | async-start | bytes 2359296 | tf_op jit(solution)/shard_map/all_to_all | solution.py:35
  18.9 0.0 copy-done.4
  18.9 4.3 %collective-permute-start = (bf16[512,512]{1,0:T(8,128)(2,1)S(1)}, bf16[512,512]{1,0:T(8,128)(2,1)S(1)}, u32[]{:S(2)}, u32[]{:S(2)}) collective-permute-start(bf16[512,512]{1,0:T(8,128)(2,1)S(1)} %copy-done.4), channel_id=1, source_target_pairs={{0,128},{128,0},{1,129},{129,1},{2,130},{130,2},{3,131},{131,3},{4... | collective-permute-start | bytes 1572872 | tf_op jit(solution)/shard_map/ppermute | solution.py:49
  23.2 41.6 %collective-permute-done = bf16[512,512]{1,0:T(8,128)(2,1)S(1)} collective-permute-done((bf16[512,512]{1,0:T(8,128)(2,1)S(1)}, bf16[512,512]{1,0:T(8,128)(2,1)S(1)}, u32[]{:S(2)}, u32[]{:S(2)}) %collective-permute-start) | collective-permute-done | bytes 524320 | tf_op jit(solution)/shard_map/ppermute | solution.py:49
  64.8 0.1 pad_maximum_fusion.1
  64.9 0.0 all-to-all-done.parcel_ref
  64.9 0.0 copy-start.2
  64.9 1.0 copy-done.2
  65.9 6.0 %project.1 = bf16[4,4,128,512]{3,2,1,0:T(8,128)(2,1)} custom-call(bf16[16,144,256]{2,1,0:T(8,128)(2,1)} %copy-done.2, bf16[256,8192]{1,0:T(8,128)(2,1)} %weight_ref.1), custom_call_target="tpu_custom_call" | custom-call | flops 536870912 | bytes 7340032 | tf_op jit(solution)/shard_map/project/pallas_call | solution.py:302
  71.9 5.9 %all-to-all-start.1 = ((bf16[4,4,128,512]{3,2,1,0:T(8,128)(2,1)}), bf16[4,4,128,512]{3,2,1,0:T(8,128)(2,1)S(1)}, u32[]{:S(2)}, u32[]{:S(2)}) async-start(bf16[4,4,128,512]{3,2,1,0:T(8,128)(2,1)} %project.1), calls=%async_computation.1 | async-start | bytes 4194304 | tf_op jit(solution)/shard_map/all_to_all | solution.py:35
  77.8 2.7 collective-permute-start.3
  80.6 0.3 collective-permute-start.2
  80.9 0.7 collective-permute-start.1
  81.6 19.8 %collective-permute-done.3 = bf16[2,512,512]{2,1,0:T(8,128)(2,1)S(1)} collective-permute-done((bf16[2,512,512]{2,1,0:T(8,128)(2,1)S(1)}, bf16[2,512,512]{2,1,0:T(8,128)(2,1)S(1)}, u32[]{:S(2)}, u32[]{:S(2)}) %collective-permute-start.3) | collective-permute-done | bytes 1048608 | tf_op jit(solution)/shard_map/ppermute | solution.py:49
  101.4 2.5 collective-permute-done.2
  103.9 25.7 %collective-permute-done.1 = bf16[2,512,512]{2,1,0:T(8,128)(2,1)S(1)} collective-permute-done((bf16[2,512,512]{2,1,0:T(8,128)(2,1)S(1)}, bf16[2,512,512]{2,1,0:T(8,128)(2,1)S(1)}, u32[]{:S(2)}, u32[]{:S(2)}) %collective-permute-start.1) | collective-permute-done | bytes 1048608 | tf_op jit(solution)/shard_map/ppermute | solution.py:49
  129.6 2.3 pad_maximum_fusion
  131.9 0.0 all-to-all-done.1
  131.9 0.6 reduce_sum.21
  132.5 0.6 collective-permute-start.5
  133.1 20.2 %all_to_all.34.along_ref = bf16[4,128,512]{2,1,0:T(8,128)(2,1)} all-to-all(bf16[4,128,512]{2,1,0:T(8,128)(2,1)S(1)} %reduce_sum.21), channel_id=1, replica_groups=mesh['zh'=2,'y'=4,'c'=2,'zl'=4,'x'=4] {'zl'}, dimensions={0} | all-to-all | bytes 1048576 | tf_op jit(solution)/shard_map/all_to_all | solution.py:35
  153.3 2.0 settle.1
  155.2 12.8 %all-gather = bf16[512,512]{1,0:T(8,128)(2,1)S(1)} all-gather(bf16[128,512]{1,0:T(8,128)(2,1)} %get-tuple-element.29), channel_id=2, replica_groups=mesh['zh'=2,'y'=4,'c'=2,'zl'=4,'x'=4] {'zl'}, dimensions={0}, use_global_device_ids=true | all-gather | bytes 655360 | tf_op jit(solution)/shard_map/all_gather | solution.py:54
  168.0 1.6 broadcast_in_dim.7
  169.6 4.1 %all-to-all-start.3 = ((bf16[16,128,512]{2,1,0:T(8,128)(2,1)}), bf16[16,128,512]{2,1,0:T(8,128)(2,1)S(1)}, u32[]{:S(2)}, u32[]{:S(2)}) async-start(bf16[16,128,512]{2,1,0:T(8,128)(2,1)} %bitcast.10), calls=%async_computation.3 | async-start | bytes 4194304 | tf_op jit(solution)/shard_map/all_to_all | solution.py:35
  173.7 0.0 copy-done.6
  173.8 8.0 %collective-permute-start.4 = (bf16[128,512]{1,0:T(8,128)(2,1)S(1)}, bf16[128,512]{1,0:T(8,128)(2,1)S(1)}, u32[]{:S(2)}, u32[]{:S(2)}) collective-permute-start(bf16[128,512]{1,0:T(8,128)(2,1)S(1)} %copy-done.6), channel_id=1, source_target_pairs={{0,0},{1,16},{2,32},{3,48},{4,64},{5,80},{6,96},{7,112},{8,128},{9... | collective-permute-start | bytes 393224 | tf_op jit(solution)/shard_map/ppermute | solution.py:440
  181.7 20.2 %collective-permute-done.4 = bf16[128,512]{1,0:T(8,128)(2,1)S(1)} collective-permute-done((bf16[128,512]{1,0:T(8,128)(2,1)S(1)}, bf16[128,512]{1,0:T(8,128)(2,1)S(1)}, u32[]{:S(2)}, u32[]{:S(2)}) %collective-permute-start.4) | collective-permute-done | bytes 131104 | tf_op jit(solution)/shard_map/ppermute | solution.py:440
  201.9 0.0 all-to-all-done.3
  201.9 0.0 collective-permute-start.8
  202.0 0.3 collective-permute-start.7
  202.2 1.2 collective-permute-start.6
  203.4 0.5 fusion.2
  204.0 2.8 collective-permute-done.8
  206.8 3.4 %collective-permute-done.7 = bf16[128,512]{1,0:T(8,128)(2,1)S(1)} collective-permute-done((bf16[128,512]{1,0:T(8,128)(2,1)S(1)}, bf16[128,512]{1,0:T(8,128)(2,1)S(1)}, u32[]{:S(2)}, u32[]{:S(2)}) %collective-permute-start.7) | collective-permute-done | bytes 131104 | tf_op jit(solution)/shard_map/ppermute | solution.py:49
  210.2 0.0 collective-permute-done.6
  210.2 0.1 pad_maximum_fusion.3
  210.3 0.0 collective-permute-done.5
  210.3 0.0 copy-done.1
  210.3 8.3 %predict.1 = (bf16[128,512]{1,0:T(8,128)(2,1)}, bf16[128,512]{1,0:T(8,128)(2,1)}, f32[8,128]{1,0:T(8,128)}) custom-call(s32[16]{0:T(128)} %get-tuple-element.47.source_ref, s32[1]{0:T(128)} %bitcast.rank_ref, s32[4]{0:T(128)} %len_ref.3, s32[4]{0:T(128)} %leaf_ref.1, bf16[4,4,128,512]{3,2,1,0:T(8,128)(2,1)} %bitcast.34, ...), custom_call_target="tpu_custom_call" | custom-call | flops 1073741824 | bytes 13631488 | tf_op jit(solution)/shard_map/predict/pallas_call | solution.py:346
  218.6 3.7 %collective-permute-start.9 = (bf16[128,512]{1,0:T(8,128)(2,1)}, bf16[128,512]{1,0:T(8,128)(2,1)S(1)}, u32[]{:S(2)}, u32[]{:S(2)}) collective-permute-start(bf16[128,512]{1,0:T(8,128)(2,1)} %get-tuple-element.39), channel_id=1, source_target_pairs={{0,128},{128,0},{1,129},{129,1},{2,130},{130,2},{3,131},{131,3},{4... | collective-permute-start | bytes 393224 | tf_op jit(solution)/shard_map/ppermute | solution.py:49
  222.3 1.6 broadcast_in_dim.8
  223.8 8.1 %all-to-all-start.4 = ((bf16[16,128,512]{2,1,0:T(8,128)(2,1)}), bf16[16,128,512]{2,1,0:T(8,128)(2,1)S(1)}, u32[]{:S(2)}, u32[]{:S(2)}) async-start(bf16[16,128,512]{2,1,0:T(8,128)(2,1)} %bitcast.33), calls=%async_computation.4 | async-start | bytes 4194304 | tf_op jit(solution)/shard_map/all_to_all | solution.py:35
  232.0 0.0 collective-permute-done.9
  232.0 0.0 copy-done.5
  232.0 4.9 %collective-permute-start.12 = (bf16[2,128,512]{2,1,0:T(8,128)(2,1)S(1)}, bf16[2,128,512]{2,1,0:T(8,128)(2,1)S(1)}, u32[]{:S(2)}, u32[]{:S(2)}) collective-permute-start(bf16[2,128,512]{2,1,0:T(8,128)(2,1)S(1)} %get-tuple-element.49), channel_id=1, source_target_pairs={{0,96},{32,0},{64,32},{96,64},{1,97},{33,1},{65,33},{97,65},{2,98}... | collective-permute-start | bytes 786440 | tf_op jit(solution)/shard_map/ppermute | solution.py:49
  236.9 1.5 collective-permute-start.11
  238.4 0.0 collective-permute-start.10
  238.4 4.4 %collective-permute-done.12 = bf16[2,128,512]{2,1,0:T(8,128)(2,1)S(1)} collective-permute-done((bf16[2,128,512]{2,1,0:T(8,128)(2,1)S(1)}, bf16[2,128,512]{2,1,0:T(8,128)(2,1)S(1)}, u32[]{:S(2)}, u32[]{:S(2)}) %collective-permute-start.12) | collective-permute-done | bytes 262176 | tf_op jit(solution)/shard_map/ppermute | solution.py:49
  242.8 2.6 collective-permute-done.11
  245.4 6.8 %collective-permute-done.10 = bf16[2,128,512]{2,1,0:T(8,128)(2,1)S(1)} collective-permute-done((bf16[2,128,512]{2,1,0:T(8,128)(2,1)S(1)}, bf16[2,128,512]{2,1,0:T(8,128)(2,1)S(1)}, u32[]{:S(2)}, u32[]{:S(2)}) %collective-permute-start.10) | collective-permute-done | bytes 262176 | tf_op jit(solution)/shard_map/ppermute | solution.py:49
  252.2 0.1 pad_maximum_fusion.2.near_ref
  252.4 0.0 copy-start.3
  252.4 0.6 collective-permute-start.13
  253.0 2.4 collective-permute-done.13.other_ref
  255.4 0.7 all-to-all-done.4.column_ref
  256.1 1.3 copy-done
  257.4 4.5 %differentiate.1 = (f32[512,512]{1,0:T(8,128)}, f32[256,128]{1,0:T(8,128)}) custom-call(s32[16]{0:T(128)} %get-tuple-element.46.source_ref, bf16[16,128,512]{2,1,0:T(8,128)(2,1)} %copy-done, bf16[4,2,128,512]{3,2,1,0:T(8,128)(2,1)} %copy-done.3, bf16[4,2,128,512]{3,2,1,0:T(8,128)(2,1)} %collective-permute-done.13.other_ref, f32[8,128]{1,0:T(8,128)} %get-tuple-element.40.loss_ref), custom_call_target="tpu_custom_call" | custom-call | flops 1073741824 | bytes 5242880 | tf_op jit(solution)/shard_map/differentiate/pallas_call | solution.py:379
  261.9 25.0 %all_to_all.35 = f32[256,1,128]{2,1,0:T(1,128)S(1)} all-to-all(f32[256,1,128]{2,1,0:T(1,128)} %bitcast.48), channel_id=1, replica_groups=mesh['zh'=2,'y'=4,'c'=2,'zl'=4,'x'=4] {'zh','y','c','zl','x'}, dimensions={0} | all-to-all | bytes 262144 | tf_op jit(solution)/shard_map/all_to_all | solution.py:35
  286.9 0.3 reduce_sum.22
  287.2 0.6 fusion.18
  289.1 4.1 %subtract_convert_fusion = (bf16[512,512]{1,0:T(8,128)(2,1)}, f32[512,512]{1,0:T(8,128)}, f32[512,512]{1,0:T(8,128)}) fusion(bf16[512,512]{1,0:T(8,128)(2,1)} %param.27, f32[512,512]{1,0:T(8,128)} %get-tuple-element.41, f32[]{:T(128)} %bitcast.28, f32[512,512]{1,0:T(8,128)} %param.28, f32[512,512]{1,0:T(8,128)} %param.29), kind=kLoop, calls=%fused_computation.5 | loop fusion | flops 4194304 | bytes 6291460 | tf_op jit(solution)/shard_map/convert_element_type | solution.py:476
  (6 shorter events, 0.0 us)
Async XLA Ops:
  0.6 18.3 %copy-start.4 = (bf16[512,512]{1,0:T(8,128)(2,1)S(1)}, bf16[512,512]{1,0:T(8,128)(2,1)}, u32[]{:S(2)}) copy-start(bf16[512,512]{1,0:T(8,128)(2,1)} %param.27) | copy-start | bytes 1572868
  9.9 55.0 %all-to-all-start = ((bf16[16,144,256]{2,1,0:T(8,128)(2,1)}), bf16[16,144,256]{2,1,0:T(8,128)(2,1)S(1)}, u32[]{:S(2)}, u32[]{:S(2)}) async-start(bf16[16,144,256]{2,1,0:T(8,128)(2,1)} %get-tuple-element.24), calls=%async_computation | async-start | bytes 2359296 | tf_op jit(solution)/shard_map/all_to_all | solution.py:35
  18.9 45.9 %collective-permute-start = (bf16[512,512]{1,0:T(8,128)(2,1)S(1)}, bf16[512,512]{1,0:T(8,128)(2,1)S(1)}, u32[]{:S(2)}, u32[]{:S(2)}) collective-permute-start(bf16[512,512]{1,0:T(8,128)(2,1)S(1)} %copy-done.4), channel_id=1, source_target_pairs={{0,128},{128,0},{1,129},{129,1},{2,130},{130,2},{3,131},{131,3},{4... | collective-permute-start | bytes 1572872 | tf_op jit(solution)/shard_map/ppermute | solution.py:49
  64.9 1.0 copy-start.2
  71.9 60.0 %all-to-all-start.1 = ((bf16[4,4,128,512]{3,2,1,0:T(8,128)(2,1)}), bf16[4,4,128,512]{3,2,1,0:T(8,128)(2,1)S(1)}, u32[]{:S(2)}, u32[]{:S(2)}) async-start(bf16[4,4,128,512]{3,2,1,0:T(8,128)(2,1)} %project.1), calls=%async_computation.1 | async-start | bytes 4194304 | tf_op jit(solution)/shard_map/all_to_all | solution.py:35
  77.8 23.6 %collective-permute-start.3 = (bf16[2,512,512]{2,1,0:T(8,128)(2,1)S(1)}, bf16[2,512,512]{2,1,0:T(8,128)(2,1)S(1)}, u32[]{:S(2)}, u32[]{:S(2)}) collective-permute-start(bf16[2,512,512]{2,1,0:T(8,128)(2,1)S(1)} %pad_maximum_fusion.1), channel_id=1, source_target_pairs={{0,96},{32,0},{64,32},{96,64},{1,97},{33,1},{65,33},{97,65},{2,98}... | collective-permute-start | bytes 3145736 | tf_op jit(solution)/shard_map/ppermute | solution.py:49
  80.6 23.3 %collective-permute-start.2 = (bf16[2,512,512]{2,1,0:T(8,128)(2,1)S(1)}, bf16[2,512,512]{2,1,0:T(8,128)(2,1)S(1)}, u32[]{:S(2)}, u32[]{:S(2)}) collective-permute-start(bf16[2,512,512]{2,1,0:T(8,128)(2,1)S(1)} %pad_maximum_fusion.1), channel_id=1, source_target_pairs={{0,64},{32,96},{64,0},{96,32},{1,65},{33,97},{65,1},{97,33},{2,66}... | collective-permute-start | bytes 3145736 | tf_op jit(solution)/shard_map/ppermute | solution.py:49
  80.9 48.7 %collective-permute-start.1 = (bf16[2,512,512]{2,1,0:T(8,128)(2,1)S(1)}, bf16[2,512,512]{2,1,0:T(8,128)(2,1)S(1)}, u32[]{:S(2)}, u32[]{:S(2)}) collective-permute-start(bf16[2,512,512]{2,1,0:T(8,128)(2,1)S(1)} %pad_maximum_fusion.1), channel_id=1, source_target_pairs={{0,32},{32,64},{64,96},{96,0},{1,33},{33,65},{65,97},{97,1},{2,34}... | collective-permute-start | bytes 3145736 | tf_op jit(solution)/shard_map/ppermute | solution.py:49
  132.5 77.8 %collective-permute-start.5 = (bf16[4,2,512,512]{3,2,1,0:T(8,128)(2,1)}, bf16[4,2,512,512]{3,2,1,0:T(8,128)(2,1)}, u32[]{:S(2)}, u32[]{:S(2)}) collective-permute-start(bf16[4,2,512,512]{3,2,1,0:T(8,128)(2,1)} %pad_maximum_fusion), channel_id=1, source_target_pairs={{0,16},{16,0},{1,17},{17,1},{2,18},{18,2},{3,19},{19,3},{4,20},{20... | collective-permute-start | bytes 12582920 | tf_op jit(solution)/shard_map/ppermute | solution.py:436
  155.2 18.5 %copy-start.6 = (bf16[128,512]{1,0:T(8,128)(2,1)S(1)}, bf16[128,512]{1,0:T(8,128)(2,1)}, u32[]{:S(2)}) copy-start(bf16[128,512]{1,0:T(8,128)(2,1)} %get-tuple-element.28) | copy-start | bytes 393220
  169.6 32.3 %all-to-all-start.3 = ((bf16[16,128,512]{2,1,0:T(8,128)(2,1)}), bf16[16,128,512]{2,1,0:T(8,128)(2,1)S(1)}, u32[]{:S(2)}, u32[]{:S(2)}) async-start(bf16[16,128,512]{2,1,0:T(8,128)(2,1)} %bitcast.10), calls=%async_computation.3 | async-start | bytes 4194304 | tf_op jit(solution)/shard_map/all_to_all | solution.py:35
  173.8 28.2 %collective-permute-start.4 = (bf16[128,512]{1,0:T(8,128)(2,1)S(1)}, bf16[128,512]{1,0:T(8,128)(2,1)S(1)}, u32[]{:S(2)}, u32[]{:S(2)}) collective-permute-start(bf16[128,512]{1,0:T(8,128)(2,1)S(1)} %copy-done.6), channel_id=1, source_target_pairs={{0,0},{1,16},{2,32},{3,48},{4,64},{5,80},{6,96},{7,112},{8,128},{9... | collective-permute-start | bytes 393224 | tf_op jit(solution)/shard_map/ppermute | solution.py:440
  201.9 8.3 %copy-start.1 = (bf16[16,128,512]{2,1,0:T(8,128)(2,1)}, bf16[16,128,512]{2,1,0:T(8,128)(2,1)S(1)}, u32[]{:S(2)}) copy-start(bf16[16,128,512]{2,1,0:T(8,128)(2,1)S(1)} %all-to-all-done.3) | copy-start | bytes 6291460
  201.9 4.8 %collective-permute-start.8 = (bf16[128,512]{1,0:T(8,128)(2,1)S(1)}, bf16[128,512]{1,0:T(8,128)(2,1)S(1)}, u32[]{:S(2)}, u32[]{:S(2)}) collective-permute-start(bf16[128,512]{1,0:T(8,128)(2,1)S(1)} %collective-permute-done.4), channel_id=1, source_target_pairs={{0,12},{4,0},{8,4},{12,8},{1,13},{5,1},{9,5},{13,9},{2,14},{6,2},{... | collective-permute-start | bytes 393224 | tf_op jit(solution)/shard_map/ppermute | solution.py:49
  202.0 8.2 %collective-permute-start.7 = (bf16[128,512]{1,0:T(8,128)(2,1)S(1)}, bf16[128,512]{1,0:T(8,128)(2,1)S(1)}, u32[]{:S(2)}, u32[]{:S(2)}) collective-permute-start(bf16[128,512]{1,0:T(8,128)(2,1)S(1)} %collective-permute-done.4), channel_id=1, source_target_pairs={{0,8},{4,12},{8,0},{12,4},{1,9},{5,13},{9,1},{13,5},{2,10},{6,14},... | collective-permute-start | bytes 393224 | tf_op jit(solution)/shard_map/ppermute | solution.py:49
  202.2 8.0 %collective-permute-start.6 = (bf16[128,512]{1,0:T(8,128)(2,1)S(1)}, bf16[128,512]{1,0:T(8,128)(2,1)S(1)}, u32[]{:S(2)}, u32[]{:S(2)}) collective-permute-start(bf16[128,512]{1,0:T(8,128)(2,1)S(1)} %collective-permute-done.4), channel_id=1, source_target_pairs={{0,4},{4,8},{8,12},{12,0},{1,5},{5,9},{9,13},{13,1},{2,6},{6,10},{... | collective-permute-start | bytes 393224 | tf_op jit(solution)/shard_map/ppermute | solution.py:49
  218.6 13.4 %copy-start.5 = (bf16[128,512]{1,0:T(8,128)(2,1)S(1)}, bf16[128,512]{1,0:T(8,128)(2,1)}, u32[]{:S(2)}) copy-start(bf16[128,512]{1,0:T(8,128)(2,1)} %get-tuple-element.39) | copy-start | bytes 393220
  218.6 13.4 %collective-permute-start.9 = (bf16[128,512]{1,0:T(8,128)(2,1)}, bf16[128,512]{1,0:T(8,128)(2,1)S(1)}, u32[]{:S(2)}, u32[]{:S(2)}) collective-permute-start(bf16[128,512]{1,0:T(8,128)(2,1)} %get-tuple-element.39), channel_id=1, source_target_pairs={{0,128},{128,0},{1,129},{129,1},{2,130},{130,2},{3,131},{131,3},{4... | collective-permute-start | bytes 393224 | tf_op jit(solution)/shard_map/ppermute | solution.py:49
  223.8 32.3 %all-to-all-start.4 = ((bf16[16,128,512]{2,1,0:T(8,128)(2,1)}), bf16[16,128,512]{2,1,0:T(8,128)(2,1)S(1)}, u32[]{:S(2)}, u32[]{:S(2)}) async-start(bf16[16,128,512]{2,1,0:T(8,128)(2,1)} %bitcast.33), calls=%async_computation.4 | async-start | bytes 4194304 | tf_op jit(solution)/shard_map/all_to_all | solution.py:35
  232.0 10.8 %collective-permute-start.12 = (bf16[2,128,512]{2,1,0:T(8,128)(2,1)S(1)}, bf16[2,128,512]{2,1,0:T(8,128)(2,1)S(1)}, u32[]{:S(2)}, u32[]{:S(2)}) collective-permute-start(bf16[2,128,512]{2,1,0:T(8,128)(2,1)S(1)} %get-tuple-element.49), channel_id=1, source_target_pairs={{0,96},{32,0},{64,32},{96,64},{1,97},{33,1},{65,33},{97,65},{2,98}... | collective-permute-start | bytes 786440 | tf_op jit(solution)/shard_map/ppermute | solution.py:49
  236.9 8.6 %collective-permute-start.11 = (bf16[2,128,512]{2,1,0:T(8,128)(2,1)S(1)}, bf16[2,128,512]{2,1,0:T(8,128)(2,1)S(1)}, u32[]{:S(2)}, u32[]{:S(2)}) collective-permute-start(bf16[2,128,512]{2,1,0:T(8,128)(2,1)S(1)} %get-tuple-element.49), channel_id=1, source_target_pairs={{0,64},{32,96},{64,0},{96,32},{1,65},{33,97},{65,1},{97,33},{2,66}... | collective-permute-start | bytes 786440 | tf_op jit(solution)/shard_map/ppermute | solution.py:49
  238.4 13.8 %collective-permute-start.10 = (bf16[2,128,512]{2,1,0:T(8,128)(2,1)S(1)}, bf16[2,128,512]{2,1,0:T(8,128)(2,1)S(1)}, u32[]{:S(2)}, u32[]{:S(2)}) collective-permute-start(bf16[2,128,512]{2,1,0:T(8,128)(2,1)S(1)} %get-tuple-element.49), channel_id=1, source_target_pairs={{0,32},{32,64},{64,96},{96,0},{1,33},{33,65},{65,97},{97,1},{2,34}... | collective-permute-start | bytes 786440 | tf_op jit(solution)/shard_map/ppermute | solution.py:49
  252.4 3.7 %copy-start.3 = (bf16[4,2,128,512]{3,2,1,0:T(8,128)(2,1)}, bf16[4,2,128,512]{3,2,1,0:T(8,128)(2,1)S(1)}, u32[]{:S(2)}) copy-start(bf16[4,2,128,512]{3,2,1,0:T(8,128)(2,1)S(1)} %pad_maximum_fusion.2.near_ref) | copy-start | bytes 3145732
  252.4 3.0 %collective-permute-start.13 = (bf16[4,2,128,512]{3,2,1,0:T(8,128)(2,1)S(1)}, bf16[4,2,128,512]{3,2,1,0:T(8,128)(2,1)}, u32[]{:S(2)}, u32[]{:S(2)}) collective-permute-start(bf16[4,2,128,512]{3,2,1,0:T(8,128)(2,1)S(1)} %pad_maximum_fusion.2.near_ref), channel_id=1, source_target_pairs={{0,16},{16,0},{1,17},{17,1},{2,18},{18,2},{3,19},{19,3},{4,20},{20... | collective-permute-start | bytes 3145736 | tf_op jit(solution)/shard_map/ppermute | solution.py:465
  256.1 1.3 copy-start

commit v4 on v3

--- a/solution.py
+++ b/solution.py
@@ -44,14 +44,12 @@
     return [(i, (i + step) % count) for i in range(count)]
 
 
+def passed(value, axis, count):
+    return [value] + [lax.ppermute(value, axis, turn(count, step)) for step in range(1, count)]
+
+
 def turns(value, axis, count):
-    return jnp.stack(
-        [value] + [lax.ppermute(value, axis, turn(count, step)) for step in range(1, count)]
-    )
-
-
-def gather(value, axis):
-    return lax.all_gather(value, axis, axis=0, tiled=True)
+    return jnp.stack(passed(value, axis, count))
 
 
 def dot(left, right, dims, **kwargs):
@@ -165,12 +163,22 @@
         out_ref[x, 0] = dot(att_ref[...], weight_ref[:, cols], ((1,), (0,))).astype(BF16)
 
 
-def settle_kernel(rank_ref, along_ref, residual_ref, gain_ref, prev_ref, mixed_ref, near_ref, table_ref):
-    mixed = residual_ref[...].astype(F32)
-    total = along_ref[0].astype(F32)
-    for term in range(1, 4):
-        total = total + along_ref[term].astype(F32)
-    mixed = mixed + total
+def fold_kernel(rank_ref, along_ref, *out_refs):
+    for step in range(4):
+        zl = lax.rem(rank_ref[0] // 4 + step, 4)
+        total = along_ref[0, zl].astype(F32)
+        for x in range(1, 4):
+            total = total + along_ref[x, zl].astype(F32)
+        out_refs[step][...] = total.astype(BF16)
+
+
+def settle_kernel(
+    rank_ref, own_ref, one_ref, two_ref, three_ref, residual_ref, gain_ref, prev_ref,
+    mixed_ref, near_ref, table_ref,
+):
+    total = own_ref[...].astype(F32) + one_ref[...].astype(F32)
+    total = total + (two_ref[...].astype(F32) + three_ref[...].astype(F32))
+    mixed = residual_ref[...].astype(F32) + total
     mixed_ref[...] = mixed
     near_ref[...] = mixed.astype(BF16)
     scaled = mixed * gain_ref[0]
@@ -183,31 +191,34 @@
 
 def predict_kernel(
     source_ref, rank_ref, len_ref, leaf_ref, far_ref, mixed_ref, gain_ref, prev_ref, reach_ref,
-    pick_ref, near_ref, other_ref, own_ref, err_ref, loss_ref, scale_ref, ahead_ref,
+    pick_ref, *refs,
 ):
-    step = pl.program_id(0)
-
-    @pl.when(step == 0)
-    def start():
-        square = jnp.zeros((128, 128), F32)
-        for zl in range(4):
-            for x in range(4):
-                part = far_ref[x, zl].astype(F32)
-                part = part * part
-                for i in range(4):
-                    square = square + part[:, i * 128 : (i + 1) * 128]
-        square = jnp.sum(square, axis=1, keepdims=True)
-        scale = lax.rsqrt(square / D + NORM_EPSILON)
-        scale_ref[...] = jnp.broadcast_to(scale, (128, 128))
-        own_ref[...] = (mixed_ref[...] * scale * gain_ref[rank_ref[0]]).astype(BF16)
+    weight_refs = refs[:16]
+    own_ref, err_ref, loss_ref, scale_ref, ahead_ref, weight_ref, sem_ref = refs[16:]
+    loads = [pltpu.make_async_copy(weight_refs[i], weight_ref.at[i], sem_ref.at[i]) for i in range(16)]
+    for load in loads:
+        load.start()
+    square = jnp.zeros((128, 128), F32)
+    for k in range(4):
+        for x in range(4):
+            part = far_ref[x, k].astype(F32)
+            part = part * part
+            for i in range(4):
+                square = square + part[:, i * 128 : (i + 1) * 128]
+    square = jnp.sum(square, axis=1, keepdims=True)
+    scale = lax.rsqrt(square / D + NORM_EPSILON)
+    scale_ref[...] = jnp.broadcast_to(scale, (128, 128))
+    own_ref[...] = (mixed_ref[...] * scale * gain_ref[rank_ref[0]]).astype(BF16)
 
     node = lax.broadcasted_iota(jnp.int32, (NODES, 1), 0)
-
-    def multiply(weight_ref):
+    for part in range(8):
+        loads[part].wait()
+        loads[part + 8].wait()
         total = jnp.zeros((128, 512), F32)
-        for i in range(4):
-            p = source_ref[step * 4 + i]
-            block = far_ref[lax.rem(p, 4), p // 4].astype(F32) * scale_ref[:, 0:1] * gain_ref[p]
+        for i in range(2):
+            p = source_ref[part * 2 + i]
+            back = lax.rem(rank_ref[0] // 4 + 4 - p // 4, 4)
+            block = far_ref[lax.rem(p, 4), back].astype(F32) * scale_ref[:, 0:1] * gain_ref[p]
             prev = prev_ref[:, pl.ds(pl.multiple_of(p * 512, 512), 512)].astype(F32)
             block = jnp.concatenate(
                 [
@@ -216,40 +227,30 @@
                 ],
                 axis=0,
             ).astype(BF16)
-            total = total + dot(block, weight_ref[i], ((1,), (0,)))
-        return total
-
-    @pl.when(step == 0)
-    def first():
-        ahead_ref[...] = multiply(near_ref)
-
-    @pl.when(step == 1)
-    def second():
-        ahead_ref[...] += multiply(near_ref)
-
-    @pl.when(step >= 2)
-    def rest():
-        ahead_ref[...] += multiply(other_ref)
-
-    @pl.when(step == 3)
-    def finish():
-        row, lane = same_request()
-        accepted = []
-        for r in range(4):
-            part = slice(r * NODES, (r + 1) * NODES)
-            path = jnp.where(lane[part] == leaf_ref[r] + r * NODES, reach_ref[part].astype(F32), 0.0)
-            path = jnp.sum(path, axis=1, keepdims=True)
-            accepted.append((1.0 + 3.0 * path) * (0.5 + len_ref[r].astype(F32) / CACHE))
-        weights = jnp.concatenate(accepted, axis=0)
-        pick = pick_ref[...].astype(F32)
-        predicted = dot(pick, ahead_ref[...], ((0,), (0,)), precision=lax.Precision.HIGHEST)
-        error = predicted - own_ref[...].astype(F32)
-        weighted = weights * error
-        joined = dot(pick, weighted, ((1,), (0,)), precision=lax.Precision.HIGHEST)
-        scale = jnp.where(row[:, 0:1] % NODES == NODES - 1, 1.0, scale_ref[:, 0:1])
-        err_ref[...] = (joined * scale).astype(BF16)
-        loss = jnp.sum(jnp.sum(weighted * error, axis=0, keepdims=True), axis=1, keepdims=True)
-        loss_ref[...] = jnp.broadcast_to(loss, (8, 128))
+            total = total + dot(block[:, :256], weight_ref[part, i], ((1,), (0,)))
+            total = total + dot(block[:, 256:], weight_ref[part + 8, i], ((1,), (0,)))
+        if part == 0:
+            ahead_ref[...] = total
+        else:
+            ahead_ref[...] += total
+
+    row, lane = same_request()
+    accepted = []
+    for r in range(4):
+        part = slice(r * NODES, (r + 1) * NODES)
+        path = jnp.where(lane[part] == leaf_ref[r] + r * NODES, reach_ref[part].astype(F32), 0.0)
+        path = jnp.sum(path, axis=1, keepdims=True)
+        accepted.append((1.0 + 3.0 * path) * (0.5 + len_ref[r].astype(F32) / CACHE))
+    weights = jnp.concatenate(accepted, axis=0)
+    pick = pick_ref[...].astype(F32)
+    predicted = dot(pick, ahead_ref[...], ((0,), (0,)), precision=lax.Precision.HIGHEST)
+    error = predicted - own_ref[...].astype(F32)
+    weighted = weights * error
+    joined = dot(pick, weighted, ((1,), (0,)), precision=lax.Precision.HIGHEST)
+    scale = jnp.where(row[:, 0:1] % NODES == NODES - 1, 1.0, scale_ref[:, 0:1])
+    err_ref[...] = (joined * scale).astype(BF16)
+    loss = jnp.sum(jnp.sum(weighted * error, axis=0, keepdims=True), axis=1, keepdims=True)
+    loss_ref[...] = jnp.broadcast_to(loss, (8, 128))
 
 
 def differentiate_kernel(source_ref, column_ref, near_ref, other_ref, loss_ref, grad_ref, pair_ref):
@@ -316,19 +317,32 @@
     )(parcel, out_weight)
 
 
-def settle(rank, along, residual, gain, prev):
+def fold(rank, along):
+    return pl.pallas_call(
+        fold_kernel,
+        out_shape=(jax.ShapeDtypeStruct((128, 512), BF16),) * 4,
+        in_specs=[in_smem(), in_vmem()],
+        out_specs=(in_vmem(),) * 4,
+        cost_estimate=pl.CostEstimate(
+            flops=16 * 128 * 512, bytes_accessed=5 << 19, transcendentals=0
+        ),
+        name="fold",
+    )(rank, along)
+
+
+def settle(rank, terms, residual, gain, prev):
+    whole = pl.BlockSpec((128, 512), lambda p, at: (0, 0))
     return pl.pallas_call(
         settle_kernel,
         grid_spec=pltpu.PrefetchScalarGridSpec(
             num_scalar_prefetch=1,
             grid=(1,),
-            in_specs=[
-                pl.BlockSpec((4, 128, 512), lambda p, at: (0, 0, 0)),
-                pl.BlockSpec((128, 512), lambda p, at: (0, 0)),
+            in_specs=[whole] * 5
+            + [
                 pl.BlockSpec((1, 1, 512), lambda p, at: (at[0], 0, 0)),
                 pl.BlockSpec((4, 512), lambda p, at: (0, at[0])),
             ],
-            out_specs=[pl.BlockSpec((128, 512), lambda p, at: (0, 0))] * 3,
+            out_specs=[whole] * 3,
         ),
         out_shape=(
             jax.ShapeDtypeStruct((128, 512), F32),
@@ -339,40 +353,33 @@
             flops=128 * 512 * 8, bytes_accessed=2 << 20, transcendentals=0
         ),
         name="settle",
-    )(rank, along, residual, gain, prev)
-
-
-def predict(source, rank, lengths, leaf, far, mixed, gain, prev, reach, pick, near, other):
+    )(rank, *terms, residual, gain, prev)
+
+
+def predict(source, rank, lengths, leaf, far, mixed, gain, prev, reach, pick, all_weight):
     return pl.pallas_call(
         predict_kernel,
-        grid=(4,),
         out_shape=(
             jax.ShapeDtypeStruct((128, 512), BF16),
             jax.ShapeDtypeStruct((128, 512), BF16),
             jax.ShapeDtypeStruct((8, 128), F32),
         ),
         in_specs=[in_smem()] * 4
-        + [
-            pl.BlockSpec((4, 4, 128, 512), lambda p: (0, 0, 0, 0)),
-            pl.BlockSpec((128, 512), lambda p: (0, 0)),
-            pl.BlockSpec((N_TP, 1, 512), lambda p: (0, 0, 0)),
-            pl.BlockSpec((4, D), lambda p: (0, 0)),
-            pl.BlockSpec((128, 128), lambda p: (0, 0)),
-            pl.BlockSpec((128, 128), lambda p: (0, 0)),
-            pl.BlockSpec((4, 512, 512), lambda p: (jnp.minimum(p, 1), 0, 0)),
-            pl.BlockSpec((4, 512, 512), lambda p: (jnp.maximum(p - 2, 0), 0, 0)),
+        + [in_vmem()] * 6
+        + [pl.BlockSpec(memory_space=pl.ANY)] * 16,
+        out_specs=(in_vmem(),) * 3,
+        scratch_shapes=[
+            pltpu.VMEM((128, 128), F32),
+            pltpu.VMEM((128, 512), F32),
+            pltpu.VMEM((16, 2, 256, 512), BF16),
+            pltpu.SemaphoreType.DMA((16,)),
         ],
-        out_specs=(
-            pl.BlockSpec((128, 512), lambda p: (0, 0)),
-            pl.BlockSpec((128, 512), lambda p: (0, 0)),
-            pl.BlockSpec((8, 128), lambda p: (0, 0)),
-        ),
-        scratch_shapes=[pltpu.VMEM((128, 128), F32), pltpu.VMEM((128, 512), F32)],
+        compiler_params=pltpu.CompilerParams(vmem_limit_bytes=32 << 20),
         cost_estimate=pl.CostEstimate(
             flops=2 * 128 * 8192 * 512, bytes_accessed=13 << 20, transcendentals=0
         ),
         name="predict",
-    )(source, rank, lengths, leaf, far, mixed, gain, prev, reach, pick, near, other)
+    )(source, rank, lengths, leaf, far, mixed, gain, prev, reach, pick, *all_weight)
 
 
 def differentiate(source, columns, near_err, other_err, loss):
@@ -421,27 +428,33 @@
     )
     place = (source % 4) * 4 + (lax.axis_index("zl") + 4 - source // 4) % 4
 
-    wide_weight = turns(draft_weight, "zh", 2)
+    half = draft_weight.shape[0] // 2
+    upper = passed(draft_weight[:half], "zh", 2)
     parcel, reach, pick = attend(
         rank, lengths, parents, queries, cache_keys, cache_values, tree_keys, tree_values
     )
     parcel = exchange(parcel, TP)
-    parcel, wide_weight = lax.optimization_barrier((parcel, wide_weight))
-    wide_weight = turns(wide_weight, "y", 4)
+    upper = jnp.stack(upper)
+    upper = passed(upper, "y", 4)
+    parcel, lower = lax.optimization_barrier((parcel, draft_weight[half:]))
+    lower = passed(lower, "zh", 2)
 
     partial_value = project(parcel, out_weight)
     along_x = exchange(partial_value, "x")
-    along_x = jnp.sum(along_x.astype(F32), axis=0).astype(BF16)
-    along_x, wide_weight = lax.optimization_barrier((along_x, wide_weight))
-    other_weight = lax.ppermute(wide_weight, "c", turn(2, 1))
-    along_z = exchange(along_x, "zl")
-    mixed, near, table = settle(rank, along_z, residual.reshape(rows, block), gain, prev_feature)
-
+    other_upper = [lax.ppermute(part, "c", turn(2, 1)) for part in upper]
+    lower = jnp.stack(lower)
+    lower = passed(lower, "y", 4)
+    terms = list(fold(rank, along_x))
+    terms[1:] = [lax.ppermute(terms[step], "zl", turn(4, step)) for step in (1, 2, 3)]
+    mixed, near, table = settle(rank, terms, residual.reshape(rows, block), gain, prev_feature)
+
+    far = turns(near, "zl", 4)
+    far, table = lax.optimization_barrier((far, table))
+    far = spread(far, "x", 4).reshape(4, 4, rows, block)
     swapped = lax.ppermute(
         table, REQ + TP, [(i * N_TP + j, j * N_TP + i) for i in range(16) for j in range(16)]
     )
-    far = gather(near[None], "zl")
-    far = spread(far, "x", 4).reshape(4, 4, rows, block)
+    other_lower = [lax.ppermute(part, "c", turn(2, 1)) for part in lower]
     swapped, far = lax.optimization_barrier((swapped, far))
     columns = turns(swapped, "zl", 4)
     own_features, scaled_err, loss = predict(
@@ -455,8 +468,7 @@
         prev_feature,
         reach,
         pick,
-        wide_weight.reshape(8, block, block),
-        other_weight.reshape(8, block, block),
+        upper + other_upper + lower + other_lower,
     )
     columns, scaled_err = lax.optimization_barrier((columns, scaled_err))
     columns = spread(columns, "x", 4).reshape(N_REQ, rows, block)

time: 295 us -> 264 us (0.89)
  waiting for transfers between devices: 133 us -> 92.1 us
  blocking collectives: 58 us -> 21.2 us
  starting transfers between devices: 55.9 us -> 92.4 us
  local copies, waits for them, and re-layouts: 6.1 us -> 15 us
    ppermute x12 -> x29, waiting for transfers between devices: 110 us -> 40.7 us  [the longest x18 34.1 us: passed(): lax.ppermute(value, axis, turn(count, step))]
    all_to_all x4, waiting for transfers between devices: 0.72 us -> 48.9 us  [exchange(): return lax.all_to_all(value, axis, 0, 0, tiled=True)]
    ppermute x12 -> x29, starting transfers between devices: 20.2 us -> 62.6 us  [the longest x18 36.6 us: passed(): lax.ppermute(value, axis, turn(count, step))]
    all_to_all x2 -> x1, blocking collectives: 45.2 us -> 21.2 us  [exchange(): return lax.all_to_all(value, axis, 0, 0, tiled=True)]
    ppermute x1, waiting for transfers between devices: 20.2 us -> 0.01 us  [body(): lax.ppermute(table, REQ + TP, [(i * N_TP + j, j * N_TP + i) for i in rang...]
    all_gather x1 -> x0, blocking collectives: 12.8 us -> none  [gather(): return lax.all_gather(value, axis, axis=0, tiled=True)]
    unnamed x14 -> x46, local copies, waits for them, and re-layouts: 2.38 us -> 11.3 us
    all_to_all x4, starting transfers between devices: 27.2 us -> 24.1 us  [exchange(): return lax.all_to_all(value, axis, 0, 0, tiled=True)]
  transfers between devices with their start and end apart: 18 -> 35, of which waited for: 12 -> 13; matrix products, arithmetic and copies ran while one was open for 2% -> 3% of each run, Pallas kernels for 1% -> 4%
where the time goes in v4:
time: 264 us; the launch traced here: 263 us
  starting transfers between devices  92.4 us (35%)
  waiting for transfers between devices  92.1 us (35%)
  Pallas kernels  30 us (11%)
  blocking collectives  21.2 us (8%)
  local copies, waits for them, and re-layouts  15 us (6%)
  other arithmetic  9 us (3%)
  between operations  3.42 us (1%)
    all_to_all x4, waiting for transfers between devices, exchange(): return lax.all_to_all(value, axis, 0, 0, tiled=True)  48.9 us
    ppermute x18, starting transfers between devices, passed(): lax.ppermute(value, axis, turn(count, step))  36.6 us
    ppermute x18, waiting for transfers between devices, passed(): lax.ppermute(value, axis, turn(count, step))  34.1 us
    all_to_all x4, starting transfers between devices, exchange(): return lax.all_to_all(value, axis, 0, 0, tiled=True)  24.1 us
    all_to_all x1, blocking collectives, exchange(): return lax.all_to_all(value, axis, 0, 0, tiled=True)  21.2 us
    ppermute x4, starting transfers between devices, body(): other_lower = [lax.ppermute(part, 'c', turn(2, 1)) for part in lower]  14 us
    unnamed x46, local copies, waits for them, and re-layouts  11.3 us
    pallas_call x1, Pallas kernels, attend(): pl.pallas_call(attend_kernel, out_shape=(jax.ShapeDtypeStruct((N_TP, 144,...  9.24 us
  transfers between devices with their start and end apart: 35, of which 13 were waited for; matrix products, arithmetic and copies ran while one was open for 3% of the time, Pallas kernels for 4%

profile of v4, /device:TPU:1, one launch (start us, length us, event | category | flops | bytes accessed | tf_op | source)
XLA Modules:
  0.0 263.0 jit_solution(9968536375131224028)
XLA Ops:
  0.7 9.2 %attend.1 = (bf16[16,144,256]{2,1,0:T(8,128)(2,1)}, bf16[128,128]{1,0:T(8,128)(2,1)}, bf16[128,128]{1,0:T(8,128)(2,1)}) custom-call(s32[1]{0:T(128)} %bitcast.rank_ref, s32[4]{0:T(128)} %len_ref.3, s32[4,32]{1,0:T(4,128)} %par_ref.1, bf16[4,32,4096]{2,1,0:T(8,128)(2,1)} %q_ref.1, bf16[4,256,512]{2,1,0:T(8,128)(2,1)} %ck_ref.1, bf16[4,256,512]{2,1,0:T(8,128)(2,1)} %cv_ref.1, ...), custom_call_target="tpu_custom_call" | custom-call | flops 536870912 | bytes 4194304 | tf_op jit(solution)/shard_map/attend/pallas_call | solution.py:285
  9.9 9.0 %all-to-all-start = ((bf16[16,144,256]{2,1,0:T(8,128)(2,1)}), bf16[16,144,256]{2,1,0:T(8,128)(2,1)S(1)}, u32[]{:S(2)}, u32[]{:S(2)}) async-start(bf16[16,144,256]{2,1,0:T(8,128)(2,1)} %get-tuple-element.28), calls=%async_computation | async-start | bytes 2359296 | tf_op jit(solution)/shard_map/all_to_all | solution.py:35
  19.0 24.4 %all-to-all-done.parcel_ref = bf16[16,144,256]{2,1,0:T(8,128)(2,1)S(1)} async-done(((bf16[16,144,256]{2,1,0:T(8,128)(2,1)}), bf16[16,144,256]{2,1,0:T(8,128)(2,1)S(1)}, u32[]{:S(2)}, u32[]{:S(2)}) %all-to-all-start) | async-done | bytes 1179680 | tf_op jit(solution)/shard_map/all_to_all | solution.py:35
  43.4 1.0 copy-done.16
  44.4 5.9 %project.1 = bf16[4,4,128,512]{3,2,1,0:T(8,128)(2,1)} custom-call(bf16[16,144,256]{2,1,0:T(8,128)(2,1)} %copy-done.16, bf16[256,8192]{1,0:T(8,128)(2,1)} %weight_ref.1), custom_call_target="tpu_custom_call" | custom-call | flops 536870912 | bytes 7340032 | tf_op jit(solution)/shard_map/project/pallas_call | solution.py:303
  50.4 4.9 %all-to-all-start.1 = ((bf16[4,4,128,512]{3,2,1,0:T(8,128)(2,1)}), bf16[4,4,128,512]{3,2,1,0:T(8,128)(2,1)S(1)}, u32[]{:S(2)}, u32[]{:S(2)}) async-start(bf16[4,4,128,512]{3,2,1,0:T(8,128)(2,1)} %project.1), calls=%async_computation.1 | async-start | bytes 4194304 | tf_op jit(solution)/shard_map/all_to_all | solution.py:35
  55.3 4.2 %collective-permute-start.7 = (bf16[256,512]{1,0:T(8,128)(2,1)S(1)}, bf16[256,512]{1,0:T(8,128)(2,1)S(1)}, u32[]{:S(2)}, u32[]{:S(2)}) collective-permute-start(bf16[256,512]{1,0:T(8,128)(2,1)S(1)} %get-tuple-element.58), channel_id=1, source_target_pairs={{0,128},{128,0},{1,129},{129,1},{2,130},{130,2},{3,131},{131,3},{4... | collective-permute-start | bytes 786440 | tf_op jit(solution)/shard_map/ppermute | solution.py:48
  59.5 19.5 %all-to-all-done.1.along_ref = bf16[4,4,128,512]{3,2,1,0:T(8,128)(2,1)S(1)} async-done(((bf16[4,4,128,512]{3,2,1,0:T(8,128)(2,1)}), bf16[4,4,128,512]{3,2,1,0:T(8,128)(2,1)S(1)}, u32[]{:S(2)}, u32[]{:S(2)}) %all-to-all-start.1) | async-done | bytes 2097184 | tf_op jit(solution)/shard_map/all_to_all | solution.py:35
  79.1 1.3 copy-done.15
  80.4 2.6 fold.1
  83.0 4.4 %collective-permute-start = (bf16[128,512]{1,0:T(8,128)(2,1)}, bf16[128,512]{1,0:T(8,128)(2,1)S(1)}, u32[]{:S(2)}, u32[]{:S(2)}) collective-permute-start(bf16[128,512]{1,0:T(8,128)(2,1)} %get-tuple-element.31), channel_id=1, source_target_pairs={{0,4},{4,8},{8,12},{12,0},{1,5},{5,9},{9,13},{13,1},{2,6},{6,10},{... | collective-permute-start | bytes 393224 | tf_op jit(solution)/shard_map/ppermute | solution.py:448
  87.4 1.4 collective-permute-start.1
  88.7 2.4 collective-permute-start.2
  91.1 6.5 %collective-permute-done.1.two_ref = bf16[128,512]{1,0:T(8,128)(2,1)S(1)} collective-permute-done((bf16[128,512]{1,0:T(8,128)(2,1)}, bf16[128,512]{1,0:T(8,128)(2,1)S(1)}, u32[]{:S(2)}, u32[]{:S(2)}) %collective-permute-start.1) | collective-permute-done | bytes 131104 | tf_op jit(solution)/shard_map/ppermute | solution.py:448
  97.6 0.6 copy-done.21
  98.3 2.1 settle.1
  100.4 4.4 %collective-permute-start.5 = (bf16[128,512]{1,0:T(8,128)(2,1)}, bf16[128,512]{1,0:T(8,128)(2,1)S(1)}, u32[]{:S(2)}, u32[]{:S(2)}) collective-permute-start(bf16[128,512]{1,0:T(8,128)(2,1)} %get-tuple-element.34), channel_id=1, source_target_pairs={{0,12},{4,0},{8,4},{12,8},{1,13},{5,1},{9,5},{13,9},{2,14},{6,2},{... | collective-permute-start | bytes 393224 | tf_op jit(solution)/shard_map/ppermute | solution.py:48
  105.1 1.6 collective-permute-start.8
  106.7 2.6 collective-permute-start.9
  109.3 7.0 %collective-permute-done.4 = bf16[128,512]{1,0:T(8,128)(2,1)S(1)} collective-permute-done((bf16[128,512]{1,0:T(8,128)(2,1)}, bf16[128,512]{1,0:T(8,128)(2,1)S(1)}, u32[]{:S(2)}, u32[]{:S(2)}) %collective-permute-start.4) | collective-permute-done | bytes 131104 | tf_op jit(solution)/shard_map/ppermute | solution.py:48
  116.3 1.0 pad_maximum_fusion.1
  117.2 1.5 broadcast_in_dim.4
  118.8 3.8 %all-to-all-start.2 = ((bf16[16,128,512]{2,1,0:T(8,128)(2,1)}), bf16[16,128,512]{2,1,0:T(8,128)(2,1)S(1)}, u32[]{:S(2)}, u32[]{:S(2)}) async-start(bf16[16,128,512]{2,1,0:T(8,128)(2,1)} %bitcast.35), calls=%async_computation.2 | async-start | bytes 4194304 | tf_op jit(solution)/shard_map/all_to_all | solution.py:35
  122.6 2.8 %collective-permute-start.10 = (bf16[2,256,512]{2,1,0:T(8,128)(2,1)S(1)}, bf16[2,256,512]{2,1,0:T(8,128)(2,1)}, u32[]{:S(2)}, u32[]{:S(2)}) collective-permute-start(bf16[2,256,512]{2,1,0:T(8,128)(2,1)S(1)} %pad_maximum_fusion.2.refs_0_), channel_id=1, source_target_pairs={{0,96},{32,0},{64,32},{96,64},{1,97},{33,1},{65,33},{97,65},{2,98}... | collective-permute-start | bytes 1572872 | tf_op jit(solution)/shard_map/ppermute | solution.py:48
  125.4 1.8 collective-permute-start.11
  127.2 4.2 %collective-permute-start.15 = (bf16[256,512]{1,0:T(8,128)(2,1)S(1)}, bf16[256,512]{1,0:T(8,128)(2,1)S(1)}, u32[]{:S(2)}, u32[]{:S(2)}) collective-permute-start(bf16[256,512]{1,0:T(8,128)(2,1)S(1)} %get-tuple-element.42), channel_id=1, source_target_pairs={{0,128},{128,0},{1,129},{129,1},{2,130},{130,2},{3,131},{131,3},{4... | collective-permute-start | bytes 786440 | tf_op jit(solution)/shard_map/ppermute | solution.py:48
  131.7 1.8 collective-permute-start.13
  133.5 6.7 %collective-permute-done.15 = bf16[256,512]{1,0:T(8,128)(2,1)S(1)} collective-permute-done((bf16[256,512]{1,0:T(8,128)(2,1)S(1)}, bf16[256,512]{1,0:T(8,128)(2,1)S(1)}, u32[]{:S(2)}, u32[]{:S(2)}) %collective-permute-start.15) | collective-permute-done | bytes 262176 | tf_op jit(solution)/shard_map/ppermute | solution.py:48
  140.2 1.0 pad_maximum_fusion.3.refs_8_
  141.3 1.6 collective-permute-start.17
  142.9 0.8 copy-done
  143.7 1.0 collective-permute-start.18
  144.7 0.8 copy-done.2
  145.5 4.9 %collective-permute-start.6 = (bf16[128,512]{1,0:T(8,128)(2,1)}, bf16[128,512]{1,0:T(8,128)(2,1)}, u32[]{:S(2)}, u32[]{:S(2)}) collective-permute-start(bf16[128,512]{1,0:T(8,128)(2,1)} %get-tuple-element.36), channel_id=1, source_target_pairs={{0,0},{1,16},{2,32},{3,48},{4,64},{5,80},{6,96},{7,112},{8,128},{9... | collective-permute-start | bytes 393224 | tf_op jit(solution)/shard_map/ppermute | solution.py:454
  150.4 0.8 copy-done.4
  151.2 4.9 %collective-permute-done.16.refs_9_ = bf16[2,256,512]{2,1,0:T(8,128)(2,1)} collective-permute-done((bf16[2,256,512]{2,1,0:T(8,128)(2,1)S(1)}, bf16[2,256,512]{2,1,0:T(8,128)(2,1)}, u32[]{:S(2)}, u32[]{:S(2)}) %collective-permute-start.16) | collective-permute-done | bytes 524320 | tf_op jit(solution)/shard_map/ppermute | solution.py:48
  156.2 12.0 %collective-permute-start.19 = (bf16[2,256,512]{2,1,0:T(8,128)(2,1)S(1)}, bf16[2,256,512]{2,1,0:T(8,128)(2,1)}, u32[]{:S(2)}, u32[]{:S(2)}) collective-permute-start(bf16[2,256,512]{2,1,0:T(8,128)(2,1)S(1)} %pad_maximum_fusion.3.refs_8_), channel_id=1, source_target_pairs={{0,16},{16,0},{1,17},{17,1},{2,18},{18,2},{3,19},{19,3},{4,20},{20... | collective-permute-start | bytes 1572872 | tf_op jit(solution)/shard_map/ppermute | solution.py:457
  168.1 0.6 collective-permute-done.17.refs_10_
  168.8 1.5 collective-permute-start.20
  170.8 3.8 %collective-permute-start.25 = (bf16[128,512]{1,0:T(8,128)(2,1)}, bf16[128,512]{1,0:T(8,128)(2,1)S(1)}, u32[]{:S(2)}, u32[]{:S(2)}) collective-permute-start(bf16[128,512]{1,0:T(8,128)(2,1)} %collective-permute-done.6), channel_id=1, source_target_pairs={{0,12},{4,0},{8,4},{12,8},{1,13},{5,1},{9,5},{13,9},{2,14},{6,2},{... | collective-permute-start | bytes 393224 | tf_op jit(solution)/shard_map/ppermute | solution.py:48
  174.6 4.0 %collective-permute-start.24 = (bf16[128,512]{1,0:T(8,128)(2,1)}, bf16[128,512]{1,0:T(8,128)(2,1)S(1)}, u32[]{:S(2)}, u32[]{:S(2)}) collective-permute-start(bf16[128,512]{1,0:T(8,128)(2,1)} %collective-permute-done.6), channel_id=1, source_target_pairs={{0,8},{4,12},{8,0},{12,4},{1,9},{5,13},{9,1},{13,5},{2,10},{6,14},... | collective-permute-start | bytes 393224 | tf_op jit(solution)/shard_map/ppermute | solution.py:48
  179.3 1.0 copy-done.1
  180.4 1.0 copy-done.3
  181.4 1.0 copy-done.5
  182.5 0.8 copy-done.10
  183.2 5.7 %predict.1 = (bf16[128,512]{1,0:T(8,128)(2,1)}, bf16[128,512]{1,0:T(8,128)(2,1)}, f32[8,128]{1,0:T(8,128)S(1)}) custom-call(s32[16]{0:T(128)S(1)} %get-tuple-element.55.source_ref, s32[1]{0:T(128)} %bitcast.rank_ref, s32[4]{0:T(128)S(1)} %copy-done.12, s32[4]{0:T(128)S(1)} %copy-done.13, bf16[4,4,128,512]{3,2,1,0:T(8,128)(2,1)S(1)} %bitcast.32, ...), custom_call_target="tpu_custom_call" | custom-call | flops 1073741824 | bytes 13631488 | tf_op jit(solution)/shard_map/predict/pallas_call | solution.py:360
  189.5 1.2 collective-permute-done.24
  190.7 1.0 pad_maximum_fusion.4
  191.7 4.3 %collective-permute-start.26 = (bf16[128,512]{1,0:T(8,128)(2,1)}, bf16[128,512]{1,0:T(8,128)(2,1)S(1)}, u32[]{:S(2)}, u32[]{:S(2)}) collective-permute-start(bf16[128,512]{1,0:T(8,128)(2,1)} %get-tuple-element.47), channel_id=1, source_target_pairs={{0,128},{128,0},{1,129},{129,1},{2,130},{130,2},{3,131},{131,3},{4... | collective-permute-start | bytes 393224 | tf_op jit(solution)/shard_map/ppermute | solution.py:48
  196.0 1.5 broadcast_in_dim.5
  197.5 6.4 %all-to-all-start.3 = ((bf16[16,128,512]{2,1,0:T(8,128)(2,1)}), bf16[16,128,512]{2,1,0:T(8,128)(2,1)S(1)}, u32[]{:S(2)}, u32[]{:S(2)}) async-start(bf16[16,128,512]{2,1,0:T(8,128)(2,1)} %bitcast.36), calls=%async_computation.3 | async-start | bytes 4194304 | tf_op jit(solution)/shard_map/all_to_all | solution.py:35
  203.9 0.9 fusion.15
  205.0 0.9 collective-permute-start.28
  206.4 4.6 %collective-permute-done.29 = bf16[2,128,512]{2,1,0:T(8,128)(2,1)S(1)} collective-permute-done((bf16[2,128,512]{2,1,0:T(8,128)(2,1)S(1)}, bf16[2,128,512]{2,1,0:T(8,128)(2,1)S(1)}, u32[]{:S(2)}, u32[]{:S(2)}) %collective-permute-start.29) | collective-permute-done | bytes 262176 | tf_op jit(solution)/shard_map/ppermute | solution.py:48
  211.0 0.9 collective-permute-done.28
  211.9 8.2 %collective-permute-done.27 = bf16[2,128,512]{2,1,0:T(8,128)(2,1)S(1)} collective-permute-done((bf16[2,128,512]{2,1,0:T(8,128)(2,1)S(1)}, bf16[2,128,512]{2,1,0:T(8,128)(2,1)S(1)}, u32[]{:S(2)}, u32[]{:S(2)}) %collective-permute-start.27) | collective-permute-done | bytes 262176 | tf_op jit(solution)/shard_map/ppermute | solution.py:48
  220.3 0.9 collective-permute-start.30
  221.1 2.4 collective-permute-done.30.other_ref
  223.5 5.0 %all-to-all-done.3.column_ref = bf16[16,128,512]{2,1,0:T(8,128)(2,1)S(1)} async-done(((bf16[16,128,512]{2,1,0:T(8,128)(2,1)}), bf16[16,128,512]{2,1,0:T(8,128)(2,1)S(1)}, u32[]{:S(2)}, u32[]{:S(2)}) %all-to-all-start.3) | async-done | bytes 2097184 | tf_op jit(solution)/shard_map/all_to_all | solution.py:35
  228.6 1.3 copy-done.14
  229.9 4.5 %differentiate.1 = (f32[512,512]{1,0:T(8,128)}, f32[256,128]{1,0:T(8,128)}) custom-call(s32[16]{0:T(128)} %get-tuple-element.54.source_ref, bf16[16,128,512]{2,1,0:T(8,128)(2,1)} %copy-done.14, bf16[4,2,128,512]{3,2,1,0:T(8,128)(2,1)} %copy-done.17, bf16[4,2,128,512]{3,2,1,0:T(8,128)(2,1)} %collective-permute-done.30.other_ref, f32[8,128]{1,0:T(8,128)} %copy-done.11), custom_call_target="tpu_custom_call" | custom-call | flops 1073741824 | bytes 5242880 | tf_op jit(solution)/shard_map/differentiate/pallas_call | solution.py:386
  234.4 21.2 %all_to_all.29 = f32[256,1,128]{2,1,0:T(1,128)S(1)} all-to-all(f32[256,1,128]{2,1,0:T(1,128)} %bitcast.44), channel_id=1, replica_groups=mesh['zh'=2,'y'=4,'c'=2,'zl'=4,'x'=4] {'zh','y','c','zl','x'}, dimensions={0} | all-to-all | bytes 262144 | tf_op jit(solution)/shard_map/all_to_all | solution.py:35
  255.8 0.6 fusion.18
  257.8 4.1 %subtract_convert_fusion = (bf16[512,512]{1,0:T(8,128)(2,1)}, f32[512,512]{1,0:T(8,128)}, f32[512,512]{1,0:T(8,128)}) fusion(bf16[512,512]{1,0:T(8,128)(2,1)} %param.27, f32[512,512]{1,0:T(8,128)} %get-tuple-element.49, f32[]{:T(128)} %bitcast.27, f32[512,512]{1,0:T(8,128)} %param.28, f32[512,512]{1,0:T(8,128)} %param.29), kind=kLoop, calls=%fused_computation.3 | loop fusion | flops 4194304 | bytes 6291460 | tf_op jit(solution)/shard_map/convert_element_type | solution.py:488
  (72 shorter events, 3.8 us)
Async XLA Ops:
  0.6 18.3 %copy-start.18 = (bf16[512,512]{1,0:T(8,128)(2,1)S(1)}, bf16[512,512]{1,0:T(8,128)(2,1)}, u32[]{:S(2)}) copy-start(bf16[512,512]{1,0:T(8,128)(2,1)} %param.27) | copy-start | bytes 1572868
  9.9 33.5 %all-to-all-start = ((bf16[16,144,256]{2,1,0:T(8,128)(2,1)}), bf16[16,144,256]{2,1,0:T(8,128)(2,1)S(1)}, u32[]{:S(2)}, u32[]{:S(2)}) async-start(bf16[16,144,256]{2,1,0:T(8,128)(2,1)} %get-tuple-element.28), calls=%async_computation | async-start | bytes 2359296 | tf_op jit(solution)/shard_map/all_to_all | solution.py:35
  19.0 108.2 %copy-start.19 = (bf16[256,512]{1,0:T(8,128)(2,1)}, bf16[256,512]{1,0:T(8,128)(2,1)S(1)}, u32[]{:S(2)}) copy-start(bf16[256,512]{1,0:T(8,128)(2,1)S(1)} %get-tuple-element.42) | copy-start | bytes 786436
  43.4 1.0 copy-start.16
  50.4 28.7 %all-to-all-start.1 = ((bf16[4,4,128,512]{3,2,1,0:T(8,128)(2,1)}), bf16[4,4,128,512]{3,2,1,0:T(8,128)(2,1)S(1)}, u32[]{:S(2)}, u32[]{:S(2)}) async-start(bf16[4,4,128,512]{3,2,1,0:T(8,128)(2,1)} %project.1), calls=%async_computation.1 | async-start | bytes 4194304 | tf_op jit(solution)/shard_map/all_to_all | solution.py:35
  55.3 49.7 %collective-permute-start.7 = (bf16[256,512]{1,0:T(8,128)(2,1)S(1)}, bf16[256,512]{1,0:T(8,128)(2,1)S(1)}, u32[]{:S(2)}, u32[]{:S(2)}) collective-permute-start(bf16[256,512]{1,0:T(8,128)(2,1)S(1)} %get-tuple-element.58), channel_id=1, source_target_pairs={{0,128},{128,0},{1,129},{129,1},{2,130},{130,2},{3,131},{131,3},{4... | collective-permute-start | bytes 786440 | tf_op jit(solution)/shard_map/ppermute | solution.py:48
  79.1 1.3 copy-start.15
  83.0 8.1 %collective-permute-start = (bf16[128,512]{1,0:T(8,128)(2,1)}, bf16[128,512]{1,0:T(8,128)(2,1)S(1)}, u32[]{:S(2)}, u32[]{:S(2)}) collective-permute-start(bf16[128,512]{1,0:T(8,128)(2,1)} %get-tuple-element.31), channel_id=1, source_target_pairs={{0,4},{4,8},{8,12},{12,0},{1,5},{5,9},{9,13},{13,1},{2,6},{6,10},{... | collective-permute-start | bytes 393224 | tf_op jit(solution)/shard_map/ppermute | solution.py:448
  87.4 10.2 %collective-permute-start.1 = (bf16[128,512]{1,0:T(8,128)(2,1)}, bf16[128,512]{1,0:T(8,128)(2,1)S(1)}, u32[]{:S(2)}, u32[]{:S(2)}) collective-permute-start(bf16[128,512]{1,0:T(8,128)(2,1)} %get-tuple-element.32), channel_id=1, source_target_pairs={{0,8},{4,12},{8,0},{12,4},{1,9},{5,13},{9,1},{13,5},{2,10},{6,14},... | collective-permute-start | bytes 393224 | tf_op jit(solution)/shard_map/ppermute | solution.py:448
  88.7 8.9 %collective-permute-start.2 = (bf16[128,512]{1,0:T(8,128)(2,1)}, bf16[128,512]{1,0:T(8,128)(2,1)S(1)}, u32[]{:S(2)}, u32[]{:S(2)}) collective-permute-start(bf16[128,512]{1,0:T(8,128)(2,1)} %get-tuple-element.33), channel_id=1, source_target_pairs={{0,12},{4,0},{8,4},{12,8},{1,13},{5,1},{9,5},{13,9},{2,14},{6,2},{... | collective-permute-start | bytes 393224 | tf_op jit(solution)/shard_map/ppermute | solution.py:448
  91.1 6.5 %copy-start.20 = (bf16[128,512]{1,0:T(8,128)(2,1)}, bf16[128,512]{1,0:T(8,128)(2,1)S(1)}, u32[]{:S(2)}) copy-start(bf16[128,512]{1,0:T(8,128)(2,1)S(1)} %collective-permute-done.one_ref) | copy-start | bytes 393220
  97.6 0.7 copy-start.21
  97.6 0.7 copy-start.22
  100.4 8.9 %collective-permute-start.5 = (bf16[128,512]{1,0:T(8,128)(2,1)}, bf16[128,512]{1,0:T(8,128)(2,1)S(1)}, u32[]{:S(2)}, u32[]{:S(2)}) collective-permute-start(bf16[128,512]{1,0:T(8,128)(2,1)} %get-tuple-element.34), channel_id=1, source_target_pairs={{0,12},{4,0},{8,4},{12,8},{1,13},{5,1},{9,5},{13,9},{2,14},{6,2},{... | collective-permute-start | bytes 393224 | tf_op jit(solution)/shard_map/ppermute | solution.py:48
  104.8 11.5 %collective-permute-start.4 = (bf16[128,512]{1,0:T(8,128)(2,1)}, bf16[128,512]{1,0:T(8,128)(2,1)S(1)}, u32[]{:S(2)}, u32[]{:S(2)}) collective-permute-start(bf16[128,512]{1,0:T(8,128)(2,1)} %get-tuple-element.34), channel_id=1, source_target_pairs={{0,8},{4,12},{8,0},{12,4},{1,9},{5,13},{9,1},{13,5},{2,10},{6,14},... | collective-permute-start | bytes 393224 | tf_op jit(solution)/shard_map/ppermute | solution.py:48
  104.8 11.5 %collective-permute-start.3 = (bf16[128,512]{1,0:T(8,128)(2,1)}, bf16[128,512]{1,0:T(8,128)(2,1)S(1)}, u32[]{:S(2)}, u32[]{:S(2)}) collective-permute-start(bf16[128,512]{1,0:T(8,128)(2,1)} %get-tuple-element.34), channel_id=1, source_target_pairs={{0,4},{4,8},{8,12},{12,0},{1,5},{5,9},{9,13},{13,1},{2,6},{6,10},{... | collective-permute-start | bytes 393224 | tf_op jit(solution)/shard_map/ppermute | solution.py:48
  105.1 26.3 %collective-permute-start.8 = (bf16[2,256,512]{2,1,0:T(8,128)(2,1)S(1)}, bf16[2,256,512]{2,1,0:T(8,128)(2,1)}, u32[]{:S(2)}, u32[]{:S(2)}) collective-permute-start(bf16[2,256,512]{2,1,0:T(8,128)(2,1)S(1)} %pad_maximum_fusion.2.refs_0_), channel_id=1, source_target_pairs={{0,32},{32,64},{64,96},{96,0},{1,33},{33,65},{65,97},{97,1},{2,34}... | collective-permute-start | bytes 1572872 | tf_op jit(solution)/shard_map/ppermute | solution.py:48
  106.7 25.0 %collective-permute-start.9 = (bf16[2,256,512]{2,1,0:T(8,128)(2,1)S(1)}, bf16[2,256,512]{2,1,0:T(8,128)(2,1)}, u32[]{:S(2)}, u32[]{:S(2)}) collective-permute-start(bf16[2,256,512]{2,1,0:T(8,128)(2,1)S(1)} %pad_maximum_fusion.2.refs_0_), channel_id=1, source_target_pairs={{0,64},{32,96},{64,0},{96,32},{1,65},{33,97},{65,1},{97,33},{2,66}... | collective-permute-start | bytes 1572872 | tf_op jit(solution)/shard_map/ppermute | solution.py:48
  118.8 60.5 %copy-start.6 = (bf16[4,8192]{1,0:T(4,128)(2,1)S(1)}, bf16[4,8192]{1,0:T(4,128)(2,1)}, u32[]{:S(2)}) copy-start(bf16[4,8192]{1,0:T(4,128)(2,1)} %prev_ref.3) | copy-start | bytes 196612
  118.8 60.5 %copy-start.7 = (f32[128,512]{1,0:T(8,128)S(1)}, f32[128,512]{1,0:T(8,128)}, u32[]{:S(2)}) copy-start(f32[128,512]{1,0:T(8,128)} %get-tuple-element.39.mixed_ref) | copy-start | bytes 786436
  118.8 60.5 %copy-start.8 = (f32[8192]{0:T(1024)S(1)}, f32[8192]{0:T(1024)}, u32[]{:S(2)}) copy-start(f32[8192]{0:T(1024)} %param.24) | copy-start | bytes 98308
  118.8 60.5 %copy-start.9 = (bf16[128,128]{1,0:T(8,128)(2,1)S(1)}, bf16[128,128]{1,0:T(8,128)(2,1)}, u32[]{:S(2)}) copy-start(bf16[128,128]{1,0:T(8,128)(2,1)} %get-tuple-element.40.reach_ref) | copy-start | bytes 98308
  118.8 60.5 %copy-start.12 = (s32[4]{0:T(128)S(1)}, s32[4]{0:T(128)}, u32[]{:S(2)}) copy-start(s32[4]{0:T(128)} %len_ref.3) | copy-start | bytes 52
  118.8 60.5 %copy-start.13 = (s32[4]{0:T(128)S(1)}, s32[4]{0:T(128)}, u32[]{:S(2)}) copy-start(s32[4]{0:T(128)} %leaf_ref.1) | copy-start | bytes 52
  118.8 51.9 %all-to-all-start.2 = ((bf16[16,128,512]{2,1,0:T(8,128)(2,1)}), bf16[16,128,512]{2,1,0:T(8,128)(2,1)S(1)}, u32[]{:S(2)}, u32[]{:S(2)}) async-start(bf16[16,128,512]{2,1,0:T(8,128)(2,1)} %bitcast.35), calls=%async_computation.2 | async-start | bytes 4194304 | tf_op jit(solution)/shard_map/all_to_all | solution.py:35
  122.6 18.7 %collective-permute-start.10 = (bf16[2,256,512]{2,1,0:T(8,128)(2,1)S(1)}, bf16[2,256,512]{2,1,0:T(8,128)(2,1)}, u32[]{:S(2)}, u32[]{:S(2)}) collective-permute-start(bf16[2,256,512]{2,1,0:T(8,128)(2,1)S(1)} %pad_maximum_fusion.2.refs_0_), channel_id=1, source_target_pairs={{0,96},{32,0},{64,32},{96,64},{1,97},{33,1},{65,33},{97,65},{2,98}... | collective-permute-start | bytes 1572872 | tf_op jit(solution)/shard_map/ppermute | solution.py:48
  125.4 17.5 %collective-permute-start.11 = (bf16[2,256,512]{2,1,0:T(8,128)(2,1)S(1)}, bf16[2,256,512]{2,1,0:T(8,128)(2,1)S(1)}, u32[]{:S(2)}, u32[]{:S(2)}) collective-permute-start(bf16[2,256,512]{2,1,0:T(8,128)(2,1)S(1)} %pad_maximum_fusion.2.refs_0_), channel_id=1, source_target_pairs={{0,16},{16,0},{1,17},{17,1},{2,18},{18,2},{3,19},{19,3},{4,20},{20... | collective-permute-start | bytes 1572872 | tf_op jit(solution)/shard_map/ppermute | solution.py:444
  127.2 13.0 %collective-permute-start.15 = (bf16[256,512]{1,0:T(8,128)(2,1)S(1)}, bf16[256,512]{1,0:T(8,128)(2,1)S(1)}, u32[]{:S(2)}, u32[]{:S(2)}) collective-permute-start(bf16[256,512]{1,0:T(8,128)(2,1)S(1)} %get-tuple-element.42), channel_id=1, source_target_pairs={{0,128},{128,0},{1,129},{129,1},{2,130},{130,2},{3,131},{131,3},{4... | collective-permute-start | bytes 786440 | tf_op jit(solution)/shard_map/ppermute | solution.py:48
  131.4 13.4 %collective-permute-start.12 = (bf16[2,256,512]{2,1,0:T(8,128)(2,1)}, bf16[2,256,512]{2,1,0:T(8,128)(2,1)S(1)}, u32[]{:S(2)}, u32[]{:S(2)}) collective-permute-start(bf16[2,256,512]{2,1,0:T(8,128)(2,1)} %collective-permute-done.8.refs_1_), channel_id=1, source_target_pairs={{0,16},{16,0},{1,17},{17,1},{2,18},{18,2},{3,19},{19,3},{4,20},{20... | collective-permute-start | bytes 1572872 | tf_op jit(solution)/shard_map/ppermute | solution.py:444
  131.7 18.8 %collective-permute-start.13 = (bf16[2,256,512]{2,1,0:T(8,128)(2,1)}, bf16[2,256,512]{2,1,0:T(8,128)(2,1)S(1)}, u32[]{:S(2)}, u32[]{:S(2)}) collective-permute-start(bf16[2,256,512]{2,1,0:T(8,128)(2,1)} %collective-permute-done.9.refs_2_), channel_id=1, source_target_pairs={{0,16},{16,0},{1,17},{17,1},{2,18},{18,2},{3,19},{19,3},{4,20},{20... | collective-permute-start | bytes 1572872 | tf_op jit(solution)/shard_map/ppermute | solution.py:444
  141.2 15.0 %collective-permute-start.16 = (bf16[2,256,512]{2,1,0:T(8,128)(2,1)S(1)}, bf16[2,256,512]{2,1,0:T(8,128)(2,1)}, u32[]{:S(2)}, u32[]{:S(2)}) collective-permute-start(bf16[2,256,512]{2,1,0:T(8,128)(2,1)S(1)} %pad_maximum_fusion.3.refs_8_), channel_id=1, source_target_pairs={{0,32},{32,64},{64,96},{96,0},{1,33},{33,65},{65,97},{97,1},{2,34}... | collective-permute-start | bytes 1572872 | tf_op jit(solution)/shard_map/ppermute | solution.py:48
  141.3 27.5 %collective-permute-start.17 = (bf16[2,256,512]{2,1,0:T(8,128)(2,1)S(1)}, bf16[2,256,512]{2,1,0:T(8,128)(2,1)}, u32[]{:S(2)}, u32[]{:S(2)}) collective-permute-start(bf16[2,256,512]{2,1,0:T(8,128)(2,1)S(1)} %pad_maximum_fusion.3.refs_8_), channel_id=1, source_target_pairs={{0,64},{32,96},{64,0},{96,32},{1,65},{33,97},{65,1},{97,33},{2,66}... | collective-permute-start | bytes 1572872 | tf_op jit(solution)/shard_map/ppermute | solution.py:48
  142.9 0.8 copy-start
  143.7 26.6 %collective-permute-start.18 = (bf16[2,256,512]{2,1,0:T(8,128)(2,1)S(1)}, bf16[2,256,512]{2,1,0:T(8,128)(2,1)}, u32[]{:S(2)}, u32[]{:S(2)}) collective-permute-start(bf16[2,256,512]{2,1,0:T(8,128)(2,1)S(1)} %pad_maximum_fusion.3.refs_8_), channel_id=1, source_target_pairs={{0,96},{32,0},{64,32},{96,64},{1,97},{33,1},{65,33},{97,65},{2,98}... | collective-permute-start | bytes 1572872 | tf_op jit(solution)/shard_map/ppermute | solution.py:48
  144.7 0.8 copy-start.2
  145.5 24.9 %collective-permute-start.6 = (bf16[128,512]{1,0:T(8,128)(2,1)}, bf16[128,512]{1,0:T(8,128)(2,1)}, u32[]{:S(2)}, u32[]{:S(2)}) collective-permute-start(bf16[128,512]{1,0:T(8,128)(2,1)} %get-tuple-element.36), channel_id=1, source_target_pairs={{0,0},{1,16},{2,32},{3,48},{4,64},{5,80},{6,96},{7,112},{8,128},{9... | collective-permute-start | bytes 393224 | tf_op jit(solution)/shard_map/ppermute | solution.py:454
  150.4 0.8 copy-start.4
  151.2 19.5 %collective-permute-start.14 = (bf16[2,256,512]{2,1,0:T(8,128)(2,1)}, bf16[2,256,512]{2,1,0:T(8,128)(2,1)}, u32[]{:S(2)}, u32[]{:S(2)}) collective-permute-start(bf16[2,256,512]{2,1,0:T(8,128)(2,1)} %collective-permute-done.10.refs_3_), channel_id=1, source_target_pairs={{0,16},{16,0},{1,17},{17,1},{2,18},{18,2},{3,19},{19,3},{4,20},{20... | collective-permute-start | bytes 1572872 | tf_op jit(solution)/shard_map/ppermute | solution.py:444
  156.2 18.4 %collective-permute-start.19 = (bf16[2,256,512]{2,1,0:T(8,128)(2,1)S(1)}, bf16[2,256,512]{2,1,0:T(8,128)(2,1)}, u32[]{:S(2)}, u32[]{:S(2)}) collective-permute-start(bf16[2,256,512]{2,1,0:T(8,128)(2,1)S(1)} %pad_maximum_fusion.3.refs_8_), channel_id=1, source_target_pairs={{0,16},{16,0},{1,17},{17,1},{2,18},{18,2},{3,19},{19,3},{4,20},{20... | collective-permute-start | bytes 1572872 | tf_op jit(solution)/shard_map/ppermute | solution.py:457
  168.8 9.8 %collective-permute-start.20 = (bf16[2,256,512]{2,1,0:T(8,128)(2,1)}, bf16[2,256,512]{2,1,0:T(8,128)(2,1)}, u32[]{:S(2)}, u32[]{:S(2)}) collective-permute-start(bf16[2,256,512]{2,1,0:T(8,128)(2,1)} %collective-permute-done.16.refs_9_), channel_id=1, source_target_pairs={{0,16},{16,0},{1,17},{17,1},{2,18},{18,2},{3,19},{19,3},{4,20},{20... | collective-permute-start | bytes 1572872 | tf_op jit(solution)/shard_map/ppermute | solution.py:457
  170.2 9.0 %collective-permute-start.21 = (bf16[2,256,512]{2,1,0:T(8,128)(2,1)}, bf16[2,256,512]{2,1,0:T(8,128)(2,1)}, u32[]{:S(2)}, u32[]{:S(2)}) collective-permute-start(bf16[2,256,512]{2,1,0:T(8,128)(2,1)} %collective-permute-done.17.refs_10_), channel_id=1, source_target_pairs={{0,16},{16,0},{1,17},{17,1},{2,18},{18,2},{3,19},{19,3},{4,20},{20... | collective-permute-start | bytes 1572872 | tf_op jit(solution)/shard_map/ppermute | solution.py:457
  170.4 8.9 %collective-permute-start.22 = (bf16[2,256,512]{2,1,0:T(8,128)(2,1)}, bf16[2,256,512]{2,1,0:T(8,128)(2,1)}, u32[]{:S(2)}, u32[]{:S(2)}) collective-permute-start(bf16[2,256,512]{2,1,0:T(8,128)(2,1)} %collective-permute-done.18.refs_11_), channel_id=1, source_target_pairs={{0,16},{16,0},{1,17},{17,1},{2,18},{18,2},{3,19},{19,3},{4,20},{20... | collective-permute-start | bytes 1572872 | tf_op jit(solution)/shard_map/ppermute | solution.py:457
  170.8 18.7 %collective-permute-start.25 = (bf16[128,512]{1,0:T(8,128)(2,1)}, bf16[128,512]{1,0:T(8,128)(2,1)S(1)}, u32[]{:S(2)}, u32[]{:S(2)}) collective-permute-start(bf16[128,512]{1,0:T(8,128)(2,1)} %collective-permute-done.6), channel_id=1, source_target_pairs={{0,12},{4,0},{8,4},{12,8},{1,13},{5,1},{9,5},{13,9},{2,14},{6,2},{... | collective-permute-start | bytes 393224 | tf_op jit(solution)/shard_map/ppermute | solution.py:48
  174.6 16.1 %collective-permute-start.24 = (bf16[128,512]{1,0:T(8,128)(2,1)}, bf16[128,512]{1,0:T(8,128)(2,1)S(1)}, u32[]{:S(2)}, u32[]{:S(2)}) collective-permute-start(bf16[128,512]{1,0:T(8,128)(2,1)} %collective-permute-done.6), channel_id=1, source_target_pairs={{0,8},{4,12},{8,0},{12,4},{1,9},{5,13},{9,1},{13,5},{2,10},{6,14},... | collective-permute-start | bytes 393224 | tf_op jit(solution)/shard_map/ppermute | solution.py:48
  178.6 12.1 %collective-permute-start.23 = (bf16[128,512]{1,0:T(8,128)(2,1)}, bf16[128,512]{1,0:T(8,128)(2,1)S(1)}, u32[]{:S(2)}, u32[]{:S(2)}) collective-permute-start(bf16[128,512]{1,0:T(8,128)(2,1)} %collective-permute-done.6), channel_id=1, source_target_pairs={{0,4},{4,8},{8,12},{12,0},{1,5},{5,9},{9,13},{13,1},{2,6},{6,10},{... | collective-permute-start | bytes 393224 | tf_op jit(solution)/shard_map/ppermute | solution.py:48
  179.3 1.0 copy-start.1
  180.4 1.0 copy-start.3
  181.4 1.0 copy-start.5
  182.5 0.8 copy-start.10
  188.9 0.6 copy-start.11
  191.7 12.3 %collective-permute-start.26 = (bf16[128,512]{1,0:T(8,128)(2,1)}, bf16[128,512]{1,0:T(8,128)(2,1)S(1)}, u32[]{:S(2)}, u32[]{:S(2)}) collective-permute-start(bf16[128,512]{1,0:T(8,128)(2,1)} %get-tuple-element.47), channel_id=1, source_target_pairs={{0,128},{128,0},{1,129},{129,1},{2,130},{130,2},{3,131},{131,3},{4... | collective-permute-start | bytes 393224 | tf_op jit(solution)/shard_map/ppermute | solution.py:48
  197.5 31.0 %all-to-all-start.3 = ((bf16[16,128,512]{2,1,0:T(8,128)(2,1)}), bf16[16,128,512]{2,1,0:T(8,128)(2,1)S(1)}, u32[]{:S(2)}, u32[]{:S(2)}) async-start(bf16[16,128,512]{2,1,0:T(8,128)(2,1)} %bitcast.36), calls=%async_computation.3 | async-start | bytes 4194304 | tf_op jit(solution)/shard_map/all_to_all | solution.py:35
  204.9 6.1 %collective-permute-start.29 = (bf16[2,128,512]{2,1,0:T(8,128)(2,1)S(1)}, bf16[2,128,512]{2,1,0:T(8,128)(2,1)S(1)}, u32[]{:S(2)}, u32[]{:S(2)}) collective-permute-start(bf16[2,128,512]{2,1,0:T(8,128)(2,1)S(1)} %get-tuple-element.60), channel_id=1, source_target_pairs={{0,96},{32,0},{64,32},{96,64},{1,97},{33,1},{65,33},{97,65},{2,98}... | collective-permute-start | bytes 786440 | tf_op jit(solution)/shard_map/ppermute | solution.py:48
  205.0 6.9 %collective-permute-start.28 = (bf16[2,128,512]{2,1,0:T(8,128)(2,1)S(1)}, bf16[2,128,512]{2,1,0:T(8,128)(2,1)S(1)}, u32[]{:S(2)}, u32[]{:S(2)}) collective-permute-start(bf16[2,128,512]{2,1,0:T(8,128)(2,1)S(1)} %get-tuple-element.60), channel_id=1, source_target_pairs={{0,64},{32,96},{64,0},{96,32},{1,65},{33,97},{65,1},{97,33},{2,66}... | collective-permute-start | bytes 786440 | tf_op jit(solution)/shard_map/ppermute | solution.py:48
  205.9 14.2 %collective-permute-start.27 = (bf16[2,128,512]{2,1,0:T(8,128)(2,1)S(1)}, bf16[2,128,512]{2,1,0:T(8,128)(2,1)S(1)}, u32[]{:S(2)}, u32[]{:S(2)}) collective-permute-start(bf16[2,128,512]{2,1,0:T(8,128)(2,1)S(1)} %get-tuple-element.60), channel_id=1, source_target_pairs={{0,32},{32,64},{64,96},{96,0},{1,33},{33,65},{65,97},{97,1},{2,34}... | collective-permute-start | bytes 786440 | tf_op jit(solution)/shard_map/ppermute | solution.py:48
  220.3 8.3 %copy-start.17 = (bf16[4,2,128,512]{3,2,1,0:T(8,128)(2,1)}, bf16[4,2,128,512]{3,2,1,0:T(8,128)(2,1)S(1)}, u32[]{:S(2)}) copy-start(bf16[4,2,128,512]{3,2,1,0:T(8,128)(2,1)S(1)} %pad_maximum_fusion.near_ref) | copy-start | bytes 3145732
  220.3 3.3 %collective-permute-start.30 = (bf16[4,2,128,512]{3,2,1,0:T(8,128)(2,1)S(1)}, bf16[4,2,128,512]{3,2,1,0:T(8,128)(2,1)}, u32[]{:S(2)}, u32[]{:S(2)}) collective-permute-start(bf16[4,2,128,512]{3,2,1,0:T(8,128)(2,1)S(1)} %pad_maximum_fusion.near_ref), channel_id=1, source_target_pairs={{0,16},{16,0},{1,17},{17,1},{2,18},{18,2},{3,19},{19,3},{4,20},{20... | collective-permute-start | bytes 3145736 | tf_op jit(solution)/shard_map/ppermute | solution.py:477
  228.5 1.3 copy-start.14

commit v5 on v4

--- a/solution.py
+++ b/solution.py
@@ -89,14 +89,16 @@
         reach = jnp.minimum(dot(reach, reach, ((1,), (0,))), 1.0).astype(BF16)
     reach_ref[...] = reach
     own = jnp.where(row % NODES == 2 * rank + lane, jnp.where(lane < 2, 1.0, 0.0), 0.0)
-    visible = dot(reach, own.astype(BF16), ((0,), (0,)))
+    stat_ref[...] = dot(reach, own.astype(BF16), ((0,), (0,)))
     scale = 1.0 / math.sqrt(HEAD)
     span = ck_ref.shape[1]
     slot = lax.broadcasted_iota(jnp.int32, (256, span), 1) + rank * span
     wide_lane = lax.broadcasted_iota(jnp.int32, (NODES, 128), 1)
-    for r in range(q_ref.shape[0]):
+
+    def attend_one(r, carry):
+        own_rows = pl.ds(pl.multiple_of(r * NODES, NODES), NODES)
         live = slot < len_ref[r]
-        seen = visible[r * NODES : (r + 1) * NODES, : tk_ref.shape[1]]
+        seen = stat_ref[own_rows, :][:, : tk_ref.shape[1]]
         seen = jnp.concatenate([seen] * 8, axis=0) > 0.5
         stats = jnp.zeros((NODES, 128), F32)
         for k in range(KV_HEADS):
@@ -126,10 +128,13 @@
             for g in range(8):
                 h = k * 8 + g
                 part = slice(g * NODES, (g + 1) * NODES)
-                out_ref[h // 2, r * NODES : (r + 1) * NODES, (h % 2) * HEAD : (h % 2 + 1) * HEAD] = value[part]
+                out_ref[h // 2, own_rows, (h % 2) * HEAD : (h % 2 + 1) * HEAD] = value[part]
                 for at, column in enumerate((top, high, low)):
                     stats = jnp.where(wide_lane == h * 4 + at, column[part], stats)
-        stat_ref[r * NODES : (r + 1) * NODES, :] = stats
+        stat_ref[own_rows, :] = stats
+        return carry
+
+    lax.fori_loop(0, q_ref.shape[0], attend_one, 0)
     turned = jnp.transpose(stat_ref[...])
     empty = jnp.zeros((8, 128), F32)
     blank = jnp.zeros((16, 128), BF16)
@@ -190,16 +195,23 @@
 
 
 def predict_kernel(
-    source_ref, rank_ref, len_ref, leaf_ref, far_ref, mixed_ref, gain_ref, prev_ref, reach_ref,
+    source_ref, rank_ref, len_ref, leaf_ref, far_own_ref, far_rest_ref, mixed_ref, gain_ref, prev_ref, reach_ref,
     pick_ref, *refs,
 ):
     weight_refs = refs[:16]
-    own_ref, err_ref, loss_ref, scale_ref, ahead_ref, weight_ref, sem_ref = refs[16:]
+    own_ref, err_ref, loss_ref, scale_ref, ahead_ref, weight_ref, sem_ref, far_ref, far_sem = refs[16:]
+    own_load = pltpu.make_async_copy(far_own_ref, far_ref.at[:, 0], far_sem.at[0])
+    rest_load = pltpu.make_async_copy(far_rest_ref, far_ref.at[:, 1:4], far_sem.at[1])
+    own_load.start()
+    rest_load.start()
     loads = [pltpu.make_async_copy(weight_refs[i], weight_ref.at[i], sem_ref.at[i]) for i in range(16)]
     for load in loads:
         load.start()
     square = jnp.zeros((128, 128), F32)
+    own_load.wait()
     for k in range(4):
+        if k == 1:
+            rest_load.wait()
         for x in range(4):
             part = far_ref[x, k].astype(F32)
             part = part * part
@@ -253,13 +265,11 @@
     loss_ref[...] = jnp.broadcast_to(loss, (8, 128))
 
 
-def differentiate_kernel(source_ref, column_ref, near_ref, other_ref, loss_ref, grad_ref, pair_ref):
-    for part in range(4):
-        left = jnp.concatenate([column_ref[source_ref[part * 4 + i]] for i in range(4)], axis=0)
-        err_ref = near_ref if part < 2 else other_ref
-        right = jnp.concatenate(
-            [err_ref[(part % 2) * 2 + i // 2, i % 2] for i in range(4)], axis=0
-        )
+def differentiate_kernel(place_ref, column_ref, e0_ref, e1_ref, e2_ref, e3_ref, loss_ref, grad_ref, pair_ref):
+    for part, err_ref in enumerate((e0_ref, e1_ref, e2_ref, e3_ref)):
+        first = (part // 2) * 8 + part % 2
+        left = jnp.concatenate([column_ref[place_ref[first + 2 * i]] for i in range(4)], axis=0)
+        right = jnp.concatenate([err_ref[i] for i in range(4)], axis=0)
         term = dot(left, right, ((0,), (0,)))
         if part == 0:
             grad_ref[...] = term
@@ -273,6 +283,23 @@
         pair_ref[i * 8 : (i + 1) * 8] = pair
 
 
+def update_kernel(
+    pair_ref, grad_ref, weight_ref, first_ref, second_ref,
+    new_weight_ref, new_first_ref, new_second_ref, loss_ref,
+):
+    total = jnp.sum(pair_ref[...], axis=0, keepdims=True)
+    norm = jnp.sqrt(total[:, 0:1]) + 1e-06
+    clipped = grad_ref[...] * jnp.minimum(1.0, D / norm)
+    new_first = BETA_ONE * first_ref[...] + (1.0 - BETA_ONE) * clipped
+    new_second = BETA_TWO * second_ref[...] + (1.0 - BETA_TWO) * clipped * clipped
+    direction = new_first / CORRECT_ONE / (jnp.sqrt(new_second / CORRECT_TWO) + 1e-08)
+    new_first_ref[...] = new_first
+    new_second_ref[...] = new_second
+    new_weight_ref[...] = (weight_ref[...].astype(F32) - LEARN_RATE * direction).astype(BF16)
+    lane = lax.broadcasted_iota(jnp.int32, (1, 128), 1)
+    loss_ref[0, 0] = jnp.sum(jnp.where(lane == 1, total, 0.0)) * (0.5 / (128 * N_REQ * D))
+
+
 def in_vmem():
     return pl.BlockSpec(memory_space=pltpu.VMEM)
 
@@ -356,7 +383,7 @@
     )(rank, *terms, residual, gain, prev)
 
 
-def predict(source, rank, lengths, leaf, far, mixed, gain, prev, reach, pick, all_weight):
+def predict(source, rank, lengths, leaf, far_own, far, mixed, gain, prev, reach, pick, all_weight):
     return pl.pallas_call(
         predict_kernel,
         out_shape=(
@@ -365,7 +392,8 @@
             jax.ShapeDtypeStruct((8, 128), F32),
         ),
         in_specs=[in_smem()] * 4
-        + [in_vmem()] * 6
+        + [pl.BlockSpec(memory_space=pl.ANY)] * 2
+        + [in_vmem()] * 5
         + [pl.BlockSpec(memory_space=pl.ANY)] * 16,
         out_specs=(in_vmem(),) * 3,
         scratch_shapes=[
@@ -373,29 +401,51 @@
             pltpu.VMEM((128, 512), F32),
             pltpu.VMEM((16, 2, 256, 512), BF16),
             pltpu.SemaphoreType.DMA((16,)),
+            pltpu.VMEM((4, 4, 128, 512), BF16),
+            pltpu.SemaphoreType.DMA((2,)),
         ],
         compiler_params=pltpu.CompilerParams(vmem_limit_bytes=32 << 20),
         cost_estimate=pl.CostEstimate(
             flops=2 * 128 * 8192 * 512, bytes_accessed=13 << 20, transcendentals=0
         ),
         name="predict",
-    )(source, rank, lengths, leaf, far, mixed, gain, prev, reach, pick, *all_weight)
-
-
-def differentiate(source, columns, near_err, other_err, loss):
+    )(source, rank, lengths, leaf, far_own, far, mixed, gain, prev, reach, pick, *all_weight)
+
+
+def differentiate(place, columns, errors, loss):
     return pl.pallas_call(
         differentiate_kernel,
         out_shape=(
             jax.ShapeDtypeStruct((512, 512), F32),
             jax.ShapeDtypeStruct((N_REQ * N_TP, 128), F32),
         ),
-        in_specs=[in_smem()] + [in_vmem()] * 4,
+        in_specs=[in_smem()] + [in_vmem()] * 6,
         out_specs=(in_vmem(), in_vmem()),
         cost_estimate=pl.CostEstimate(
             flops=2 * 2048 * 512 * 512, bytes_accessed=5 << 20, transcendentals=0
         ),
         name="differentiate",
-    )(source, columns, near_err, other_err, loss)
+    )(place, columns, *errors, loss)
+
+
+def update(pair, gradient, weight, first, second):
+    part = pl.BlockSpec((128, 512), lambda p: (p, 0))
+    return pl.pallas_call(
+        update_kernel,
+        grid=(4,),
+        out_shape=(
+            jax.ShapeDtypeStruct((512, 512), BF16),
+            jax.ShapeDtypeStruct((512, 512), F32),
+            jax.ShapeDtypeStruct((512, 512), F32),
+            jax.ShapeDtypeStruct((1, 1), F32),
+        ),
+        in_specs=[pl.BlockSpec((N_REQ * N_TP, 128), lambda p: (0, 0))] + [part] * 4,
+        out_specs=(part, part, part, in_smem()),
+        cost_estimate=pl.CostEstimate(
+            flops=20 * 512 * 512, bytes_accessed=6 << 20, transcendentals=512 * 512
+        ),
+        name="update",
+    )(pair, gradient, weight, first, second)
 
 
 def body(
@@ -428,16 +478,18 @@
     )
     place = (source % 4) * 4 + (lax.axis_index("zl") + 4 - source // 4) % 4
 
-    half = draft_weight.shape[0] // 2
-    upper = passed(draft_weight[:half], "zh", 2)
     parcel, reach, pick = attend(
         rank, lengths, parents, queries, cache_keys, cache_values, tree_keys, tree_values
     )
     parcel = exchange(parcel, TP)
+    half = draft_weight.shape[0] // 2
+    parcel, upper, lower = lax.optimization_barrier(
+        (parcel, draft_weight[:half], draft_weight[half:])
+    )
+    upper = passed(upper, "zh", 2)
+    lower = passed(lower, "zh", 2)
     upper = jnp.stack(upper)
     upper = passed(upper, "y", 4)
-    parcel, lower = lax.optimization_barrier((parcel, draft_weight[half:]))
-    lower = passed(lower, "zh", 2)
 
     partial_value = project(parcel, out_weight)
     along_x = exchange(partial_value, "x")
@@ -448,20 +500,21 @@
     terms[1:] = [lax.ppermute(terms[step], "zl", turn(4, step)) for step in (1, 2, 3)]
     mixed, near, table = settle(rank, terms, residual.reshape(rows, block), gain, prev_feature)
 
-    far = turns(near, "zl", 4)
-    far, table = lax.optimization_barrier((far, table))
-    far = spread(far, "x", 4).reshape(4, 4, rows, block)
+    far = passed(near, "zl", 4)[1:]
+    far_own = spread(near[None], "x", 4)
+    far = jnp.stack(far)
+    far = spread(far, "x", 4).reshape(4, 3, rows, block)
     swapped = lax.ppermute(
         table, REQ + TP, [(i * N_TP + j, j * N_TP + i) for i in range(16) for j in range(16)]
     )
     other_lower = [lax.ppermute(part, "c", turn(2, 1)) for part in lower]
-    swapped, far = lax.optimization_barrier((swapped, far))
     columns = turns(swapped, "zl", 4)
     own_features, scaled_err, loss = predict(
         source,
         rank,
         lengths,
         accepted_leaf,
+        far_own,
         far,
         mixed,
         gain,
@@ -472,26 +525,22 @@
     )
     columns, scaled_err = lax.optimization_barrier((columns, scaled_err))
     columns = spread(columns, "x", 4).reshape(N_REQ, rows, block)
-    near_err = turns(scaled_err, "zh", 2)
-    near_err = turns(near_err, "y", 4)
-    other_err = lax.ppermute(near_err, "c", turn(2, 1))
-    gradient, pair = differentiate(place, columns, near_err, other_err, loss)
-    pair = jnp.sum(exchange(pair, REQ + TP), axis=0)
-    square_total, error_total = pair[0], pair[1]
-    draft_loss = 0.5 * error_total / (rows * N_REQ * D)
-    grad_norm = jnp.sqrt(square_total) + 1e-06
-    clip_factor = jnp.minimum(1.0, D / grad_norm)
-    clipped = gradient * clip_factor
-    new_first = BETA_ONE * first_moment + (1.0 - BETA_ONE) * clipped
-    new_second = BETA_TWO * second_moment + (1.0 - BETA_TWO) * clipped * clipped
-    direction = new_first / CORRECT_ONE / (jnp.sqrt(new_second / CORRECT_TWO) + 1e-08)
-    new_weight = (draft_weight.astype(F32) - LEARN_RATE * direction).astype(BF16)
+    far_err = lax.ppermute(scaled_err, "zh", turn(2, 1))
+    err = passed(scaled_err, "y", 4)
+    far_err = passed(far_err, "y", 4)
+    err, far_err = jnp.stack(err), jnp.stack(far_err)
+    errors = [err, far_err] + [lax.ppermute(part, "c", turn(2, 1)) for part in (err, far_err)]
+    gradient, pair = differentiate(place, columns, errors, loss)
+    pair = exchange(pair, REQ + TP)
+    new_weight, new_first, new_second, draft_loss = update(
+        pair, gradient, draft_weight, first_moment, second_moment
+    )
     return (
         own_features.reshape(requests, NODES, block),
         new_weight,
         new_first,
         new_second,
-        draft_loss,
+        draft_loss.reshape(()),
     )
 
 

time: 264 us -> 272 us (1.030)
  starting transfers between devices: 92.4 us -> 112 us
  waiting for transfers between devices: 92.1 us -> 76.9 us
  other arithmetic: 9 us -> 2.77 us
  Pallas kernels: 30 us -> 35.1 us
  blocking collectives: 21.2 us -> 25.6 us
    ppermute x18 -> x20, waiting for transfers between devices: 34.1 us -> 19.1 us  [passed(): lax.ppermute(value, axis, turn(count, step))]
    ppermute x1 -> x3, starting transfers between devices: 0.87 us -> 14 us  [the longest x1 11.5 us: body(): far_err = lax.ppermute(scaled_err, 'zh', turn(2, 1))]
    ppermute x4, starting transfers between devices: 3.9 us -> 11.7 us  [body(): other_upper = [lax.ppermute(part, 'c', turn(2, 1)) for part in upper]]
    ppermute x1, waiting for transfers between devices: 0.01 us -> 7.45 us  [body(): lax.ppermute(table, REQ + TP, [(i * N_TP + j, j * N_TP + i) for i in rang...]
    all_to_all x4 -> x5, waiting for transfers between devices: 48.9 us -> 44 us  [exchange(): return lax.all_to_all(value, axis, 0, 0, tiled=True)]
    pallas_call x0 -> x1, Pallas kernels: none -> 4.83 us  [update(): pl.pallas_call(update_kernel, grid=(4,), out_shape=(jax.ShapeDtypeStruct(...]
    all_to_all x1, blocking collectives: 21.2 us -> 25.6 us  [exchange(): return lax.all_to_all(value, axis, 0, 0, tiled=True)]
    convert_element_type x1 -> x0, other arithmetic: 4.11 us -> none  [body(): (draft_weight.astype(F32) - LEARN_RATE * direction).astype(BF16)]
  transfers between devices with their start and end apart: 35 -> 40, of which waited for: 13 -> 12; matrix products, arithmetic and copies ran while one was open for 3% -> 2% of each run, Pallas kernels for 4% -> 2%
where the time goes in v5:
time: 272 us; the launch traced here: 271 us
  starting transfers between devices  112 us (41%)
  waiting for transfers between devices  76.9 us (28%)
  Pallas kernels  35.1 us (13%)
  blocking collectives  25.6 us (9%)
  local copies, waits for them, and re-layouts  17.6 us (6%)
  other arithmetic  2.77 us (1%)
    all_to_all x5, waiting for transfers between devices, exchange(): return lax.all_to_all(value, axis, 0, 0, tiled=True)  44 us
    ppermute x20, starting transfers between devices, passed(): lax.ppermute(value, axis, turn(count, step))  38.9 us
    all_to_all x5, starting transfers between devices, exchange(): return lax.all_to_all(value, axis, 0, 0, tiled=True)  25.7 us
    all_to_all x1, blocking collectives, exchange(): return lax.all_to_all(value, axis, 0, 0, tiled=True)  25.6 us
    ppermute x20, waiting for transfers between devices, passed(): lax.ppermute(value, axis, turn(count, step))  19.1 us
    unnamed x68, local copies, waits for them, and re-layouts  13 us
    ppermute x4, starting transfers between devices, body(): other_upper = [lax.ppermute(part, 'c', turn(2, 1)) for part in upper]  11.7 us
    ppermute x1, starting transfers between devices, body(): far_err = lax.ppermute(scaled_err, 'zh', turn(2, 1))  11.5 us
  transfers between devices with their start and end apart: 40, of which 12 were waited for; matrix products, arithmetic and copies ran while one was open for 2% of the time, Pallas kernels for 2%

profile of v5, /device:TPU:1, one launch (start us, length us, event | category | flops | bytes accessed | tf_op | source)
XLA Modules:
  0.0 271.1 jit_solution(3586823021193839313)
XLA Ops:
  0.7 9.6 %attend.1 = (bf16[16,144,256]{2,1,0:T(8,128)(2,1)}, bf16[128,128]{1,0:T(8,128)(2,1)}, bf16[128,128]{1,0:T(8,128)(2,1)}) custom-call(s32[1]{0:T(128)} %bitcast.rank_ref, s32[4]{0:T(128)} %len_ref.3, s32[4,32]{1,0:T(4,128)} %par_ref.1, bf16[4,32,4096]{2,1,0:T(8,128)(2,1)} %q_ref.1, bf16[4,256,512]{2,1,0:T(8,128)(2,1)} %ck_ref.1, bf16[4,256,512]{2,1,0:T(8,128)(2,1)} %cv_ref.1, ...), custom_call_target="tpu_custom_call" | custom-call | flops 536870912 | bytes 4194304 | tf_op jit(solution)/shard_map/attend/pallas_call | solution.py:312
  10.2 9.0 %all-to-all-start = ((bf16[16,144,256]{2,1,0:T(8,128)(2,1)}), bf16[16,144,256]{2,1,0:T(8,128)(2,1)S(1)}, u32[]{:S(2)}, u32[]{:S(2)}) async-start(bf16[16,144,256]{2,1,0:T(8,128)(2,1)} %get-tuple-element.29), calls=%async_computation | async-start | bytes 2359296 | tf_op jit(solution)/shard_map/all_to_all | solution.py:35
  19.3 24.4 %all-to-all-done.parcel_ref = bf16[16,144,256]{2,1,0:T(8,128)(2,1)S(1)} async-done(((bf16[16,144,256]{2,1,0:T(8,128)(2,1)}), bf16[16,144,256]{2,1,0:T(8,128)(2,1)S(1)}, u32[]{:S(2)}, u32[]{:S(2)}) %all-to-all-start) | async-done | bytes 1179680 | tf_op jit(solution)/shard_map/all_to_all | solution.py:35
  43.7 1.0 copy-done.20
  44.8 6.0 %project.1 = bf16[4,4,128,512]{3,2,1,0:T(8,128)(2,1)} custom-call(bf16[16,144,256]{2,1,0:T(8,128)(2,1)} %copy-done.20, bf16[256,8192]{1,0:T(8,128)(2,1)} %weight_ref.2), custom_call_target="tpu_custom_call" | custom-call | flops 536870912 | bytes 7340032 | tf_op jit(solution)/shard_map/project/pallas_call | solution.py:330
  50.7 4.9 %all-to-all-start.1 = ((bf16[4,4,128,512]{3,2,1,0:T(8,128)(2,1)}), bf16[4,4,128,512]{3,2,1,0:T(8,128)(2,1)S(1)}, u32[]{:S(2)}, u32[]{:S(2)}) async-start(bf16[4,4,128,512]{3,2,1,0:T(8,128)(2,1)} %project.1), calls=%async_computation.1 | async-start | bytes 4194304 | tf_op jit(solution)/shard_map/all_to_all | solution.py:35
  55.7 4.2 %collective-permute-start.6 = (bf16[256,512]{1,0:T(8,128)(2,1)S(1)}, bf16[256,512]{1,0:T(8,128)(2,1)S(1)}, u32[]{:S(2)}, u32[]{:S(2)}) collective-permute-start(bf16[256,512]{1,0:T(8,128)(2,1)S(1)} %get-tuple-element.39), channel_id=1, source_target_pairs={{0,128},{128,0},{1,129},{129,1},{2,130},{130,2},{3,131},{131,3},{4... | collective-permute-start | bytes 786440 | tf_op jit(solution)/shard_map/ppermute | solution.py:48
  59.9 19.5 %all-to-all-done.1.along_ref = bf16[4,4,128,512]{3,2,1,0:T(8,128)(2,1)S(1)} async-done(((bf16[4,4,128,512]{3,2,1,0:T(8,128)(2,1)}), bf16[4,4,128,512]{3,2,1,0:T(8,128)(2,1)S(1)}, u32[]{:S(2)}, u32[]{:S(2)}) %all-to-all-start.1) | async-done | bytes 2097184 | tf_op jit(solution)/shard_map/all_to_all | solution.py:35
  79.4 1.3 copy-done.19
  80.7 2.6 fold.1
  83.3 4.4 %collective-permute-start = (bf16[128,512]{1,0:T(8,128)(2,1)}, bf16[128,512]{1,0:T(8,128)(2,1)S(1)}, u32[]{:S(2)}, u32[]{:S(2)}) collective-permute-start(bf16[128,512]{1,0:T(8,128)(2,1)} %get-tuple-element.32), channel_id=1, source_target_pairs={{0,4},{4,8},{8,12},{12,0},{1,5},{5,9},{9,13},{13,1},{2,6},{6,10},{... | collective-permute-start | bytes 393224 | tf_op jit(solution)/shard_map/ppermute | solution.py:500
  87.7 1.3 collective-permute-start.1
  89.0 2.4 collective-permute-start.2
  91.4 4.2 %collective-permute-start.14 = (bf16[256,512]{1,0:T(8,128)(2,1)S(1)}, bf16[256,512]{1,0:T(8,128)(2,1)S(1)}, u32[]{:S(2)}, u32[]{:S(2)}) collective-permute-start(bf16[256,512]{1,0:T(8,128)(2,1)S(1)} %get-tuple-element.40), channel_id=1, source_target_pairs={{0,128},{128,0},{1,129},{129,1},{2,130},{130,2},{3,131},{131,3},{4... | collective-permute-start | bytes 786440 | tf_op jit(solution)/shard_map/ppermute | solution.py:48
  95.6 3.3 %collective-permute-done.1.two_ref = bf16[128,512]{1,0:T(8,128)(2,1)S(1)} collective-permute-done((bf16[128,512]{1,0:T(8,128)(2,1)}, bf16[128,512]{1,0:T(8,128)(2,1)S(1)}, u32[]{:S(2)}, u32[]{:S(2)}) %collective-permute-start.1) | collective-permute-done | bytes 131104 | tf_op jit(solution)/shard_map/ppermute | solution.py:500
  99.0 0.6 copy-done.28
  99.7 2.1 settle.1
  101.7 14.6 %collective-permute-start.5 = (bf16[128,512]{1,0:T(8,128)(2,1)}, bf16[128,512]{1,0:T(8,128)(2,1)S(1)}, u32[]{:S(2)}, u32[]{:S(2)}) collective-permute-start(bf16[128,512]{1,0:T(8,128)(2,1)} %get-tuple-element.35), channel_id=1, source_target_pairs={{0,12},{4,0},{8,4},{12,8},{1,13},{5,1},{9,5},{13,9},{2,14},{6,2},{... | collective-permute-start | bytes 393224 | tf_op jit(solution)/shard_map/ppermute | solution.py:48
  116.3 1.4 collective-permute-start.7
  117.7 2.6 collective-permute-start.8
  120.3 1.1 collective-permute-start.9
  121.4 3.4 %collective-permute-start.10 = (bf16[2,256,512]{2,1,0:T(8,128)(2,1)S(1)}, bf16[2,256,512]{2,1,0:T(8,128)(2,1)}, u32[]{:S(2)}, u32[]{:S(2)}) collective-permute-start(bf16[2,256,512]{2,1,0:T(8,128)(2,1)S(1)} %pad_maximum_fusion.refs_0_), channel_id=1, source_target_pairs={{0,16},{16,0},{1,17},{17,1},{2,18},{18,2},{3,19},{19,3},{4,20},{20... | collective-permute-start | bytes 1572872 | tf_op jit(solution)/shard_map/ppermute | solution.py:496
  124.8 1.7 reshape.47
  126.6 3.5 %all-to-all-start.2 = ((bf16[4,128,512]{2,1,0:T(8,128)(2,1)}), bf16[4,128,512]{2,1,0:T(8,128)(2,1)S(1)}, u32[]{:S(2)}, u32[]{:S(2)}) async-start(bf16[4,128,512]{2,1,0:T(8,128)(2,1)} %reshape.47), calls=%async_computation.2 | async-start | bytes 1048576 | tf_op jit(solution)/shard_map/all_to_all | solution.py:35
  130.4 5.9 %collective-permute-done.3 = bf16[128,512]{1,0:T(8,128)(2,1)S(1)} collective-permute-done((bf16[128,512]{1,0:T(8,128)(2,1)S(1)}, bf16[128,512]{1,0:T(8,128)(2,1)S(1)}, u32[]{:S(2)}, u32[]{:S(2)}) %collective-permute-start.3) | collective-permute-done | bytes 131104 | tf_op jit(solution)/shard_map/ppermute | solution.py:48
  136.8 3.2 %collective-permute-start.16 = (bf16[2,256,512]{2,1,0:T(8,128)(2,1)S(1)}, bf16[2,256,512]{2,1,0:T(8,128)(2,1)}, u32[]{:S(2)}, u32[]{:S(2)}) collective-permute-start(bf16[2,256,512]{2,1,0:T(8,128)(2,1)S(1)} %pad_maximum_fusion.1.refs_8_), channel_id=1, source_target_pairs={{0,64},{32,96},{64,0},{96,32},{1,65},{33,97},{65,1},{97,33},{2,66}... | collective-permute-start | bytes 1572872 | tf_op jit(solution)/shard_map/ppermute | solution.py:48
  140.0 1.2 collective-permute-done.8.refs_2_
  141.1 1.3 broadcast_in_dim.4
  142.5 3.9 %all-to-all-start.3 = ((bf16[12,128,512]{2,1,0:T(8,128)(2,1)}), bf16[12,128,512]{2,1,0:T(8,128)(2,1)S(1)}, u32[]{:S(2)}, u32[]{:S(2)}) async-start(bf16[12,128,512]{2,1,0:T(8,128)(2,1)} %bitcast.36), calls=%async_computation.3 | async-start | bytes 3145728 | tf_op jit(solution)/shard_map/all_to_all | solution.py:35
  146.4 6.2 %collective-permute-start.18 = (bf16[2,256,512]{2,1,0:T(8,128)(2,1)S(1)}, bf16[2,256,512]{2,1,0:T(8,128)(2,1)S(1)}, u32[]{:S(2)}, u32[]{:S(2)}) collective-permute-start(bf16[2,256,512]{2,1,0:T(8,128)(2,1)S(1)} %pad_maximum_fusion.1.refs_8_), channel_id=1, source_target_pairs={{0,16},{16,0},{1,17},{17,1},{2,18},{18,2},{3,19},{19,3},{4,20},{20... | collective-permute-start | bytes 1572872 | tf_op jit(solution)/shard_map/ppermute | solution.py:510
  152.7 4.6 %collective-permute-done.15.refs_9_ = bf16[2,256,512]{2,1,0:T(8,128)(2,1)} collective-permute-done((bf16[2,256,512]{2,1,0:T(8,128)(2,1)S(1)}, bf16[2,256,512]{2,1,0:T(8,128)(2,1)}, u32[]{:S(2)}, u32[]{:S(2)}) %collective-permute-start.15) | collective-permute-done | bytes 524320 | tf_op jit(solution)/shard_map/ppermute | solution.py:48
  157.2 2.9 %collective-permute-start.22 = (bf16[128,512]{1,0:T(8,128)(2,1)}, bf16[128,512]{1,0:T(8,128)(2,1)S(1)}, u32[]{:S(2)}, u32[]{:S(2)}) collective-permute-start(bf16[128,512]{1,0:T(8,128)(2,1)} %get-tuple-element.42), channel_id=1, source_target_pairs={{0,0},{1,16},{2,32},{3,48},{4,64},{5,80},{6,96},{7,112},{8,128},{9... | collective-permute-start | bytes 393224 | tf_op jit(solution)/shard_map/ppermute | solution.py:507
  160.1 7.5 %collective-permute-done.22 = bf16[128,512]{1,0:T(8,128)(2,1)S(1)} collective-permute-done((bf16[128,512]{1,0:T(8,128)(2,1)}, bf16[128,512]{1,0:T(8,128)(2,1)S(1)}, u32[]{:S(2)}, u32[]{:S(2)}) %collective-permute-start.22) | collective-permute-done | bytes 131104 | tf_op jit(solution)/shard_map/ppermute | solution.py:507
  167.6 2.8 %collective-permute-start.25 = (bf16[128,512]{1,0:T(8,128)(2,1)S(1)}, bf16[128,512]{1,0:T(8,128)(2,1)S(1)}, u32[]{:S(2)}, u32[]{:S(2)}) collective-permute-start(bf16[128,512]{1,0:T(8,128)(2,1)S(1)} %collective-permute-done.22), channel_id=1, source_target_pairs={{0,12},{4,0},{8,4},{12,8},{1,13},{5,1},{9,5},{13,9},{2,14},{6,2},{... | collective-permute-start | bytes 393224 | tf_op jit(solution)/shard_map/ppermute | solution.py:48
  170.7 0.9 copy-done.4
  171.6 8.2 %collective-permute-start.12 = (bf16[2,256,512]{2,1,0:T(8,128)(2,1)}, bf16[2,256,512]{2,1,0:T(8,128)(2,1)}, u32[]{:S(2)}, u32[]{:S(2)}) collective-permute-start(bf16[2,256,512]{2,1,0:T(8,128)(2,1)} %copy-done.2), channel_id=1, source_target_pairs={{0,16},{16,0},{1,17},{17,1},{2,18},{18,2},{3,19},{19,3},{4,20},{20... | collective-permute-start | bytes 1572872 | tf_op jit(solution)/shard_map/ppermute | solution.py:496
  179.8 0.8 copy-done.6
  181.1 3.5 %collective-permute-start.20 = (bf16[2,256,512]{2,1,0:T(8,128)(2,1)}, bf16[2,256,512]{2,1,0:T(8,128)(2,1)}, u32[]{:S(2)}, u32[]{:S(2)}) collective-permute-start(bf16[2,256,512]{2,1,0:T(8,128)(2,1)} %collective-permute-done.16.refs_10_), channel_id=1, source_target_pairs={{0,16},{16,0},{1,17},{17,1},{2,18},{18,2},{3,19},{19,3},{4,20},{20... | collective-permute-start | bytes 1572872 | tf_op jit(solution)/shard_map/ppermute | solution.py:510
  184.7 0.7 copy-done.33
  186.5 1.9 pad_maximum_fusion.2
  188.6 1.0 copy-done.1
  189.6 1.0 copy-done.3
  190.6 1.0 copy-done.5
  191.7 1.0 copy-done.7
  192.7 0.8 copy-done.14
  193.5 5.6 %predict.1 = (bf16[128,512]{1,0:T(8,128)(2,1)}, bf16[128,512]{1,0:T(8,128)(2,1)S(1)}, f32[8,128]{1,0:T(8,128)S(1)}) custom-call(s32[16]{0:T(128)S(1)} %get-tuple-element.54.source_ref, s32[1]{0:T(128)} %bitcast.rank_ref, s32[4]{0:T(128)S(1)} %copy-done.16, s32[4]{0:T(128)S(1)} %copy-done.17, bf16[4,128,512]{2,1,0:T(8,128)(2,1)S(1)} %all-to-all-done.2.far_own_ref, ...), custom_call_target="tpu_custom_call" | custom-call | flops 1073741824 | bytes 13631488 | tf_op jit(solution)/shard_map/predict/pallas_call | solution.py:387
  199.1 0.6 copy-done.11
  199.7 1.5 broadcast_in_dim.5
  201.3 4.4 %all-to-all-start.4 = ((bf16[16,128,512]{2,1,0:T(8,128)(2,1)}), bf16[16,128,512]{2,1,0:T(8,128)(2,1)S(1)}, u32[]{:S(2)}, u32[]{:S(2)}) async-start(bf16[16,128,512]{2,1,0:T(8,128)(2,1)} %bitcast.35), calls=%async_computation.4 | async-start | bytes 4194304 | tf_op jit(solution)/shard_map/all_to_all | solution.py:35
  205.7 11.5 %collective-permute-start.29 = (bf16[128,512]{1,0:T(8,128)(2,1)S(1)}, bf16[128,512]{1,0:T(8,128)(2,1)S(1)}, u32[]{:S(2)}, u32[]{:S(2)}) collective-permute-start(bf16[128,512]{1,0:T(8,128)(2,1)S(1)} %copy-done.12), channel_id=1, source_target_pairs={{0,128},{128,0},{1,129},{129,1},{2,130},{130,2},{3,131},{131,3},{4... | collective-permute-start | bytes 393224 | tf_op jit(solution)/shard_map/ppermute | solution.py:528
  217.2 1.5 collective-permute-start.26
  218.6 2.1 collective-permute-done.29
  220.8 1.1 collective-permute-start.32
  222.2 0.9 collective-permute-start.30
  223.2 4.5 %collective-permute-done.26 = bf16[128,512]{1,0:T(8,128)(2,1)S(1)} collective-permute-done((bf16[128,512]{1,0:T(8,128)(2,1)S(1)}, bf16[128,512]{1,0:T(8,128)(2,1)S(1)}, u32[]{:S(2)}, u32[]{:S(2)}) %collective-permute-start.26) | collective-permute-done | bytes 131104 | tf_op jit(solution)/shard_map/ppermute | solution.py:48
  227.7 0.8 collective-permute-start.33
  228.5 2.8 %collective-permute-done.30 = bf16[128,512]{1,0:T(8,128)(2,1)S(1)} collective-permute-done((bf16[128,512]{1,0:T(8,128)(2,1)S(1)}, bf16[128,512]{1,0:T(8,128)(2,1)S(1)}, u32[]{:S(2)}, u32[]{:S(2)}) %collective-permute-start.30) | collective-permute-done | bytes 131104 | tf_op jit(solution)/shard_map/ppermute | solution.py:48
  231.4 1.8 collective-permute-start.34
  233.2 0.8 copy-done.25
  234.0 0.9 collective-permute-done.34.e3_ref
  234.9 1.3 copy-done.18
  236.2 4.5 %differentiate.1 = (f32[512,512]{1,0:T(8,128)}, f32[256,128]{1,0:T(8,128)}) custom-call(s32[16]{0:T(128)} %get-tuple-element.53.place_ref, bf16[16,128,512]{2,1,0:T(8,128)(2,1)} %copy-done.18, bf16[4,128,512]{2,1,0:T(8,128)(2,1)} %copy-done.22, bf16[4,128,512]{2,1,0:T(8,128)(2,1)} %copy-done.23, bf16[4,128,512]{2,1,0:T(8,128)(2,1)} %copy-done.25, ...), custom_call_target="tpu_custom_call" | custom-call | flops 1073741824 | bytes 5242880 | tf_op jit(solution)/shard_map/differentiate/pallas_call | solution.py:416
  240.7 25.6 %all_to_all.36 = f32[256,1,128]{2,1,0:T(1,128)} all-to-all(f32[256,1,128]{2,1,0:T(1,128)} %bitcast.43), channel_id=1, replica_groups=mesh['zh'=2,'y'=4,'c'=2,'zl'=4,'x'=4] {'zh','y','c','zl','x'}, dimensions={0} | all-to-all | bytes 262144 | tf_op jit(solution)/shard_map/all_to_all | solution.py:35
  266.2 4.8 %update.1 = (bf16[512,512]{1,0:T(8,128)(2,1)}, f32[512,512]{1,0:T(8,128)}, f32[512,512]{1,0:T(8,128)}, f32[1,1]{1,0:T(1,128)}) custom-call(f32[256,128]{1,0:T(8,128)} %bitcast.39, f32[512,512]{1,0:T(8,128)} %get-tuple-element.48.grad_ref, bf16[512,512]{1,0:T(8,128)(2,1)} %weight_ref.3, f32[512,512]{1,0:T(8,128)} %first_ref.1, f32[512,512]{1,0:T(8,128)} %second_ref.1), custom_call_target="tpu_custom_call" | custom-call | flops 5242880 | bytes 6291456 | tf_op jit(solution)/shard_map/update/pallas_call | solution.py:433
  (103 shorter events, 3.9 us)
Async XLA Ops:
  0.6 18.6 %copy-start.24 = (bf16[512,512]{1,0:T(8,128)(2,1)S(1)}, bf16[512,512]{1,0:T(8,128)(2,1)}, u32[]{:S(2)}) copy-start(bf16[512,512]{1,0:T(8,128)(2,1)} %weight_ref.3) | copy-start | bytes 1572868
  10.2 33.5 %all-to-all-start = ((bf16[16,144,256]{2,1,0:T(8,128)(2,1)}), bf16[16,144,256]{2,1,0:T(8,128)(2,1)S(1)}, u32[]{:S(2)}, u32[]{:S(2)}) async-start(bf16[16,144,256]{2,1,0:T(8,128)(2,1)} %get-tuple-element.29), calls=%async_computation | async-start | bytes 2359296 | tf_op jit(solution)/shard_map/all_to_all | solution.py:35
  50.7 28.7 %all-to-all-start.1 = ((bf16[4,4,128,512]{3,2,1,0:T(8,128)(2,1)}), bf16[4,4,128,512]{3,2,1,0:T(8,128)(2,1)S(1)}, u32[]{:S(2)}, u32[]{:S(2)}) async-start(bf16[4,4,128,512]{3,2,1,0:T(8,128)(2,1)} %project.1), calls=%async_computation.1 | async-start | bytes 4194304 | tf_op jit(solution)/shard_map/all_to_all | solution.py:35
  55.7 60.6 %collective-permute-start.6 = (bf16[256,512]{1,0:T(8,128)(2,1)S(1)}, bf16[256,512]{1,0:T(8,128)(2,1)S(1)}, u32[]{:S(2)}, u32[]{:S(2)}) collective-permute-start(bf16[256,512]{1,0:T(8,128)(2,1)S(1)} %get-tuple-element.39), channel_id=1, source_target_pairs={{0,128},{128,0},{1,129},{129,1},{2,130},{130,2},{3,131},{131,3},{4... | collective-permute-start | bytes 786440 | tf_op jit(solution)/shard_map/ppermute | solution.py:48
  79.4 1.3 copy-start.19
  83.3 12.3 %collective-permute-start = (bf16[128,512]{1,0:T(8,128)(2,1)}, bf16[128,512]{1,0:T(8,128)(2,1)S(1)}, u32[]{:S(2)}, u32[]{:S(2)}) collective-permute-start(bf16[128,512]{1,0:T(8,128)(2,1)} %get-tuple-element.32), channel_id=1, source_target_pairs={{0,4},{4,8},{8,12},{12,0},{1,5},{5,9},{9,13},{13,1},{2,6},{6,10},{... | collective-permute-start | bytes 393224 | tf_op jit(solution)/shard_map/ppermute | solution.py:500
  87.7 11.3 %collective-permute-start.1 = (bf16[128,512]{1,0:T(8,128)(2,1)}, bf16[128,512]{1,0:T(8,128)(2,1)S(1)}, u32[]{:S(2)}, u32[]{:S(2)}) collective-permute-start(bf16[128,512]{1,0:T(8,128)(2,1)} %get-tuple-element.33), channel_id=1, source_target_pairs={{0,8},{4,12},{8,0},{12,4},{1,9},{5,13},{9,1},{13,5},{2,10},{6,14},... | collective-permute-start | bytes 393224 | tf_op jit(solution)/shard_map/ppermute | solution.py:500
  89.0 9.9 %collective-permute-start.2 = (bf16[128,512]{1,0:T(8,128)(2,1)}, bf16[128,512]{1,0:T(8,128)(2,1)S(1)}, u32[]{:S(2)}, u32[]{:S(2)}) collective-permute-start(bf16[128,512]{1,0:T(8,128)(2,1)} %get-tuple-element.34), channel_id=1, source_target_pairs={{0,12},{4,0},{8,4},{12,8},{1,13},{5,1},{9,5},{13,9},{2,14},{6,2},{... | collective-permute-start | bytes 393224 | tf_op jit(solution)/shard_map/ppermute | solution.py:500
  91.4 30.0 %collective-permute-start.14 = (bf16[256,512]{1,0:T(8,128)(2,1)S(1)}, bf16[256,512]{1,0:T(8,128)(2,1)S(1)}, u32[]{:S(2)}, u32[]{:S(2)}) collective-permute-start(bf16[256,512]{1,0:T(8,128)(2,1)S(1)} %get-tuple-element.40), channel_id=1, source_target_pairs={{0,128},{128,0},{1,129},{129,1},{2,130},{130,2},{3,131},{131,3},{4... | collective-permute-start | bytes 786440 | tf_op jit(solution)/shard_map/ppermute | solution.py:48
  95.6 3.4 %copy-start.27 = (bf16[128,512]{1,0:T(8,128)(2,1)}, bf16[128,512]{1,0:T(8,128)(2,1)S(1)}, u32[]{:S(2)}) copy-start(bf16[128,512]{1,0:T(8,128)(2,1)S(1)} %collective-permute-done.one_ref) | copy-start | bytes 393220
  101.7 28.3 %copy-start.26 = (bf16[128,512]{1,0:T(8,128)(2,1)S(1)}, bf16[128,512]{1,0:T(8,128)(2,1)}, u32[]{:S(2)}) copy-start(bf16[128,512]{1,0:T(8,128)(2,1)} %get-tuple-element.35) | copy-start | bytes 393220
  101.7 19.7 %collective-permute-start.5 = (bf16[128,512]{1,0:T(8,128)(2,1)}, bf16[128,512]{1,0:T(8,128)(2,1)S(1)}, u32[]{:S(2)}, u32[]{:S(2)}) collective-permute-start(bf16[128,512]{1,0:T(8,128)(2,1)} %get-tuple-element.35), channel_id=1, source_target_pairs={{0,12},{4,0},{8,4},{12,8},{1,13},{5,1},{9,5},{13,9},{2,14},{6,2},{... | collective-permute-start | bytes 393224 | tf_op jit(solution)/shard_map/ppermute | solution.py:48
  116.3 20.4 %collective-permute-start.7 = (bf16[2,256,512]{2,1,0:T(8,128)(2,1)S(1)}, bf16[2,256,512]{2,1,0:T(8,128)(2,1)S(1)}, u32[]{:S(2)}, u32[]{:S(2)}) collective-permute-start(bf16[2,256,512]{2,1,0:T(8,128)(2,1)S(1)} %pad_maximum_fusion.refs_0_), channel_id=1, source_target_pairs={{0,32},{32,64},{64,96},{96,0},{1,33},{33,65},{65,97},{97,1},{2,34}... | collective-permute-start | bytes 1572872 | tf_op jit(solution)/shard_map/ppermute | solution.py:48
  117.7 23.4 %collective-permute-start.8 = (bf16[2,256,512]{2,1,0:T(8,128)(2,1)S(1)}, bf16[2,256,512]{2,1,0:T(8,128)(2,1)S(1)}, u32[]{:S(2)}, u32[]{:S(2)}) collective-permute-start(bf16[2,256,512]{2,1,0:T(8,128)(2,1)S(1)} %pad_maximum_fusion.refs_0_), channel_id=1, source_target_pairs={{0,64},{32,96},{64,0},{96,32},{1,65},{33,97},{65,1},{97,33},{2,66}... | collective-permute-start | bytes 1572872 | tf_op jit(solution)/shard_map/ppermute | solution.py:48
  120.3 26.0 %collective-permute-start.9 = (bf16[2,256,512]{2,1,0:T(8,128)(2,1)S(1)}, bf16[2,256,512]{2,1,0:T(8,128)(2,1)}, u32[]{:S(2)}, u32[]{:S(2)}) collective-permute-start(bf16[2,256,512]{2,1,0:T(8,128)(2,1)S(1)} %pad_maximum_fusion.refs_0_), channel_id=1, source_target_pairs={{0,96},{32,0},{64,32},{96,64},{1,97},{33,1},{65,33},{97,65},{2,98}... | collective-permute-start | bytes 1572872 | tf_op jit(solution)/shard_map/ppermute | solution.py:48
  121.4 8.6 %collective-permute-start.4 = (bf16[128,512]{1,0:T(8,128)(2,1)}, bf16[128,512]{1,0:T(8,128)(2,1)S(1)}, u32[]{:S(2)}, u32[]{:S(2)}) collective-permute-start(bf16[128,512]{1,0:T(8,128)(2,1)} %get-tuple-element.35), channel_id=1, source_target_pairs={{0,8},{4,12},{8,0},{12,4},{1,9},{5,13},{9,1},{13,5},{2,10},{6,14},... | collective-permute-start | bytes 393224 | tf_op jit(solution)/shard_map/ppermute | solution.py:48
  121.4 31.1 %collective-permute-start.10 = (bf16[2,256,512]{2,1,0:T(8,128)(2,1)S(1)}, bf16[2,256,512]{2,1,0:T(8,128)(2,1)}, u32[]{:S(2)}, u32[]{:S(2)}) collective-permute-start(bf16[2,256,512]{2,1,0:T(8,128)(2,1)S(1)} %pad_maximum_fusion.refs_0_), channel_id=1, source_target_pairs={{0,16},{16,0},{1,17},{17,1},{2,18},{18,2},{3,19},{19,3},{4,20},{20... | collective-permute-start | bytes 1572872 | tf_op jit(solution)/shard_map/ppermute | solution.py:496
  126.6 14.6 %all-to-all-start.2 = ((bf16[4,128,512]{2,1,0:T(8,128)(2,1)}), bf16[4,128,512]{2,1,0:T(8,128)(2,1)S(1)}, u32[]{:S(2)}, u32[]{:S(2)}) async-start(bf16[4,128,512]{2,1,0:T(8,128)(2,1)} %reshape.47), calls=%async_computation.2 | async-start | bytes 1048576 | tf_op jit(solution)/shard_map/all_to_all | solution.py:35
  130.1 6.3 %collective-permute-start.3 = (bf16[128,512]{1,0:T(8,128)(2,1)S(1)}, bf16[128,512]{1,0:T(8,128)(2,1)S(1)}, u32[]{:S(2)}, u32[]{:S(2)}) collective-permute-start(bf16[128,512]{1,0:T(8,128)(2,1)S(1)} %copy-done.26), channel_id=1, source_target_pairs={{0,4},{4,8},{8,12},{12,0},{1,5},{5,9},{9,13},{13,1},{2,6},{6,10},{... | collective-permute-start | bytes 393224 | tf_op jit(solution)/shard_map/ppermute | solution.py:48
  136.3 20.9 %collective-permute-start.15 = (bf16[2,256,512]{2,1,0:T(8,128)(2,1)S(1)}, bf16[2,256,512]{2,1,0:T(8,128)(2,1)}, u32[]{:S(2)}, u32[]{:S(2)}) collective-permute-start(bf16[2,256,512]{2,1,0:T(8,128)(2,1)S(1)} %pad_maximum_fusion.1.refs_8_), channel_id=1, source_target_pairs={{0,32},{32,64},{64,96},{96,0},{1,33},{33,65},{65,97},{97,1},{2,34}... | collective-permute-start | bytes 1572872 | tf_op jit(solution)/shard_map/ppermute | solution.py:48
  136.8 5.7 %copy-start = (bf16[2,256,512]{2,1,0:T(8,128)(2,1)}, bf16[2,256,512]{2,1,0:T(8,128)(2,1)S(1)}, u32[]{:S(2)}) copy-start(bf16[2,256,512]{2,1,0:T(8,128)(2,1)S(1)} %collective-permute-done.7.refs_1_) | copy-start | bytes 1572868
  136.8 33.6 %collective-permute-start.16 = (bf16[2,256,512]{2,1,0:T(8,128)(2,1)S(1)}, bf16[2,256,512]{2,1,0:T(8,128)(2,1)}, u32[]{:S(2)}, u32[]{:S(2)}) collective-permute-start(bf16[2,256,512]{2,1,0:T(8,128)(2,1)S(1)} %pad_maximum_fusion.1.refs_8_), channel_id=1, source_target_pairs={{0,64},{32,96},{64,0},{96,32},{1,65},{33,97},{65,1},{97,33},{2,66}... | collective-permute-start | bytes 1572872 | tf_op jit(solution)/shard_map/ppermute | solution.py:48
  141.1 1.4 copy-start.2
  141.1 29.2 %collective-permute-start.17 = (bf16[2,256,512]{2,1,0:T(8,128)(2,1)S(1)}, bf16[2,256,512]{2,1,0:T(8,128)(2,1)}, u32[]{:S(2)}, u32[]{:S(2)}) collective-permute-start(bf16[2,256,512]{2,1,0:T(8,128)(2,1)S(1)} %pad_maximum_fusion.1.refs_8_), channel_id=1, source_target_pairs={{0,96},{32,0},{64,32},{96,64},{1,97},{33,1},{65,33},{97,65},{2,98}... | collective-permute-start | bytes 1572872 | tf_op jit(solution)/shard_map/ppermute | solution.py:48
  142.4 46.1 %copy-start.8 = (bf16[4,8192]{1,0:T(4,128)(2,1)S(1)}, bf16[4,8192]{1,0:T(4,128)(2,1)}, u32[]{:S(2)}) copy-start(bf16[4,8192]{1,0:T(4,128)(2,1)} %prev_ref.3) | copy-start | bytes 196612
  142.4 46.1 %copy-start.9 = (f32[128,512]{1,0:T(8,128)S(1)}, f32[128,512]{1,0:T(8,128)}, u32[]{:S(2)}) copy-start(f32[128,512]{1,0:T(8,128)} %get-tuple-element.36.mixed_ref) | copy-start | bytes 786436
  142.4 46.1 %copy-start.10 = (f32[8192]{0:T(1024)S(1)}, f32[8192]{0:T(1024)}, u32[]{:S(2)}) copy-start(f32[8192]{0:T(1024)} %param.24) | copy-start | bytes 98308
  142.4 46.1 %copy-start.13 = (bf16[128,128]{1,0:T(8,128)(2,1)S(1)}, bf16[128,128]{1,0:T(8,128)(2,1)}, u32[]{:S(2)}) copy-start(bf16[128,128]{1,0:T(8,128)(2,1)} %get-tuple-element.37.reach_ref) | copy-start | bytes 98308
  142.4 46.1 %copy-start.16 = (s32[4]{0:T(128)S(1)}, s32[4]{0:T(128)}, u32[]{:S(2)}) copy-start(s32[4]{0:T(128)} %len_ref.3) | copy-start | bytes 52
  142.5 46.1 %copy-start.17 = (s32[4]{0:T(128)S(1)}, s32[4]{0:T(128)}, u32[]{:S(2)}) copy-start(s32[4]{0:T(128)} %leaf_ref.1) | copy-start | bytes 52
  142.5 46.0 %all-to-all-start.3 = ((bf16[12,128,512]{2,1,0:T(8,128)(2,1)}), bf16[12,128,512]{2,1,0:T(8,128)(2,1)S(1)}, u32[]{:S(2)}, u32[]{:S(2)}) async-start(bf16[12,128,512]{2,1,0:T(8,128)(2,1)} %bitcast.36), calls=%async_computation.3 | async-start | bytes 3145728 | tf_op jit(solution)/shard_map/all_to_all | solution.py:35
  146.4 24.4 %collective-permute-start.18 = (bf16[2,256,512]{2,1,0:T(8,128)(2,1)S(1)}, bf16[2,256,512]{2,1,0:T(8,128)(2,1)S(1)}, u32[]{:S(2)}, u32[]{:S(2)}) collective-permute-start(bf16[2,256,512]{2,1,0:T(8,128)(2,1)S(1)} %pad_maximum_fusion.1.refs_8_), channel_id=1, source_target_pairs={{0,16},{16,0},{1,17},{17,1},{2,18},{18,2},{3,19},{19,3},{4,20},{20... | collective-permute-start | bytes 1572872 | tf_op jit(solution)/shard_map/ppermute | solution.py:510
  152.6 27.2 %collective-permute-start.11 = (bf16[2,256,512]{2,1,0:T(8,128)(2,1)}, bf16[2,256,512]{2,1,0:T(8,128)(2,1)S(1)}, u32[]{:S(2)}, u32[]{:S(2)}) collective-permute-start(bf16[2,256,512]{2,1,0:T(8,128)(2,1)} %copy-done), channel_id=1, source_target_pairs={{0,16},{16,0},{1,17},{17,1},{2,18},{18,2},{3,19},{19,3},{4,20},{20... | collective-permute-start | bytes 1572872 | tf_op jit(solution)/shard_map/ppermute | solution.py:496
  157.2 10.3 %collective-permute-start.22 = (bf16[128,512]{1,0:T(8,128)(2,1)}, bf16[128,512]{1,0:T(8,128)(2,1)S(1)}, u32[]{:S(2)}, u32[]{:S(2)}) collective-permute-start(bf16[128,512]{1,0:T(8,128)(2,1)} %get-tuple-element.42), channel_id=1, source_target_pairs={{0,0},{1,16},{2,32},{3,48},{4,64},{5,80},{6,96},{7,112},{8,128},{9... | collective-permute-start | bytes 393224 | tf_op jit(solution)/shard_map/ppermute | solution.py:507
  167.6 12.2 %copy-start.30 = (bf16[128,512]{1,0:T(8,128)(2,1)}, bf16[128,512]{1,0:T(8,128)(2,1)S(1)}, u32[]{:S(2)}) copy-start(bf16[128,512]{1,0:T(8,128)(2,1)S(1)} %collective-permute-done.22) | copy-start | bytes 393220
  167.6 13.0 %collective-permute-start.25 = (bf16[128,512]{1,0:T(8,128)(2,1)S(1)}, bf16[128,512]{1,0:T(8,128)(2,1)S(1)}, u32[]{:S(2)}, u32[]{:S(2)}) collective-permute-start(bf16[128,512]{1,0:T(8,128)(2,1)S(1)} %collective-permute-done.22), channel_id=1, source_target_pairs={{0,12},{4,0},{8,4},{12,8},{1,13},{5,1},{9,5},{13,9},{2,14},{6,2},{... | collective-permute-start | bytes 393224 | tf_op jit(solution)/shard_map/ppermute | solution.py:48
  170.4 10.7 %collective-permute-start.24 = (bf16[128,512]{1,0:T(8,128)(2,1)S(1)}, bf16[128,512]{1,0:T(8,128)(2,1)S(1)}, u32[]{:S(2)}, u32[]{:S(2)}) collective-permute-start(bf16[128,512]{1,0:T(8,128)(2,1)S(1)} %collective-permute-done.22), channel_id=1, source_target_pairs={{0,8},{4,12},{8,0},{12,4},{1,9},{5,13},{9,1},{13,5},{2,10},{6,14},... | collective-permute-start | bytes 393224 | tf_op jit(solution)/shard_map/ppermute | solution.py:48
  170.4 14.3 %collective-permute-start.23 = (bf16[128,512]{1,0:T(8,128)(2,1)S(1)}, bf16[128,512]{1,0:T(8,128)(2,1)S(1)}, u32[]{:S(2)}, u32[]{:S(2)}) collective-permute-start(bf16[128,512]{1,0:T(8,128)(2,1)S(1)} %collective-permute-done.22), channel_id=1, source_target_pairs={{0,4},{4,8},{8,12},{12,0},{1,5},{5,9},{9,13},{13,1},{2,6},{6,10},{... | collective-permute-start | bytes 393224 | tf_op jit(solution)/shard_map/ppermute | solution.py:48
  171.6 16.8 %collective-permute-start.12 = (bf16[2,256,512]{2,1,0:T(8,128)(2,1)}, bf16[2,256,512]{2,1,0:T(8,128)(2,1)}, u32[]{:S(2)}, u32[]{:S(2)}) collective-permute-start(bf16[2,256,512]{2,1,0:T(8,128)(2,1)} %copy-done.2), channel_id=1, source_target_pairs={{0,16},{16,0},{1,17},{17,1},{2,18},{18,2},{3,19},{19,3},{4,20},{20... | collective-permute-start | bytes 1572872 | tf_op jit(solution)/shard_map/ppermute | solution.py:496
  180.6 7.9 %collective-permute-start.13 = (bf16[2,256,512]{2,1,0:T(8,128)(2,1)}, bf16[2,256,512]{2,1,0:T(8,128)(2,1)}, u32[]{:S(2)}, u32[]{:S(2)}) collective-permute-start(bf16[2,256,512]{2,1,0:T(8,128)(2,1)} %collective-permute-done.9.refs_3_), channel_id=1, source_target_pairs={{0,16},{16,0},{1,17},{17,1},{2,18},{18,2},{3,19},{19,3},{4,20},{20... | collective-permute-start | bytes 1572872 | tf_op jit(solution)/shard_map/ppermute | solution.py:496
  180.6 4.0 %copy-start.31 = (bf16[128,512]{1,0:T(8,128)(2,1)}, bf16[128,512]{1,0:T(8,128)(2,1)S(1)}, u32[]{:S(2)}) copy-start(bf16[128,512]{1,0:T(8,128)(2,1)S(1)} %collective-permute-done.25) | copy-start | bytes 393220
  180.6 7.9 %collective-permute-start.19 = (bf16[2,256,512]{2,1,0:T(8,128)(2,1)}, bf16[2,256,512]{2,1,0:T(8,128)(2,1)}, u32[]{:S(2)}, u32[]{:S(2)}) collective-permute-start(bf16[2,256,512]{2,1,0:T(8,128)(2,1)} %collective-permute-done.15.refs_9_), channel_id=1, source_target_pairs={{0,16},{16,0},{1,17},{17,1},{2,18},{18,2},{3,19},{19,3},{4,20},{20... | collective-permute-start | bytes 1572872 | tf_op jit(solution)/shard_map/ppermute | solution.py:510
  181.1 3.5 %copy-start.32 = (bf16[128,512]{1,0:T(8,128)(2,1)}, bf16[128,512]{1,0:T(8,128)(2,1)S(1)}, u32[]{:S(2)}) copy-start(bf16[128,512]{1,0:T(8,128)(2,1)S(1)} %collective-permute-done.24) | copy-start | bytes 393220
  181.1 7.3 %collective-permute-start.20 = (bf16[2,256,512]{2,1,0:T(8,128)(2,1)}, bf16[2,256,512]{2,1,0:T(8,128)(2,1)}, u32[]{:S(2)}, u32[]{:S(2)}) collective-permute-start(bf16[2,256,512]{2,1,0:T(8,128)(2,1)} %collective-permute-done.16.refs_10_), channel_id=1, source_target_pairs={{0,16},{16,0},{1,17},{17,1},{2,18},{18,2},{3,19},{19,3},{4,20},{20... | collective-permute-start | bytes 1572872 | tf_op jit(solution)/shard_map/ppermute | solution.py:510
  185.3 3.2 %collective-permute-start.21 = (bf16[2,256,512]{2,1,0:T(8,128)(2,1)}, bf16[2,256,512]{2,1,0:T(8,128)(2,1)}, u32[]{:S(2)}, u32[]{:S(2)}) collective-permute-start(bf16[2,256,512]{2,1,0:T(8,128)(2,1)} %collective-permute-done.17.refs_11_), channel_id=1, source_target_pairs={{0,16},{16,0},{1,17},{17,1},{2,18},{18,2},{3,19},{19,3},{4,20},{20... | collective-permute-start | bytes 1572872 | tf_op jit(solution)/shard_map/ppermute | solution.py:510
  188.5 1.0 copy-start.1
  189.6 1.0 copy-start.3
  190.6 1.0 copy-start.5
  193.5 6.3 %copy-start.21 = (bf16[4,128,512]{2,1,0:T(8,128)(2,1)S(1)}, bf16[4,128,512]{2,1,0:T(8,128)(2,1)}, u32[]{:S(2)}) copy-start(bf16[4,128,512]{2,1,0:T(8,128)(2,1)} %pad_maximum_fusion.2) | copy-start | bytes 1572868
  199.7 1.5 copy-start.15
  201.3 4.4 %copy-start.12 = (bf16[128,512]{1,0:T(8,128)(2,1)S(1)}, bf16[128,512]{1,0:T(8,128)(2,1)}, u32[]{:S(2)}) copy-start(bf16[128,512]{1,0:T(8,128)(2,1)} %copy-done.11) | copy-start | bytes 393220
  201.3 33.6 %all-to-all-start.4 = ((bf16[16,128,512]{2,1,0:T(8,128)(2,1)}), bf16[16,128,512]{2,1,0:T(8,128)(2,1)S(1)}, u32[]{:S(2)}, u32[]{:S(2)}) async-start(bf16[16,128,512]{2,1,0:T(8,128)(2,1)} %bitcast.35), calls=%async_computation.4 | async-start | bytes 4194304 | tf_op jit(solution)/shard_map/all_to_all | solution.py:35
  205.7 15.1 %collective-permute-start.29 = (bf16[128,512]{1,0:T(8,128)(2,1)S(1)}, bf16[128,512]{1,0:T(8,128)(2,1)S(1)}, u32[]{:S(2)}, u32[]{:S(2)}) collective-permute-start(bf16[128,512]{1,0:T(8,128)(2,1)S(1)} %copy-done.12), channel_id=1, source_target_pairs={{0,128},{128,0},{1,129},{129,1},{2,130},{130,2},{3,131},{131,3},{4... | collective-permute-start | bytes 393224 | tf_op jit(solution)/shard_map/ppermute | solution.py:528
  217.2 5.1 %collective-permute-start.28 = (bf16[128,512]{1,0:T(8,128)(2,1)S(1)}, bf16[128,512]{1,0:T(8,128)(2,1)S(1)}, u32[]{:S(2)}, u32[]{:S(2)}) collective-permute-start(bf16[128,512]{1,0:T(8,128)(2,1)S(1)} %copy-done.12), channel_id=1, source_target_pairs={{0,96},{32,0},{64,32},{96,64},{1,97},{33,1},{65,33},{97,65},{2,98}... | collective-permute-start | bytes 393224 | tf_op jit(solution)/shard_map/ppermute | solution.py:48
  217.2 6.0 %collective-permute-start.27 = (bf16[128,512]{1,0:T(8,128)(2,1)S(1)}, bf16[128,512]{1,0:T(8,128)(2,1)S(1)}, u32[]{:S(2)}, u32[]{:S(2)}) collective-permute-start(bf16[128,512]{1,0:T(8,128)(2,1)S(1)} %copy-done.12), channel_id=1, source_target_pairs={{0,64},{32,96},{64,0},{96,32},{1,65},{33,97},{65,1},{97,33},{2,66}... | collective-permute-start | bytes 393224 | tf_op jit(solution)/shard_map/ppermute | solution.py:48
  217.2 10.5 %collective-permute-start.26 = (bf16[128,512]{1,0:T(8,128)(2,1)S(1)}, bf16[128,512]{1,0:T(8,128)(2,1)S(1)}, u32[]{:S(2)}, u32[]{:S(2)}) collective-permute-start(bf16[128,512]{1,0:T(8,128)(2,1)S(1)} %copy-done.12), channel_id=1, source_target_pairs={{0,32},{32,64},{64,96},{96,0},{1,33},{33,65},{65,97},{97,1},{2,34}... | collective-permute-start | bytes 393224 | tf_op jit(solution)/shard_map/ppermute | solution.py:48
  220.8 7.7 %collective-permute-start.32 = (bf16[128,512]{1,0:T(8,128)(2,1)S(1)}, bf16[128,512]{1,0:T(8,128)(2,1)S(1)}, u32[]{:S(2)}, u32[]{:S(2)}) collective-permute-start(bf16[128,512]{1,0:T(8,128)(2,1)S(1)} %collective-permute-done.29), channel_id=1, source_target_pairs={{0,96},{32,0},{64,32},{96,64},{1,97},{33,1},{65,33},{97,65},{2,98}... | collective-permute-start | bytes 393224 | tf_op jit(solution)/shard_map/ppermute | solution.py:48
  221.8 6.7 %collective-permute-start.31 = (bf16[128,512]{1,0:T(8,128)(2,1)S(1)}, bf16[128,512]{1,0:T(8,128)(2,1)S(1)}, u32[]{:S(2)}, u32[]{:S(2)}) collective-permute-start(bf16[128,512]{1,0:T(8,128)(2,1)S(1)} %collective-permute-done.29), channel_id=1, source_target_pairs={{0,64},{32,96},{64,0},{96,32},{1,65},{33,97},{65,1},{97,33},{2,66}... | collective-permute-start | bytes 393224 | tf_op jit(solution)/shard_map/ppermute | solution.py:48
  222.2 9.1 %collective-permute-start.30 = (bf16[128,512]{1,0:T(8,128)(2,1)S(1)}, bf16[128,512]{1,0:T(8,128)(2,1)S(1)}, u32[]{:S(2)}, u32[]{:S(2)}) collective-permute-start(bf16[128,512]{1,0:T(8,128)(2,1)S(1)} %collective-permute-done.29), channel_id=1, source_target_pairs={{0,32},{32,64},{64,96},{96,0},{1,33},{33,65},{65,97},{97,1},{2,34}... | collective-permute-start | bytes 393224 | tf_op jit(solution)/shard_map/ppermute | solution.py:48
  227.7 7.2 %copy-start.22 = (bf16[4,128,512]{2,1,0:T(8,128)(2,1)}, bf16[4,128,512]{2,1,0:T(8,128)(2,1)S(1)}, u32[]{:S(2)}) copy-start(bf16[4,128,512]{2,1,0:T(8,128)(2,1)S(1)} %pad_maximum_fusion.3.e0_ref) | copy-start | bytes 1572868
  227.7 5.5 %collective-permute-start.33 = (bf16[4,128,512]{2,1,0:T(8,128)(2,1)S(1)}, bf16[4,128,512]{2,1,0:T(8,128)(2,1)S(1)}, u32[]{:S(2)}, u32[]{:S(2)}) collective-permute-start(bf16[4,128,512]{2,1,0:T(8,128)(2,1)S(1)} %pad_maximum_fusion.3.e0_ref), channel_id=1, source_target_pairs={{0,16},{16,0},{1,17},{17,1},{2,18},{18,2},{3,19},{19,3},{4,20},{20... | collective-permute-start | bytes 1572872 | tf_op jit(solution)/shard_map/ppermute | solution.py:532
  231.4 3.5 %copy-start.23 = (bf16[4,128,512]{2,1,0:T(8,128)(2,1)}, bf16[4,128,512]{2,1,0:T(8,128)(2,1)S(1)}, u32[]{:S(2)}) copy-start(bf16[4,128,512]{2,1,0:T(8,128)(2,1)S(1)} %pad_maximum_fusion.4.e1_ref) | copy-start | bytes 1572868
  231.4 3.4 %collective-permute-start.34 = (bf16[4,128,512]{2,1,0:T(8,128)(2,1)S(1)}, bf16[4,128,512]{2,1,0:T(8,128)(2,1)}, u32[]{:S(2)}, u32[]{:S(2)}) collective-permute-start(bf16[4,128,512]{2,1,0:T(8,128)(2,1)S(1)} %pad_maximum_fusion.4.e1_ref), channel_id=1, source_target_pairs={{0,16},{16,0},{1,17},{17,1},{2,18},{18,2},{3,19},{19,3},{4,20},{20... | collective-permute-start | bytes 1572872 | tf_op jit(solution)/shard_map/ppermute | solution.py:532
  234.9 1.3 copy-start.18
  (10 other events, 7.9 us)

commit v6 on v5

--- a/solution.py
+++ b/solution.py
@@ -8,6 +8,7 @@
 from jax.sharding import Mesh
 from jax.sharding import PartitionSpec as P
 
+HEADS = 32
 KV_HEADS = 4
 HEAD = 128
 NODES = 32
@@ -66,82 +67,86 @@
     rank_ref, len_ref, par_ref, q_ref, ck_ref, cv_ref, tk_ref, tv_ref,
     out_ref, reach_ref, pick_ref, stat_ref,
 ):
+    r = pl.program_id(0)
     rank = rank_ref[0]
-    row, lane = same_request()
-    base = (lane // NODES) * NODES
-    tile = jnp.where(
-        lax.broadcasted_iota(jnp.int32, (NODES, 128), 0)
-        == lax.broadcasted_iota(jnp.int32, (NODES, 128), 1) % NODES,
-        1.0,
-        0.0,
-    )
-    wide = dot(par_ref[...].astype(F32).astype(BF16), tile.astype(BF16), ((1,), (0,)))
-    lane_request = lax.broadcasted_iota(jnp.int32, (1, 128), 1) // NODES
-    parent = wide[0:1]
-    for r in range(1, 4):
-        parent = jnp.where(lane_request == r, wide[r : r + 1], parent)
-    parent = parent.astype(jnp.int32)
-    rooted = jnp.where(parent < 0, NODES - 1, parent)
-    pick_ref[...] = jnp.where(row == base + rooted, 1.0, 0.0).astype(BF16)
-    up = jnp.where(row == base + parent, jnp.where(parent >= 0, 1.0, 0.0), 0.0)
-    reach = (jnp.where(row == lane, 1.0, 0.0) + up).astype(BF16)
-    for _ in range((NODES - 1).bit_length()):
-        reach = jnp.minimum(dot(reach, reach, ((1,), (0,))), 1.0).astype(BF16)
-    reach_ref[...] = reach
-    own = jnp.where(row % NODES == 2 * rank + lane, jnp.where(lane < 2, 1.0, 0.0), 0.0)
-    stat_ref[...] = dot(reach, own.astype(BF16), ((0,), (0,)))
+
+    @pl.when(r == 0)
+    def trees():
+        row, lane = same_request()
+        base = (lane // NODES) * NODES
+        tile = jnp.where(
+            lax.broadcasted_iota(jnp.int32, (NODES, 128), 0)
+            == lax.broadcasted_iota(jnp.int32, (NODES, 128), 1) % NODES,
+            1.0,
+            0.0,
+        )
+        wide = dot(par_ref[...].astype(F32).astype(BF16), tile.astype(BF16), ((1,), (0,)))
+        lane_request = lax.broadcasted_iota(jnp.int32, (1, 128), 1) // NODES
+        parent = wide[0:1]
+        for r in range(1, 4):
+            parent = jnp.where(lane_request == r, wide[r : r + 1], parent)
+        parent = parent.astype(jnp.int32)
+        rooted = jnp.where(parent < 0, NODES - 1, parent)
+        pick_ref[...] = jnp.where(row == base + rooted, 1.0, 0.0).astype(BF16)
+        up = jnp.where(row == base + parent, jnp.where(parent >= 0, 1.0, 0.0), 0.0)
+        reach = (jnp.where(row == lane, 1.0, 0.0) + up).astype(BF16)
+        for _ in range((NODES - 1).bit_length()):
+            reach = jnp.minimum(dot(reach, reach, ((1,), (0,))), 1.0).astype(BF16)
+        reach_ref[...] = reach
+        own = jnp.where(row % NODES == 2 * rank + lane, jnp.where(lane < 2, 1.0, 0.0), 0.0)
+        stat_ref[...] = dot(reach, own.astype(BF16), ((0,), (0,)))
+
     scale = 1.0 / math.sqrt(HEAD)
     span = ck_ref.shape[1]
     slot = lax.broadcasted_iota(jnp.int32, (256, span), 1) + rank * span
     wide_lane = lax.broadcasted_iota(jnp.int32, (NODES, 128), 1)
 
-    def attend_one(r, carry):
-        own_rows = pl.ds(pl.multiple_of(r * NODES, NODES), NODES)
-        live = slot < len_ref[r]
-        seen = stat_ref[own_rows, :][:, : tk_ref.shape[1]]
-        seen = jnp.concatenate([seen] * 8, axis=0) > 0.5
-        stats = jnp.zeros((NODES, 128), F32)
-        for k in range(KV_HEADS):
-            head = slice(k * HEAD, (k + 1) * HEAD)
-            query = jnp.concatenate(
-                [q_ref[r, :, (k * 8 + g) * HEAD : (k * 8 + g + 1) * HEAD] for g in range(8)], axis=0
-            )
-            scores = dot(query, ck_ref[r, :, head], ((1,), (1,))) * scale
-            tree = dot(query, tk_ref[r, :, head], ((1,), (1,))) * scale
-            scores = jnp.where(live, scores, NEG_FILL)
-            tree = jnp.where(seen, tree, NEG_FILL)
-            top = jnp.maximum(
-                jnp.max(scores, axis=1, keepdims=True), jnp.max(tree, axis=1, keepdims=True)
-            )
-            top = top.astype(BF16).astype(F32)
-            probs = jnp.where(live, jnp.exp(scores - top), 0.0).astype(BF16)
-            tree = jnp.where(seen, jnp.exp(tree - top), 0.0).astype(BF16)
-            total = jnp.sum(probs.astype(F32), axis=1, keepdims=True) + jnp.sum(
-                tree.astype(F32), axis=1, keepdims=True
-            )
-            high = total.astype(BF16).astype(F32)
-            low = total - high
-            value = dot(probs, cv_ref[r, :, head], ((1,), (0,))) + dot(
-                tree, tv_ref[r, :, head], ((1,), (0,))
-            )
-            value = value.astype(BF16)
-            for g in range(8):
-                h = k * 8 + g
-                part = slice(g * NODES, (g + 1) * NODES)
-                out_ref[h // 2, own_rows, (h % 2) * HEAD : (h % 2 + 1) * HEAD] = value[part]
-                for at, column in enumerate((top, high, low)):
-                    stats = jnp.where(wide_lane == h * 4 + at, column[part], stats)
-        stat_ref[own_rows, :] = stats
-        return carry
-
-    lax.fori_loop(0, q_ref.shape[0], attend_one, 0)
-    turned = jnp.transpose(stat_ref[...])
-    empty = jnp.zeros((8, 128), F32)
-    blank = jnp.zeros((16, 128), BF16)
-    for owner in range(N_TP):
-        block = jnp.concatenate([turned[owner * 8 : (owner + 1) * 8], empty], axis=0)
-        out_ref[owner, 128:144, 0:128] = block.astype(BF16)
-        out_ref[owner, 128:144, 128:256] = blank
+    own_rows = pl.ds(pl.multiple_of(r * NODES, NODES), NODES)
+    live = slot < len_ref[r]
+    seen = stat_ref[own_rows, :][:, : tk_ref.shape[1]]
+    seen = jnp.concatenate([seen] * 8, axis=0) > 0.5
+    stats = jnp.zeros((NODES, 128), F32)
+    for k in range(KV_HEADS):
+        head = slice(k * HEAD, (k + 1) * HEAD)
+        query = jnp.concatenate(
+            [q_ref[0, :, (k * 8 + g) * HEAD : (k * 8 + g + 1) * HEAD] for g in range(8)], axis=0
+        )
+        scores = dot(query, ck_ref[0, :, head], ((1,), (1,))) * scale
+        tree = dot(query, tk_ref[0, :, head], ((1,), (1,))) * scale
+        scores = jnp.where(live, scores, NEG_FILL)
+        tree = jnp.where(seen, tree, NEG_FILL)
+        top = jnp.maximum(
+            jnp.max(scores, axis=1, keepdims=True), jnp.max(tree, axis=1, keepdims=True)
+        )
+        top = jnp.maximum(top, 0.5 * NEG_FILL).astype(BF16).astype(F32)
+        probs = jnp.exp(scores - top).astype(BF16)
+        tree = jnp.exp(tree - top).astype(BF16)
+        total = jnp.sum(probs.astype(F32), axis=1, keepdims=True) + jnp.sum(
+            tree.astype(F32), axis=1, keepdims=True
+        )
+        high = total.astype(BF16).astype(F32)
+        low = total - high
+        value = dot(probs, cv_ref[0, :, head], ((1,), (0,))) + dot(
+            tree, tv_ref[0, :, head], ((1,), (0,))
+        )
+        value = value.astype(BF16)
+        for g in range(8):
+            h = k * 8 + g
+            part = slice(g * NODES, (g + 1) * NODES)
+            out_ref[h // 2, own_rows, (h % 2) * HEAD : (h % 2 + 1) * HEAD] = value[part]
+            for at, column in enumerate((top, high, low)):
+                stats = jnp.where(wide_lane == h * 4 + at, column[part], stats)
+    stat_ref[own_rows, :] = stats
+
+    @pl.when(r == 3)
+    def statistics():
+        turned = jnp.transpose(stat_ref[...])
+        empty = jnp.zeros((8, 128), F32)
+        blank = jnp.zeros((16, 128), BF16)
+        for owner in range(N_TP):
+            block = jnp.concatenate([turned[owner * 8 : (owner + 1) * 8], empty], axis=0)
+            out_ref[owner, 128:144, 0:128] = block.astype(BF16)
+            out_ref[owner, 128:144, 128:256] = blank
 
 
 def project_kernel(parcel_ref, weight_ref, out_ref, att_ref):
@@ -316,8 +321,20 @@
             jax.ShapeDtypeStruct((128, 128), BF16),
             jax.ShapeDtypeStruct((128, 128), BF16),
         ),
-        in_specs=[in_smem(), in_smem()] + [in_vmem()] * 6,
-        out_specs=(in_vmem(), in_vmem(), in_vmem()),
+        grid=(4,),
+        in_specs=[
+            in_smem(),
+            in_smem(),
+            pl.BlockSpec((4, NODES), lambda r: (0, 0)),
+            pl.BlockSpec((1, NODES, HEADS * HEAD), lambda r: (r, 0, 0)),
+        ]
+        + [pl.BlockSpec((1, 256, KV_HEADS * HEAD), lambda r: (r, 0, 0))] * 2
+        + [pl.BlockSpec((1, 2, KV_HEADS * HEAD), lambda r: (r, 0, 0))] * 2,
+        out_specs=(
+            pl.BlockSpec((N_TP, 144, 2 * HEAD), lambda r: (0, 0, 0)),
+            pl.BlockSpec((128, 128), lambda r: (0, 0)),
+            pl.BlockSpec((128, 128), lambda r: (0, 0)),
+        ),
         scratch_shapes=[pltpu.VMEM((128, 128), F32)],
         cost_estimate=pl.CostEstimate(
             flops=2 * 2 * 16 * 256 * 256 * 128, bytes_accessed=4 << 20, transcendentals=16 * 256 * 256
@@ -509,6 +526,7 @@
     )
     other_lower = [lax.ppermute(part, "c", turn(2, 1)) for part in lower]
     columns = turns(swapped, "zl", 4)
+    columns = spread(columns, "x", 4).reshape(N_REQ, rows, block)
     own_features, scaled_err, loss = predict(
         source,
         rank,
@@ -523,8 +541,6 @@
         pick,
         upper + other_upper + lower + other_lower,
     )
-    columns, scaled_err = lax.optimization_barrier((columns, scaled_err))
-    columns = spread(columns, "x", 4).reshape(N_REQ, rows, block)
     far_err = lax.ppermute(scaled_err, "zh", turn(2, 1))
     err = passed(scaled_err, "y", 4)
     far_err = passed(far_err, "y", 4)

time: 272 us -> 282 us (1.037)
  blocking collectives: 25.6 us -> 54.2 us
  waiting for transfers between devices: 76.9 us -> 69 us
  starting transfers between devices: 112 us -> 105 us
  local copies, waits for them, and re-layouts: 17.6 us -> 13.5 us
    all_to_all x1 -> x2, blocking collectives: 25.6 us -> 54.2 us  [exchange(): return lax.all_to_all(value, axis, 0, 0, tiled=True)]
    all_to_all x5 -> x4, waiting for transfers between devices: 44 us -> 24.5 us  [exchange(): return lax.all_to_all(value, axis, 0, 0, tiled=True)]
    ppermute x20, waiting for transfers between devices: 19.1 us -> 31.4 us  [passed(): lax.ppermute(value, axis, turn(count, step))]
    ppermute x1, starting transfers between devices: 11.5 us -> 0.1 us  [body(): far_err = lax.ppermute(scaled_err, 'zh', turn(2, 1))]
    ppermute x4, starting transfers between devices: 10.8 us -> 1.3 us  [body(): other_lower = [lax.ppermute(part, 'c', turn(2, 1)) for part in lower]]
    ppermute x20, starting transfers between devices: 38.9 us -> 46.6 us  [passed(): lax.ppermute(value, axis, turn(count, step))]
    ppermute x1, starting transfers between devices: 2.87 us -> 9.51 us  [body(): lax.ppermute(table, REQ + TP, [(i * N_TP + j, j * N_TP + i) for i in rang...]
    unnamed x68 -> x52, local copies, waits for them, and re-layouts: 13 us -> 7.83 us
  transfers between devices with their start and end apart: 40 -> 39, of which waited for: 12 -> 14; matrix products, arithmetic and copies ran while one was open for 2% -> 3% of each run, Pallas kernels for 2% -> 2%
where the time goes in v6:
time: 282 us; the launch traced here: 281 us
  starting transfers between devices  105 us (37%)
  waiting for transfers between devices  69 us (24%)
  blocking collectives  54.2 us (19%)
  Pallas kernels  34.3 us (12%)
  local copies, waits for them, and re-layouts  13.5 us (5%)
  other arithmetic  3.6 us (1%)
    all_to_all x2, blocking collectives, exchange(): return lax.all_to_all(value, axis, 0, 0, tiled=True)  54.2 us
    ppermute x20, starting transfers between devices, passed(): lax.ppermute(value, axis, turn(count, step))  46.6 us
    ppermute x20, waiting for transfers between devices, passed(): lax.ppermute(value, axis, turn(count, step))  31.4 us
    all_to_all x4, waiting for transfers between devices, exchange(): return lax.all_to_all(value, axis, 0, 0, tiled=True)  24.5 us
    all_to_all x4, starting transfers between devices, exchange(): return lax.all_to_all(value, axis, 0, 0, tiled=True)  21.4 us
    ppermute x4, starting transfers between devices, body(): other_upper = [lax.ppermute(part, 'c', turn(2, 1)) for part in upper]  10.3 us
    ppermute x1, starting transfers between devices, body(): lax.ppermute(table, REQ + TP, [(i * N_TP + j, j * N_TP + i) for i in rang...  9.51 us
    pallas_call x1, Pallas kernels, attend(): pl.pallas_call(attend_kernel, out_shape=(jax.ShapeDtypeStruct((N_TP, 144,...  8.91 us
  transfers between devices with their start and end apart: 39, of which 14 were waited for; matrix products, arithmetic and copies ran while one was open for 3% of the time, Pallas kernels for 2%

profile of v6, /device:TPU:1, one launch (start us, length us, event | category | flops | bytes accessed | tf_op | source)
XLA Modules:
  0.0 281.0 jit_solution(15419355430237536730)
XLA Ops:
  0.7 8.9 %attend.1 = (bf16[16,144,256]{2,1,0:T(8,128)(2,1)}, bf16[128,128]{1,0:T(8,128)(2,1)}, bf16[128,128]{1,0:T(8,128)(2,1)}) custom-call(s32[1]{0:T(128)} %bitcast.rank_ref, s32[4]{0:T(128)} %len_ref.3, s32[4,32]{1,0:T(4,128)} %par_ref.1, bf16[4,32,4096]{2,1,0:T(8,128)(2,1)} %q_ref.1, bf16[4,256,512]{2,1,0:T(8,128)(2,1)} %ck_ref.1, bf16[4,256,512]{2,1,0:T(8,128)(2,1)} %cv_ref.1, ...), custom_call_target="tpu_custom_call" | custom-call | flops 536870912 | bytes 4194304 | tf_op jit(solution)/shard_map/attend/pallas_call | solution.py:317
  9.6 9.0 %all-to-all-start = ((bf16[16,144,256]{2,1,0:T(8,128)(2,1)}), bf16[16,144,256]{2,1,0:T(8,128)(2,1)S(1)}, u32[]{:S(2)}, u32[]{:S(2)}) async-start(bf16[16,144,256]{2,1,0:T(8,128)(2,1)} %get-tuple-element.27), calls=%async_computation | async-start | bytes 2359296 | tf_op jit(solution)/shard_map/all_to_all | solution.py:36
  18.6 24.4 %all-to-all-done.parcel_ref = bf16[16,144,256]{2,1,0:T(8,128)(2,1)S(1)} async-done(((bf16[16,144,256]{2,1,0:T(8,128)(2,1)}), bf16[16,144,256]{2,1,0:T(8,128)(2,1)S(1)}, u32[]{:S(2)}, u32[]{:S(2)}) %all-to-all-start) | async-done | bytes 1179680 | tf_op jit(solution)/shard_map/all_to_all | solution.py:36
  43.1 1.0 copy-done.14
  44.1 6.0 %project.1 = bf16[4,4,128,512]{3,2,1,0:T(8,128)(2,1)} custom-call(bf16[16,144,256]{2,1,0:T(8,128)(2,1)} %copy-done.14, bf16[256,8192]{1,0:T(8,128)(2,1)} %weight_ref.2), custom_call_target="tpu_custom_call" | custom-call | flops 536870912 | bytes 7340032 | tf_op jit(solution)/shard_map/project/pallas_call | solution.py:347
  50.1 29.0 %all_to_all.36.along_ref = bf16[4,4,128,512]{3,2,1,0:T(8,128)(2,1)} all-to-all(bf16[4,4,128,512]{3,2,1,0:T(8,128)(2,1)} %project.1), channel_id=1, replica_groups=mesh['zh'=2,'y'=4,'c'=2,'zl'=4,'x'=4] {'x'}, dimensions={0} | all-to-all | bytes 4194304 | tf_op jit(solution)/shard_map/all_to_all | solution.py:36
  79.1 2.6 fold.1
  81.6 3.6 %collective-permute-start = (bf16[128,512]{1,0:T(8,128)(2,1)}, bf16[128,512]{1,0:T(8,128)(2,1)S(1)}, u32[]{:S(2)}, u32[]{:S(2)}) collective-permute-start(bf16[128,512]{1,0:T(8,128)(2,1)} %get-tuple-element.30), channel_id=1, source_target_pairs={{0,4},{4,8},{8,12},{12,0},{1,5},{5,9},{9,13},{13,1},{2,6},{6,10},{... | collective-permute-start | bytes 393224 | tf_op jit(solution)/shard_map/ppermute | solution.py:517
  85.3 2.6 collective-permute-start.1
  87.8 2.4 collective-permute-start.2
  90.2 3.6 %collective-permute-done.1.two_ref = bf16[128,512]{1,0:T(8,128)(2,1)S(1)} collective-permute-done((bf16[128,512]{1,0:T(8,128)(2,1)}, bf16[128,512]{1,0:T(8,128)(2,1)S(1)}, u32[]{:S(2)}, u32[]{:S(2)}) %collective-permute-start.1) | collective-permute-done | bytes 131104 | tf_op jit(solution)/shard_map/ppermute | solution.py:517
  94.5 2.1 settle.1
  96.6 1.7 reshape.47
  98.3 3.5 %all-to-all-start.2 = ((bf16[4,128,512]{2,1,0:T(8,128)(2,1)}), bf16[4,128,512]{2,1,0:T(8,128)(2,1)S(1)}, u32[]{:S(2)}, u32[]{:S(2)}) async-start(bf16[4,128,512]{2,1,0:T(8,128)(2,1)} %reshape.47), calls=%async_computation.2 | async-start | bytes 1048576 | tf_op jit(solution)/shard_map/all_to_all | solution.py:36
  101.8 4.3 %collective-permute-start.6 = (bf16[256,512]{1,0:T(8,128)(2,1)S(1)}, bf16[256,512]{1,0:T(8,128)(2,1)S(1)}, u32[]{:S(2)}, u32[]{:S(2)}) collective-permute-start(bf16[256,512]{1,0:T(8,128)(2,1)S(1)} %get-tuple-element.37), channel_id=1, source_target_pairs={{0,128},{128,0},{1,129},{129,1},{2,130},{130,2},{3,131},{131,3},{4... | collective-permute-start | bytes 786440 | tf_op jit(solution)/shard_map/ppermute | solution.py:49
  106.1 4.7 %collective-permute-start.3 = (bf16[128,512]{1,0:T(8,128)(2,1)}, bf16[128,512]{1,0:T(8,128)(2,1)S(1)}, u32[]{:S(2)}, u32[]{:S(2)}) collective-permute-start(bf16[128,512]{1,0:T(8,128)(2,1)} %get-tuple-element.33), channel_id=1, source_target_pairs={{0,4},{4,8},{8,12},{12,0},{1,5},{5,9},{9,13},{13,1},{2,6},{6,10},{... | collective-permute-start | bytes 393224 | tf_op jit(solution)/shard_map/ppermute | solution.py:49
  110.8 2.7 collective-permute-start.4
  113.5 1.2 collective-permute-start.14
  114.7 10.3 %collective-permute-done.3 = bf16[128,512]{1,0:T(8,128)(2,1)S(1)} collective-permute-done((bf16[128,512]{1,0:T(8,128)(2,1)}, bf16[128,512]{1,0:T(8,128)(2,1)S(1)}, u32[]{:S(2)}, u32[]{:S(2)}) %collective-permute-start.3) | collective-permute-done | bytes 131104 | tf_op jit(solution)/shard_map/ppermute | solution.py:49
  125.0 14.8 %collective-permute-done.4 = bf16[128,512]{1,0:T(8,128)(2,1)S(1)} collective-permute-done((bf16[128,512]{1,0:T(8,128)(2,1)}, bf16[128,512]{1,0:T(8,128)(2,1)S(1)}, u32[]{:S(2)}, u32[]{:S(2)}) %collective-permute-start.4) | collective-permute-done | bytes 131104 | tf_op jit(solution)/shard_map/ppermute | solution.py:49
  139.8 1.3 broadcast_in_dim.4
  141.1 4.3 %all-to-all-start.3 = ((bf16[12,128,512]{2,1,0:T(8,128)(2,1)}), bf16[12,128,512]{2,1,0:T(8,128)(2,1)S(1)}, u32[]{:S(2)}, u32[]{:S(2)}) async-start(bf16[12,128,512]{2,1,0:T(8,128)(2,1)} %bitcast.36), calls=%async_computation.3 | async-start | bytes 3145728 | tf_op jit(solution)/shard_map/all_to_all | solution.py:36
  145.4 0.7 copy-done.21
  146.1 1.0 pad_maximum_fusion.refs_0_
  147.1 1.4 collective-permute-start.7
  148.5 2.6 collective-permute-start.8
  151.1 1.1 collective-permute-start.9
  152.2 0.7 copy-done.20
  152.9 1.0 pad_maximum_fusion.1.refs_8_
  154.3 9.5 %collective-permute-start.22 = (bf16[128,512]{1,0:T(8,128)(2,1)S(1)}, bf16[128,512]{1,0:T(8,128)(2,1)S(1)}, u32[]{:S(2)}, u32[]{:S(2)}) collective-permute-start(bf16[128,512]{1,0:T(8,128)(2,1)S(1)} %copy-done.25), channel_id=1, source_target_pairs={{0,0},{1,16},{2,32},{3,48},{4,64},{5,80},{6,96},{7,112},{8,128},{9... | collective-permute-start | bytes 393224 | tf_op jit(solution)/shard_map/ppermute | solution.py:524
  163.9 3.2 %collective-permute-done.22 = bf16[128,512]{1,0:T(8,128)(2,1)S(1)} collective-permute-done((bf16[128,512]{1,0:T(8,128)(2,1)S(1)}, bf16[128,512]{1,0:T(8,128)(2,1)S(1)}, u32[]{:S(2)}, u32[]{:S(2)}) %collective-permute-start.22) | collective-permute-done | bytes 131104 | tf_op jit(solution)/shard_map/ppermute | solution.py:524
  167.1 5.8 %collective-permute-start.23 = (bf16[128,512]{1,0:T(8,128)(2,1)S(1)}, bf16[128,512]{1,0:T(8,128)(2,1)S(1)}, u32[]{:S(2)}, u32[]{:S(2)}) collective-permute-start(bf16[128,512]{1,0:T(8,128)(2,1)S(1)} %collective-permute-done.22), channel_id=1, source_target_pairs={{0,4},{4,8},{8,12},{12,0},{1,5},{5,9},{9,13},{13,1},{2,6},{6,10},{... | collective-permute-start | bytes 393224 | tf_op jit(solution)/shard_map/ppermute | solution.py:49
  172.9 2.0 collective-permute-start.24
  175.0 8.4 %collective-permute-start.25 = (bf16[128,512]{1,0:T(8,128)(2,1)S(1)}, bf16[128,512]{1,0:T(8,128)(2,1)S(1)}, u32[]{:S(2)}, u32[]{:S(2)}) collective-permute-start(bf16[128,512]{1,0:T(8,128)(2,1)S(1)} %collective-permute-done.22), channel_id=1, source_target_pairs={{0,12},{4,0},{8,4},{12,8},{1,13},{5,1},{9,5},{13,9},{2,14},{6,2},{... | collective-permute-start | bytes 393224 | tf_op jit(solution)/shard_map/ppermute | solution.py:49
  183.5 0.8 collective-permute-start.17
  184.3 8.9 %collective-permute-start.10 = (bf16[2,256,512]{2,1,0:T(8,128)(2,1)S(1)}, bf16[2,256,512]{2,1,0:T(8,128)(2,1)}, u32[]{:S(2)}, u32[]{:S(2)}) collective-permute-start(bf16[2,256,512]{2,1,0:T(8,128)(2,1)S(1)} %pad_maximum_fusion.refs_0_), channel_id=1, source_target_pairs={{0,16},{16,0},{1,17},{17,1},{2,18},{18,2},{3,19},{19,3},{4,20},{20... | collective-permute-start | bytes 1572872 | tf_op jit(solution)/shard_map/ppermute | solution.py:513
  194.0 0.9 pad_maximum_fusion.2
  194.9 2.6 broadcast_in_dim.5
  197.5 4.6 %all-to-all-start.4 = ((bf16[16,128,512]{2,1,0:T(8,128)(2,1)}), bf16[16,128,512]{2,1,0:T(8,128)(2,1)}, u32[]{:S(2)}, u32[]{:S(2)}) async-start(bf16[16,128,512]{2,1,0:T(8,128)(2,1)} %bitcast.35), calls=%async_computation.4 | async-start | bytes 4194304 | tf_op jit(solution)/shard_map/all_to_all | solution.py:36
  202.7 5.6 %collective-permute-done.17.refs_11_ = bf16[2,256,512]{2,1,0:T(8,128)(2,1)} collective-permute-done((bf16[2,256,512]{2,1,0:T(8,128)(2,1)S(1)}, bf16[2,256,512]{2,1,0:T(8,128)(2,1)}, u32[]{:S(2)}, u32[]{:S(2)}) %collective-permute-start.17) | collective-permute-done | bytes 524320 | tf_op jit(solution)/shard_map/ppermute | solution.py:49
  208.2 0.8 collective-permute-start.13
  210.2 0.7 collective-permute-done.13.refs_7_
  210.9 0.7 collective-permute-done.19.refs_13_
  211.7 0.7 collective-permute-done.20.refs_14_
  212.4 0.7 collective-permute-done.21.refs_15_
  213.2 1.0 copy-done.1
  214.2 1.0 copy-done.3
  215.3 1.0 copy-done.5
  216.3 0.8 copy-done.10
  217.1 5.5 %predict.1 = (bf16[128,512]{1,0:T(8,128)(2,1)}, bf16[128,512]{1,0:T(8,128)(2,1)S(1)}, f32[8,128]{1,0:T(8,128)S(1)}) custom-call(s32[16]{0:T(128)S(1)} %get-tuple-element.50.source_ref, s32[1]{0:T(128)} %bitcast.rank_ref, s32[4]{0:T(128)S(1)} %copy-done.12, s32[4]{0:T(128)S(1)} %copy-done.13, bf16[4,128,512]{2,1,0:T(8,128)(2,1)S(1)} %all-to-all-done.2.far_own_ref, ...), custom_call_target="tpu_custom_call" | custom-call | flops 1073741824 | bytes 13631488 | tf_op jit(solution)/shard_map/predict/pallas_call | solution.py:404
  222.6 2.7 collective-permute-start.26
  225.4 3.1 %collective-permute-start.27 = (bf16[128,512]{1,0:T(8,128)(2,1)S(1)}, bf16[128,512]{1,0:T(8,128)(2,1)S(1)}, u32[]{:S(2)}, u32[]{:S(2)}) collective-permute-start(bf16[128,512]{1,0:T(8,128)(2,1)S(1)} %get-tuple-element.41), channel_id=1, source_target_pairs={{0,64},{32,96},{64,0},{96,32},{1,65},{33,97},{65,1},{97,33},{2,66}... | collective-permute-start | bytes 393224 | tf_op jit(solution)/shard_map/ppermute | solution.py:49
  228.5 1.0 collective-permute-start.28
  229.5 1.7 collective-permute-done.29
  231.2 3.4 %collective-permute-start.31 = (bf16[128,512]{1,0:T(8,128)(2,1)S(1)}, bf16[128,512]{1,0:T(8,128)(2,1)S(1)}, u32[]{:S(2)}, u32[]{:S(2)}) collective-permute-start(bf16[128,512]{1,0:T(8,128)(2,1)S(1)} %collective-permute-done.29), channel_id=1, source_target_pairs={{0,64},{32,96},{64,0},{96,32},{1,65},{33,97},{65,1},{97,33},{2,66}... | collective-permute-start | bytes 393224 | tf_op jit(solution)/shard_map/ppermute | solution.py:49
  234.6 0.9 collective-permute-start.32
  235.6 3.2 %collective-permute-start.33 = (bf16[4,128,512]{2,1,0:T(8,128)(2,1)S(1)}, bf16[4,128,512]{2,1,0:T(8,128)(2,1)S(1)}, u32[]{:S(2)}, u32[]{:S(2)}) collective-permute-start(bf16[4,128,512]{2,1,0:T(8,128)(2,1)S(1)} %pad_maximum_fusion.3.e0_ref), channel_id=1, source_target_pairs={{0,16},{16,0},{1,17},{17,1},{2,18},{18,2},{3,19},{19,3},{4,20},{20... | collective-permute-start | bytes 1572872 | tf_op jit(solution)/shard_map/ppermute | solution.py:548
  238.7 0.7 collective-permute-done.31
  239.5 4.4 %collective-permute-start.34 = (bf16[4,128,512]{2,1,0:T(8,128)(2,1)S(1)}, bf16[4,128,512]{2,1,0:T(8,128)(2,1)S(1)}, u32[]{:S(2)}, u32[]{:S(2)}) collective-permute-start(bf16[4,128,512]{2,1,0:T(8,128)(2,1)S(1)} %pad_maximum_fusion.4.e1_ref), channel_id=1, source_target_pairs={{0,16},{16,0},{1,17},{17,1},{2,18},{18,2},{3,19},{19,3},{4,20},{20... | collective-permute-start | bytes 1572872 | tf_op jit(solution)/shard_map/ppermute | solution.py:548
  244.0 1.5 collective-permute-done.34.e3_ref
  245.5 0.8 copy-done.19
  246.3 4.5 %differentiate.1 = (f32[512,512]{1,0:T(8,128)}, f32[256,128]{1,0:T(8,128)}) custom-call(s32[16]{0:T(128)} %get-tuple-element.49.place_ref, bf16[16,128,512]{2,1,0:T(8,128)(2,1)} %all-to-all-done.4.column_ref, bf16[4,128,512]{2,1,0:T(8,128)(2,1)} %copy-done.15, bf16[4,128,512]{2,1,0:T(8,128)(2,1)} %copy-done.16, bf16[4,128,512]{2,1,0:T(8,128)(2,1)} %copy-done.18, ...), custom_call_target="tpu_custom_call" | custom-call | flops 1073741824 | bytes 5242880 | tf_op jit(solution)/shard_map/differentiate/pallas_call | solution.py:433
  250.8 25.3 %all_to_all.37 = f32[256,1,128]{2,1,0:T(1,128)} all-to-all(f32[256,1,128]{2,1,0:T(1,128)} %bitcast.43), channel_id=1, replica_groups=mesh['zh'=2,'y'=4,'c'=2,'zl'=4,'x'=4] {'zh','y','c','zl','x'}, dimensions={0} | all-to-all | bytes 262144 | tf_op jit(solution)/shard_map/all_to_all | solution.py:36
  276.1 4.8 %update.1 = (bf16[512,512]{1,0:T(8,128)(2,1)}, f32[512,512]{1,0:T(8,128)}, f32[512,512]{1,0:T(8,128)}, f32[1,1]{1,0:T(1,128)}) custom-call(f32[256,128]{1,0:T(8,128)} %bitcast.39, f32[512,512]{1,0:T(8,128)} %get-tuple-element.44.grad_ref, bf16[512,512]{1,0:T(8,128)(2,1)} %weight_ref.3, f32[512,512]{1,0:T(8,128)} %first_ref.1, f32[512,512]{1,0:T(8,128)} %second_ref.1), custom_call_target="tpu_custom_call" | custom-call | flops 5242880 | bytes 6291456 | tf_op jit(solution)/shard_map/update/pallas_call | solution.py:450
  (86 shorter events, 4.1 us)
Async XLA Ops:
  0.6 17.9 %copy-start.17 = (bf16[512,512]{1,0:T(8,128)(2,1)S(1)}, bf16[512,512]{1,0:T(8,128)(2,1)}, u32[]{:S(2)}) copy-start(bf16[512,512]{1,0:T(8,128)(2,1)} %weight_ref.3) | copy-start | bytes 1572868
  9.6 33.5 %all-to-all-start = ((bf16[16,144,256]{2,1,0:T(8,128)(2,1)}), bf16[16,144,256]{2,1,0:T(8,128)(2,1)S(1)}, u32[]{:S(2)}, u32[]{:S(2)}) async-start(bf16[16,144,256]{2,1,0:T(8,128)(2,1)} %get-tuple-element.27), calls=%async_computation | async-start | bytes 2359296 | tf_op jit(solution)/shard_map/all_to_all | solution.py:36
  43.1 1.0 copy-start.14
  81.6 8.6 %collective-permute-start = (bf16[128,512]{1,0:T(8,128)(2,1)}, bf16[128,512]{1,0:T(8,128)(2,1)S(1)}, u32[]{:S(2)}, u32[]{:S(2)}) collective-permute-start(bf16[128,512]{1,0:T(8,128)(2,1)} %get-tuple-element.30), channel_id=1, source_target_pairs={{0,4},{4,8},{8,12},{12,0},{1,5},{5,9},{9,13},{13,1},{2,6},{6,10},{... | collective-permute-start | bytes 393224 | tf_op jit(solution)/shard_map/ppermute | solution.py:517
  85.3 8.5 %collective-permute-start.1 = (bf16[128,512]{1,0:T(8,128)(2,1)}, bf16[128,512]{1,0:T(8,128)(2,1)S(1)}, u32[]{:S(2)}, u32[]{:S(2)}) collective-permute-start(bf16[128,512]{1,0:T(8,128)(2,1)} %get-tuple-element.31), channel_id=1, source_target_pairs={{0,8},{4,12},{8,0},{12,4},{1,9},{5,13},{9,1},{13,5},{2,10},{6,14},... | collective-permute-start | bytes 393224 | tf_op jit(solution)/shard_map/ppermute | solution.py:517
  87.8 6.0 %collective-permute-start.2 = (bf16[128,512]{1,0:T(8,128)(2,1)}, bf16[128,512]{1,0:T(8,128)(2,1)S(1)}, u32[]{:S(2)}, u32[]{:S(2)}) collective-permute-start(bf16[128,512]{1,0:T(8,128)(2,1)} %get-tuple-element.32), channel_id=1, source_target_pairs={{0,12},{4,0},{8,4},{12,8},{1,13},{5,1},{9,5},{13,9},{2,14},{6,2},{... | collective-permute-start | bytes 393224 | tf_op jit(solution)/shard_map/ppermute | solution.py:517
  90.2 3.7 %copy-start.22 = (bf16[128,512]{1,0:T(8,128)(2,1)}, bf16[128,512]{1,0:T(8,128)(2,1)S(1)}, u32[]{:S(2)}) copy-start(bf16[128,512]{1,0:T(8,128)(2,1)S(1)} %collective-permute-done.one_ref) | copy-start | bytes 393220
  93.8 0.7 copy-start.23
  98.3 41.5 %all-to-all-start.2 = ((bf16[4,128,512]{2,1,0:T(8,128)(2,1)}), bf16[4,128,512]{2,1,0:T(8,128)(2,1)S(1)}, u32[]{:S(2)}, u32[]{:S(2)}) async-start(bf16[4,128,512]{2,1,0:T(8,128)(2,1)} %reshape.47), calls=%async_computation.2 | async-start | bytes 1048576 | tf_op jit(solution)/shard_map/all_to_all | solution.py:36
  101.8 43.6 %collective-permute-start.6 = (bf16[256,512]{1,0:T(8,128)(2,1)S(1)}, bf16[256,512]{1,0:T(8,128)(2,1)S(1)}, u32[]{:S(2)}, u32[]{:S(2)}) collective-permute-start(bf16[256,512]{1,0:T(8,128)(2,1)S(1)} %get-tuple-element.37), channel_id=1, source_target_pairs={{0,128},{128,0},{1,129},{129,1},{2,130},{130,2},{3,131},{131,3},{4... | collective-permute-start | bytes 786440 | tf_op jit(solution)/shard_map/ppermute | solution.py:49
  106.1 18.9 %collective-permute-start.3 = (bf16[128,512]{1,0:T(8,128)(2,1)}, bf16[128,512]{1,0:T(8,128)(2,1)S(1)}, u32[]{:S(2)}, u32[]{:S(2)}) collective-permute-start(bf16[128,512]{1,0:T(8,128)(2,1)} %get-tuple-element.33), channel_id=1, source_target_pairs={{0,4},{4,8},{8,12},{12,0},{1,5},{5,9},{9,13},{13,1},{2,6},{6,10},{... | collective-permute-start | bytes 393224 | tf_op jit(solution)/shard_map/ppermute | solution.py:49
  110.8 28.9 %collective-permute-start.4 = (bf16[128,512]{1,0:T(8,128)(2,1)}, bf16[128,512]{1,0:T(8,128)(2,1)S(1)}, u32[]{:S(2)}, u32[]{:S(2)}) collective-permute-start(bf16[128,512]{1,0:T(8,128)(2,1)} %get-tuple-element.33), channel_id=1, source_target_pairs={{0,8},{4,12},{8,0},{12,4},{1,9},{5,13},{9,1},{13,5},{2,10},{6,14},... | collective-permute-start | bytes 393224 | tf_op jit(solution)/shard_map/ppermute | solution.py:49
  113.5 26.2 %collective-permute-start.5 = (bf16[128,512]{1,0:T(8,128)(2,1)}, bf16[128,512]{1,0:T(8,128)(2,1)S(1)}, u32[]{:S(2)}, u32[]{:S(2)}) collective-permute-start(bf16[128,512]{1,0:T(8,128)(2,1)} %get-tuple-element.33), channel_id=1, source_target_pairs={{0,12},{4,0},{8,4},{12,8},{1,13},{5,1},{9,5},{13,9},{2,14},{6,2},{... | collective-permute-start | bytes 393224 | tf_op jit(solution)/shard_map/ppermute | solution.py:49
  113.5 38.6 %collective-permute-start.14 = (bf16[256,512]{1,0:T(8,128)(2,1)S(1)}, bf16[256,512]{1,0:T(8,128)(2,1)S(1)}, u32[]{:S(2)}, u32[]{:S(2)}) collective-permute-start(bf16[256,512]{1,0:T(8,128)(2,1)S(1)} %get-tuple-element.38), channel_id=1, source_target_pairs={{0,128},{128,0},{1,129},{129,1},{2,130},{130,2},{3,131},{131,3},{4... | collective-permute-start | bytes 786440 | tf_op jit(solution)/shard_map/ppermute | solution.py:49
  141.1 13.2 %copy-start.25 = (bf16[128,512]{1,0:T(8,128)(2,1)S(1)}, bf16[128,512]{1,0:T(8,128)(2,1)}, u32[]{:S(2)}) copy-start(bf16[128,512]{1,0:T(8,128)(2,1)} %get-tuple-element.40) | copy-start | bytes 393220
  141.1 53.8 %all-to-all-start.3 = ((bf16[12,128,512]{2,1,0:T(8,128)(2,1)}), bf16[12,128,512]{2,1,0:T(8,128)(2,1)S(1)}, u32[]{:S(2)}, u32[]{:S(2)}) async-start(bf16[12,128,512]{2,1,0:T(8,128)(2,1)} %bitcast.36), calls=%async_computation.3 | async-start | bytes 3145728 | tf_op jit(solution)/shard_map/all_to_all | solution.py:36
  145.4 0.7 copy-start.21
  147.1 25.8 %collective-permute-start.7 = (bf16[2,256,512]{2,1,0:T(8,128)(2,1)S(1)}, bf16[2,256,512]{2,1,0:T(8,128)(2,1)}, u32[]{:S(2)}, u32[]{:S(2)}) collective-permute-start(bf16[2,256,512]{2,1,0:T(8,128)(2,1)S(1)} %pad_maximum_fusion.refs_0_), channel_id=1, source_target_pairs={{0,32},{32,64},{64,96},{96,0},{1,33},{33,65},{65,97},{97,1},{2,34}... | collective-permute-start | bytes 1572872 | tf_op jit(solution)/shard_map/ppermute | solution.py:49
  148.5 26.5 %collective-permute-start.8 = (bf16[2,256,512]{2,1,0:T(8,128)(2,1)S(1)}, bf16[2,256,512]{2,1,0:T(8,128)(2,1)S(1)}, u32[]{:S(2)}, u32[]{:S(2)}) collective-permute-start(bf16[2,256,512]{2,1,0:T(8,128)(2,1)S(1)} %pad_maximum_fusion.refs_0_), channel_id=1, source_target_pairs={{0,64},{32,96},{64,0},{96,32},{1,65},{33,97},{65,1},{97,33},{2,66}... | collective-permute-start | bytes 1572872 | tf_op jit(solution)/shard_map/ppermute | solution.py:49
  151.1 32.3 %collective-permute-start.9 = (bf16[2,256,512]{2,1,0:T(8,128)(2,1)S(1)}, bf16[2,256,512]{2,1,0:T(8,128)(2,1)S(1)}, u32[]{:S(2)}, u32[]{:S(2)}) collective-permute-start(bf16[2,256,512]{2,1,0:T(8,128)(2,1)S(1)} %pad_maximum_fusion.refs_0_), channel_id=1, source_target_pairs={{0,96},{32,0},{64,32},{96,64},{1,97},{33,1},{65,33},{97,65},{2,98}... | collective-permute-start | bytes 1572872 | tf_op jit(solution)/shard_map/ppermute | solution.py:49
  152.2 0.7 copy-start.20
  153.9 29.6 %collective-permute-start.15 = (bf16[2,256,512]{2,1,0:T(8,128)(2,1)S(1)}, bf16[2,256,512]{2,1,0:T(8,128)(2,1)S(1)}, u32[]{:S(2)}, u32[]{:S(2)}) collective-permute-start(bf16[2,256,512]{2,1,0:T(8,128)(2,1)S(1)} %pad_maximum_fusion.1.refs_8_), channel_id=1, source_target_pairs={{0,32},{32,64},{64,96},{96,0},{1,33},{33,65},{65,97},{97,1},{2,34}... | collective-permute-start | bytes 1572872 | tf_op jit(solution)/shard_map/ppermute | solution.py:49
  154.3 12.7 %collective-permute-start.22 = (bf16[128,512]{1,0:T(8,128)(2,1)S(1)}, bf16[128,512]{1,0:T(8,128)(2,1)S(1)}, u32[]{:S(2)}, u32[]{:S(2)}) collective-permute-start(bf16[128,512]{1,0:T(8,128)(2,1)S(1)} %copy-done.25), channel_id=1, source_target_pairs={{0,0},{1,16},{2,32},{3,48},{4,64},{5,80},{6,96},{7,112},{8,128},{9... | collective-permute-start | bytes 393224 | tf_op jit(solution)/shard_map/ppermute | solution.py:524
  167.1 17.2 %collective-permute-start.23 = (bf16[128,512]{1,0:T(8,128)(2,1)S(1)}, bf16[128,512]{1,0:T(8,128)(2,1)S(1)}, u32[]{:S(2)}, u32[]{:S(2)}) collective-permute-start(bf16[128,512]{1,0:T(8,128)(2,1)S(1)} %collective-permute-done.22), channel_id=1, source_target_pairs={{0,4},{4,8},{8,12},{12,0},{1,5},{5,9},{9,13},{13,1},{2,6},{6,10},{... | collective-permute-start | bytes 393224 | tf_op jit(solution)/shard_map/ppermute | solution.py:49
  172.9 20.3 %collective-permute-start.24 = (bf16[128,512]{1,0:T(8,128)(2,1)S(1)}, bf16[128,512]{1,0:T(8,128)(2,1)S(1)}, u32[]{:S(2)}, u32[]{:S(2)}) collective-permute-start(bf16[128,512]{1,0:T(8,128)(2,1)S(1)} %collective-permute-done.22), channel_id=1, source_target_pairs={{0,8},{4,12},{8,0},{12,4},{1,9},{5,13},{9,1},{13,5},{2,10},{6,14},... | collective-permute-start | bytes 393224 | tf_op jit(solution)/shard_map/ppermute | solution.py:49
  175.0 19.0 %copy-start = (bf16[2,256,512]{2,1,0:T(8,128)(2,1)}, bf16[2,256,512]{2,1,0:T(8,128)(2,1)S(1)}, u32[]{:S(2)}) copy-start(bf16[2,256,512]{2,1,0:T(8,128)(2,1)S(1)} %collective-permute-done.8.refs_2_) | copy-start | bytes 1572868
  175.0 18.9 %collective-permute-start.25 = (bf16[128,512]{1,0:T(8,128)(2,1)S(1)}, bf16[128,512]{1,0:T(8,128)(2,1)S(1)}, u32[]{:S(2)}, u32[]{:S(2)}) collective-permute-start(bf16[128,512]{1,0:T(8,128)(2,1)S(1)} %collective-permute-done.22), channel_id=1, source_target_pairs={{0,12},{4,0},{8,4},{12,8},{1,13},{5,1},{9,5},{13,9},{2,14},{6,2},{... | collective-permute-start | bytes 393224 | tf_op jit(solution)/shard_map/ppermute | solution.py:49
  183.4 10.6 %copy-start.2 = (bf16[2,256,512]{2,1,0:T(8,128)(2,1)}, bf16[2,256,512]{2,1,0:T(8,128)(2,1)S(1)}, u32[]{:S(2)}) copy-start(bf16[2,256,512]{2,1,0:T(8,128)(2,1)S(1)} %collective-permute-done.9.refs_3_) | copy-start | bytes 1572868
  183.4 18.7 %collective-permute-start.16 = (bf16[2,256,512]{2,1,0:T(8,128)(2,1)S(1)}, bf16[2,256,512]{2,1,0:T(8,128)(2,1)}, u32[]{:S(2)}, u32[]{:S(2)}) collective-permute-start(bf16[2,256,512]{2,1,0:T(8,128)(2,1)S(1)} %pad_maximum_fusion.1.refs_8_), channel_id=1, source_target_pairs={{0,64},{32,96},{64,0},{96,32},{1,65},{33,97},{65,1},{97,33},{2,66}... | collective-permute-start | bytes 1572872 | tf_op jit(solution)/shard_map/ppermute | solution.py:49
  183.4 9.8 %copy-start.4 = (bf16[2,256,512]{2,1,0:T(8,128)(2,1)}, bf16[2,256,512]{2,1,0:T(8,128)(2,1)S(1)}, u32[]{:S(2)}) copy-start(bf16[2,256,512]{2,1,0:T(8,128)(2,1)S(1)} %collective-permute-done.15.refs_9_) | copy-start | bytes 1572868
  183.5 24.8 %collective-permute-start.17 = (bf16[2,256,512]{2,1,0:T(8,128)(2,1)S(1)}, bf16[2,256,512]{2,1,0:T(8,128)(2,1)}, u32[]{:S(2)}, u32[]{:S(2)}) collective-permute-start(bf16[2,256,512]{2,1,0:T(8,128)(2,1)S(1)} %pad_maximum_fusion.1.refs_8_), channel_id=1, source_target_pairs={{0,96},{32,0},{64,32},{96,64},{1,97},{33,1},{65,33},{97,65},{2,98}... | collective-permute-start | bytes 1572872 | tf_op jit(solution)/shard_map/ppermute | solution.py:49
  184.3 24.7 %collective-permute-start.10 = (bf16[2,256,512]{2,1,0:T(8,128)(2,1)S(1)}, bf16[2,256,512]{2,1,0:T(8,128)(2,1)}, u32[]{:S(2)}, u32[]{:S(2)}) collective-permute-start(bf16[2,256,512]{2,1,0:T(8,128)(2,1)S(1)} %pad_maximum_fusion.refs_0_), channel_id=1, source_target_pairs={{0,16},{16,0},{1,17},{17,1},{2,18},{18,2},{3,19},{19,3},{4,20},{20... | collective-permute-start | bytes 1572872 | tf_op jit(solution)/shard_map/ppermute | solution.py:513
  193.2 15.8 %collective-permute-start.18 = (bf16[2,256,512]{2,1,0:T(8,128)(2,1)S(1)}, bf16[2,256,512]{2,1,0:T(8,128)(2,1)}, u32[]{:S(2)}, u32[]{:S(2)}) collective-permute-start(bf16[2,256,512]{2,1,0:T(8,128)(2,1)S(1)} %pad_maximum_fusion.1.refs_8_), channel_id=1, source_target_pairs={{0,16},{16,0},{1,17},{17,1},{2,18},{18,2},{3,19},{19,3},{4,20},{20... | collective-permute-start | bytes 1572872 | tf_op jit(solution)/shard_map/ppermute | solution.py:527
  193.9 15.6 %collective-permute-start.11 = (bf16[2,256,512]{2,1,0:T(8,128)(2,1)}, bf16[2,256,512]{2,1,0:T(8,128)(2,1)}, u32[]{:S(2)}, u32[]{:S(2)}) collective-permute-start(bf16[2,256,512]{2,1,0:T(8,128)(2,1)} %collective-permute-done.7.refs_1_), channel_id=1, source_target_pairs={{0,16},{16,0},{1,17},{17,1},{2,18},{18,2},{3,19},{19,3},{4,20},{20... | collective-permute-start | bytes 1572872 | tf_op jit(solution)/shard_map/ppermute | solution.py:513
  197.5 15.7 %copy-start.6 = (bf16[4,8192]{1,0:T(4,128)(2,1)S(1)}, bf16[4,8192]{1,0:T(4,128)(2,1)}, u32[]{:S(2)}) copy-start(bf16[4,8192]{1,0:T(4,128)(2,1)} %prev_ref.3) | copy-start | bytes 196612
  197.5 15.7 %copy-start.7 = (f32[128,512]{1,0:T(8,128)S(1)}, f32[128,512]{1,0:T(8,128)}, u32[]{:S(2)}) copy-start(f32[128,512]{1,0:T(8,128)} %get-tuple-element.34.mixed_ref) | copy-start | bytes 786436
  197.5 15.7 %copy-start.8 = (f32[8192]{0:T(1024)S(1)}, f32[8192]{0:T(1024)}, u32[]{:S(2)}) copy-start(f32[8192]{0:T(1024)} %param.24) | copy-start | bytes 98308
  197.5 15.7 %copy-start.9 = (bf16[128,128]{1,0:T(8,128)(2,1)S(1)}, bf16[128,128]{1,0:T(8,128)(2,1)}, u32[]{:S(2)}) copy-start(bf16[128,128]{1,0:T(8,128)(2,1)} %get-tuple-element.35.reach_ref) | copy-start | bytes 98308
  197.5 15.7 %copy-start.12 = (s32[4]{0:T(128)S(1)}, s32[4]{0:T(128)}, u32[]{:S(2)}) copy-start(s32[4]{0:T(128)} %len_ref.3) | copy-start | bytes 52
  197.5 15.7 %copy-start.13 = (s32[4]{0:T(128)S(1)}, s32[4]{0:T(128)}, u32[]{:S(2)}) copy-start(s32[4]{0:T(128)} %leaf_ref.1) | copy-start | bytes 52
  197.5 46.4 %all-to-all-start.4 = ((bf16[16,128,512]{2,1,0:T(8,128)(2,1)}), bf16[16,128,512]{2,1,0:T(8,128)(2,1)}, u32[]{:S(2)}, u32[]{:S(2)}) async-start(bf16[16,128,512]{2,1,0:T(8,128)(2,1)} %bitcast.35), calls=%async_computation.4 | async-start | bytes 4194304 | tf_op jit(solution)/shard_map/all_to_all | solution.py:36
  202.2 8.0 %collective-permute-start.12 = (bf16[2,256,512]{2,1,0:T(8,128)(2,1)}, bf16[2,256,512]{2,1,0:T(8,128)(2,1)}, u32[]{:S(2)}, u32[]{:S(2)}) collective-permute-start(bf16[2,256,512]{2,1,0:T(8,128)(2,1)} %copy-done), channel_id=1, source_target_pairs={{0,16},{16,0},{1,17},{17,1},{2,18},{18,2},{3,19},{19,3},{4,20},{20... | collective-permute-start | bytes 1572872 | tf_op jit(solution)/shard_map/ppermute | solution.py:513
  208.2 2.7 collective-permute-start.13
  209.0 2.6 collective-permute-start.19
  209.0 3.4 %collective-permute-start.20 = (bf16[2,256,512]{2,1,0:T(8,128)(2,1)}, bf16[2,256,512]{2,1,0:T(8,128)(2,1)}, u32[]{:S(2)}, u32[]{:S(2)}) collective-permute-start(bf16[2,256,512]{2,1,0:T(8,128)(2,1)} %collective-permute-done.16.refs_10_), channel_id=1, source_target_pairs={{0,16},{16,0},{1,17},{17,1},{2,18},{18,2},{3,19},{19,3},{4,20},{20... | collective-permute-start | bytes 1572872 | tf_op jit(solution)/shard_map/ppermute | solution.py:527
  209.5 3.6 %collective-permute-start.21 = (bf16[2,256,512]{2,1,0:T(8,128)(2,1)}, bf16[2,256,512]{2,1,0:T(8,128)(2,1)}, u32[]{:S(2)}, u32[]{:S(2)}) collective-permute-start(bf16[2,256,512]{2,1,0:T(8,128)(2,1)} %collective-permute-done.17.refs_11_), channel_id=1, source_target_pairs={{0,16},{16,0},{1,17},{17,1},{2,18},{18,2},{3,19},{19,3},{4,20},{20... | collective-permute-start | bytes 1572872 | tf_op jit(solution)/shard_map/ppermute | solution.py:527
  213.2 1.0 copy-start.1
  214.2 1.0 copy-start.3
  215.3 1.0 copy-start.5
  216.3 0.8 copy-start.10
  222.5 13.0 %copy-start.11 = (f32[8,128]{1,0:T(8,128)}, f32[8,128]{1,0:T(8,128)S(1)}, u32[]{:S(2)}) copy-start(f32[8,128]{1,0:T(8,128)S(1)} %get-tuple-element.42.loss_ref) | copy-start | bytes 12292
  222.5 8.7 %collective-permute-start.29 = (bf16[128,512]{1,0:T(8,128)(2,1)S(1)}, bf16[128,512]{1,0:T(8,128)(2,1)S(1)}, u32[]{:S(2)}, u32[]{:S(2)}) collective-permute-start(bf16[128,512]{1,0:T(8,128)(2,1)S(1)} %get-tuple-element.41), channel_id=1, source_target_pairs={{0,128},{128,0},{1,129},{129,1},{2,130},{130,2},{3,131},{131,3},{4... | collective-permute-start | bytes 393224 | tf_op jit(solution)/shard_map/ppermute | solution.py:544
  222.6 11.9 %collective-permute-start.26 = (bf16[128,512]{1,0:T(8,128)(2,1)S(1)}, bf16[128,512]{1,0:T(8,128)(2,1)S(1)}, u32[]{:S(2)}, u32[]{:S(2)}) collective-permute-start(bf16[128,512]{1,0:T(8,128)(2,1)S(1)} %get-tuple-element.41), channel_id=1, source_target_pairs={{0,32},{32,64},{64,96},{96,0},{1,33},{33,65},{65,97},{97,1},{2,34}... | collective-permute-start | bytes 393224 | tf_op jit(solution)/shard_map/ppermute | solution.py:49
  225.4 10.1 %collective-permute-start.27 = (bf16[128,512]{1,0:T(8,128)(2,1)S(1)}, bf16[128,512]{1,0:T(8,128)(2,1)S(1)}, u32[]{:S(2)}, u32[]{:S(2)}) collective-permute-start(bf16[128,512]{1,0:T(8,128)(2,1)S(1)} %get-tuple-element.41), channel_id=1, source_target_pairs={{0,64},{32,96},{64,0},{96,32},{1,65},{33,97},{65,1},{97,33},{2,66}... | collective-permute-start | bytes 393224 | tf_op jit(solution)/shard_map/ppermute | solution.py:49
  228.5 7.0 %collective-permute-start.28 = (bf16[128,512]{1,0:T(8,128)(2,1)S(1)}, bf16[128,512]{1,0:T(8,128)(2,1)S(1)}, u32[]{:S(2)}, u32[]{:S(2)}) collective-permute-start(bf16[128,512]{1,0:T(8,128)(2,1)S(1)} %get-tuple-element.41), channel_id=1, source_target_pairs={{0,96},{32,0},{64,32},{96,64},{1,97},{33,1},{65,33},{97,65},{2,98}... | collective-permute-start | bytes 393224 | tf_op jit(solution)/shard_map/ppermute | solution.py:49
  231.2 7.5 %collective-permute-start.30 = (bf16[128,512]{1,0:T(8,128)(2,1)S(1)}, bf16[128,512]{1,0:T(8,128)(2,1)S(1)}, u32[]{:S(2)}, u32[]{:S(2)}) collective-permute-start(bf16[128,512]{1,0:T(8,128)(2,1)S(1)} %collective-permute-done.29), channel_id=1, source_target_pairs={{0,32},{32,64},{64,96},{96,0},{1,33},{33,65},{65,97},{97,1},{2,34}... | collective-permute-start | bytes 393224 | tf_op jit(solution)/shard_map/ppermute | solution.py:49
  231.2 8.2 %collective-permute-start.31 = (bf16[128,512]{1,0:T(8,128)(2,1)S(1)}, bf16[128,512]{1,0:T(8,128)(2,1)S(1)}, u32[]{:S(2)}, u32[]{:S(2)}) collective-permute-start(bf16[128,512]{1,0:T(8,128)(2,1)S(1)} %collective-permute-done.29), channel_id=1, source_target_pairs={{0,64},{32,96},{64,0},{96,32},{1,65},{33,97},{65,1},{97,33},{2,66}... | collective-permute-start | bytes 393224 | tf_op jit(solution)/shard_map/ppermute | solution.py:49
  234.6 4.9 %collective-permute-start.32 = (bf16[128,512]{1,0:T(8,128)(2,1)S(1)}, bf16[128,512]{1,0:T(8,128)(2,1)S(1)}, u32[]{:S(2)}, u32[]{:S(2)}) collective-permute-start(bf16[128,512]{1,0:T(8,128)(2,1)S(1)} %collective-permute-done.29), channel_id=1, source_target_pairs={{0,96},{32,0},{64,32},{96,64},{1,97},{33,1},{65,33},{97,65},{2,98}... | collective-permute-start | bytes 393224 | tf_op jit(solution)/shard_map/ppermute | solution.py:49
  235.6 9.9 %copy-start.15 = (bf16[4,128,512]{2,1,0:T(8,128)(2,1)}, bf16[4,128,512]{2,1,0:T(8,128)(2,1)S(1)}, u32[]{:S(2)}) copy-start(bf16[4,128,512]{2,1,0:T(8,128)(2,1)S(1)} %pad_maximum_fusion.3.e0_ref) | copy-start | bytes 1572868
  235.6 8.4 %collective-permute-start.33 = (bf16[4,128,512]{2,1,0:T(8,128)(2,1)S(1)}, bf16[4,128,512]{2,1,0:T(8,128)(2,1)S(1)}, u32[]{:S(2)}, u32[]{:S(2)}) collective-permute-start(bf16[4,128,512]{2,1,0:T(8,128)(2,1)S(1)} %pad_maximum_fusion.3.e0_ref), channel_id=1, source_target_pairs={{0,16},{16,0},{1,17},{17,1},{2,18},{18,2},{3,19},{19,3},{4,20},{20... | collective-permute-start | bytes 1572872 | tf_op jit(solution)/shard_map/ppermute | solution.py:548
  239.5 6.0 %copy-start.16 = (bf16[4,128,512]{2,1,0:T(8,128)(2,1)}, bf16[4,128,512]{2,1,0:T(8,128)(2,1)S(1)}, u32[]{:S(2)}) copy-start(bf16[4,128,512]{2,1,0:T(8,128)(2,1)S(1)} %pad_maximum_fusion.4.e1_ref) | copy-start | bytes 1572868
  239.5 6.0 %collective-permute-start.34 = (bf16[4,128,512]{2,1,0:T(8,128)(2,1)S(1)}, bf16[4,128,512]{2,1,0:T(8,128)(2,1)S(1)}, u32[]{:S(2)}, u32[]{:S(2)}) collective-permute-start(bf16[4,128,512]{2,1,0:T(8,128)(2,1)S(1)} %pad_maximum_fusion.4.e1_ref), channel_id=1, source_target_pairs={{0,16},{16,0},{1,17},{17,1},{2,18},{18,2},{3,19},{19,3},{4,20},{20... | collective-permute-start | bytes 1572872 | tf_op jit(solution)/shard_map/ppermute | solution.py:548
  244.0 1.5 copy-start.18
  245.5 0.8 copy-start.19
  (1 other events, 0.7 us)

commit v7 on v6

--- a/solution.py
+++ b/solution.py
@@ -47,10 +47,6 @@
 
 def passed(value, axis, count):
     return [value] + [lax.ppermute(value, axis, turn(count, step)) for step in range(1, count)]
-
-
-def turns(value, axis, count):
-    return jnp.stack(passed(value, axis, count))
 
 
 def dot(left, right, dims, **kwargs):
@@ -149,9 +145,12 @@
             out_ref[owner, 128:144, 128:256] = blank
 
 
-def project_kernel(parcel_ref, weight_ref, out_ref, att_ref):
+def project_kernel(from_ref, weight_ref, out_ref, att_ref, parcel_ref, sem_ref):
     @pl.when(pl.program_id(0) == 0)
     def join():
+        load = pltpu.make_async_copy(from_ref, parcel_ref, sem_ref.at[0])
+        load.start()
+        load.wait()
         stats = jnp.concatenate(
             [parcel_ref[src, 128:144, 0:128].astype(F32)[0:8] for src in range(N_TP)], axis=0
         )
@@ -173,7 +172,13 @@
         out_ref[x, 0] = dot(att_ref[...], weight_ref[:, cols], ((1,), (0,))).astype(BF16)
 
 
-def fold_kernel(rank_ref, along_ref, *out_refs):
+def fold_kernel(rank_ref, from_ref, *refs):
+    out_refs, (along_ref, sem_ref) = refs[:4], refs[4:]
+    loads = [pltpu.make_async_copy(from_ref.at[x], along_ref.at[x], sem_ref.at[x]) for x in range(4)]
+    for load in loads:
+        load.start()
+    for load in loads:
+        load.wait()
     for step in range(4):
         zl = lax.rem(rank_ref[0] // 4 + step, 4)
         total = along_ref[0, zl].astype(F32)
@@ -270,11 +275,19 @@
     loss_ref[...] = jnp.broadcast_to(loss, (8, 128))
 
 
-def differentiate_kernel(place_ref, column_ref, e0_ref, e1_ref, e2_ref, e3_ref, loss_ref, grad_ref, pair_ref):
-    for part, err_ref in enumerate((e0_ref, e1_ref, e2_ref, e3_ref)):
+def differentiate_kernel(place_ref, *refs):
+    loss_ref, grad_ref, pair_ref, column_ref, sem_ref = refs[8:]
+    column_loads = [
+        pltpu.make_async_copy(refs[i], column_ref.at[pl.ds(4 * i, 4)], sem_ref.at[i]) for i in range(4)
+    ]
+    for load in column_loads:
+        load.start()
+    for load in column_loads:
+        load.wait()
+    for part in range(4):
         first = (part // 2) * 8 + part % 2
         left = jnp.concatenate([column_ref[place_ref[first + 2 * i]] for i in range(4)], axis=0)
-        right = jnp.concatenate([err_ref[i] for i in range(4)], axis=0)
+        right = jnp.concatenate([refs[4 + part][i] for i in range(4)], axis=0)
         term = dot(left, right, ((0,), (0,)))
         if part == 0:
             grad_ref[...] = term
@@ -349,11 +362,15 @@
         grid=(4,),
         out_shape=jax.ShapeDtypeStruct((4, 4, 128, 512), BF16),
         in_specs=[
-            pl.BlockSpec((N_TP, 144, 2 * HEAD), lambda p: (0, 0, 0)),
+            pl.BlockSpec(memory_space=pl.ANY),
             pl.BlockSpec((2 * HEAD, 2048), lambda p: (0, p)),
         ],
         out_specs=pl.BlockSpec((4, 1, 128, 512), lambda p: (0, p, 0, 0)),
-        scratch_shapes=[pltpu.VMEM((128, 2 * HEAD), BF16)],
+        scratch_shapes=[
+            pltpu.VMEM((128, 2 * HEAD), BF16),
+            pltpu.VMEM((N_TP, 144, 2 * HEAD), BF16),
+            pltpu.SemaphoreType.DMA((1,)),
+        ],
         cost_estimate=pl.CostEstimate(
             flops=2 * 128 * 256 * 8192, bytes_accessed=7 << 20, transcendentals=0
         ),
@@ -365,8 +382,9 @@
     return pl.pallas_call(
         fold_kernel,
         out_shape=(jax.ShapeDtypeStruct((128, 512), BF16),) * 4,
-        in_specs=[in_smem(), in_vmem()],
+        in_specs=[in_smem(), pl.BlockSpec(memory_space=pl.ANY)],
         out_specs=(in_vmem(),) * 4,
+        scratch_shapes=[pltpu.VMEM((4, 4, 128, 512), BF16), pltpu.SemaphoreType.DMA((4,))],
         cost_estimate=pl.CostEstimate(
             flops=16 * 128 * 512, bytes_accessed=5 << 19, transcendentals=0
         ),
@@ -436,13 +454,17 @@
             jax.ShapeDtypeStruct((512, 512), F32),
             jax.ShapeDtypeStruct((N_REQ * N_TP, 128), F32),
         ),
-        in_specs=[in_smem()] + [in_vmem()] * 6,
+        in_specs=[in_smem()] + [pl.BlockSpec(memory_space=pl.ANY)] * 4 + [in_vmem()] * 5,
         out_specs=(in_vmem(), in_vmem()),
+        scratch_shapes=[
+            pltpu.VMEM((16, 128, 512), BF16),
+            pltpu.SemaphoreType.DMA((4,)),
+        ],
         cost_estimate=pl.CostEstimate(
             flops=2 * 2048 * 512 * 512, bytes_accessed=5 << 20, transcendentals=0
         ),
         name="differentiate",
-    )(place, columns, *errors, loss)
+    )(place, *columns, *errors, loss)
 
 
 def update(pair, gradient, weight, first, second):
@@ -493,7 +515,9 @@
     source = (
         ((zh + piece % 2) % 2) * 8 + ((y + 4 - (piece // 2) % 4) % 4) * 2 + (c + piece // 8) % 2
     )
-    place = (source % 4) * 4 + (lax.axis_index("zl") + 4 - source // 4) % 4
+    place = ((lax.axis_index("x") + 4 - source % 4) % 4) * 4 + (
+        lax.axis_index("zl") + 4 - source // 4
+    ) % 4
 
     parcel, reach, pick = attend(
         rank, lengths, parents, queries, cache_keys, cache_values, tree_keys, tree_values
@@ -525,8 +549,9 @@
         table, REQ + TP, [(i * N_TP + j, j * N_TP + i) for i in range(16) for j in range(16)]
     )
     other_lower = [lax.ppermute(part, "c", turn(2, 1)) for part in lower]
-    columns = turns(swapped, "zl", 4)
-    columns = spread(columns, "x", 4).reshape(N_REQ, rows, block)
+    columns = passed(swapped, "zl", 4)
+    columns = jnp.stack(columns)
+    columns = passed(columns, "x", 4)
     own_features, scaled_err, loss = predict(
         source,
         rank,

time: 282 us -> 263 us (0.933)
  blocking collectives: 54.2 us -> 24.1 us
  waiting for transfers between devices: 69 us -> 78.2 us
    all_to_all x2 -> x1, blocking collectives: 54.2 us -> 24.1 us  [exchange(): return lax.all_to_all(value, axis, 0, 0, tiled=True)]
    all_to_all x4, waiting for transfers between devices: 24.5 us -> 42.8 us  [exchange(): return lax.all_to_all(value, axis, 0, 0, tiled=True)]
    ppermute x1, starting transfers between devices: 9.51 us -> 3.19 us  [body(): lax.ppermute(table, REQ + TP, [(i * N_TP + j, j * N_TP + i) for i in rang...]
    ppermute x20 -> x23, starting transfers between devices: 46.6 us -> 52.5 us  [passed(): lax.ppermute(value, axis, turn(count, step))]
    unnamed x52 -> x62, local copies, waits for them, and re-layouts: 7.83 us -> 12.8 us
    ppermute x2, starting transfers between devices: 7.59 us -> 3.74 us  [body(): lax.ppermute(part, 'c', turn(2, 1))]
    ppermute x20 -> x23, waiting for transfers between devices: 31.4 us -> 29.8 us  [passed(): lax.ppermute(value, axis, turn(count, step))]
  transfers between devices with their start and end apart: 39 -> 42, of which waited for: 14 -> 13; matrix products, arithmetic and copies ran while one was open for 3% -> 2% of each run, Pallas kernels for 2% -> 4%
where the time goes in v7:
time: 263 us; the launch traced here: 262 us
  starting transfers between devices  104 us (40%)
  waiting for transfers between devices  78.2 us (30%)
  Pallas kernels  36.2 us (14%)
  blocking collectives  24.1 us (9%)
  local copies, waits for them, and re-layouts  15.8 us (6%)
    ppermute x23, starting transfers between devices, passed(): lax.ppermute(value, axis, turn(count, step))  52.5 us
    all_to_all x4, waiting for transfers between devices, exchange(): return lax.all_to_all(value, axis, 0, 0, tiled=True)  42.8 us
    ppermute x23, waiting for transfers between devices, passed(): lax.ppermute(value, axis, turn(count, step))  29.8 us
    all_to_all x1, blocking collectives, exchange(): return lax.all_to_all(value, axis, 0, 0, tiled=True)  24.1 us
    all_to_all x4, starting transfers between devices, exchange(): return lax.all_to_all(value, axis, 0, 0, tiled=True)  21.9 us
    unnamed x62, local copies, waits for them, and re-layouts  12.8 us
    ppermute x4, starting transfers between devices, body(): other_upper = [lax.ppermute(part, 'c', turn(2, 1)) for part in upper]  12.5 us
    pallas_call x1, Pallas kernels, attend(): pl.pallas_call(attend_kernel, out_shape=(jax.ShapeDtypeStruct((N_TP, 144,...  8.84 us
  transfers between devices with their start and end apart: 42, of which 13 were waited for; matrix products, arithmetic and copies ran while one was open for 2% of the time, Pallas kernels for 4%

profile of v7, /device:TPU:1, one launch (start us, length us, event | category | flops | bytes accessed | tf_op | source)
XLA Modules:
  0.0 261.6 jit_solution(3399518940454565314)
XLA Ops:
  0.6 8.8 %attend.1 = (bf16[16,144,256]{2,1,0:T(8,128)(2,1)}, bf16[128,128]{1,0:T(8,128)(2,1)}, bf16[128,128]{1,0:T(8,128)(2,1)}) custom-call(s32[1]{0:T(128)} %bitcast.rank_ref, s32[4]{0:T(128)} %len_ref.3, s32[4,32]{1,0:T(4,128)} %par_ref.1, bf16[4,32,4096]{2,1,0:T(8,128)(2,1)} %q_ref.1, bf16[4,256,512]{2,1,0:T(8,128)(2,1)} %ck_ref.1, bf16[4,256,512]{2,1,0:T(8,128)(2,1)} %cv_ref.1, ...), custom_call_target="tpu_custom_call" | custom-call | flops 536870912 | bytes 4194304 | tf_op jit(solution)/shard_map/attend/pallas_call | solution.py:330
  9.5 9.1 %all-to-all-start = ((bf16[16,144,256]{2,1,0:T(8,128)(2,1)}), bf16[16,144,256]{2,1,0:T(8,128)(2,1)S(1)}, u32[]{:S(2)}, u32[]{:S(2)}) async-start(bf16[16,144,256]{2,1,0:T(8,128)(2,1)} %get-tuple-element.27), calls=%async_computation | async-start | bytes 2359296 | tf_op jit(solution)/shard_map/all_to_all | solution.py:36
  18.7 24.4 %all-to-all-done.from_ref = bf16[16,144,256]{2,1,0:T(8,128)(2,1)S(1)} async-done(((bf16[16,144,256]{2,1,0:T(8,128)(2,1)}), bf16[16,144,256]{2,1,0:T(8,128)(2,1)S(1)}, u32[]{:S(2)}, u32[]{:S(2)}) %all-to-all-start) | async-done | bytes 1179680 | tf_op jit(solution)/shard_map/all_to_all | solution.py:36
  43.1 1.0 copy-done.17
  44.2 7.0 %project.1 = bf16[4,4,128,512]{3,2,1,0:T(8,128)(2,1)} custom-call(bf16[16,144,256]{2,1,0:T(8,128)(2,1)} %copy-done.17, bf16[256,8192]{1,0:T(8,128)(2,1)} %weight_ref.2), custom_call_target="tpu_custom_call" | custom-call | flops 536870912 | bytes 7340032 | tf_op jit(solution)/shard_map/project/pallas_call | solution.py:360
  51.2 5.0 %all-to-all-start.1 = ((bf16[4,4,128,512]{3,2,1,0:T(8,128)(2,1)}), bf16[4,4,128,512]{3,2,1,0:T(8,128)(2,1)S(1)}, u32[]{:S(2)}, u32[]{:S(2)}) async-start(bf16[4,4,128,512]{3,2,1,0:T(8,128)(2,1)} %project.1), calls=%async_computation.1 | async-start | bytes 4194304 | tf_op jit(solution)/shard_map/all_to_all | solution.py:36
  56.1 4.2 %collective-permute-start.6 = (bf16[256,512]{1,0:T(8,128)(2,1)S(1)}, bf16[256,512]{1,0:T(8,128)(2,1)S(1)}, u32[]{:S(2)}, u32[]{:S(2)}) collective-permute-start(bf16[256,512]{1,0:T(8,128)(2,1)S(1)} %get-tuple-element.37), channel_id=1, source_target_pairs={{0,128},{128,0},{1,129},{129,1},{2,130},{130,2},{3,131},{131,3},{4... | collective-permute-start | bytes 786440 | tf_op jit(solution)/shard_map/ppermute | solution.py:49
  60.3 1.2 collective-permute-start.14
  61.5 18.4 %all-to-all-done.1.from_ref = bf16[4,4,128,512]{3,2,1,0:T(8,128)(2,1)S(1)} async-done(((bf16[4,4,128,512]{3,2,1,0:T(8,128)(2,1)}), bf16[4,4,128,512]{3,2,1,0:T(8,128)(2,1)S(1)}, u32[]{:S(2)}, u32[]{:S(2)}) %all-to-all-start.1) | async-done | bytes 2097184 | tf_op jit(solution)/shard_map/all_to_all | solution.py:36
  79.9 1.3 copy-done.16
  81.2 2.5 fold.1
  83.7 4.5 %collective-permute-start = (bf16[128,512]{1,0:T(8,128)(2,1)}, bf16[128,512]{1,0:T(8,128)(2,1)S(1)}, u32[]{:S(2)}, u32[]{:S(2)}) collective-permute-start(bf16[128,512]{1,0:T(8,128)(2,1)} %get-tuple-element.30), channel_id=1, source_target_pairs={{0,4},{4,8},{8,12},{12,0},{1,5},{5,9},{9,13},{13,1},{2,6},{6,10},{... | collective-permute-start | bytes 393224 | tf_op jit(solution)/shard_map/ppermute | solution.py:541
  88.2 1.4 collective-permute-start.1
  89.6 2.3 collective-permute-start.2
  91.9 1.4 collective-permute-start.7
  93.3 2.6 collective-permute-start.8
  95.9 2.5 collective-permute-done.1.two_ref
  98.4 2.7 %collective-permute-start.9 = (bf16[2,256,512]{2,1,0:T(8,128)(2,1)S(1)}, bf16[2,256,512]{2,1,0:T(8,128)(2,1)}, u32[]{:S(2)}, u32[]{:S(2)}) collective-permute-start(bf16[2,256,512]{2,1,0:T(8,128)(2,1)S(1)} %pad_maximum_fusion.refs_0_), channel_id=1, source_target_pairs={{0,96},{32,0},{64,32},{96,64},{1,97},{33,1},{65,33},{97,65},{2,98}... | collective-permute-start | bytes 1572872 | tf_op jit(solution)/shard_map/ppermute | solution.py:49
  101.7 2.1 settle.1
  103.9 2.0 collective-permute-start.3
  106.0 1.7 reshape.43
  107.7 3.5 %all-to-all-start.2 = ((bf16[4,128,512]{2,1,0:T(8,128)(2,1)}), bf16[4,128,512]{2,1,0:T(8,128)(2,1)S(1)}, u32[]{:S(2)}, u32[]{:S(2)}) async-start(bf16[4,128,512]{2,1,0:T(8,128)(2,1)} %reshape.43), calls=%async_computation.2 | async-start | bytes 1048576 | tf_op jit(solution)/shard_map/all_to_all | solution.py:36
  111.3 3.1 %collective-permute-start.4 = (bf16[128,512]{1,0:T(8,128)(2,1)S(1)}, bf16[128,512]{1,0:T(8,128)(2,1)S(1)}, u32[]{:S(2)}, u32[]{:S(2)}) collective-permute-start(bf16[128,512]{1,0:T(8,128)(2,1)S(1)} %copy-done.29), channel_id=1, source_target_pairs={{0,8},{4,12},{8,0},{12,4},{1,9},{5,13},{9,1},{13,5},{2,10},{6,14},... | collective-permute-start | bytes 393224 | tf_op jit(solution)/shard_map/ppermute | solution.py:49
  114.4 3.9 %collective-permute-done.4 = bf16[128,512]{1,0:T(8,128)(2,1)S(1)} collective-permute-done((bf16[128,512]{1,0:T(8,128)(2,1)S(1)}, bf16[128,512]{1,0:T(8,128)(2,1)S(1)}, u32[]{:S(2)}, u32[]{:S(2)}) %collective-permute-start.4) | collective-permute-done | bytes 131104 | tf_op jit(solution)/shard_map/ppermute | solution.py:49
  118.3 2.5 collective-permute-start.5
  120.8 1.9 collective-permute-done.5
  122.8 1.8 collective-permute-start.16
  124.6 1.3 broadcast_in_dim.2
  125.9 4.4 %all-to-all-start.3 = ((bf16[12,128,512]{2,1,0:T(8,128)(2,1)}), bf16[12,128,512]{2,1,0:T(8,128)(2,1)S(1)}, u32[]{:S(2)}, u32[]{:S(2)}) async-start(bf16[12,128,512]{2,1,0:T(8,128)(2,1)} %bitcast.34), calls=%async_computation.3 | async-start | bytes 3145728 | tf_op jit(solution)/shard_map/all_to_all | solution.py:36
  130.8 5.2 %collective-permute-start.10 = (bf16[2,256,512]{2,1,0:T(8,128)(2,1)S(1)}, bf16[2,256,512]{2,1,0:T(8,128)(2,1)S(1)}, u32[]{:S(2)}, u32[]{:S(2)}) collective-permute-start(bf16[2,256,512]{2,1,0:T(8,128)(2,1)S(1)} %pad_maximum_fusion.refs_0_), channel_id=1, source_target_pairs={{0,16},{16,0},{1,17},{17,1},{2,18},{18,2},{3,19},{19,3},{4,20},{20... | collective-permute-start | bytes 1572872 | tf_op jit(solution)/shard_map/ppermute | solution.py:537
  136.5 2.0 collective-permute-done.16.refs_10_
  138.5 4.1 %collective-permute-start.12 = (bf16[2,256,512]{2,1,0:T(8,128)(2,1)}, bf16[2,256,512]{2,1,0:T(8,128)(2,1)S(1)}, u32[]{:S(2)}, u32[]{:S(2)}) collective-permute-start(bf16[2,256,512]{2,1,0:T(8,128)(2,1)} %collective-permute-done.8.refs_2_), channel_id=1, source_target_pairs={{0,16},{16,0},{1,17},{17,1},{2,18},{18,2},{3,19},{19,3},{4,20},{20... | collective-permute-start | bytes 1572872 | tf_op jit(solution)/shard_map/ppermute | solution.py:537
  142.6 4.7 %collective-permute-done.17.refs_11_ = bf16[2,256,512]{2,1,0:T(8,128)(2,1)} collective-permute-done((bf16[2,256,512]{2,1,0:T(8,128)(2,1)S(1)}, bf16[2,256,512]{2,1,0:T(8,128)(2,1)}, u32[]{:S(2)}, u32[]{:S(2)}) %collective-permute-start.17) | collective-permute-done | bytes 524320 | tf_op jit(solution)/shard_map/ppermute | solution.py:49
  147.3 2.8 %collective-permute-start.13 = (bf16[2,256,512]{2,1,0:T(8,128)(2,1)}, bf16[2,256,512]{2,1,0:T(8,128)(2,1)}, u32[]{:S(2)}, u32[]{:S(2)}) collective-permute-start(bf16[2,256,512]{2,1,0:T(8,128)(2,1)} %collective-permute-done.9.refs_3_), channel_id=1, source_target_pairs={{0,16},{16,0},{1,17},{17,1},{2,18},{18,2},{3,19},{19,3},{4,20},{20... | collective-permute-start | bytes 1572872 | tf_op jit(solution)/shard_map/ppermute | solution.py:537
  150.1 0.8 copy-done
  150.9 0.8 copy-done.2
  152.3 0.8 copy-done.4
  153.1 0.8 copy-done.6
  153.9 3.2 %collective-permute-start.22 = (bf16[128,512]{1,0:T(8,128)(2,1)}, bf16[128,512]{1,0:T(8,128)(2,1)}, u32[]{:S(2)}, u32[]{:S(2)}) collective-permute-start(bf16[128,512]{1,0:T(8,128)(2,1)} %get-tuple-element.40), channel_id=1, source_target_pairs={{0,0},{1,16},{2,32},{3,48},{4,64},{5,80},{6,96},{7,112},{8,128},{9... | collective-permute-start | bytes 393224 | tf_op jit(solution)/shard_map/ppermute | solution.py:548
  157.6 3.1 %collective-permute-done.22 = bf16[128,512]{1,0:T(8,128)(2,1)} collective-permute-done((bf16[128,512]{1,0:T(8,128)(2,1)}, bf16[128,512]{1,0:T(8,128)(2,1)}, u32[]{:S(2)}, u32[]{:S(2)}) %collective-permute-start.22) | collective-permute-done | bytes 131104 | tf_op jit(solution)/shard_map/ppermute | solution.py:548
  160.7 4.9 %collective-permute-start.23 = (bf16[128,512]{1,0:T(8,128)(2,1)}, bf16[128,512]{1,0:T(8,128)(2,1)}, u32[]{:S(2)}, u32[]{:S(2)}) collective-permute-start(bf16[128,512]{1,0:T(8,128)(2,1)} %collective-permute-done.22), channel_id=1, source_target_pairs={{0,4},{4,8},{8,12},{12,0},{1,5},{5,9},{9,13},{13,1},{2,6},{6,10},{... | collective-permute-start | bytes 393224 | tf_op jit(solution)/shard_map/ppermute | solution.py:49
  165.5 6.1 %collective-permute-start.24 = (bf16[128,512]{1,0:T(8,128)(2,1)}, bf16[128,512]{1,0:T(8,128)(2,1)}, u32[]{:S(2)}, u32[]{:S(2)}) collective-permute-start(bf16[128,512]{1,0:T(8,128)(2,1)} %collective-permute-done.22), channel_id=1, source_target_pairs={{0,8},{4,12},{8,0},{12,4},{1,9},{5,13},{9,1},{13,5},{2,10},{6,14},... | collective-permute-start | bytes 393224 | tf_op jit(solution)/shard_map/ppermute | solution.py:49
  171.7 1.0 copy-done.1
  172.8 1.0 copy-done.3
  173.8 1.0 copy-done.5
  174.8 1.0 copy-done.7
  176.6 5.5 %predict.1 = (bf16[128,512]{1,0:T(8,128)(2,1)}, bf16[128,512]{1,0:T(8,128)(2,1)S(1)}, f32[8,128]{1,0:T(8,128)S(1)}) custom-call(s32[16]{0:T(128)S(1)} %get-tuple-element.50.source_ref, s32[1]{0:T(128)} %bitcast.rank_ref, s32[4]{0:T(128)S(1)} %copy-done.14, s32[4]{0:T(128)S(1)} %copy-done.15, bf16[4,128,512]{2,1,0:T(8,128)(2,1)S(1)} %all-to-all-done.2.far_own_ref, ...), custom_call_target="tpu_custom_call" | custom-call | flops 1073741824 | bytes 13631488 | tf_op jit(solution)/shard_map/predict/pallas_call | solution.py:422
  182.2 1.6 collective-permute-start.32
  183.8 1.7 collective-permute-start.25
  185.8 4.8 %collective-permute-start.30 = (bf16[128,512]{1,0:T(8,128)(2,1)S(1)}, bf16[128,512]{1,0:T(8,128)(2,1)S(1)}, u32[]{:S(2)}, u32[]{:S(2)}) collective-permute-start(bf16[128,512]{1,0:T(8,128)(2,1)S(1)} %get-tuple-element.41), channel_id=1, source_target_pairs={{0,64},{32,96},{64,0},{96,32},{1,65},{33,97},{65,1},{97,33},{2,66}... | collective-permute-start | bytes 393224 | tf_op jit(solution)/shard_map/ppermute | solution.py:49
  191.2 0.9 collective-permute-start.33
  192.3 5.7 %collective-permute-start.34 = (bf16[128,512]{1,0:T(8,128)(2,1)S(1)}, bf16[128,512]{1,0:T(8,128)(2,1)S(1)}, u32[]{:S(2)}, u32[]{:S(2)}) collective-permute-start(bf16[128,512]{1,0:T(8,128)(2,1)S(1)} %collective-permute-done.32), channel_id=1, source_target_pairs={{0,64},{32,96},{64,0},{96,32},{1,65},{33,97},{65,1},{97,33},{2,66}... | collective-permute-start | bytes 393224 | tf_op jit(solution)/shard_map/ppermute | solution.py:49
  198.5 1.1 pad_maximum_fusion.2.refs_0_
  200.4 2.2 collective-permute-start.27
  202.7 2.0 collective-permute-start.28
  204.8 3.6 %collective-permute-start.36 = (bf16[4,128,512]{2,1,0:T(8,128)(2,1)S(1)}, bf16[4,128,512]{2,1,0:T(8,128)(2,1)S(1)}, u32[]{:S(2)}, u32[]{:S(2)}) collective-permute-start(bf16[4,128,512]{2,1,0:T(8,128)(2,1)S(1)} %pad_maximum_fusion.3.refs_4_), channel_id=1, source_target_pairs={{0,16},{16,0},{1,17},{17,1},{2,18},{18,2},{3,19},{19,3},{4,20},{20... | collective-permute-start | bytes 1572872 | tf_op jit(solution)/shard_map/ppermute | solution.py:573
  208.6 4.7 %collective-permute-done.26.refs_1_ = bf16[4,128,512]{2,1,0:T(8,128)(2,1)S(1)} collective-permute-done((bf16[4,128,512]{2,1,0:T(8,128)(2,1)S(1)}, bf16[4,128,512]{2,1,0:T(8,128)(2,1)S(1)}, u32[]{:S(2)}, u32[]{:S(2)}) %collective-permute-start.26) | collective-permute-done | bytes 524320 | tf_op jit(solution)/shard_map/ppermute | solution.py:49
  213.3 9.8 %collective-permute-done.27.refs_2_ = bf16[4,128,512]{2,1,0:T(8,128)(2,1)S(1)} collective-permute-done((bf16[4,128,512]{2,1,0:T(8,128)(2,1)S(1)}, bf16[4,128,512]{2,1,0:T(8,128)(2,1)S(1)}, u32[]{:S(2)}, u32[]{:S(2)}) %collective-permute-start.27) | collective-permute-done | bytes 524320 | tf_op jit(solution)/shard_map/ppermute | solution.py:49
  223.1 2.5 collective-permute-done.28.refs_3_
  225.6 0.8 copy-done.25
  226.4 0.8 copy-done.26
  227.2 5.4 %differentiate.1 = (f32[512,512]{1,0:T(8,128)}, f32[256,128]{1,0:T(8,128)}) custom-call(s32[16]{0:T(128)} %get-tuple-element.49.place_ref, bf16[4,128,512]{2,1,0:T(8,128)(2,1)} %copy-done.18, bf16[4,128,512]{2,1,0:T(8,128)(2,1)} %copy-done.22, bf16[4,128,512]{2,1,0:T(8,128)(2,1)} %copy-done.23, bf16[4,128,512]{2,1,0:T(8,128)(2,1)} %copy-done.24, ...), custom_call_target="tpu_custom_call" | custom-call | flops 1073741824 | bytes 5242880 | tf_op jit(solution)/shard_map/differentiate/pallas_call | solution.py:451
  232.6 24.1 %all_to_all.31 = f32[256,1,128]{2,1,0:T(1,128)} all-to-all(f32[256,1,128]{2,1,0:T(1,128)} %bitcast.41), channel_id=1, replica_groups=mesh['zh'=2,'y'=4,'c'=2,'zl'=4,'x'=4] {'zh','y','c','zl','x'}, dimensions={0} | all-to-all | bytes 262144 | tf_op jit(solution)/shard_map/all_to_all | solution.py:36
  256.7 4.8 %update.1 = (bf16[512,512]{1,0:T(8,128)(2,1)}, f32[512,512]{1,0:T(8,128)}, f32[512,512]{1,0:T(8,128)}, f32[1,1]{1,0:T(1,128)}) custom-call(f32[256,128]{1,0:T(8,128)} %bitcast.37, f32[512,512]{1,0:T(8,128)} %get-tuple-element.44.grad_ref, bf16[512,512]{1,0:T(8,128)(2,1)} %weight_ref.3, f32[512,512]{1,0:T(8,128)} %first_ref.1, f32[512,512]{1,0:T(8,128)} %second_ref.1), custom_call_target="tpu_custom_call" | custom-call | flops 5242880 | bytes 6291456 | tf_op jit(solution)/shard_map/update/pallas_call | solution.py:472
  (100 shorter events, 6.5 us)
Async XLA Ops:
  9.5 9.2 %copy-start.21 = (bf16[512,512]{1,0:T(8,128)(2,1)S(1)}, bf16[512,512]{1,0:T(8,128)(2,1)}, u32[]{:S(2)}) copy-start(bf16[512,512]{1,0:T(8,128)(2,1)} %weight_ref.3) | copy-start | bytes 1572868
  9.5 33.7 %all-to-all-start = ((bf16[16,144,256]{2,1,0:T(8,128)(2,1)}), bf16[16,144,256]{2,1,0:T(8,128)(2,1)S(1)}, u32[]{:S(2)}, u32[]{:S(2)}) async-start(bf16[16,144,256]{2,1,0:T(8,128)(2,1)} %get-tuple-element.27), calls=%async_computation | async-start | bytes 2359296 | tf_op jit(solution)/shard_map/all_to_all | solution.py:36
  51.2 28.7 %all-to-all-start.1 = ((bf16[4,4,128,512]{3,2,1,0:T(8,128)(2,1)}), bf16[4,4,128,512]{3,2,1,0:T(8,128)(2,1)S(1)}, u32[]{:S(2)}, u32[]{:S(2)}) async-start(bf16[4,4,128,512]{3,2,1,0:T(8,128)(2,1)} %project.1), calls=%async_computation.1 | async-start | bytes 4194304 | tf_op jit(solution)/shard_map/all_to_all | solution.py:36
  56.1 35.8 %collective-permute-start.6 = (bf16[256,512]{1,0:T(8,128)(2,1)S(1)}, bf16[256,512]{1,0:T(8,128)(2,1)S(1)}, u32[]{:S(2)}, u32[]{:S(2)}) collective-permute-start(bf16[256,512]{1,0:T(8,128)(2,1)S(1)} %get-tuple-element.37), channel_id=1, source_target_pairs={{0,128},{128,0},{1,129},{129,1},{2,130},{130,2},{3,131},{131,3},{4... | collective-permute-start | bytes 786440 | tf_op jit(solution)/shard_map/ppermute | solution.py:49
  60.3 45.5 %collective-permute-start.14 = (bf16[256,512]{1,0:T(8,128)(2,1)S(1)}, bf16[256,512]{1,0:T(8,128)(2,1)S(1)}, u32[]{:S(2)}, u32[]{:S(2)}) collective-permute-start(bf16[256,512]{1,0:T(8,128)(2,1)S(1)} %get-tuple-element.38), channel_id=1, source_target_pairs={{0,128},{128,0},{1,129},{129,1},{2,130},{130,2},{3,131},{131,3},{4... | collective-permute-start | bytes 786440 | tf_op jit(solution)/shard_map/ppermute | solution.py:49
  79.9 1.3 copy-start.16
  83.7 9.6 %collective-permute-start = (bf16[128,512]{1,0:T(8,128)(2,1)}, bf16[128,512]{1,0:T(8,128)(2,1)S(1)}, u32[]{:S(2)}, u32[]{:S(2)}) collective-permute-start(bf16[128,512]{1,0:T(8,128)(2,1)} %get-tuple-element.30), channel_id=1, source_target_pairs={{0,4},{4,8},{8,12},{12,0},{1,5},{5,9},{9,13},{13,1},{2,6},{6,10},{... | collective-permute-start | bytes 393224 | tf_op jit(solution)/shard_map/ppermute | solution.py:541
  88.2 10.2 %collective-permute-start.1 = (bf16[128,512]{1,0:T(8,128)(2,1)}, bf16[128,512]{1,0:T(8,128)(2,1)S(1)}, u32[]{:S(2)}, u32[]{:S(2)}) collective-permute-start(bf16[128,512]{1,0:T(8,128)(2,1)} %get-tuple-element.31), channel_id=1, source_target_pairs={{0,8},{4,12},{8,0},{12,4},{1,9},{5,13},{9,1},{13,5},{2,10},{6,14},... | collective-permute-start | bytes 393224 | tf_op jit(solution)/shard_map/ppermute | solution.py:541
  89.6 11.5 %collective-permute-start.2 = (bf16[128,512]{1,0:T(8,128)(2,1)}, bf16[128,512]{1,0:T(8,128)(2,1)S(1)}, u32[]{:S(2)}, u32[]{:S(2)}) collective-permute-start(bf16[128,512]{1,0:T(8,128)(2,1)} %get-tuple-element.32), channel_id=1, source_target_pairs={{0,12},{4,0},{8,4},{12,8},{1,13},{5,1},{9,5},{13,9},{2,14},{6,2},{... | collective-permute-start | bytes 393224 | tf_op jit(solution)/shard_map/ppermute | solution.py:541
  91.9 38.4 %collective-permute-start.7 = (bf16[2,256,512]{2,1,0:T(8,128)(2,1)S(1)}, bf16[2,256,512]{2,1,0:T(8,128)(2,1)}, u32[]{:S(2)}, u32[]{:S(2)}) collective-permute-start(bf16[2,256,512]{2,1,0:T(8,128)(2,1)S(1)} %pad_maximum_fusion.refs_0_), channel_id=1, source_target_pairs={{0,32},{32,64},{64,96},{96,0},{1,33},{33,65},{65,97},{97,1},{2,34}... | collective-permute-start | bytes 1572872 | tf_op jit(solution)/shard_map/ppermute | solution.py:49
  93.3 7.8 %copy-start.27 = (bf16[128,512]{1,0:T(8,128)(2,1)}, bf16[128,512]{1,0:T(8,128)(2,1)S(1)}, u32[]{:S(2)}) copy-start(bf16[128,512]{1,0:T(8,128)(2,1)S(1)} %collective-permute-done.one_ref) | copy-start | bytes 393220
  93.3 37.5 %collective-permute-start.8 = (bf16[2,256,512]{2,1,0:T(8,128)(2,1)S(1)}, bf16[2,256,512]{2,1,0:T(8,128)(2,1)}, u32[]{:S(2)}, u32[]{:S(2)}) collective-permute-start(bf16[2,256,512]{2,1,0:T(8,128)(2,1)S(1)} %pad_maximum_fusion.refs_0_), channel_id=1, source_target_pairs={{0,64},{32,96},{64,0},{96,32},{1,65},{33,97},{65,1},{97,33},{2,66}... | collective-permute-start | bytes 1572872 | tf_op jit(solution)/shard_map/ppermute | solution.py:49
  98.4 2.7 %copy-start.28 = (bf16[128,512]{1,0:T(8,128)(2,1)}, bf16[128,512]{1,0:T(8,128)(2,1)S(1)}, u32[]{:S(2)}) copy-start(bf16[128,512]{1,0:T(8,128)(2,1)S(1)} %collective-permute-done.1.two_ref) | copy-start | bytes 393220
  98.4 37.6 %collective-permute-start.9 = (bf16[2,256,512]{2,1,0:T(8,128)(2,1)S(1)}, bf16[2,256,512]{2,1,0:T(8,128)(2,1)}, u32[]{:S(2)}, u32[]{:S(2)}) collective-permute-start(bf16[2,256,512]{2,1,0:T(8,128)(2,1)S(1)} %pad_maximum_fusion.refs_0_), channel_id=1, source_target_pairs={{0,96},{32,0},{64,32},{96,64},{1,97},{33,1},{65,33},{97,65},{2,98}... | collective-permute-start | bytes 1572872 | tf_op jit(solution)/shard_map/ppermute | solution.py:49
  103.9 7.4 %copy-start.29 = (bf16[128,512]{1,0:T(8,128)(2,1)S(1)}, bf16[128,512]{1,0:T(8,128)(2,1)}, u32[]{:S(2)}) copy-start(bf16[128,512]{1,0:T(8,128)(2,1)} %get-tuple-element.33) | copy-start | bytes 393220
  103.9 7.4 %collective-permute-start.3 = (bf16[128,512]{1,0:T(8,128)(2,1)}, bf16[128,512]{1,0:T(8,128)(2,1)S(1)}, u32[]{:S(2)}, u32[]{:S(2)}) collective-permute-start(bf16[128,512]{1,0:T(8,128)(2,1)} %get-tuple-element.33), channel_id=1, source_target_pairs={{0,4},{4,8},{8,12},{12,0},{1,5},{5,9},{9,13},{13,1},{2,6},{6,10},{... | collective-permute-start | bytes 393224 | tf_op jit(solution)/shard_map/ppermute | solution.py:49
  105.9 30.2 %collective-permute-start.15 = (bf16[2,256,512]{2,1,0:T(8,128)(2,1)S(1)}, bf16[2,256,512]{2,1,0:T(8,128)(2,1)}, u32[]{:S(2)}, u32[]{:S(2)}) collective-permute-start(bf16[2,256,512]{2,1,0:T(8,128)(2,1)S(1)} %pad_maximum_fusion.1.refs_8_), channel_id=1, source_target_pairs={{0,32},{32,64},{64,96},{96,0},{1,33},{33,65},{65,97},{97,1},{2,34}... | collective-permute-start | bytes 1572872 | tf_op jit(solution)/shard_map/ppermute | solution.py:49
  107.7 16.9 %all-to-all-start.2 = ((bf16[4,128,512]{2,1,0:T(8,128)(2,1)}), bf16[4,128,512]{2,1,0:T(8,128)(2,1)S(1)}, u32[]{:S(2)}, u32[]{:S(2)}) async-start(bf16[4,128,512]{2,1,0:T(8,128)(2,1)} %reshape.43), calls=%async_computation.2 | async-start | bytes 1048576 | tf_op jit(solution)/shard_map/all_to_all | solution.py:36
  111.3 7.0 %collective-permute-start.4 = (bf16[128,512]{1,0:T(8,128)(2,1)S(1)}, bf16[128,512]{1,0:T(8,128)(2,1)S(1)}, u32[]{:S(2)}, u32[]{:S(2)}) collective-permute-start(bf16[128,512]{1,0:T(8,128)(2,1)S(1)} %copy-done.29), channel_id=1, source_target_pairs={{0,8},{4,12},{8,0},{12,4},{1,9},{5,13},{9,1},{13,5},{2,10},{6,14},... | collective-permute-start | bytes 393224 | tf_op jit(solution)/shard_map/ppermute | solution.py:49
  118.3 4.4 %collective-permute-start.5 = (bf16[128,512]{1,0:T(8,128)(2,1)S(1)}, bf16[128,512]{1,0:T(8,128)(2,1)S(1)}, u32[]{:S(2)}, u32[]{:S(2)}) collective-permute-start(bf16[128,512]{1,0:T(8,128)(2,1)S(1)} %copy-done.29), channel_id=1, source_target_pairs={{0,12},{4,0},{8,4},{12,8},{1,13},{5,1},{9,5},{13,9},{2,14},{6,2},{... | collective-permute-start | bytes 393224 | tf_op jit(solution)/shard_map/ppermute | solution.py:49
  122.8 15.7 %collective-permute-start.16 = (bf16[2,256,512]{2,1,0:T(8,128)(2,1)S(1)}, bf16[2,256,512]{2,1,0:T(8,128)(2,1)}, u32[]{:S(2)}, u32[]{:S(2)}) collective-permute-start(bf16[2,256,512]{2,1,0:T(8,128)(2,1)S(1)} %pad_maximum_fusion.1.refs_8_), channel_id=1, source_target_pairs={{0,64},{32,96},{64,0},{96,32},{1,65},{33,97},{65,1},{97,33},{2,66}... | collective-permute-start | bytes 1572872 | tf_op jit(solution)/shard_map/ppermute | solution.py:49
  125.9 45.8 %copy-start.8 = (bf16[4,8192]{1,0:T(4,128)(2,1)S(1)}, bf16[4,8192]{1,0:T(4,128)(2,1)}, u32[]{:S(2)}) copy-start(bf16[4,8192]{1,0:T(4,128)(2,1)} %prev_ref.3) | copy-start | bytes 196612
  125.9 45.8 %copy-start.9 = (f32[128,512]{1,0:T(8,128)S(1)}, f32[128,512]{1,0:T(8,128)}, u32[]{:S(2)}) copy-start(f32[128,512]{1,0:T(8,128)} %get-tuple-element.34.mixed_ref) | copy-start | bytes 786436
  125.9 45.8 %copy-start.10 = (f32[8192]{0:T(1024)S(1)}, f32[8192]{0:T(1024)}, u32[]{:S(2)}) copy-start(f32[8192]{0:T(1024)} %param.24) | copy-start | bytes 98308
  125.9 45.8 %copy-start.11 = (bf16[128,128]{1,0:T(8,128)(2,1)S(1)}, bf16[128,128]{1,0:T(8,128)(2,1)}, u32[]{:S(2)}) copy-start(bf16[128,128]{1,0:T(8,128)(2,1)} %get-tuple-element.35.reach_ref) | copy-start | bytes 98308
  125.9 45.8 %copy-start.14 = (s32[4]{0:T(128)S(1)}, s32[4]{0:T(128)}, u32[]{:S(2)}) copy-start(s32[4]{0:T(128)} %len_ref.3) | copy-start | bytes 52
  125.9 45.8 %copy-start.15 = (s32[4]{0:T(128)S(1)}, s32[4]{0:T(128)}, u32[]{:S(2)}) copy-start(s32[4]{0:T(128)} %leaf_ref.1) | copy-start | bytes 52
  125.9 45.7 %all-to-all-start.3 = ((bf16[12,128,512]{2,1,0:T(8,128)(2,1)}), bf16[12,128,512]{2,1,0:T(8,128)(2,1)S(1)}, u32[]{:S(2)}, u32[]{:S(2)}) async-start(bf16[12,128,512]{2,1,0:T(8,128)(2,1)} %bitcast.34), calls=%async_computation.3 | async-start | bytes 3145728 | tf_op jit(solution)/shard_map/all_to_all | solution.py:36
  130.3 17.0 %collective-permute-start.17 = (bf16[2,256,512]{2,1,0:T(8,128)(2,1)S(1)}, bf16[2,256,512]{2,1,0:T(8,128)(2,1)}, u32[]{:S(2)}, u32[]{:S(2)}) collective-permute-start(bf16[2,256,512]{2,1,0:T(8,128)(2,1)S(1)} %pad_maximum_fusion.1.refs_8_), channel_id=1, source_target_pairs={{0,96},{32,0},{64,32},{96,64},{1,97},{33,1},{65,33},{97,65},{2,98}... | collective-permute-start | bytes 1572872 | tf_op jit(solution)/shard_map/ppermute | solution.py:49
  130.8 19.3 %collective-permute-start.10 = (bf16[2,256,512]{2,1,0:T(8,128)(2,1)S(1)}, bf16[2,256,512]{2,1,0:T(8,128)(2,1)S(1)}, u32[]{:S(2)}, u32[]{:S(2)}) collective-permute-start(bf16[2,256,512]{2,1,0:T(8,128)(2,1)S(1)} %pad_maximum_fusion.refs_0_), channel_id=1, source_target_pairs={{0,16},{16,0},{1,17},{17,1},{2,18},{18,2},{3,19},{19,3},{4,20},{20... | collective-permute-start | bytes 1572872 | tf_op jit(solution)/shard_map/ppermute | solution.py:537
  136.0 15.0 %collective-permute-start.18 = (bf16[2,256,512]{2,1,0:T(8,128)(2,1)S(1)}, bf16[2,256,512]{2,1,0:T(8,128)(2,1)S(1)}, u32[]{:S(2)}, u32[]{:S(2)}) collective-permute-start(bf16[2,256,512]{2,1,0:T(8,128)(2,1)S(1)} %pad_maximum_fusion.1.refs_8_), channel_id=1, source_target_pairs={{0,16},{16,0},{1,17},{17,1},{2,18},{18,2},{3,19},{19,3},{4,20},{20... | collective-permute-start | bytes 1572872 | tf_op jit(solution)/shard_map/ppermute | solution.py:551
  136.1 16.2 %collective-permute-start.11 = (bf16[2,256,512]{2,1,0:T(8,128)(2,1)}, bf16[2,256,512]{2,1,0:T(8,128)(2,1)S(1)}, u32[]{:S(2)}, u32[]{:S(2)}) collective-permute-start(bf16[2,256,512]{2,1,0:T(8,128)(2,1)} %collective-permute-done.7.refs_1_), channel_id=1, source_target_pairs={{0,16},{16,0},{1,17},{17,1},{2,18},{18,2},{3,19},{19,3},{4,20},{20... | collective-permute-start | bytes 1572872 | tf_op jit(solution)/shard_map/ppermute | solution.py:537
  138.5 14.6 %collective-permute-start.12 = (bf16[2,256,512]{2,1,0:T(8,128)(2,1)}, bf16[2,256,512]{2,1,0:T(8,128)(2,1)S(1)}, u32[]{:S(2)}, u32[]{:S(2)}) collective-permute-start(bf16[2,256,512]{2,1,0:T(8,128)(2,1)} %collective-permute-done.8.refs_2_), channel_id=1, source_target_pairs={{0,16},{16,0},{1,17},{17,1},{2,18},{18,2},{3,19},{19,3},{4,20},{20... | collective-permute-start | bytes 1572872 | tf_op jit(solution)/shard_map/ppermute | solution.py:537
  147.3 18.2 %collective-permute-start.13 = (bf16[2,256,512]{2,1,0:T(8,128)(2,1)}, bf16[2,256,512]{2,1,0:T(8,128)(2,1)}, u32[]{:S(2)}, u32[]{:S(2)}) collective-permute-start(bf16[2,256,512]{2,1,0:T(8,128)(2,1)} %collective-permute-done.9.refs_3_), channel_id=1, source_target_pairs={{0,16},{16,0},{1,17},{17,1},{2,18},{18,2},{3,19},{19,3},{4,20},{20... | collective-permute-start | bytes 1572872 | tf_op jit(solution)/shard_map/ppermute | solution.py:537
  150.9 20.7 %collective-permute-start.19 = (bf16[2,256,512]{2,1,0:T(8,128)(2,1)}, bf16[2,256,512]{2,1,0:T(8,128)(2,1)}, u32[]{:S(2)}, u32[]{:S(2)}) collective-permute-start(bf16[2,256,512]{2,1,0:T(8,128)(2,1)} %collective-permute-done.15.refs_9_), channel_id=1, source_target_pairs={{0,16},{16,0},{1,17},{17,1},{2,18},{18,2},{3,19},{19,3},{4,20},{20... | collective-permute-start | bytes 1572872 | tf_op jit(solution)/shard_map/ppermute | solution.py:551
  151.8 19.9 %collective-permute-start.20 = (bf16[2,256,512]{2,1,0:T(8,128)(2,1)}, bf16[2,256,512]{2,1,0:T(8,128)(2,1)}, u32[]{:S(2)}, u32[]{:S(2)}) collective-permute-start(bf16[2,256,512]{2,1,0:T(8,128)(2,1)} %collective-permute-done.16.refs_10_), channel_id=1, source_target_pairs={{0,16},{16,0},{1,17},{17,1},{2,18},{18,2},{3,19},{19,3},{4,20},{20... | collective-permute-start | bytes 1572872 | tf_op jit(solution)/shard_map/ppermute | solution.py:551
  153.1 18.6 %collective-permute-start.21 = (bf16[2,256,512]{2,1,0:T(8,128)(2,1)}, bf16[2,256,512]{2,1,0:T(8,128)(2,1)}, u32[]{:S(2)}, u32[]{:S(2)}) collective-permute-start(bf16[2,256,512]{2,1,0:T(8,128)(2,1)} %collective-permute-done.17.refs_11_), channel_id=1, source_target_pairs={{0,16},{16,0},{1,17},{17,1},{2,18},{18,2},{3,19},{19,3},{4,20},{20... | collective-permute-start | bytes 1572872 | tf_op jit(solution)/shard_map/ppermute | solution.py:551
  153.9 6.8 %collective-permute-start.22 = (bf16[128,512]{1,0:T(8,128)(2,1)}, bf16[128,512]{1,0:T(8,128)(2,1)}, u32[]{:S(2)}, u32[]{:S(2)}) collective-permute-start(bf16[128,512]{1,0:T(8,128)(2,1)} %get-tuple-element.40), channel_id=1, source_target_pairs={{0,0},{1,16},{2,32},{3,48},{4,64},{5,80},{6,96},{7,112},{8,128},{9... | collective-permute-start | bytes 393224 | tf_op jit(solution)/shard_map/ppermute | solution.py:548
  160.7 25.1 %collective-permute-start.23 = (bf16[128,512]{1,0:T(8,128)(2,1)}, bf16[128,512]{1,0:T(8,128)(2,1)}, u32[]{:S(2)}, u32[]{:S(2)}) collective-permute-start(bf16[128,512]{1,0:T(8,128)(2,1)} %collective-permute-done.22), channel_id=1, source_target_pairs={{0,4},{4,8},{8,12},{12,0},{1,5},{5,9},{9,13},{13,1},{2,6},{6,10},{... | collective-permute-start | bytes 393224 | tf_op jit(solution)/shard_map/ppermute | solution.py:49
  165.5 25.1 %collective-permute-start.24 = (bf16[128,512]{1,0:T(8,128)(2,1)}, bf16[128,512]{1,0:T(8,128)(2,1)}, u32[]{:S(2)}, u32[]{:S(2)}) collective-permute-start(bf16[128,512]{1,0:T(8,128)(2,1)} %collective-permute-done.22), channel_id=1, source_target_pairs={{0,8},{4,12},{8,0},{12,4},{1,9},{5,13},{9,1},{13,5},{2,10},{6,14},... | collective-permute-start | bytes 393224 | tf_op jit(solution)/shard_map/ppermute | solution.py:49
  171.7 1.0 copy-start.1
  172.8 1.0 copy-start.3
  173.8 1.0 copy-start.5
  174.8 1.0 copy-start.7
  182.2 26.3 %copy-start.13 = (f32[8,128]{1,0:T(8,128)}, f32[8,128]{1,0:T(8,128)S(1)}, u32[]{:S(2)}) copy-start(f32[8,128]{1,0:T(8,128)S(1)} %get-tuple-element.42.refs_8_) | copy-start | bytes 12292
  182.2 9.1 %collective-permute-start.32 = (bf16[128,512]{1,0:T(8,128)(2,1)S(1)}, bf16[128,512]{1,0:T(8,128)(2,1)S(1)}, u32[]{:S(2)}, u32[]{:S(2)}) collective-permute-start(bf16[128,512]{1,0:T(8,128)(2,1)S(1)} %get-tuple-element.41), channel_id=1, source_target_pairs={{0,128},{128,0},{1,129},{129,1},{2,130},{130,2},{3,131},{131,3},{4... | collective-permute-start | bytes 393224 | tf_op jit(solution)/shard_map/ppermute | solution.py:569
  183.8 8.5 %collective-permute-start.25 = (bf16[128,512]{1,0:T(8,128)(2,1)}, bf16[128,512]{1,0:T(8,128)(2,1)S(1)}, u32[]{:S(2)}, u32[]{:S(2)}) collective-permute-start(bf16[128,512]{1,0:T(8,128)(2,1)} %collective-permute-done.22), channel_id=1, source_target_pairs={{0,12},{4,0},{8,4},{12,8},{1,13},{5,1},{9,5},{13,9},{2,14},{6,2},{... | collective-permute-start | bytes 393224 | tf_op jit(solution)/shard_map/ppermute | solution.py:49
  185.5 12.5 %collective-permute-start.29 = (bf16[128,512]{1,0:T(8,128)(2,1)S(1)}, bf16[128,512]{1,0:T(8,128)(2,1)S(1)}, u32[]{:S(2)}, u32[]{:S(2)}) collective-permute-start(bf16[128,512]{1,0:T(8,128)(2,1)S(1)} %get-tuple-element.41), channel_id=1, source_target_pairs={{0,32},{32,64},{64,96},{96,0},{1,33},{33,65},{65,97},{97,1},{2,34}... | collective-permute-start | bytes 393224 | tf_op jit(solution)/shard_map/ppermute | solution.py:49
  185.8 13.8 %collective-permute-start.30 = (bf16[128,512]{1,0:T(8,128)(2,1)S(1)}, bf16[128,512]{1,0:T(8,128)(2,1)S(1)}, u32[]{:S(2)}, u32[]{:S(2)}) collective-permute-start(bf16[128,512]{1,0:T(8,128)(2,1)S(1)} %get-tuple-element.41), channel_id=1, source_target_pairs={{0,64},{32,96},{64,0},{96,32},{1,65},{33,97},{65,1},{97,33},{2,66}... | collective-permute-start | bytes 393224 | tf_op jit(solution)/shard_map/ppermute | solution.py:49
  190.6 9.7 %collective-permute-start.31 = (bf16[128,512]{1,0:T(8,128)(2,1)S(1)}, bf16[128,512]{1,0:T(8,128)(2,1)S(1)}, u32[]{:S(2)}, u32[]{:S(2)}) collective-permute-start(bf16[128,512]{1,0:T(8,128)(2,1)S(1)} %get-tuple-element.41), channel_id=1, source_target_pairs={{0,96},{32,0},{64,32},{96,64},{1,97},{33,1},{65,33},{97,65},{2,98}... | collective-permute-start | bytes 393224 | tf_op jit(solution)/shard_map/ppermute | solution.py:49
  191.2 11.5 %collective-permute-start.33 = (bf16[128,512]{1,0:T(8,128)(2,1)S(1)}, bf16[128,512]{1,0:T(8,128)(2,1)S(1)}, u32[]{:S(2)}, u32[]{:S(2)}) collective-permute-start(bf16[128,512]{1,0:T(8,128)(2,1)S(1)} %collective-permute-done.32), channel_id=1, source_target_pairs={{0,32},{32,64},{64,96},{96,0},{1,33},{33,65},{65,97},{97,1},{2,34}... | collective-permute-start | bytes 393224 | tf_op jit(solution)/shard_map/ppermute | solution.py:49
  192.3 12.5 %collective-permute-start.34 = (bf16[128,512]{1,0:T(8,128)(2,1)S(1)}, bf16[128,512]{1,0:T(8,128)(2,1)S(1)}, u32[]{:S(2)}, u32[]{:S(2)}) collective-permute-start(bf16[128,512]{1,0:T(8,128)(2,1)S(1)} %collective-permute-done.32), channel_id=1, source_target_pairs={{0,64},{32,96},{64,0},{96,32},{1,65},{33,97},{65,1},{97,33},{2,66}... | collective-permute-start | bytes 393224 | tf_op jit(solution)/shard_map/ppermute | solution.py:49
  198.0 10.4 %collective-permute-start.35 = (bf16[128,512]{1,0:T(8,128)(2,1)S(1)}, bf16[128,512]{1,0:T(8,128)(2,1)S(1)}, u32[]{:S(2)}, u32[]{:S(2)}) collective-permute-start(bf16[128,512]{1,0:T(8,128)(2,1)S(1)} %collective-permute-done.32), channel_id=1, source_target_pairs={{0,96},{32,0},{64,32},{96,64},{1,97},{33,1},{65,33},{97,65},{2,98}... | collective-permute-start | bytes 393224 | tf_op jit(solution)/shard_map/ppermute | solution.py:49
  199.6 27.6 %copy-start.18 = (bf16[4,128,512]{2,1,0:T(8,128)(2,1)}, bf16[4,128,512]{2,1,0:T(8,128)(2,1)S(1)}, u32[]{:S(2)}) copy-start(bf16[4,128,512]{2,1,0:T(8,128)(2,1)S(1)} %pad_maximum_fusion.2.refs_0_) | copy-start | bytes 1572868
  199.6 13.7 %collective-permute-start.26 = (bf16[4,128,512]{2,1,0:T(8,128)(2,1)S(1)}, bf16[4,128,512]{2,1,0:T(8,128)(2,1)S(1)}, u32[]{:S(2)}, u32[]{:S(2)}) collective-permute-start(bf16[4,128,512]{2,1,0:T(8,128)(2,1)S(1)} %pad_maximum_fusion.2.refs_0_), channel_id=1, source_target_pairs={{0,1},{1,2},{2,3},{3,0},{4,5},{5,6},{6,7},{7,4},{8,9},{9,10},{10,1... | collective-permute-start | bytes 1572872 | tf_op jit(solution)/shard_map/ppermute | solution.py:49
  200.4 22.7 %collective-permute-start.27 = (bf16[4,128,512]{2,1,0:T(8,128)(2,1)S(1)}, bf16[4,128,512]{2,1,0:T(8,128)(2,1)S(1)}, u32[]{:S(2)}, u32[]{:S(2)}) collective-permute-start(bf16[4,128,512]{2,1,0:T(8,128)(2,1)S(1)} %pad_maximum_fusion.2.refs_0_), channel_id=1, source_target_pairs={{0,2},{1,3},{2,0},{3,1},{4,6},{5,7},{6,4},{7,5},{8,10},{9,11},{10,... | collective-permute-start | bytes 1572872 | tf_op jit(solution)/shard_map/ppermute | solution.py:49
  202.7 24.5 %copy-start.19 = (bf16[4,128,512]{2,1,0:T(8,128)(2,1)}, bf16[4,128,512]{2,1,0:T(8,128)(2,1)S(1)}, u32[]{:S(2)}) copy-start(bf16[4,128,512]{2,1,0:T(8,128)(2,1)S(1)} %pad_maximum_fusion.3.refs_4_) | copy-start | bytes 1572868
  202.7 22.8 %collective-permute-start.28 = (bf16[4,128,512]{2,1,0:T(8,128)(2,1)S(1)}, bf16[4,128,512]{2,1,0:T(8,128)(2,1)S(1)}, u32[]{:S(2)}, u32[]{:S(2)}) collective-permute-start(bf16[4,128,512]{2,1,0:T(8,128)(2,1)S(1)} %pad_maximum_fusion.2.refs_0_), channel_id=1, source_target_pairs={{0,3},{1,0},{2,1},{3,2},{4,7},{5,4},{6,5},{7,6},{8,11},{9,8},{10,9... | collective-permute-start | bytes 1572872 | tf_op jit(solution)/shard_map/ppermute | solution.py:49
  204.8 20.8 %collective-permute-start.36 = (bf16[4,128,512]{2,1,0:T(8,128)(2,1)S(1)}, bf16[4,128,512]{2,1,0:T(8,128)(2,1)S(1)}, u32[]{:S(2)}, u32[]{:S(2)}) collective-permute-start(bf16[4,128,512]{2,1,0:T(8,128)(2,1)S(1)} %pad_maximum_fusion.3.refs_4_), channel_id=1, source_target_pairs={{0,16},{16,0},{1,17},{17,1},{2,18},{18,2},{3,19},{19,3},{4,20},{20... | collective-permute-start | bytes 1572872 | tf_op jit(solution)/shard_map/ppermute | solution.py:573
  208.5 18.7 %copy-start.20 = (bf16[4,128,512]{2,1,0:T(8,128)(2,1)}, bf16[4,128,512]{2,1,0:T(8,128)(2,1)S(1)}, u32[]{:S(2)}) copy-start(bf16[4,128,512]{2,1,0:T(8,128)(2,1)S(1)} %pad_maximum_fusion.4.refs_5_) | copy-start | bytes 1572868
  208.5 17.1 %collective-permute-start.37 = (bf16[4,128,512]{2,1,0:T(8,128)(2,1)S(1)}, bf16[4,128,512]{2,1,0:T(8,128)(2,1)S(1)}, u32[]{:S(2)}, u32[]{:S(2)}) collective-permute-start(bf16[4,128,512]{2,1,0:T(8,128)(2,1)S(1)} %pad_maximum_fusion.4.refs_5_), channel_id=1, source_target_pairs={{0,16},{16,0},{1,17},{17,1},{2,18},{18,2},{3,19},{19,3},{4,20},{20... | collective-permute-start | bytes 1572872 | tf_op jit(solution)/shard_map/ppermute | solution.py:573
  213.3 13.9 %copy-start.22 = (bf16[4,128,512]{2,1,0:T(8,128)(2,1)}, bf16[4,128,512]{2,1,0:T(8,128)(2,1)S(1)}, u32[]{:S(2)}) copy-start(bf16[4,128,512]{2,1,0:T(8,128)(2,1)S(1)} %collective-permute-done.26.refs_1_) | copy-start | bytes 1572868
  223.1 4.1 %copy-start.23 = (bf16[4,128,512]{2,1,0:T(8,128)(2,1)}, bf16[4,128,512]{2,1,0:T(8,128)(2,1)S(1)}, u32[]{:S(2)}) copy-start(bf16[4,128,512]{2,1,0:T(8,128)(2,1)S(1)} %collective-permute-done.27.refs_2_) | copy-start | bytes 1572868
  225.6 1.6 copy-start.24
  (9 other events, 7.3 us)

commit v8 on v6

--- a/solution.py
+++ b/solution.py
@@ -36,21 +36,12 @@
     return lax.all_to_all(value, axis, 0, 0, tiled=True)
 
 
-def spread(value, axis, count):
-    wide = jnp.broadcast_to(value[None], (count, *value.shape))
-    return exchange(wide.reshape(count * value.shape[0], *value.shape[1:]), axis)
-
-
 def turn(count, step):
     return [(i, (i + step) % count) for i in range(count)]
 
 
 def passed(value, axis, count):
     return [value] + [lax.ppermute(value, axis, turn(count, step)) for step in range(1, count)]
-
-
-def turns(value, axis, count):
-    return jnp.stack(passed(value, axis, count))
 
 
 def dot(left, right, dims, **kwargs):
@@ -65,7 +56,7 @@
 
 def attend_kernel(
     rank_ref, len_ref, par_ref, q_ref, ck_ref, cv_ref, tk_ref, tv_ref,
-    out_ref, reach_ref, pick_ref, stat_ref,
+    out_ref, maps_ref, stat_ref,
 ):
     r = pl.program_id(0)
     rank = rank_ref[0]
@@ -87,12 +78,12 @@
             parent = jnp.where(lane_request == r, wide[r : r + 1], parent)
         parent = parent.astype(jnp.int32)
         rooted = jnp.where(parent < 0, NODES - 1, parent)
-        pick_ref[...] = jnp.where(row == base + rooted, 1.0, 0.0).astype(BF16)
+        maps_ref[128:256] = jnp.where(row == base + rooted, 1.0, 0.0).astype(BF16)
         up = jnp.where(row == base + parent, jnp.where(parent >= 0, 1.0, 0.0), 0.0)
         reach = (jnp.where(row == lane, 1.0, 0.0) + up).astype(BF16)
         for _ in range((NODES - 1).bit_length()):
             reach = jnp.minimum(dot(reach, reach, ((1,), (0,))), 1.0).astype(BF16)
-        reach_ref[...] = reach
+        maps_ref[0:128] = reach
         own = jnp.where(row % NODES == 2 * rank + lane, jnp.where(lane < 2, 1.0, 0.0), 0.0)
         stat_ref[...] = dot(reach, own.astype(BF16), ((0,), (0,)))
 
@@ -184,13 +175,16 @@
 
 def settle_kernel(
     rank_ref, own_ref, one_ref, two_ref, three_ref, residual_ref, gain_ref, prev_ref,
-    mixed_ref, near_ref, table_ref,
+    mixed_ref, near_ref, wide_ref, table_ref,
 ):
     total = own_ref[...].astype(F32) + one_ref[...].astype(F32)
     total = total + (two_ref[...].astype(F32) + three_ref[...].astype(F32))
     mixed = residual_ref[...].astype(F32) + total
     mixed_ref[...] = mixed
-    near_ref[...] = mixed.astype(BF16)
+    near = mixed.astype(BF16)
+    near_ref[...] = near
+    for x in range(4):
+        wide_ref[x] = near
     scaled = mixed * gain_ref[0]
     node = lax.broadcasted_iota(jnp.int32, (NODES, 1), 0)
     prev = prev_ref[...].astype(F32)
@@ -200,8 +194,8 @@
 
 
 def predict_kernel(
-    source_ref, rank_ref, len_ref, leaf_ref, far_own_ref, far_rest_ref, mixed_ref, gain_ref, prev_ref, reach_ref,
-    pick_ref, *refs,
+    source_ref, rank_ref, len_ref, leaf_ref, far_own_ref, far_rest_ref, mixed_ref, gain_ref, prev_ref, maps_ref,
+    *refs,
 ):
     weight_refs = refs[:16]
     own_ref, err_ref, loss_ref, scale_ref, ahead_ref, weight_ref, sem_ref, far_ref, far_sem = refs[16:]
@@ -255,11 +249,11 @@
     accepted = []
     for r in range(4):
         part = slice(r * NODES, (r + 1) * NODES)
-        path = jnp.where(lane[part] == leaf_ref[r] + r * NODES, reach_ref[part].astype(F32), 0.0)
+        path = jnp.where(lane[part] == leaf_ref[r] + r * NODES, maps_ref[part].astype(F32), 0.0)
         path = jnp.sum(path, axis=1, keepdims=True)
         accepted.append((1.0 + 3.0 * path) * (0.5 + len_ref[r].astype(F32) / CACHE))
     weights = jnp.concatenate(accepted, axis=0)
-    pick = pick_ref[...].astype(F32)
+    pick = maps_ref[128:256].astype(F32)
     predicted = dot(pick, ahead_ref[...], ((0,), (0,)), precision=lax.Precision.HIGHEST)
     error = predicted - own_ref[...].astype(F32)
     weighted = weights * error
@@ -318,8 +312,7 @@
         attend_kernel,
         out_shape=(
             jax.ShapeDtypeStruct((N_TP, 144, 2 * HEAD), BF16),
-            jax.ShapeDtypeStruct((128, 128), BF16),
-            jax.ShapeDtypeStruct((128, 128), BF16),
+            jax.ShapeDtypeStruct((256, 128), BF16),
         ),
         grid=(4,),
         in_specs=[
@@ -332,8 +325,7 @@
         + [pl.BlockSpec((1, 2, KV_HEADS * HEAD), lambda r: (r, 0, 0))] * 2,
         out_specs=(
             pl.BlockSpec((N_TP, 144, 2 * HEAD), lambda r: (0, 0, 0)),
-            pl.BlockSpec((128, 128), lambda r: (0, 0)),
-            pl.BlockSpec((128, 128), lambda r: (0, 0)),
+            pl.BlockSpec((256, 128), lambda r: (0, 0)),
         ),
         scratch_shapes=[pltpu.VMEM((128, 128), F32)],
         cost_estimate=pl.CostEstimate(
@@ -386,11 +378,17 @@
                 pl.BlockSpec((1, 1, 512), lambda p, at: (at[0], 0, 0)),
                 pl.BlockSpec((4, 512), lambda p, at: (0, at[0])),
             ],
-            out_specs=[whole] * 3,
+            out_specs=[
+                whole,
+                whole,
+                pl.BlockSpec((4, 128, 512), lambda p, at: (0, 0, 0)),
+                whole,
+            ],
         ),
         out_shape=(
             jax.ShapeDtypeStruct((128, 512), F32),
             jax.ShapeDtypeStruct((128, 512), BF16),
+            jax.ShapeDtypeStruct((4, 128, 512), BF16),
             jax.ShapeDtypeStruct((128, 512), BF16),
         ),
         cost_estimate=pl.CostEstimate(
@@ -400,7 +398,7 @@
     )(rank, *terms, residual, gain, prev)
 
 
-def predict(source, rank, lengths, leaf, far_own, far, mixed, gain, prev, reach, pick, all_weight):
+def predict(source, rank, lengths, leaf, far_own, far, mixed, gain, prev, maps, all_weight):
     return pl.pallas_call(
         predict_kernel,
         out_shape=(
@@ -410,7 +408,7 @@
         ),
         in_specs=[in_smem()] * 4
         + [pl.BlockSpec(memory_space=pl.ANY)] * 2
-        + [in_vmem()] * 5
+        + [in_vmem()] * 4
         + [pl.BlockSpec(memory_space=pl.ANY)] * 16,
         out_specs=(in_vmem(),) * 3,
         scratch_shapes=[
@@ -426,7 +424,7 @@
             flops=2 * 128 * 8192 * 512, bytes_accessed=13 << 20, transcendentals=0
         ),
         name="predict",
-    )(source, rank, lengths, leaf, far_own, far, mixed, gain, prev, reach, pick, *all_weight)
+    )(source, rank, lengths, leaf, far_own, far, mixed, gain, prev, maps, *all_weight)
 
 
 def differentiate(place, columns, errors, loss):
@@ -495,7 +493,7 @@
     )
     place = (source % 4) * 4 + (lax.axis_index("zl") + 4 - source // 4) % 4
 
-    parcel, reach, pick = attend(
+    parcel, maps = attend(
         rank, lengths, parents, queries, cache_keys, cache_values, tree_keys, tree_values
     )
     parcel = exchange(parcel, TP)
@@ -515,18 +513,21 @@
     lower = passed(lower, "y", 4)
     terms = list(fold(rank, along_x))
     terms[1:] = [lax.ppermute(terms[step], "zl", turn(4, step)) for step in (1, 2, 3)]
-    mixed, near, table = settle(rank, terms, residual.reshape(rows, block), gain, prev_feature)
+    mixed, near, wide, table = settle(rank, terms, residual.reshape(rows, block), gain, prev_feature)
 
     far = passed(near, "zl", 4)[1:]
-    far_own = spread(near[None], "x", 4)
+    far_own = exchange(wide, "x")
     far = jnp.stack(far)
-    far = spread(far, "x", 4).reshape(4, 3, rows, block)
+    far = jnp.broadcast_to(far[None], (4, 3, rows, block)).reshape(12, rows, block)
+    far = exchange(far, "x").reshape(4, 3, rows, block)
     swapped = lax.ppermute(
         table, REQ + TP, [(i * N_TP + j, j * N_TP + i) for i in range(16) for j in range(16)]
     )
     other_lower = [lax.ppermute(part, "c", turn(2, 1)) for part in lower]
-    columns = turns(swapped, "zl", 4)
-    columns = spread(columns, "x", 4).reshape(N_REQ, rows, block)
+    columns = passed(swapped, "zl", 4)
+    columns = jnp.stack(columns)
+    columns = jnp.broadcast_to(columns[None], (4, 4, rows, block)).reshape(16, rows, block)
+    columns = exchange(columns, "x")
     own_features, scaled_err, loss = predict(
         source,
         rank,
@@ -537,8 +538,7 @@
         mixed,
         gain,
         prev_feature,
-        reach,
-        pick,
+        maps,
         upper + other_upper + lower + other_lower,
     )
     far_err = lax.ppermute(scaled_err, "zh", turn(2, 1))

time: 282 us -> 280 us (level)
    unnamed x52 -> x50, local copies, waits for them, and re-layouts: 7.83 us -> 7.91 us
where the time goes in v8:
time: 280 us; the launch traced here: 279 us
  starting transfers between devices  106 us (38%)
  waiting for transfers between devices  68.8 us (25%)
  blocking collectives  54.1 us (19%)
  Pallas kernels  34.4 us (12%)
  local copies, waits for them, and re-layouts  11.9 us (4%)
  other arithmetic  3.59 us (1%)
    all_to_all x2, blocking collectives, exchange(): return lax.all_to_all(value, axis, 0, 0, tiled=True)  54.1 us
    ppermute x20, starting transfers between devices, passed(): lax.ppermute(value, axis, turn(count, step))  46.8 us
    ppermute x20, waiting for transfers between devices, passed(): lax.ppermute(value, axis, turn(count, step))  31.5 us
    all_to_all x4, waiting for transfers between devices, exchange(): return lax.all_to_all(value, axis, 0, 0, tiled=True)  24.5 us
    all_to_all x4, starting transfers between devices, exchange(): return lax.all_to_all(value, axis, 0, 0, tiled=True)  21.4 us
    ppermute x4, starting transfers between devices, body(): other_upper = [lax.ppermute(part, 'c', turn(2, 1)) for part in upper]  10.2 us
    ppermute x1, starting transfers between devices, body(): lax.ppermute(table, REQ + TP, [(i * N_TP + j, j * N_TP + i) for i in rang...  9.69 us
    pallas_call x1, Pallas kernels, attend(): pl.pallas_call(attend_kernel, out_shape=(jax.ShapeDtypeStruct((N_TP, 144,...  8.91 us
  transfers between devices with their start and end apart: 39, of which 14 were waited for; matrix products, arithmetic and copies ran while one was open for 3% of the time, Pallas kernels for 2%

profile of v8, /device:TPU:1, one launch (start us, length us, event | category | flops | bytes accessed | tf_op | source)
XLA Modules:
  0.0 279.4 jit_solution(13674351691442231754)
XLA Ops:
  0.7 8.9 %attend.1 = (bf16[16,144,256]{2,1,0:T(8,128)(2,1)}, bf16[256,128]{1,0:T(8,128)(2,1)}) custom-call(s32[1]{0:T(128)} %bitcast.rank_ref, s32[4]{0:T(128)} %len_ref.3, s32[4,32]{1,0:T(4,128)} %par_ref.1, bf16[4,32,4096]{2,1,0:T(8,128)(2,1)} %q_ref.1, bf16[4,256,512]{2,1,0:T(8,128)(2,1)} %ck_ref.1, bf16[4,256,512]{2,1,0:T(8,128)(2,1)} %cv_ref.1, ...), custom_call_target="tpu_custom_call" | custom-call | flops 536870912 | bytes 4194304 | tf_op jit(solution)/shard_map/attend/pallas_call | solution.py:311
  9.6 9.0 %all-to-all-start = ((bf16[16,144,256]{2,1,0:T(8,128)(2,1)}), bf16[16,144,256]{2,1,0:T(8,128)(2,1)S(1)}, u32[]{:S(2)}, u32[]{:S(2)}) async-start(bf16[16,144,256]{2,1,0:T(8,128)(2,1)} %get-tuple-element.27), calls=%async_computation | async-start | bytes 2359296 | tf_op jit(solution)/shard_map/all_to_all | solution.py:36
  18.6 24.4 %all-to-all-done.parcel_ref = bf16[16,144,256]{2,1,0:T(8,128)(2,1)S(1)} async-done(((bf16[16,144,256]{2,1,0:T(8,128)(2,1)}), bf16[16,144,256]{2,1,0:T(8,128)(2,1)S(1)}, u32[]{:S(2)}, u32[]{:S(2)}) %all-to-all-start) | async-done | bytes 1179680 | tf_op jit(solution)/shard_map/all_to_all | solution.py:36
  43.1 1.0 copy-done.13
  44.1 6.0 %project.1 = bf16[4,4,128,512]{3,2,1,0:T(8,128)(2,1)} custom-call(bf16[16,144,256]{2,1,0:T(8,128)(2,1)} %copy-done.13, bf16[256,8192]{1,0:T(8,128)(2,1)} %weight_ref.2), custom_call_target="tpu_custom_call" | custom-call | flops 536870912 | bytes 7340032 | tf_op jit(solution)/shard_map/project/pallas_call | solution.py:339
  50.1 29.0 %all_to_all.36.along_ref = bf16[4,4,128,512]{3,2,1,0:T(8,128)(2,1)} all-to-all(bf16[4,4,128,512]{3,2,1,0:T(8,128)(2,1)} %project.1), channel_id=1, replica_groups=mesh['zh'=2,'y'=4,'c'=2,'zl'=4,'x'=4] {'x'}, dimensions={0} | all-to-all | bytes 4194304 | tf_op jit(solution)/shard_map/all_to_all | solution.py:36
  79.1 2.6 fold.1
  81.6 3.7 %collective-permute-start = (bf16[128,512]{1,0:T(8,128)(2,1)}, bf16[128,512]{1,0:T(8,128)(2,1)S(1)}, u32[]{:S(2)}, u32[]{:S(2)}) collective-permute-start(bf16[128,512]{1,0:T(8,128)(2,1)} %get-tuple-element.30), channel_id=1, source_target_pairs={{0,4},{4,8},{8,12},{12,0},{1,5},{5,9},{9,13},{13,1},{2,6},{6,10},{... | collective-permute-start | bytes 393224 | tf_op jit(solution)/shard_map/ppermute | solution.py:515
  85.3 2.5 collective-permute-start.1
  87.8 2.4 collective-permute-start.2
  90.2 3.6 %collective-permute-done.1.two_ref = bf16[128,512]{1,0:T(8,128)(2,1)S(1)} collective-permute-done((bf16[128,512]{1,0:T(8,128)(2,1)}, bf16[128,512]{1,0:T(8,128)(2,1)S(1)}, u32[]{:S(2)}, u32[]{:S(2)}) %collective-permute-start.1) | collective-permute-done | bytes 131104 | tf_op jit(solution)/shard_map/ppermute | solution.py:515
  94.5 2.2 settle.1
  96.7 3.5 %all-to-all-start.2 = ((bf16[4,128,512]{2,1,0:T(8,128)(2,1)}), bf16[4,128,512]{2,1,0:T(8,128)(2,1)S(1)}, u32[]{:S(2)}, u32[]{:S(2)}) async-start(bf16[4,128,512]{2,1,0:T(8,128)(2,1)} %get-tuple-element.33), calls=%async_computation.2 | async-start | bytes 1048576 | tf_op jit(solution)/shard_map/all_to_all | solution.py:36
  100.2 4.3 %collective-permute-start.6 = (bf16[256,512]{1,0:T(8,128)(2,1)S(1)}, bf16[256,512]{1,0:T(8,128)(2,1)S(1)}, u32[]{:S(2)}, u32[]{:S(2)}) collective-permute-start(bf16[256,512]{1,0:T(8,128)(2,1)S(1)} %get-tuple-element.37), channel_id=1, source_target_pairs={{0,128},{128,0},{1,129},{129,1},{2,130},{130,2},{3,131},{131,3},{4... | collective-permute-start | bytes 786440 | tf_op jit(solution)/shard_map/ppermute | solution.py:44
  104.5 4.7 %collective-permute-start.3 = (bf16[128,512]{1,0:T(8,128)(2,1)}, bf16[128,512]{1,0:T(8,128)(2,1)S(1)}, u32[]{:S(2)}, u32[]{:S(2)}) collective-permute-start(bf16[128,512]{1,0:T(8,128)(2,1)} %get-tuple-element.34), channel_id=1, source_target_pairs={{0,4},{4,8},{8,12},{12,0},{1,5},{5,9},{9,13},{13,1},{2,6},{6,10},{... | collective-permute-start | bytes 393224 | tf_op jit(solution)/shard_map/ppermute | solution.py:44
  109.2 2.7 collective-permute-start.4
  111.9 1.2 collective-permute-start.14
  113.1 10.2 %collective-permute-done.3 = bf16[128,512]{1,0:T(8,128)(2,1)S(1)} collective-permute-done((bf16[128,512]{1,0:T(8,128)(2,1)}, bf16[128,512]{1,0:T(8,128)(2,1)S(1)}, u32[]{:S(2)}, u32[]{:S(2)}) %collective-permute-start.3) | collective-permute-done | bytes 131104 | tf_op jit(solution)/shard_map/ppermute | solution.py:44
  123.3 14.9 %collective-permute-done.4 = bf16[128,512]{1,0:T(8,128)(2,1)S(1)} collective-permute-done((bf16[128,512]{1,0:T(8,128)(2,1)}, bf16[128,512]{1,0:T(8,128)(2,1)S(1)}, u32[]{:S(2)}, u32[]{:S(2)}) %collective-permute-start.4) | collective-permute-done | bytes 131104 | tf_op jit(solution)/shard_map/ppermute | solution.py:44
  138.2 1.3 broadcast_in_dim.4
  139.6 4.3 %all-to-all-start.3 = ((bf16[12,128,512]{2,1,0:T(8,128)(2,1)}), bf16[12,128,512]{2,1,0:T(8,128)(2,1)S(1)}, u32[]{:S(2)}, u32[]{:S(2)}) async-start(bf16[12,128,512]{2,1,0:T(8,128)(2,1)} %bitcast.36), calls=%async_computation.3 | async-start | bytes 3145728 | tf_op jit(solution)/shard_map/all_to_all | solution.py:36
  143.8 0.7 copy-done.20
  144.5 1.0 pad_maximum_fusion.refs_0_
  145.5 1.4 collective-permute-start.7
  146.9 2.7 collective-permute-start.8
  149.6 1.1 collective-permute-start.9
  150.6 0.7 copy-done.19
  151.3 1.0 pad_maximum_fusion.1.refs_8_
  152.8 9.7 %collective-permute-start.22 = (bf16[128,512]{1,0:T(8,128)(2,1)S(1)}, bf16[128,512]{1,0:T(8,128)(2,1)S(1)}, u32[]{:S(2)}, u32[]{:S(2)}) collective-permute-start(bf16[128,512]{1,0:T(8,128)(2,1)S(1)} %copy-done.24), channel_id=1, source_target_pairs={{0,0},{1,16},{2,32},{3,48},{4,64},{5,80},{6,96},{7,112},{8,128},{9... | collective-permute-start | bytes 393224 | tf_op jit(solution)/shard_map/ppermute | solution.py:523
  162.5 2.9 %collective-permute-done.22 = bf16[128,512]{1,0:T(8,128)(2,1)S(1)} collective-permute-done((bf16[128,512]{1,0:T(8,128)(2,1)S(1)}, bf16[128,512]{1,0:T(8,128)(2,1)S(1)}, u32[]{:S(2)}, u32[]{:S(2)}) %collective-permute-start.22) | collective-permute-done | bytes 131104 | tf_op jit(solution)/shard_map/ppermute | solution.py:523
  165.4 6.0 %collective-permute-start.23 = (bf16[128,512]{1,0:T(8,128)(2,1)S(1)}, bf16[128,512]{1,0:T(8,128)(2,1)S(1)}, u32[]{:S(2)}, u32[]{:S(2)}) collective-permute-start(bf16[128,512]{1,0:T(8,128)(2,1)S(1)} %collective-permute-done.22), channel_id=1, source_target_pairs={{0,4},{4,8},{8,12},{12,0},{1,5},{5,9},{9,13},{13,1},{2,6},{6,10},{... | collective-permute-start | bytes 393224 | tf_op jit(solution)/shard_map/ppermute | solution.py:44
  171.4 2.1 collective-permute-start.24
  173.5 8.4 %collective-permute-start.25 = (bf16[128,512]{1,0:T(8,128)(2,1)S(1)}, bf16[128,512]{1,0:T(8,128)(2,1)S(1)}, u32[]{:S(2)}, u32[]{:S(2)}) collective-permute-start(bf16[128,512]{1,0:T(8,128)(2,1)S(1)} %collective-permute-done.22), channel_id=1, source_target_pairs={{0,12},{4,0},{8,4},{12,8},{1,13},{5,1},{9,5},{13,9},{2,14},{6,2},{... | collective-permute-start | bytes 393224 | tf_op jit(solution)/shard_map/ppermute | solution.py:44
  182.0 0.8 collective-permute-start.17
  182.8 8.8 %collective-permute-start.10 = (bf16[2,256,512]{2,1,0:T(8,128)(2,1)S(1)}, bf16[2,256,512]{2,1,0:T(8,128)(2,1)}, u32[]{:S(2)}, u32[]{:S(2)}) collective-permute-start(bf16[2,256,512]{2,1,0:T(8,128)(2,1)S(1)} %pad_maximum_fusion.refs_0_), channel_id=1, source_target_pairs={{0,16},{16,0},{1,17},{17,1},{2,18},{18,2},{3,19},{19,3},{4,20},{20... | collective-permute-start | bytes 1572872 | tf_op jit(solution)/shard_map/ppermute | solution.py:511
  191.5 0.7 collective-permute-start.18
  192.3 0.9 pad_maximum_fusion.2
  193.2 2.6 broadcast_in_dim.5
  195.8 4.6 %all-to-all-start.4 = ((bf16[16,128,512]{2,1,0:T(8,128)(2,1)}), bf16[16,128,512]{2,1,0:T(8,128)(2,1)}, u32[]{:S(2)}, u32[]{:S(2)}) async-start(bf16[16,128,512]{2,1,0:T(8,128)(2,1)} %bitcast.35), calls=%async_computation.4 | async-start | bytes 4194304 | tf_op jit(solution)/shard_map/all_to_all | solution.py:36
  201.0 5.7 %collective-permute-done.17.refs_11_ = bf16[2,256,512]{2,1,0:T(8,128)(2,1)} collective-permute-done((bf16[2,256,512]{2,1,0:T(8,128)(2,1)S(1)}, bf16[2,256,512]{2,1,0:T(8,128)(2,1)}, u32[]{:S(2)}, u32[]{:S(2)}) %collective-permute-start.17) | collective-permute-done | bytes 524320 | tf_op jit(solution)/shard_map/ppermute | solution.py:44
  206.7 0.8 collective-permute-start.13
  208.6 0.7 collective-permute-done.13.refs_7_
  209.4 0.7 collective-permute-done.19.refs_13_
  210.1 0.7 collective-permute-done.20.refs_14_
  210.9 0.7 collective-permute-done.21.refs_15_
  211.7 1.0 copy-done.1
  212.7 1.0 copy-done.3
  213.7 1.0 copy-done.5
  214.8 0.8 copy-done.9
  215.6 5.5 %predict.1 = (bf16[128,512]{1,0:T(8,128)(2,1)}, bf16[128,512]{1,0:T(8,128)(2,1)S(1)}, f32[8,128]{1,0:T(8,128)S(1)}) custom-call(s32[16]{0:T(128)S(1)} %get-tuple-element.50.source_ref, s32[1]{0:T(128)} %bitcast.rank_ref, s32[4]{0:T(128)S(1)} %copy-done.11, s32[4]{0:T(128)S(1)} %copy-done.12, bf16[4,128,512]{2,1,0:T(8,128)(2,1)S(1)} %all-to-all-done.2.far_own_ref, ...), custom_call_target="tpu_custom_call" | custom-call | flops 1073741824 | bytes 13631488 | tf_op jit(solution)/shard_map/predict/pallas_call | solution.py:402
  221.2 2.7 collective-permute-start.26
  223.9 3.1 %collective-permute-start.27 = (bf16[128,512]{1,0:T(8,128)(2,1)S(1)}, bf16[128,512]{1,0:T(8,128)(2,1)S(1)}, u32[]{:S(2)}, u32[]{:S(2)}) collective-permute-start(bf16[128,512]{1,0:T(8,128)(2,1)S(1)} %get-tuple-element.41), channel_id=1, source_target_pairs={{0,64},{32,96},{64,0},{96,32},{1,65},{33,97},{65,1},{97,33},{2,66}... | collective-permute-start | bytes 393224 | tf_op jit(solution)/shard_map/ppermute | solution.py:44
  227.0 1.0 collective-permute-start.28
  228.0 1.8 collective-permute-done.29
  229.8 3.3 %collective-permute-start.31 = (bf16[128,512]{1,0:T(8,128)(2,1)S(1)}, bf16[128,512]{1,0:T(8,128)(2,1)S(1)}, u32[]{:S(2)}, u32[]{:S(2)}) collective-permute-start(bf16[128,512]{1,0:T(8,128)(2,1)S(1)} %collective-permute-done.29), channel_id=1, source_target_pairs={{0,64},{32,96},{64,0},{96,32},{1,65},{33,97},{65,1},{97,33},{2,66}... | collective-permute-start | bytes 393224 | tf_op jit(solution)/shard_map/ppermute | solution.py:44
  233.1 0.9 collective-permute-start.32
  234.1 3.2 %collective-permute-start.33 = (bf16[4,128,512]{2,1,0:T(8,128)(2,1)S(1)}, bf16[4,128,512]{2,1,0:T(8,128)(2,1)S(1)}, u32[]{:S(2)}, u32[]{:S(2)}) collective-permute-start(bf16[4,128,512]{2,1,0:T(8,128)(2,1)S(1)} %pad_maximum_fusion.3.e0_ref), channel_id=1, source_target_pairs={{0,16},{16,0},{1,17},{17,1},{2,18},{18,2},{3,19},{19,3},{4,20},{20... | collective-permute-start | bytes 1572872 | tf_op jit(solution)/shard_map/ppermute | solution.py:548
  237.3 0.7 collective-permute-done.31
  238.0 4.5 %collective-permute-start.34 = (bf16[4,128,512]{2,1,0:T(8,128)(2,1)S(1)}, bf16[4,128,512]{2,1,0:T(8,128)(2,1)S(1)}, u32[]{:S(2)}, u32[]{:S(2)}) collective-permute-start(bf16[4,128,512]{2,1,0:T(8,128)(2,1)S(1)} %pad_maximum_fusion.4.e1_ref), channel_id=1, source_target_pairs={{0,16},{16,0},{1,17},{17,1},{2,18},{18,2},{3,19},{19,3},{4,20},{20... | collective-permute-start | bytes 1572872 | tf_op jit(solution)/shard_map/ppermute | solution.py:548
  242.5 1.5 collective-permute-done.34.e3_ref
  244.1 0.8 copy-done.18
  244.8 4.5 %differentiate.1 = (f32[512,512]{1,0:T(8,128)}, f32[256,128]{1,0:T(8,128)}) custom-call(s32[16]{0:T(128)} %get-tuple-element.49.place_ref, bf16[16,128,512]{2,1,0:T(8,128)(2,1)} %all-to-all-done.4.column_ref, bf16[4,128,512]{2,1,0:T(8,128)(2,1)} %copy-done.14, bf16[4,128,512]{2,1,0:T(8,128)(2,1)} %copy-done.15, bf16[4,128,512]{2,1,0:T(8,128)(2,1)} %copy-done.17, ...), custom_call_target="tpu_custom_call" | custom-call | flops 1073741824 | bytes 5242880 | tf_op jit(solution)/shard_map/differentiate/pallas_call | solution.py:431
  249.3 25.2 %all_to_all.37 = f32[256,1,128]{2,1,0:T(1,128)} all-to-all(f32[256,1,128]{2,1,0:T(1,128)} %bitcast.43), channel_id=1, replica_groups=mesh['zh'=2,'y'=4,'c'=2,'zl'=4,'x'=4] {'zh','y','c','zl','x'}, dimensions={0} | all-to-all | bytes 262144 | tf_op jit(solution)/shard_map/all_to_all | solution.py:36
  274.5 4.8 %update.1 = (bf16[512,512]{1,0:T(8,128)(2,1)}, f32[512,512]{1,0:T(8,128)}, f32[512,512]{1,0:T(8,128)}, f32[1,1]{1,0:T(1,128)}) custom-call(f32[256,128]{1,0:T(8,128)} %bitcast.39, f32[512,512]{1,0:T(8,128)} %get-tuple-element.44.grad_ref, bf16[512,512]{1,0:T(8,128)(2,1)} %weight_ref.3, f32[512,512]{1,0:T(8,128)} %first_ref.1, f32[512,512]{1,0:T(8,128)} %second_ref.1), custom_call_target="tpu_custom_call" | custom-call | flops 5242880 | bytes 6291456 | tf_op jit(solution)/shard_map/update/pallas_call | solution.py:448
  (83 shorter events, 3.4 us)
Async XLA Ops:
  0.6 17.9 %copy-start.16 = (bf16[512,512]{1,0:T(8,128)(2,1)S(1)}, bf16[512,512]{1,0:T(8,128)(2,1)}, u32[]{:S(2)}) copy-start(bf16[512,512]{1,0:T(8,128)(2,1)} %weight_ref.3) | copy-start | bytes 1572868
  9.6 33.5 %all-to-all-start = ((bf16[16,144,256]{2,1,0:T(8,128)(2,1)}), bf16[16,144,256]{2,1,0:T(8,128)(2,1)S(1)}, u32[]{:S(2)}, u32[]{:S(2)}) async-start(bf16[16,144,256]{2,1,0:T(8,128)(2,1)} %get-tuple-element.27), calls=%async_computation | async-start | bytes 2359296 | tf_op jit(solution)/shard_map/all_to_all | solution.py:36
  43.1 1.0 copy-start.13
  81.6 8.6 %collective-permute-start = (bf16[128,512]{1,0:T(8,128)(2,1)}, bf16[128,512]{1,0:T(8,128)(2,1)S(1)}, u32[]{:S(2)}, u32[]{:S(2)}) collective-permute-start(bf16[128,512]{1,0:T(8,128)(2,1)} %get-tuple-element.30), channel_id=1, source_target_pairs={{0,4},{4,8},{8,12},{12,0},{1,5},{5,9},{9,13},{13,1},{2,6},{6,10},{... | collective-permute-start | bytes 393224 | tf_op jit(solution)/shard_map/ppermute | solution.py:515
  85.3 8.5 %collective-permute-start.1 = (bf16[128,512]{1,0:T(8,128)(2,1)}, bf16[128,512]{1,0:T(8,128)(2,1)S(1)}, u32[]{:S(2)}, u32[]{:S(2)}) collective-permute-start(bf16[128,512]{1,0:T(8,128)(2,1)} %get-tuple-element.31), channel_id=1, source_target_pairs={{0,8},{4,12},{8,0},{12,4},{1,9},{5,13},{9,1},{13,5},{2,10},{6,14},... | collective-permute-start | bytes 393224 | tf_op jit(solution)/shard_map/ppermute | solution.py:515
  87.8 6.0 %collective-permute-start.2 = (bf16[128,512]{1,0:T(8,128)(2,1)}, bf16[128,512]{1,0:T(8,128)(2,1)S(1)}, u32[]{:S(2)}, u32[]{:S(2)}) collective-permute-start(bf16[128,512]{1,0:T(8,128)(2,1)} %get-tuple-element.32), channel_id=1, source_target_pairs={{0,12},{4,0},{8,4},{12,8},{1,13},{5,1},{9,5},{13,9},{2,14},{6,2},{... | collective-permute-start | bytes 393224 | tf_op jit(solution)/shard_map/ppermute | solution.py:515
  90.2 3.7 %copy-start.21 = (bf16[128,512]{1,0:T(8,128)(2,1)}, bf16[128,512]{1,0:T(8,128)(2,1)S(1)}, u32[]{:S(2)}) copy-start(bf16[128,512]{1,0:T(8,128)(2,1)S(1)} %collective-permute-done.one_ref) | copy-start | bytes 393220
  93.8 0.7 copy-start.22
  93.9 0.7 copy-start.23
  96.7 41.5 %all-to-all-start.2 = ((bf16[4,128,512]{2,1,0:T(8,128)(2,1)}), bf16[4,128,512]{2,1,0:T(8,128)(2,1)S(1)}, u32[]{:S(2)}, u32[]{:S(2)}) async-start(bf16[4,128,512]{2,1,0:T(8,128)(2,1)} %get-tuple-element.33), calls=%async_computation.2 | async-start | bytes 1048576 | tf_op jit(solution)/shard_map/all_to_all | solution.py:36
  100.2 43.6 %collective-permute-start.6 = (bf16[256,512]{1,0:T(8,128)(2,1)S(1)}, bf16[256,512]{1,0:T(8,128)(2,1)S(1)}, u32[]{:S(2)}, u32[]{:S(2)}) collective-permute-start(bf16[256,512]{1,0:T(8,128)(2,1)S(1)} %get-tuple-element.37), channel_id=1, source_target_pairs={{0,128},{128,0},{1,129},{129,1},{2,130},{130,2},{3,131},{131,3},{4... | collective-permute-start | bytes 786440 | tf_op jit(solution)/shard_map/ppermute | solution.py:44
  104.5 18.8 %collective-permute-start.3 = (bf16[128,512]{1,0:T(8,128)(2,1)}, bf16[128,512]{1,0:T(8,128)(2,1)S(1)}, u32[]{:S(2)}, u32[]{:S(2)}) collective-permute-start(bf16[128,512]{1,0:T(8,128)(2,1)} %get-tuple-element.34), channel_id=1, source_target_pairs={{0,4},{4,8},{8,12},{12,0},{1,5},{5,9},{9,13},{13,1},{2,6},{6,10},{... | collective-permute-start | bytes 393224 | tf_op jit(solution)/shard_map/ppermute | solution.py:44
  109.2 29.0 %collective-permute-start.4 = (bf16[128,512]{1,0:T(8,128)(2,1)}, bf16[128,512]{1,0:T(8,128)(2,1)S(1)}, u32[]{:S(2)}, u32[]{:S(2)}) collective-permute-start(bf16[128,512]{1,0:T(8,128)(2,1)} %get-tuple-element.34), channel_id=1, source_target_pairs={{0,8},{4,12},{8,0},{12,4},{1,9},{5,13},{9,1},{13,5},{2,10},{6,14},... | collective-permute-start | bytes 393224 | tf_op jit(solution)/shard_map/ppermute | solution.py:44
  111.9 26.3 %collective-permute-start.5 = (bf16[128,512]{1,0:T(8,128)(2,1)}, bf16[128,512]{1,0:T(8,128)(2,1)S(1)}, u32[]{:S(2)}, u32[]{:S(2)}) collective-permute-start(bf16[128,512]{1,0:T(8,128)(2,1)} %get-tuple-element.34), channel_id=1, source_target_pairs={{0,12},{4,0},{8,4},{12,8},{1,13},{5,1},{9,5},{13,9},{2,14},{6,2},{... | collective-permute-start | bytes 393224 | tf_op jit(solution)/shard_map/ppermute | solution.py:44
  111.9 38.7 %collective-permute-start.14 = (bf16[256,512]{1,0:T(8,128)(2,1)S(1)}, bf16[256,512]{1,0:T(8,128)(2,1)S(1)}, u32[]{:S(2)}, u32[]{:S(2)}) collective-permute-start(bf16[256,512]{1,0:T(8,128)(2,1)S(1)} %get-tuple-element.38), channel_id=1, source_target_pairs={{0,128},{128,0},{1,129},{129,1},{2,130},{130,2},{3,131},{131,3},{4... | collective-permute-start | bytes 786440 | tf_op jit(solution)/shard_map/ppermute | solution.py:44
  139.6 13.3 %copy-start.24 = (bf16[128,512]{1,0:T(8,128)(2,1)S(1)}, bf16[128,512]{1,0:T(8,128)(2,1)}, u32[]{:S(2)}) copy-start(bf16[128,512]{1,0:T(8,128)(2,1)} %get-tuple-element.40) | copy-start | bytes 393220
  139.6 53.6 %all-to-all-start.3 = ((bf16[12,128,512]{2,1,0:T(8,128)(2,1)}), bf16[12,128,512]{2,1,0:T(8,128)(2,1)S(1)}, u32[]{:S(2)}, u32[]{:S(2)}) async-start(bf16[12,128,512]{2,1,0:T(8,128)(2,1)} %bitcast.36), calls=%async_computation.3 | async-start | bytes 3145728 | tf_op jit(solution)/shard_map/all_to_all | solution.py:36
  143.8 0.7 copy-start.20
  145.5 25.9 %collective-permute-start.7 = (bf16[2,256,512]{2,1,0:T(8,128)(2,1)S(1)}, bf16[2,256,512]{2,1,0:T(8,128)(2,1)}, u32[]{:S(2)}, u32[]{:S(2)}) collective-permute-start(bf16[2,256,512]{2,1,0:T(8,128)(2,1)S(1)} %pad_maximum_fusion.refs_0_), channel_id=1, source_target_pairs={{0,32},{32,64},{64,96},{96,0},{1,33},{33,65},{65,97},{97,1},{2,34}... | collective-permute-start | bytes 1572872 | tf_op jit(solution)/shard_map/ppermute | solution.py:44
  146.9 26.6 %collective-permute-start.8 = (bf16[2,256,512]{2,1,0:T(8,128)(2,1)S(1)}, bf16[2,256,512]{2,1,0:T(8,128)(2,1)S(1)}, u32[]{:S(2)}, u32[]{:S(2)}) collective-permute-start(bf16[2,256,512]{2,1,0:T(8,128)(2,1)S(1)} %pad_maximum_fusion.refs_0_), channel_id=1, source_target_pairs={{0,64},{32,96},{64,0},{96,32},{1,65},{33,97},{65,1},{97,33},{2,66}... | collective-permute-start | bytes 1572872 | tf_op jit(solution)/shard_map/ppermute | solution.py:44
  149.6 32.4 %collective-permute-start.9 = (bf16[2,256,512]{2,1,0:T(8,128)(2,1)S(1)}, bf16[2,256,512]{2,1,0:T(8,128)(2,1)S(1)}, u32[]{:S(2)}, u32[]{:S(2)}) collective-permute-start(bf16[2,256,512]{2,1,0:T(8,128)(2,1)S(1)} %pad_maximum_fusion.refs_0_), channel_id=1, source_target_pairs={{0,96},{32,0},{64,32},{96,64},{1,97},{33,1},{65,33},{97,65},{2,98}... | collective-permute-start | bytes 1572872 | tf_op jit(solution)/shard_map/ppermute | solution.py:44
  150.6 0.7 copy-start.19
  152.3 29.6 %collective-permute-start.15 = (bf16[2,256,512]{2,1,0:T(8,128)(2,1)S(1)}, bf16[2,256,512]{2,1,0:T(8,128)(2,1)S(1)}, u32[]{:S(2)}, u32[]{:S(2)}) collective-permute-start(bf16[2,256,512]{2,1,0:T(8,128)(2,1)S(1)} %pad_maximum_fusion.1.refs_8_), channel_id=1, source_target_pairs={{0,32},{32,64},{64,96},{96,0},{1,33},{33,65},{65,97},{97,1},{2,34}... | collective-permute-start | bytes 1572872 | tf_op jit(solution)/shard_map/ppermute | solution.py:44
  152.8 12.6 %collective-permute-start.22 = (bf16[128,512]{1,0:T(8,128)(2,1)S(1)}, bf16[128,512]{1,0:T(8,128)(2,1)S(1)}, u32[]{:S(2)}, u32[]{:S(2)}) collective-permute-start(bf16[128,512]{1,0:T(8,128)(2,1)S(1)} %copy-done.24), channel_id=1, source_target_pairs={{0,0},{1,16},{2,32},{3,48},{4,64},{5,80},{6,96},{7,112},{8,128},{9... | collective-permute-start | bytes 393224 | tf_op jit(solution)/shard_map/ppermute | solution.py:523
  165.4 17.4 %collective-permute-start.23 = (bf16[128,512]{1,0:T(8,128)(2,1)S(1)}, bf16[128,512]{1,0:T(8,128)(2,1)S(1)}, u32[]{:S(2)}, u32[]{:S(2)}) collective-permute-start(bf16[128,512]{1,0:T(8,128)(2,1)S(1)} %collective-permute-done.22), channel_id=1, source_target_pairs={{0,4},{4,8},{8,12},{12,0},{1,5},{5,9},{9,13},{13,1},{2,6},{6,10},{... | collective-permute-start | bytes 393224 | tf_op jit(solution)/shard_map/ppermute | solution.py:44
  171.4 20.1 %collective-permute-start.24 = (bf16[128,512]{1,0:T(8,128)(2,1)S(1)}, bf16[128,512]{1,0:T(8,128)(2,1)S(1)}, u32[]{:S(2)}, u32[]{:S(2)}) collective-permute-start(bf16[128,512]{1,0:T(8,128)(2,1)S(1)} %collective-permute-done.22), channel_id=1, source_target_pairs={{0,8},{4,12},{8,0},{12,4},{1,9},{5,13},{9,1},{13,5},{2,10},{6,14},... | collective-permute-start | bytes 393224 | tf_op jit(solution)/shard_map/ppermute | solution.py:44
  173.5 18.8 %copy-start = (bf16[2,256,512]{2,1,0:T(8,128)(2,1)}, bf16[2,256,512]{2,1,0:T(8,128)(2,1)S(1)}, u32[]{:S(2)}) copy-start(bf16[2,256,512]{2,1,0:T(8,128)(2,1)S(1)} %collective-permute-done.8.refs_2_) | copy-start | bytes 1572868
  173.5 18.7 %collective-permute-start.25 = (bf16[128,512]{1,0:T(8,128)(2,1)S(1)}, bf16[128,512]{1,0:T(8,128)(2,1)S(1)}, u32[]{:S(2)}, u32[]{:S(2)}) collective-permute-start(bf16[128,512]{1,0:T(8,128)(2,1)S(1)} %collective-permute-done.22), channel_id=1, source_target_pairs={{0,12},{4,0},{8,4},{12,8},{1,13},{5,1},{9,5},{13,9},{2,14},{6,2},{... | collective-permute-start | bytes 393224 | tf_op jit(solution)/shard_map/ppermute | solution.py:44
  181.9 10.4 %copy-start.2 = (bf16[2,256,512]{2,1,0:T(8,128)(2,1)}, bf16[2,256,512]{2,1,0:T(8,128)(2,1)S(1)}, u32[]{:S(2)}) copy-start(bf16[2,256,512]{2,1,0:T(8,128)(2,1)S(1)} %collective-permute-done.9.refs_3_) | copy-start | bytes 1572868
  181.9 18.5 %collective-permute-start.16 = (bf16[2,256,512]{2,1,0:T(8,128)(2,1)S(1)}, bf16[2,256,512]{2,1,0:T(8,128)(2,1)}, u32[]{:S(2)}, u32[]{:S(2)}) collective-permute-start(bf16[2,256,512]{2,1,0:T(8,128)(2,1)S(1)} %pad_maximum_fusion.1.refs_8_), channel_id=1, source_target_pairs={{0,64},{32,96},{64,0},{96,32},{1,65},{33,97},{65,1},{97,33},{2,66}... | collective-permute-start | bytes 1572872 | tf_op jit(solution)/shard_map/ppermute | solution.py:44
  181.9 9.6 %copy-start.4 = (bf16[2,256,512]{2,1,0:T(8,128)(2,1)}, bf16[2,256,512]{2,1,0:T(8,128)(2,1)S(1)}, u32[]{:S(2)}) copy-start(bf16[2,256,512]{2,1,0:T(8,128)(2,1)S(1)} %collective-permute-done.15.refs_9_) | copy-start | bytes 1572868
  182.0 24.7 %collective-permute-start.17 = (bf16[2,256,512]{2,1,0:T(8,128)(2,1)S(1)}, bf16[2,256,512]{2,1,0:T(8,128)(2,1)}, u32[]{:S(2)}, u32[]{:S(2)}) collective-permute-start(bf16[2,256,512]{2,1,0:T(8,128)(2,1)S(1)} %pad_maximum_fusion.1.refs_8_), channel_id=1, source_target_pairs={{0,96},{32,0},{64,32},{96,64},{1,97},{33,1},{65,33},{97,65},{2,98}... | collective-permute-start | bytes 1572872 | tf_op jit(solution)/shard_map/ppermute | solution.py:44
  182.8 24.7 %collective-permute-start.10 = (bf16[2,256,512]{2,1,0:T(8,128)(2,1)S(1)}, bf16[2,256,512]{2,1,0:T(8,128)(2,1)}, u32[]{:S(2)}, u32[]{:S(2)}) collective-permute-start(bf16[2,256,512]{2,1,0:T(8,128)(2,1)S(1)} %pad_maximum_fusion.refs_0_), channel_id=1, source_target_pairs={{0,16},{16,0},{1,17},{17,1},{2,18},{18,2},{3,19},{19,3},{4,20},{20... | collective-permute-start | bytes 1572872 | tf_op jit(solution)/shard_map/ppermute | solution.py:511
  191.5 16.0 %collective-permute-start.18 = (bf16[2,256,512]{2,1,0:T(8,128)(2,1)S(1)}, bf16[2,256,512]{2,1,0:T(8,128)(2,1)}, u32[]{:S(2)}, u32[]{:S(2)}) collective-permute-start(bf16[2,256,512]{2,1,0:T(8,128)(2,1)S(1)} %pad_maximum_fusion.1.refs_8_), channel_id=1, source_target_pairs={{0,16},{16,0},{1,17},{17,1},{2,18},{18,2},{3,19},{19,3},{4,20},{20... | collective-permute-start | bytes 1572872 | tf_op jit(solution)/shard_map/ppermute | solution.py:526
  192.2 15.8 %collective-permute-start.11 = (bf16[2,256,512]{2,1,0:T(8,128)(2,1)}, bf16[2,256,512]{2,1,0:T(8,128)(2,1)}, u32[]{:S(2)}, u32[]{:S(2)}) collective-permute-start(bf16[2,256,512]{2,1,0:T(8,128)(2,1)} %collective-permute-done.7.refs_1_), channel_id=1, source_target_pairs={{0,16},{16,0},{1,17},{17,1},{2,18},{18,2},{3,19},{19,3},{4,20},{20... | collective-permute-start | bytes 1572872 | tf_op jit(solution)/shard_map/ppermute | solution.py:511
  195.8 15.8 %copy-start.6 = (bf16[4,8192]{1,0:T(4,128)(2,1)S(1)}, bf16[4,8192]{1,0:T(4,128)(2,1)}, u32[]{:S(2)}) copy-start(bf16[4,8192]{1,0:T(4,128)(2,1)} %prev_ref.3) | copy-start | bytes 196612
  195.8 15.8 %copy-start.7 = (f32[128,512]{1,0:T(8,128)S(1)}, f32[128,512]{1,0:T(8,128)}, u32[]{:S(2)}) copy-start(f32[128,512]{1,0:T(8,128)} %get-tuple-element.35.mixed_ref) | copy-start | bytes 786436
  195.8 15.8 %copy-start.8 = (f32[8192]{0:T(1024)S(1)}, f32[8192]{0:T(1024)}, u32[]{:S(2)}) copy-start(f32[8192]{0:T(1024)} %param.24) | copy-start | bytes 98308
  195.8 15.8 %copy-start.11 = (s32[4]{0:T(128)S(1)}, s32[4]{0:T(128)}, u32[]{:S(2)}) copy-start(s32[4]{0:T(128)} %len_ref.3) | copy-start | bytes 52
  195.8 15.8 %copy-start.12 = (s32[4]{0:T(128)S(1)}, s32[4]{0:T(128)}, u32[]{:S(2)}) copy-start(s32[4]{0:T(128)} %leaf_ref.1) | copy-start | bytes 52
  195.8 46.7 %all-to-all-start.4 = ((bf16[16,128,512]{2,1,0:T(8,128)(2,1)}), bf16[16,128,512]{2,1,0:T(8,128)(2,1)}, u32[]{:S(2)}, u32[]{:S(2)}) async-start(bf16[16,128,512]{2,1,0:T(8,128)(2,1)} %bitcast.35), calls=%async_computation.4 | async-start | bytes 4194304 | tf_op jit(solution)/shard_map/all_to_all | solution.py:36
  200.4 8.2 %collective-permute-start.12 = (bf16[2,256,512]{2,1,0:T(8,128)(2,1)}, bf16[2,256,512]{2,1,0:T(8,128)(2,1)}, u32[]{:S(2)}, u32[]{:S(2)}) collective-permute-start(bf16[2,256,512]{2,1,0:T(8,128)(2,1)} %copy-done), channel_id=1, source_target_pairs={{0,16},{16,0},{1,17},{17,1},{2,18},{18,2},{3,19},{19,3},{4,20},{20... | collective-permute-start | bytes 1572872 | tf_op jit(solution)/shard_map/ppermute | solution.py:511
  206.7 2.7 collective-permute-start.13
  207.5 2.6 collective-permute-start.19
  207.5 3.4 %collective-permute-start.20 = (bf16[2,256,512]{2,1,0:T(8,128)(2,1)}, bf16[2,256,512]{2,1,0:T(8,128)(2,1)}, u32[]{:S(2)}, u32[]{:S(2)}) collective-permute-start(bf16[2,256,512]{2,1,0:T(8,128)(2,1)} %collective-permute-done.16.refs_10_), channel_id=1, source_target_pairs={{0,16},{16,0},{1,17},{17,1},{2,18},{18,2},{3,19},{19,3},{4,20},{20... | collective-permute-start | bytes 1572872 | tf_op jit(solution)/shard_map/ppermute | solution.py:526
  208.0 3.6 %collective-permute-start.21 = (bf16[2,256,512]{2,1,0:T(8,128)(2,1)}, bf16[2,256,512]{2,1,0:T(8,128)(2,1)}, u32[]{:S(2)}, u32[]{:S(2)}) collective-permute-start(bf16[2,256,512]{2,1,0:T(8,128)(2,1)} %collective-permute-done.17.refs_11_), channel_id=1, source_target_pairs={{0,16},{16,0},{1,17},{17,1},{2,18},{18,2},{3,19},{19,3},{4,20},{20... | collective-permute-start | bytes 1572872 | tf_op jit(solution)/shard_map/ppermute | solution.py:526
  211.6 1.0 copy-start.1
  212.7 1.0 copy-start.3
  213.7 1.0 copy-start.5
  214.8 0.8 copy-start.9
  221.1 13.0 %copy-start.10 = (f32[8,128]{1,0:T(8,128)}, f32[8,128]{1,0:T(8,128)S(1)}, u32[]{:S(2)}) copy-start(f32[8,128]{1,0:T(8,128)S(1)} %get-tuple-element.42.loss_ref) | copy-start | bytes 12292
  221.1 8.7 %collective-permute-start.29 = (bf16[128,512]{1,0:T(8,128)(2,1)S(1)}, bf16[128,512]{1,0:T(8,128)(2,1)S(1)}, u32[]{:S(2)}, u32[]{:S(2)}) collective-permute-start(bf16[128,512]{1,0:T(8,128)(2,1)S(1)} %get-tuple-element.41), channel_id=1, source_target_pairs={{0,128},{128,0},{1,129},{129,1},{2,130},{130,2},{3,131},{131,3},{4... | collective-permute-start | bytes 393224 | tf_op jit(solution)/shard_map/ppermute | solution.py:544
  221.2 11.9 %collective-permute-start.26 = (bf16[128,512]{1,0:T(8,128)(2,1)S(1)}, bf16[128,512]{1,0:T(8,128)(2,1)S(1)}, u32[]{:S(2)}, u32[]{:S(2)}) collective-permute-start(bf16[128,512]{1,0:T(8,128)(2,1)S(1)} %get-tuple-element.41), channel_id=1, source_target_pairs={{0,32},{32,64},{64,96},{96,0},{1,33},{33,65},{65,97},{97,1},{2,34}... | collective-permute-start | bytes 393224 | tf_op jit(solution)/shard_map/ppermute | solution.py:44
  223.9 10.1 %collective-permute-start.27 = (bf16[128,512]{1,0:T(8,128)(2,1)S(1)}, bf16[128,512]{1,0:T(8,128)(2,1)S(1)}, u32[]{:S(2)}, u32[]{:S(2)}) collective-permute-start(bf16[128,512]{1,0:T(8,128)(2,1)S(1)} %get-tuple-element.41), channel_id=1, source_target_pairs={{0,64},{32,96},{64,0},{96,32},{1,65},{33,97},{65,1},{97,33},{2,66}... | collective-permute-start | bytes 393224 | tf_op jit(solution)/shard_map/ppermute | solution.py:44
  227.0 7.0 %collective-permute-start.28 = (bf16[128,512]{1,0:T(8,128)(2,1)S(1)}, bf16[128,512]{1,0:T(8,128)(2,1)S(1)}, u32[]{:S(2)}, u32[]{:S(2)}) collective-permute-start(bf16[128,512]{1,0:T(8,128)(2,1)S(1)} %get-tuple-element.41), channel_id=1, source_target_pairs={{0,96},{32,0},{64,32},{96,64},{1,97},{33,1},{65,33},{97,65},{2,98}... | collective-permute-start | bytes 393224 | tf_op jit(solution)/shard_map/ppermute | solution.py:44
  229.8 7.5 %collective-permute-start.30 = (bf16[128,512]{1,0:T(8,128)(2,1)S(1)}, bf16[128,512]{1,0:T(8,128)(2,1)S(1)}, u32[]{:S(2)}, u32[]{:S(2)}) collective-permute-start(bf16[128,512]{1,0:T(8,128)(2,1)S(1)} %collective-permute-done.29), channel_id=1, source_target_pairs={{0,32},{32,64},{64,96},{96,0},{1,33},{33,65},{65,97},{97,1},{2,34}... | collective-permute-start | bytes 393224 | tf_op jit(solution)/shard_map/ppermute | solution.py:44
  229.8 8.2 %collective-permute-start.31 = (bf16[128,512]{1,0:T(8,128)(2,1)S(1)}, bf16[128,512]{1,0:T(8,128)(2,1)S(1)}, u32[]{:S(2)}, u32[]{:S(2)}) collective-permute-start(bf16[128,512]{1,0:T(8,128)(2,1)S(1)} %collective-permute-done.29), channel_id=1, source_target_pairs={{0,64},{32,96},{64,0},{96,32},{1,65},{33,97},{65,1},{97,33},{2,66}... | collective-permute-start | bytes 393224 | tf_op jit(solution)/shard_map/ppermute | solution.py:44
  233.1 4.9 %collective-permute-start.32 = (bf16[128,512]{1,0:T(8,128)(2,1)S(1)}, bf16[128,512]{1,0:T(8,128)(2,1)S(1)}, u32[]{:S(2)}, u32[]{:S(2)}) collective-permute-start(bf16[128,512]{1,0:T(8,128)(2,1)S(1)} %collective-permute-done.29), channel_id=1, source_target_pairs={{0,96},{32,0},{64,32},{96,64},{1,97},{33,1},{65,33},{97,65},{2,98}... | collective-permute-start | bytes 393224 | tf_op jit(solution)/shard_map/ppermute | solution.py:44
  234.1 10.0 %copy-start.14 = (bf16[4,128,512]{2,1,0:T(8,128)(2,1)}, bf16[4,128,512]{2,1,0:T(8,128)(2,1)S(1)}, u32[]{:S(2)}) copy-start(bf16[4,128,512]{2,1,0:T(8,128)(2,1)S(1)} %pad_maximum_fusion.3.e0_ref) | copy-start | bytes 1572868
  234.1 8.5 %collective-permute-start.33 = (bf16[4,128,512]{2,1,0:T(8,128)(2,1)S(1)}, bf16[4,128,512]{2,1,0:T(8,128)(2,1)S(1)}, u32[]{:S(2)}, u32[]{:S(2)}) collective-permute-start(bf16[4,128,512]{2,1,0:T(8,128)(2,1)S(1)} %pad_maximum_fusion.3.e0_ref), channel_id=1, source_target_pairs={{0,16},{16,0},{1,17},{17,1},{2,18},{18,2},{3,19},{19,3},{4,20},{20... | collective-permute-start | bytes 1572872 | tf_op jit(solution)/shard_map/ppermute | solution.py:548
  238.0 6.0 %copy-start.15 = (bf16[4,128,512]{2,1,0:T(8,128)(2,1)}, bf16[4,128,512]{2,1,0:T(8,128)(2,1)S(1)}, u32[]{:S(2)}) copy-start(bf16[4,128,512]{2,1,0:T(8,128)(2,1)S(1)} %pad_maximum_fusion.4.e1_ref) | copy-start | bytes 1572868
  238.0 6.0 %collective-permute-start.34 = (bf16[4,128,512]{2,1,0:T(8,128)(2,1)S(1)}, bf16[4,128,512]{2,1,0:T(8,128)(2,1)S(1)}, u32[]{:S(2)}, u32[]{:S(2)}) collective-permute-start(bf16[4,128,512]{2,1,0:T(8,128)(2,1)S(1)} %pad_maximum_fusion.4.e1_ref), channel_id=1, source_target_pairs={{0,16},{16,0},{1,17},{17,1},{2,18},{18,2},{3,19},{19,3},{4,20},{20... | collective-permute-start | bytes 1572872 | tf_op jit(solution)/shard_map/ppermute | solution.py:548
  242.5 1.5 copy-start.17
  244.0 0.8 copy-start.18

commit v9 on v8

--- a/solution.py
+++ b/solution.py
@@ -194,20 +194,24 @@
 
 
 def predict_kernel(
-    source_ref, rank_ref, len_ref, leaf_ref, far_own_ref, far_rest_ref, mixed_ref, gain_ref, prev_ref, maps_ref,
+    source_ref, rank_ref, len_ref, leaf_ref, far_own_ref, far_rest_ref, mixed_ref, gain_ref, prev_ref, maps_from_ref,
     *refs,
 ):
     weight_refs = refs[:16]
-    own_ref, err_ref, loss_ref, scale_ref, ahead_ref, weight_ref, sem_ref, far_ref, far_sem = refs[16:]
+    own_ref, err_ref, loss_ref, scale_ref, ahead_ref, weight_ref, sem_ref, far_ref, far_sem = refs[16:25]
+    maps_ref = refs[25]
+    maps_load = pltpu.make_async_copy(maps_from_ref, maps_ref, far_sem.at[2])
     own_load = pltpu.make_async_copy(far_own_ref, far_ref.at[:, 0], far_sem.at[0])
     rest_load = pltpu.make_async_copy(far_rest_ref, far_ref.at[:, 1:4], far_sem.at[1])
     own_load.start()
     rest_load.start()
+    maps_load.start()
     loads = [pltpu.make_async_copy(weight_refs[i], weight_ref.at[i], sem_ref.at[i]) for i in range(16)]
     for load in loads:
         load.start()
     square = jnp.zeros((128, 128), F32)
     own_load.wait()
+    maps_load.wait()
     for k in range(4):
         if k == 1:
             rest_load.wait()
@@ -408,8 +412,8 @@
         ),
         in_specs=[in_smem()] * 4
         + [pl.BlockSpec(memory_space=pl.ANY)] * 2
-        + [in_vmem()] * 4
-        + [pl.BlockSpec(memory_space=pl.ANY)] * 16,
+        + [in_vmem()] * 3
+        + [pl.BlockSpec(memory_space=pl.ANY)] * 17,
         out_specs=(in_vmem(),) * 3,
         scratch_shapes=[
             pltpu.VMEM((128, 128), F32),
@@ -417,7 +421,8 @@
             pltpu.VMEM((16, 2, 256, 512), BF16),
             pltpu.SemaphoreType.DMA((16,)),
             pltpu.VMEM((4, 4, 128, 512), BF16),
-            pltpu.SemaphoreType.DMA((2,)),
+            pltpu.SemaphoreType.DMA((3,)),
+            pltpu.VMEM((256, 128), BF16),
         ],
         compiler_params=pltpu.CompilerParams(vmem_limit_bytes=32 << 20),
         cost_estimate=pl.CostEstimate(

time: 280 us -> 281 us (level)
  no operation moved by 1% of the time
where the time goes in v9:
time: 281 us; the launch traced here: 280 us
  starting transfers between devices  106 us (38%)
  waiting for transfers between devices  68.8 us (24%)
  blocking collectives  54.1 us (19%)
  Pallas kernels  34.5 us (12%)
  local copies, waits for them, and re-layouts  11.9 us (4%)
  other arithmetic  3.59 us (1%)
    all_to_all x2, blocking collectives, exchange(): return lax.all_to_all(value, axis, 0, 0, tiled=True)  54.1 us
    ppermute x20, starting transfers between devices, passed(): lax.ppermute(value, axis, turn(count, step))  46.8 us
    ppermute x20, waiting for transfers between devices, passed(): lax.ppermute(value, axis, turn(count, step))  31.5 us
    all_to_all x4, waiting for transfers between devices, exchange(): return lax.all_to_all(value, axis, 0, 0, tiled=True)  24.5 us
    all_to_all x4, starting transfers between devices, exchange(): return lax.all_to_all(value, axis, 0, 0, tiled=True)  21.4 us
    ppermute x4, starting transfers between devices, body(): other_upper = [lax.ppermute(part, 'c', turn(2, 1)) for part in upper]  10.2 us
    ppermute x1, starting transfers between devices, body(): lax.ppermute(table, REQ + TP, [(i * N_TP + j, j * N_TP + i) for i in rang...  9.69 us
    pallas_call x1, Pallas kernels, attend(): pl.pallas_call(attend_kernel, out_shape=(jax.ShapeDtypeStruct((N_TP, 144,...  8.91 us
  transfers between devices with their start and end apart: 39, of which 14 were waited for; matrix products, arithmetic and copies ran while one was open for 3% of the time, Pallas kernels for 2%

profile of v9, /device:TPU:1, one launch (start us, length us, event | category | flops | bytes accessed | tf_op | source)
XLA Modules:
  0.0 279.5 jit_solution(10853149535866321532)
XLA Ops:
  0.7 8.9 %attend.1 = (bf16[16,144,256]{2,1,0:T(8,128)(2,1)}, bf16[256,128]{1,0:T(8,128)(2,1)}) custom-call(s32[1]{0:T(128)} %bitcast.rank_ref, s32[4]{0:T(128)} %len_ref.3, s32[4,32]{1,0:T(4,128)} %par_ref.1, bf16[4,32,4096]{2,1,0:T(8,128)(2,1)} %q_ref.1, bf16[4,256,512]{2,1,0:T(8,128)(2,1)} %ck_ref.1, bf16[4,256,512]{2,1,0:T(8,128)(2,1)} %cv_ref.1, ...), custom_call_target="tpu_custom_call" | custom-call | flops 536870912 | bytes 4194304 | tf_op jit(solution)/shard_map/attend/pallas_call | solution.py:315
  9.6 9.0 %all-to-all-start = ((bf16[16,144,256]{2,1,0:T(8,128)(2,1)}), bf16[16,144,256]{2,1,0:T(8,128)(2,1)S(1)}, u32[]{:S(2)}, u32[]{:S(2)}) async-start(bf16[16,144,256]{2,1,0:T(8,128)(2,1)} %get-tuple-element.27), calls=%async_computation | async-start | bytes 2359296 | tf_op jit(solution)/shard_map/all_to_all | solution.py:36
  18.6 24.4 %all-to-all-done.parcel_ref = bf16[16,144,256]{2,1,0:T(8,128)(2,1)S(1)} async-done(((bf16[16,144,256]{2,1,0:T(8,128)(2,1)}), bf16[16,144,256]{2,1,0:T(8,128)(2,1)S(1)}, u32[]{:S(2)}, u32[]{:S(2)}) %all-to-all-start) | async-done | bytes 1179680 | tf_op jit(solution)/shard_map/all_to_all | solution.py:36
  43.1 1.0 copy-done.13
  44.1 6.0 %project.1 = bf16[4,4,128,512]{3,2,1,0:T(8,128)(2,1)} custom-call(bf16[16,144,256]{2,1,0:T(8,128)(2,1)} %copy-done.13, bf16[256,8192]{1,0:T(8,128)(2,1)} %weight_ref.2), custom_call_target="tpu_custom_call" | custom-call | flops 536870912 | bytes 7340032 | tf_op jit(solution)/shard_map/project/pallas_call | solution.py:343
  50.1 29.0 %all_to_all.36.along_ref = bf16[4,4,128,512]{3,2,1,0:T(8,128)(2,1)} all-to-all(bf16[4,4,128,512]{3,2,1,0:T(8,128)(2,1)} %project.1), channel_id=1, replica_groups=mesh['zh'=2,'y'=4,'c'=2,'zl'=4,'x'=4] {'x'}, dimensions={0} | all-to-all | bytes 4194304 | tf_op jit(solution)/shard_map/all_to_all | solution.py:36
  79.1 2.6 fold.1
  81.6 3.7 %collective-permute-start = (bf16[128,512]{1,0:T(8,128)(2,1)}, bf16[128,512]{1,0:T(8,128)(2,1)S(1)}, u32[]{:S(2)}, u32[]{:S(2)}) collective-permute-start(bf16[128,512]{1,0:T(8,128)(2,1)} %get-tuple-element.30), channel_id=1, source_target_pairs={{0,4},{4,8},{8,12},{12,0},{1,5},{5,9},{9,13},{13,1},{2,6},{6,10},{... | collective-permute-start | bytes 393224 | tf_op jit(solution)/shard_map/ppermute | solution.py:520
  85.3 2.5 collective-permute-start.1
  87.8 2.4 collective-permute-start.2
  90.2 3.6 %collective-permute-done.1.two_ref = bf16[128,512]{1,0:T(8,128)(2,1)S(1)} collective-permute-done((bf16[128,512]{1,0:T(8,128)(2,1)}, bf16[128,512]{1,0:T(8,128)(2,1)S(1)}, u32[]{:S(2)}, u32[]{:S(2)}) %collective-permute-start.1) | collective-permute-done | bytes 131104 | tf_op jit(solution)/shard_map/ppermute | solution.py:520
  94.5 2.2 settle.1
  96.7 3.5 %all-to-all-start.2 = ((bf16[4,128,512]{2,1,0:T(8,128)(2,1)}), bf16[4,128,512]{2,1,0:T(8,128)(2,1)S(1)}, u32[]{:S(2)}, u32[]{:S(2)}) async-start(bf16[4,128,512]{2,1,0:T(8,128)(2,1)} %get-tuple-element.33), calls=%async_computation.2 | async-start | bytes 1048576 | tf_op jit(solution)/shard_map/all_to_all | solution.py:36
  100.2 4.3 %collective-permute-start.6 = (bf16[256,512]{1,0:T(8,128)(2,1)S(1)}, bf16[256,512]{1,0:T(8,128)(2,1)S(1)}, u32[]{:S(2)}, u32[]{:S(2)}) collective-permute-start(bf16[256,512]{1,0:T(8,128)(2,1)S(1)} %get-tuple-element.37), channel_id=1, source_target_pairs={{0,128},{128,0},{1,129},{129,1},{2,130},{130,2},{3,131},{131,3},{4... | collective-permute-start | bytes 786440 | tf_op jit(solution)/shard_map/ppermute | solution.py:44
  104.5 4.7 %collective-permute-start.3 = (bf16[128,512]{1,0:T(8,128)(2,1)}, bf16[128,512]{1,0:T(8,128)(2,1)S(1)}, u32[]{:S(2)}, u32[]{:S(2)}) collective-permute-start(bf16[128,512]{1,0:T(8,128)(2,1)} %get-tuple-element.34), channel_id=1, source_target_pairs={{0,4},{4,8},{8,12},{12,0},{1,5},{5,9},{9,13},{13,1},{2,6},{6,10},{... | collective-permute-start | bytes 393224 | tf_op jit(solution)/shard_map/ppermute | solution.py:44
  109.2 2.7 collective-permute-start.4
  111.9 1.2 collective-permute-start.14
  113.1 10.2 %collective-permute-done.3 = bf16[128,512]{1,0:T(8,128)(2,1)S(1)} collective-permute-done((bf16[128,512]{1,0:T(8,128)(2,1)}, bf16[128,512]{1,0:T(8,128)(2,1)S(1)}, u32[]{:S(2)}, u32[]{:S(2)}) %collective-permute-start.3) | collective-permute-done | bytes 131104 | tf_op jit(solution)/shard_map/ppermute | solution.py:44
  123.3 14.9 %collective-permute-done.4 = bf16[128,512]{1,0:T(8,128)(2,1)S(1)} collective-permute-done((bf16[128,512]{1,0:T(8,128)(2,1)}, bf16[128,512]{1,0:T(8,128)(2,1)S(1)}, u32[]{:S(2)}, u32[]{:S(2)}) %collective-permute-start.4) | collective-permute-done | bytes 131104 | tf_op jit(solution)/shard_map/ppermute | solution.py:44
  138.2 1.3 broadcast_in_dim.4
  139.6 4.3 %all-to-all-start.3 = ((bf16[12,128,512]{2,1,0:T(8,128)(2,1)}), bf16[12,128,512]{2,1,0:T(8,128)(2,1)S(1)}, u32[]{:S(2)}, u32[]{:S(2)}) async-start(bf16[12,128,512]{2,1,0:T(8,128)(2,1)} %bitcast.36), calls=%async_computation.3 | async-start | bytes 3145728 | tf_op jit(solution)/shard_map/all_to_all | solution.py:36
  143.8 0.7 copy-done.20
  144.5 1.0 pad_maximum_fusion.refs_0_
  145.5 1.4 collective-permute-start.7
  146.9 2.7 collective-permute-start.8
  149.6 1.1 collective-permute-start.9
  150.6 0.7 copy-done.19
  151.3 1.0 pad_maximum_fusion.1.refs_8_
  152.8 9.7 %collective-permute-start.22 = (bf16[128,512]{1,0:T(8,128)(2,1)S(1)}, bf16[128,512]{1,0:T(8,128)(2,1)S(1)}, u32[]{:S(2)}, u32[]{:S(2)}) collective-permute-start(bf16[128,512]{1,0:T(8,128)(2,1)S(1)} %copy-done.24), channel_id=1, source_target_pairs={{0,0},{1,16},{2,32},{3,48},{4,64},{5,80},{6,96},{7,112},{8,128},{9... | collective-permute-start | bytes 393224 | tf_op jit(solution)/shard_map/ppermute | solution.py:528
  162.5 2.9 %collective-permute-done.22 = bf16[128,512]{1,0:T(8,128)(2,1)S(1)} collective-permute-done((bf16[128,512]{1,0:T(8,128)(2,1)S(1)}, bf16[128,512]{1,0:T(8,128)(2,1)S(1)}, u32[]{:S(2)}, u32[]{:S(2)}) %collective-permute-start.22) | collective-permute-done | bytes 131104 | tf_op jit(solution)/shard_map/ppermute | solution.py:528
  165.4 6.0 %collective-permute-start.23 = (bf16[128,512]{1,0:T(8,128)(2,1)S(1)}, bf16[128,512]{1,0:T(8,128)(2,1)S(1)}, u32[]{:S(2)}, u32[]{:S(2)}) collective-permute-start(bf16[128,512]{1,0:T(8,128)(2,1)S(1)} %collective-permute-done.22), channel_id=1, source_target_pairs={{0,4},{4,8},{8,12},{12,0},{1,5},{5,9},{9,13},{13,1},{2,6},{6,10},{... | collective-permute-start | bytes 393224 | tf_op jit(solution)/shard_map/ppermute | solution.py:44
  171.4 2.1 collective-permute-start.24
  173.5 8.4 %collective-permute-start.25 = (bf16[128,512]{1,0:T(8,128)(2,1)S(1)}, bf16[128,512]{1,0:T(8,128)(2,1)S(1)}, u32[]{:S(2)}, u32[]{:S(2)}) collective-permute-start(bf16[128,512]{1,0:T(8,128)(2,1)S(1)} %collective-permute-done.22), channel_id=1, source_target_pairs={{0,12},{4,0},{8,4},{12,8},{1,13},{5,1},{9,5},{13,9},{2,14},{6,2},{... | collective-permute-start | bytes 393224 | tf_op jit(solution)/shard_map/ppermute | solution.py:44
  182.0 0.8 collective-permute-start.17
  182.8 8.8 %collective-permute-start.10 = (bf16[2,256,512]{2,1,0:T(8,128)(2,1)S(1)}, bf16[2,256,512]{2,1,0:T(8,128)(2,1)}, u32[]{:S(2)}, u32[]{:S(2)}) collective-permute-start(bf16[2,256,512]{2,1,0:T(8,128)(2,1)S(1)} %pad_maximum_fusion.refs_0_), channel_id=1, source_target_pairs={{0,16},{16,0},{1,17},{17,1},{2,18},{18,2},{3,19},{19,3},{4,20},{20... | collective-permute-start | bytes 1572872 | tf_op jit(solution)/shard_map/ppermute | solution.py:516
  191.5 0.7 collective-permute-start.18
  192.3 0.9 pad_maximum_fusion.2
  193.2 2.6 broadcast_in_dim.5
  195.8 4.6 %all-to-all-start.4 = ((bf16[16,128,512]{2,1,0:T(8,128)(2,1)}), bf16[16,128,512]{2,1,0:T(8,128)(2,1)}, u32[]{:S(2)}, u32[]{:S(2)}) async-start(bf16[16,128,512]{2,1,0:T(8,128)(2,1)} %bitcast.35), calls=%async_computation.4 | async-start | bytes 4194304 | tf_op jit(solution)/shard_map/all_to_all | solution.py:36
  201.0 5.7 %collective-permute-done.17.refs_11_ = bf16[2,256,512]{2,1,0:T(8,128)(2,1)} collective-permute-done((bf16[2,256,512]{2,1,0:T(8,128)(2,1)S(1)}, bf16[2,256,512]{2,1,0:T(8,128)(2,1)}, u32[]{:S(2)}, u32[]{:S(2)}) %collective-permute-start.17) | collective-permute-done | bytes 524320 | tf_op jit(solution)/shard_map/ppermute | solution.py:44
  206.7 0.8 collective-permute-start.13
  208.6 0.7 collective-permute-done.13.refs_7_
  209.4 0.7 collective-permute-done.19.refs_13_
  210.1 0.7 collective-permute-done.20.refs_14_
  210.9 0.7 collective-permute-done.21.refs_15_
  211.7 1.0 copy-done.1
  212.7 1.0 copy-done.3
  213.7 1.0 copy-done.5
  214.8 0.8 copy-done.9
  215.6 5.6 %predict.1 = (bf16[128,512]{1,0:T(8,128)(2,1)}, bf16[128,512]{1,0:T(8,128)(2,1)S(1)}, f32[8,128]{1,0:T(8,128)S(1)}) custom-call(s32[16]{0:T(128)S(1)} %get-tuple-element.50.source_ref, s32[1]{0:T(128)} %bitcast.rank_ref, s32[4]{0:T(128)S(1)} %copy-done.11, s32[4]{0:T(128)S(1)} %copy-done.12, bf16[4,128,512]{2,1,0:T(8,128)(2,1)S(1)} %all-to-all-done.2.far_own_ref, ...), custom_call_target="tpu_custom_call" | custom-call | flops 1073741824 | bytes 13631488 | tf_op jit(solution)/shard_map/predict/pallas_call | solution.py:406
  221.3 2.7 collective-permute-start.26
  224.0 3.1 %collective-permute-start.27 = (bf16[128,512]{1,0:T(8,128)(2,1)S(1)}, bf16[128,512]{1,0:T(8,128)(2,1)S(1)}, u32[]{:S(2)}, u32[]{:S(2)}) collective-permute-start(bf16[128,512]{1,0:T(8,128)(2,1)S(1)} %get-tuple-element.41), channel_id=1, source_target_pairs={{0,64},{32,96},{64,0},{96,32},{1,65},{33,97},{65,1},{97,33},{2,66}... | collective-permute-start | bytes 393224 | tf_op jit(solution)/shard_map/ppermute | solution.py:44
  227.1 1.0 collective-permute-start.28
  228.1 1.8 collective-permute-done.29
  229.9 3.3 %collective-permute-start.31 = (bf16[128,512]{1,0:T(8,128)(2,1)S(1)}, bf16[128,512]{1,0:T(8,128)(2,1)S(1)}, u32[]{:S(2)}, u32[]{:S(2)}) collective-permute-start(bf16[128,512]{1,0:T(8,128)(2,1)S(1)} %collective-permute-done.29), channel_id=1, source_target_pairs={{0,64},{32,96},{64,0},{96,32},{1,65},{33,97},{65,1},{97,33},{2,66}... | collective-permute-start | bytes 393224 | tf_op jit(solution)/shard_map/ppermute | solution.py:44
  233.2 0.8 collective-permute-start.32
  234.2 3.2 %collective-permute-start.33 = (bf16[4,128,512]{2,1,0:T(8,128)(2,1)S(1)}, bf16[4,128,512]{2,1,0:T(8,128)(2,1)S(1)}, u32[]{:S(2)}, u32[]{:S(2)}) collective-permute-start(bf16[4,128,512]{2,1,0:T(8,128)(2,1)S(1)} %pad_maximum_fusion.3.e0_ref), channel_id=1, source_target_pairs={{0,16},{16,0},{1,17},{17,1},{2,18},{18,2},{3,19},{19,3},{4,20},{20... | collective-permute-start | bytes 1572872 | tf_op jit(solution)/shard_map/ppermute | solution.py:553
  237.4 0.7 collective-permute-done.31
  238.2 4.4 %collective-permute-start.34 = (bf16[4,128,512]{2,1,0:T(8,128)(2,1)S(1)}, bf16[4,128,512]{2,1,0:T(8,128)(2,1)S(1)}, u32[]{:S(2)}, u32[]{:S(2)}) collective-permute-start(bf16[4,128,512]{2,1,0:T(8,128)(2,1)S(1)} %pad_maximum_fusion.4.e1_ref), channel_id=1, source_target_pairs={{0,16},{16,0},{1,17},{17,1},{2,18},{18,2},{3,19},{19,3},{4,20},{20... | collective-permute-start | bytes 1572872 | tf_op jit(solution)/shard_map/ppermute | solution.py:553
  242.6 1.5 collective-permute-done.34.e3_ref
  244.2 0.8 copy-done.18
  245.0 4.5 %differentiate.1 = (f32[512,512]{1,0:T(8,128)}, f32[256,128]{1,0:T(8,128)}) custom-call(s32[16]{0:T(128)} %get-tuple-element.49.place_ref, bf16[16,128,512]{2,1,0:T(8,128)(2,1)} %all-to-all-done.4.column_ref, bf16[4,128,512]{2,1,0:T(8,128)(2,1)} %copy-done.14, bf16[4,128,512]{2,1,0:T(8,128)(2,1)} %copy-done.15, bf16[4,128,512]{2,1,0:T(8,128)(2,1)} %copy-done.17, ...), custom_call_target="tpu_custom_call" | custom-call | flops 1073741824 | bytes 5242880 | tf_op jit(solution)/shard_map/differentiate/pallas_call | solution.py:436
  249.4 25.2 %all_to_all.37 = f32[256,1,128]{2,1,0:T(1,128)} all-to-all(f32[256,1,128]{2,1,0:T(1,128)} %bitcast.43), channel_id=1, replica_groups=mesh['zh'=2,'y'=4,'c'=2,'zl'=4,'x'=4] {'zh','y','c','zl','x'}, dimensions={0} | all-to-all | bytes 262144 | tf_op jit(solution)/shard_map/all_to_all | solution.py:36
  274.6 4.8 %update.1 = (bf16[512,512]{1,0:T(8,128)(2,1)}, f32[512,512]{1,0:T(8,128)}, f32[512,512]{1,0:T(8,128)}, f32[1,1]{1,0:T(1,128)}) custom-call(f32[256,128]{1,0:T(8,128)} %bitcast.39, f32[512,512]{1,0:T(8,128)} %get-tuple-element.44.grad_ref, bf16[512,512]{1,0:T(8,128)(2,1)} %weight_ref.3, f32[512,512]{1,0:T(8,128)} %first_ref.1, f32[512,512]{1,0:T(8,128)} %second_ref.1), custom_call_target="tpu_custom_call" | custom-call | flops 5242880 | bytes 6291456 | tf_op jit(solution)/shard_map/update/pallas_call | solution.py:453
  (83 shorter events, 3.4 us)
Async XLA Ops:
  0.6 17.9 %copy-start.16 = (bf16[512,512]{1,0:T(8,128)(2,1)S(1)}, bf16[512,512]{1,0:T(8,128)(2,1)}, u32[]{:S(2)}) copy-start(bf16[512,512]{1,0:T(8,128)(2,1)} %weight_ref.3) | copy-start | bytes 1572868
  9.6 33.5 %all-to-all-start = ((bf16[16,144,256]{2,1,0:T(8,128)(2,1)}), bf16[16,144,256]{2,1,0:T(8,128)(2,1)S(1)}, u32[]{:S(2)}, u32[]{:S(2)}) async-start(bf16[16,144,256]{2,1,0:T(8,128)(2,1)} %get-tuple-element.27), calls=%async_computation | async-start | bytes 2359296 | tf_op jit(solution)/shard_map/all_to_all | solution.py:36
  43.1 1.0 copy-start.13
  81.6 8.6 %collective-permute-start = (bf16[128,512]{1,0:T(8,128)(2,1)}, bf16[128,512]{1,0:T(8,128)(2,1)S(1)}, u32[]{:S(2)}, u32[]{:S(2)}) collective-permute-start(bf16[128,512]{1,0:T(8,128)(2,1)} %get-tuple-element.30), channel_id=1, source_target_pairs={{0,4},{4,8},{8,12},{12,0},{1,5},{5,9},{9,13},{13,1},{2,6},{6,10},{... | collective-permute-start | bytes 393224 | tf_op jit(solution)/shard_map/ppermute | solution.py:520
  85.3 8.5 %collective-permute-start.1 = (bf16[128,512]{1,0:T(8,128)(2,1)}, bf16[128,512]{1,0:T(8,128)(2,1)S(1)}, u32[]{:S(2)}, u32[]{:S(2)}) collective-permute-start(bf16[128,512]{1,0:T(8,128)(2,1)} %get-tuple-element.31), channel_id=1, source_target_pairs={{0,8},{4,12},{8,0},{12,4},{1,9},{5,13},{9,1},{13,5},{2,10},{6,14},... | collective-permute-start | bytes 393224 | tf_op jit(solution)/shard_map/ppermute | solution.py:520
  87.8 6.0 %collective-permute-start.2 = (bf16[128,512]{1,0:T(8,128)(2,1)}, bf16[128,512]{1,0:T(8,128)(2,1)S(1)}, u32[]{:S(2)}, u32[]{:S(2)}) collective-permute-start(bf16[128,512]{1,0:T(8,128)(2,1)} %get-tuple-element.32), channel_id=1, source_target_pairs={{0,12},{4,0},{8,4},{12,8},{1,13},{5,1},{9,5},{13,9},{2,14},{6,2},{... | collective-permute-start | bytes 393224 | tf_op jit(solution)/shard_map/ppermute | solution.py:520
  90.2 3.7 %copy-start.21 = (bf16[128,512]{1,0:T(8,128)(2,1)}, bf16[128,512]{1,0:T(8,128)(2,1)S(1)}, u32[]{:S(2)}) copy-start(bf16[128,512]{1,0:T(8,128)(2,1)S(1)} %collective-permute-done.one_ref) | copy-start | bytes 393220
  93.8 0.7 copy-start.22
  93.9 0.7 copy-start.23
  96.7 41.5 %all-to-all-start.2 = ((bf16[4,128,512]{2,1,0:T(8,128)(2,1)}), bf16[4,128,512]{2,1,0:T(8,128)(2,1)S(1)}, u32[]{:S(2)}, u32[]{:S(2)}) async-start(bf16[4,128,512]{2,1,0:T(8,128)(2,1)} %get-tuple-element.33), calls=%async_computation.2 | async-start | bytes 1048576 | tf_op jit(solution)/shard_map/all_to_all | solution.py:36
  100.2 43.6 %collective-permute-start.6 = (bf16[256,512]{1,0:T(8,128)(2,1)S(1)}, bf16[256,512]{1,0:T(8,128)(2,1)S(1)}, u32[]{:S(2)}, u32[]{:S(2)}) collective-permute-start(bf16[256,512]{1,0:T(8,128)(2,1)S(1)} %get-tuple-element.37), channel_id=1, source_target_pairs={{0,128},{128,0},{1,129},{129,1},{2,130},{130,2},{3,131},{131,3},{4... | collective-permute-start | bytes 786440 | tf_op jit(solution)/shard_map/ppermute | solution.py:44
  104.5 18.8 %collective-permute-start.3 = (bf16[128,512]{1,0:T(8,128)(2,1)}, bf16[128,512]{1,0:T(8,128)(2,1)S(1)}, u32[]{:S(2)}, u32[]{:S(2)}) collective-permute-start(bf16[128,512]{1,0:T(8,128)(2,1)} %get-tuple-element.34), channel_id=1, source_target_pairs={{0,4},{4,8},{8,12},{12,0},{1,5},{5,9},{9,13},{13,1},{2,6},{6,10},{... | collective-permute-start | bytes 393224 | tf_op jit(solution)/shard_map/ppermute | solution.py:44
  109.2 29.0 %collective-permute-start.4 = (bf16[128,512]{1,0:T(8,128)(2,1)}, bf16[128,512]{1,0:T(8,128)(2,1)S(1)}, u32[]{:S(2)}, u32[]{:S(2)}) collective-permute-start(bf16[128,512]{1,0:T(8,128)(2,1)} %get-tuple-element.34), channel_id=1, source_target_pairs={{0,8},{4,12},{8,0},{12,4},{1,9},{5,13},{9,1},{13,5},{2,10},{6,14},... | collective-permute-start | bytes 393224 | tf_op jit(solution)/shard_map/ppermute | solution.py:44
  111.9 26.3 %collective-permute-start.5 = (bf16[128,512]{1,0:T(8,128)(2,1)}, bf16[128,512]{1,0:T(8,128)(2,1)S(1)}, u32[]{:S(2)}, u32[]{:S(2)}) collective-permute-start(bf16[128,512]{1,0:T(8,128)(2,1)} %get-tuple-element.34), channel_id=1, source_target_pairs={{0,12},{4,0},{8,4},{12,8},{1,13},{5,1},{9,5},{13,9},{2,14},{6,2},{... | collective-permute-start | bytes 393224 | tf_op jit(solution)/shard_map/ppermute | solution.py:44
  111.9 38.7 %collective-permute-start.14 = (bf16[256,512]{1,0:T(8,128)(2,1)S(1)}, bf16[256,512]{1,0:T(8,128)(2,1)S(1)}, u32[]{:S(2)}, u32[]{:S(2)}) collective-permute-start(bf16[256,512]{1,0:T(8,128)(2,1)S(1)} %get-tuple-element.38), channel_id=1, source_target_pairs={{0,128},{128,0},{1,129},{129,1},{2,130},{130,2},{3,131},{131,3},{4... | collective-permute-start | bytes 786440 | tf_op jit(solution)/shard_map/ppermute | solution.py:44
  139.6 13.3 %copy-start.24 = (bf16[128,512]{1,0:T(8,128)(2,1)S(1)}, bf16[128,512]{1,0:T(8,128)(2,1)}, u32[]{:S(2)}) copy-start(bf16[128,512]{1,0:T(8,128)(2,1)} %get-tuple-element.40) | copy-start | bytes 393220
  139.6 53.6 %all-to-all-start.3 = ((bf16[12,128,512]{2,1,0:T(8,128)(2,1)}), bf16[12,128,512]{2,1,0:T(8,128)(2,1)S(1)}, u32[]{:S(2)}, u32[]{:S(2)}) async-start(bf16[12,128,512]{2,1,0:T(8,128)(2,1)} %bitcast.36), calls=%async_computation.3 | async-start | bytes 3145728 | tf_op jit(solution)/shard_map/all_to_all | solution.py:36
  143.8 0.7 copy-start.20
  145.5 25.9 %collective-permute-start.7 = (bf16[2,256,512]{2,1,0:T(8,128)(2,1)S(1)}, bf16[2,256,512]{2,1,0:T(8,128)(2,1)}, u32[]{:S(2)}, u32[]{:S(2)}) collective-permute-start(bf16[2,256,512]{2,1,0:T(8,128)(2,1)S(1)} %pad_maximum_fusion.refs_0_), channel_id=1, source_target_pairs={{0,32},{32,64},{64,96},{96,0},{1,33},{33,65},{65,97},{97,1},{2,34}... | collective-permute-start | bytes 1572872 | tf_op jit(solution)/shard_map/ppermute | solution.py:44
  146.9 26.6 %collective-permute-start.8 = (bf16[2,256,512]{2,1,0:T(8,128)(2,1)S(1)}, bf16[2,256,512]{2,1,0:T(8,128)(2,1)S(1)}, u32[]{:S(2)}, u32[]{:S(2)}) collective-permute-start(bf16[2,256,512]{2,1,0:T(8,128)(2,1)S(1)} %pad_maximum_fusion.refs_0_), channel_id=1, source_target_pairs={{0,64},{32,96},{64,0},{96,32},{1,65},{33,97},{65,1},{97,33},{2,66}... | collective-permute-start | bytes 1572872 | tf_op jit(solution)/shard_map/ppermute | solution.py:44
  149.6 32.4 %collective-permute-start.9 = (bf16[2,256,512]{2,1,0:T(8,128)(2,1)S(1)}, bf16[2,256,512]{2,1,0:T(8,128)(2,1)S(1)}, u32[]{:S(2)}, u32[]{:S(2)}) collective-permute-start(bf16[2,256,512]{2,1,0:T(8,128)(2,1)S(1)} %pad_maximum_fusion.refs_0_), channel_id=1, source_target_pairs={{0,96},{32,0},{64,32},{96,64},{1,97},{33,1},{65,33},{97,65},{2,98}... | collective-permute-start | bytes 1572872 | tf_op jit(solution)/shard_map/ppermute | solution.py:44
  150.6 0.7 copy-start.19
  152.3 29.6 %collective-permute-start.15 = (bf16[2,256,512]{2,1,0:T(8,128)(2,1)S(1)}, bf16[2,256,512]{2,1,0:T(8,128)(2,1)S(1)}, u32[]{:S(2)}, u32[]{:S(2)}) collective-permute-start(bf16[2,256,512]{2,1,0:T(8,128)(2,1)S(1)} %pad_maximum_fusion.1.refs_8_), channel_id=1, source_target_pairs={{0,32},{32,64},{64,96},{96,0},{1,33},{33,65},{65,97},{97,1},{2,34}... | collective-permute-start | bytes 1572872 | tf_op jit(solution)/shard_map/ppermute | solution.py:44
  152.8 12.6 %collective-permute-start.22 = (bf16[128,512]{1,0:T(8,128)(2,1)S(1)}, bf16[128,512]{1,0:T(8,128)(2,1)S(1)}, u32[]{:S(2)}, u32[]{:S(2)}) collective-permute-start(bf16[128,512]{1,0:T(8,128)(2,1)S(1)} %copy-done.24), channel_id=1, source_target_pairs={{0,0},{1,16},{2,32},{3,48},{4,64},{5,80},{6,96},{7,112},{8,128},{9... | collective-permute-start | bytes 393224 | tf_op jit(solution)/shard_map/ppermute | solution.py:528
  165.4 17.4 %collective-permute-start.23 = (bf16[128,512]{1,0:T(8,128)(2,1)S(1)}, bf16[128,512]{1,0:T(8,128)(2,1)S(1)}, u32[]{:S(2)}, u32[]{:S(2)}) collective-permute-start(bf16[128,512]{1,0:T(8,128)(2,1)S(1)} %collective-permute-done.22), channel_id=1, source_target_pairs={{0,4},{4,8},{8,12},{12,0},{1,5},{5,9},{9,13},{13,1},{2,6},{6,10},{... | collective-permute-start | bytes 393224 | tf_op jit(solution)/shard_map/ppermute | solution.py:44
  171.4 20.1 %collective-permute-start.24 = (bf16[128,512]{1,0:T(8,128)(2,1)S(1)}, bf16[128,512]{1,0:T(8,128)(2,1)S(1)}, u32[]{:S(2)}, u32[]{:S(2)}) collective-permute-start(bf16[128,512]{1,0:T(8,128)(2,1)S(1)} %collective-permute-done.22), channel_id=1, source_target_pairs={{0,8},{4,12},{8,0},{12,4},{1,9},{5,13},{9,1},{13,5},{2,10},{6,14},... | collective-permute-start | bytes 393224 | tf_op jit(solution)/shard_map/ppermute | solution.py:44
  173.5 18.8 %copy-start = (bf16[2,256,512]{2,1,0:T(8,128)(2,1)}, bf16[2,256,512]{2,1,0:T(8,128)(2,1)S(1)}, u32[]{:S(2)}) copy-start(bf16[2,256,512]{2,1,0:T(8,128)(2,1)S(1)} %collective-permute-done.8.refs_2_) | copy-start | bytes 1572868
  173.5 18.7 %collective-permute-start.25 = (bf16[128,512]{1,0:T(8,128)(2,1)S(1)}, bf16[128,512]{1,0:T(8,128)(2,1)S(1)}, u32[]{:S(2)}, u32[]{:S(2)}) collective-permute-start(bf16[128,512]{1,0:T(8,128)(2,1)S(1)} %collective-permute-done.22), channel_id=1, source_target_pairs={{0,12},{4,0},{8,4},{12,8},{1,13},{5,1},{9,5},{13,9},{2,14},{6,2},{... | collective-permute-start | bytes 393224 | tf_op jit(solution)/shard_map/ppermute | solution.py:44
  181.9 10.4 %copy-start.2 = (bf16[2,256,512]{2,1,0:T(8,128)(2,1)}, bf16[2,256,512]{2,1,0:T(8,128)(2,1)S(1)}, u32[]{:S(2)}) copy-start(bf16[2,256,512]{2,1,0:T(8,128)(2,1)S(1)} %collective-permute-done.9.refs_3_) | copy-start | bytes 1572868
  181.9 18.5 %collective-permute-start.16 = (bf16[2,256,512]{2,1,0:T(8,128)(2,1)S(1)}, bf16[2,256,512]{2,1,0:T(8,128)(2,1)}, u32[]{:S(2)}, u32[]{:S(2)}) collective-permute-start(bf16[2,256,512]{2,1,0:T(8,128)(2,1)S(1)} %pad_maximum_fusion.1.refs_8_), channel_id=1, source_target_pairs={{0,64},{32,96},{64,0},{96,32},{1,65},{33,97},{65,1},{97,33},{2,66}... | collective-permute-start | bytes 1572872 | tf_op jit(solution)/shard_map/ppermute | solution.py:44
  181.9 9.6 %copy-start.4 = (bf16[2,256,512]{2,1,0:T(8,128)(2,1)}, bf16[2,256,512]{2,1,0:T(8,128)(2,1)S(1)}, u32[]{:S(2)}) copy-start(bf16[2,256,512]{2,1,0:T(8,128)(2,1)S(1)} %collective-permute-done.15.refs_9_) | copy-start | bytes 1572868
  182.0 24.7 %collective-permute-start.17 = (bf16[2,256,512]{2,1,0:T(8,128)(2,1)S(1)}, bf16[2,256,512]{2,1,0:T(8,128)(2,1)}, u32[]{:S(2)}, u32[]{:S(2)}) collective-permute-start(bf16[2,256,512]{2,1,0:T(8,128)(2,1)S(1)} %pad_maximum_fusion.1.refs_8_), channel_id=1, source_target_pairs={{0,96},{32,0},{64,32},{96,64},{1,97},{33,1},{65,33},{97,65},{2,98}... | collective-permute-start | bytes 1572872 | tf_op jit(solution)/shard_map/ppermute | solution.py:44
  182.8 24.7 %collective-permute-start.10 = (bf16[2,256,512]{2,1,0:T(8,128)(2,1)S(1)}, bf16[2,256,512]{2,1,0:T(8,128)(2,1)}, u32[]{:S(2)}, u32[]{:S(2)}) collective-permute-start(bf16[2,256,512]{2,1,0:T(8,128)(2,1)S(1)} %pad_maximum_fusion.refs_0_), channel_id=1, source_target_pairs={{0,16},{16,0},{1,17},{17,1},{2,18},{18,2},{3,19},{19,3},{4,20},{20... | collective-permute-start | bytes 1572872 | tf_op jit(solution)/shard_map/ppermute | solution.py:516
  191.5 16.0 %collective-permute-start.18 = (bf16[2,256,512]{2,1,0:T(8,128)(2,1)S(1)}, bf16[2,256,512]{2,1,0:T(8,128)(2,1)}, u32[]{:S(2)}, u32[]{:S(2)}) collective-permute-start(bf16[2,256,512]{2,1,0:T(8,128)(2,1)S(1)} %pad_maximum_fusion.1.refs_8_), channel_id=1, source_target_pairs={{0,16},{16,0},{1,17},{17,1},{2,18},{18,2},{3,19},{19,3},{4,20},{20... | collective-permute-start | bytes 1572872 | tf_op jit(solution)/shard_map/ppermute | solution.py:531
  192.2 15.8 %collective-permute-start.11 = (bf16[2,256,512]{2,1,0:T(8,128)(2,1)}, bf16[2,256,512]{2,1,0:T(8,128)(2,1)}, u32[]{:S(2)}, u32[]{:S(2)}) collective-permute-start(bf16[2,256,512]{2,1,0:T(8,128)(2,1)} %collective-permute-done.7.refs_1_), channel_id=1, source_target_pairs={{0,16},{16,0},{1,17},{17,1},{2,18},{18,2},{3,19},{19,3},{4,20},{20... | collective-permute-start | bytes 1572872 | tf_op jit(solution)/shard_map/ppermute | solution.py:516
  195.8 15.8 %copy-start.6 = (bf16[4,8192]{1,0:T(4,128)(2,1)S(1)}, bf16[4,8192]{1,0:T(4,128)(2,1)}, u32[]{:S(2)}) copy-start(bf16[4,8192]{1,0:T(4,128)(2,1)} %prev_ref.3) | copy-start | bytes 196612
  195.8 15.8 %copy-start.7 = (f32[128,512]{1,0:T(8,128)S(1)}, f32[128,512]{1,0:T(8,128)}, u32[]{:S(2)}) copy-start(f32[128,512]{1,0:T(8,128)} %get-tuple-element.35.mixed_ref) | copy-start | bytes 786436
  195.8 15.8 %copy-start.8 = (f32[8192]{0:T(1024)S(1)}, f32[8192]{0:T(1024)}, u32[]{:S(2)}) copy-start(f32[8192]{0:T(1024)} %param.24) | copy-start | bytes 98308
  195.8 15.8 %copy-start.11 = (s32[4]{0:T(128)S(1)}, s32[4]{0:T(128)}, u32[]{:S(2)}) copy-start(s32[4]{0:T(128)} %len_ref.3) | copy-start | bytes 52
  195.8 15.8 %copy-start.12 = (s32[4]{0:T(128)S(1)}, s32[4]{0:T(128)}, u32[]{:S(2)}) copy-start(s32[4]{0:T(128)} %leaf_ref.1) | copy-start | bytes 52
  195.8 46.8 %all-to-all-start.4 = ((bf16[16,128,512]{2,1,0:T(8,128)(2,1)}), bf16[16,128,512]{2,1,0:T(8,128)(2,1)}, u32[]{:S(2)}, u32[]{:S(2)}) async-start(bf16[16,128,512]{2,1,0:T(8,128)(2,1)} %bitcast.35), calls=%async_computation.4 | async-start | bytes 4194304 | tf_op jit(solution)/shard_map/all_to_all | solution.py:36
  200.4 8.2 %collective-permute-start.12 = (bf16[2,256,512]{2,1,0:T(8,128)(2,1)}, bf16[2,256,512]{2,1,0:T(8,128)(2,1)}, u32[]{:S(2)}, u32[]{:S(2)}) collective-permute-start(bf16[2,256,512]{2,1,0:T(8,128)(2,1)} %copy-done), channel_id=1, source_target_pairs={{0,16},{16,0},{1,17},{17,1},{2,18},{18,2},{3,19},{19,3},{4,20},{20... | collective-permute-start | bytes 1572872 | tf_op jit(solution)/shard_map/ppermute | solution.py:516
  206.7 2.7 collective-permute-start.13
  207.5 2.6 collective-permute-start.19
  207.5 3.4 %collective-permute-start.20 = (bf16[2,256,512]{2,1,0:T(8,128)(2,1)}, bf16[2,256,512]{2,1,0:T(8,128)(2,1)}, u32[]{:S(2)}, u32[]{:S(2)}) collective-permute-start(bf16[2,256,512]{2,1,0:T(8,128)(2,1)} %collective-permute-done.16.refs_10_), channel_id=1, source_target_pairs={{0,16},{16,0},{1,17},{17,1},{2,18},{18,2},{3,19},{19,3},{4,20},{20... | collective-permute-start | bytes 1572872 | tf_op jit(solution)/shard_map/ppermute | solution.py:531
  208.0 3.6 %collective-permute-start.21 = (bf16[2,256,512]{2,1,0:T(8,128)(2,1)}, bf16[2,256,512]{2,1,0:T(8,128)(2,1)}, u32[]{:S(2)}, u32[]{:S(2)}) collective-permute-start(bf16[2,256,512]{2,1,0:T(8,128)(2,1)} %collective-permute-done.17.refs_11_), channel_id=1, source_target_pairs={{0,16},{16,0},{1,17},{17,1},{2,18},{18,2},{3,19},{19,3},{4,20},{20... | collective-permute-start | bytes 1572872 | tf_op jit(solution)/shard_map/ppermute | solution.py:531
  211.6 1.0 copy-start.1
  212.7 1.0 copy-start.3
  213.7 1.0 copy-start.5
  214.8 0.8 copy-start.9
  221.2 13.0 %copy-start.10 = (f32[8,128]{1,0:T(8,128)}, f32[8,128]{1,0:T(8,128)S(1)}, u32[]{:S(2)}) copy-start(f32[8,128]{1,0:T(8,128)S(1)} %get-tuple-element.42.loss_ref) | copy-start | bytes 12292
  221.2 8.7 %collective-permute-start.29 = (bf16[128,512]{1,0:T(8,128)(2,1)S(1)}, bf16[128,512]{1,0:T(8,128)(2,1)S(1)}, u32[]{:S(2)}, u32[]{:S(2)}) collective-permute-start(bf16[128,512]{1,0:T(8,128)(2,1)S(1)} %get-tuple-element.41), channel_id=1, source_target_pairs={{0,128},{128,0},{1,129},{129,1},{2,130},{130,2},{3,131},{131,3},{4... | collective-permute-start | bytes 393224 | tf_op jit(solution)/shard_map/ppermute | solution.py:549
  221.3 11.9 %collective-permute-start.26 = (bf16[128,512]{1,0:T(8,128)(2,1)S(1)}, bf16[128,512]{1,0:T(8,128)(2,1)S(1)}, u32[]{:S(2)}, u32[]{:S(2)}) collective-permute-start(bf16[128,512]{1,0:T(8,128)(2,1)S(1)} %get-tuple-element.41), channel_id=1, source_target_pairs={{0,32},{32,64},{64,96},{96,0},{1,33},{33,65},{65,97},{97,1},{2,34}... | collective-permute-start | bytes 393224 | tf_op jit(solution)/shard_map/ppermute | solution.py:44
  224.0 10.1 %collective-permute-start.27 = (bf16[128,512]{1,0:T(8,128)(2,1)S(1)}, bf16[128,512]{1,0:T(8,128)(2,1)S(1)}, u32[]{:S(2)}, u32[]{:S(2)}) collective-permute-start(bf16[128,512]{1,0:T(8,128)(2,1)S(1)} %get-tuple-element.41), channel_id=1, source_target_pairs={{0,64},{32,96},{64,0},{96,32},{1,65},{33,97},{65,1},{97,33},{2,66}... | collective-permute-start | bytes 393224 | tf_op jit(solution)/shard_map/ppermute | solution.py:44
  227.1 7.0 %collective-permute-start.28 = (bf16[128,512]{1,0:T(8,128)(2,1)S(1)}, bf16[128,512]{1,0:T(8,128)(2,1)S(1)}, u32[]{:S(2)}, u32[]{:S(2)}) collective-permute-start(bf16[128,512]{1,0:T(8,128)(2,1)S(1)} %get-tuple-element.41), channel_id=1, source_target_pairs={{0,96},{32,0},{64,32},{96,64},{1,97},{33,1},{65,33},{97,65},{2,98}... | collective-permute-start | bytes 393224 | tf_op jit(solution)/shard_map/ppermute | solution.py:44
  229.9 7.5 %collective-permute-start.30 = (bf16[128,512]{1,0:T(8,128)(2,1)S(1)}, bf16[128,512]{1,0:T(8,128)(2,1)S(1)}, u32[]{:S(2)}, u32[]{:S(2)}) collective-permute-start(bf16[128,512]{1,0:T(8,128)(2,1)S(1)} %collective-permute-done.29), channel_id=1, source_target_pairs={{0,32},{32,64},{64,96},{96,0},{1,33},{33,65},{65,97},{97,1},{2,34}... | collective-permute-start | bytes 393224 | tf_op jit(solution)/shard_map/ppermute | solution.py:44
  229.9 8.2 %collective-permute-start.31 = (bf16[128,512]{1,0:T(8,128)(2,1)S(1)}, bf16[128,512]{1,0:T(8,128)(2,1)S(1)}, u32[]{:S(2)}, u32[]{:S(2)}) collective-permute-start(bf16[128,512]{1,0:T(8,128)(2,1)S(1)} %collective-permute-done.29), channel_id=1, source_target_pairs={{0,64},{32,96},{64,0},{96,32},{1,65},{33,97},{65,1},{97,33},{2,66}... | collective-permute-start | bytes 393224 | tf_op jit(solution)/shard_map/ppermute | solution.py:44
  233.2 4.9 %collective-permute-start.32 = (bf16[128,512]{1,0:T(8,128)(2,1)S(1)}, bf16[128,512]{1,0:T(8,128)(2,1)S(1)}, u32[]{:S(2)}, u32[]{:S(2)}) collective-permute-start(bf16[128,512]{1,0:T(8,128)(2,1)S(1)} %collective-permute-done.29), channel_id=1, source_target_pairs={{0,96},{32,0},{64,32},{96,64},{1,97},{33,1},{65,33},{97,65},{2,98}... | collective-permute-start | bytes 393224 | tf_op jit(solution)/shard_map/ppermute | solution.py:44
  234.2 10.0 %copy-start.14 = (bf16[4,128,512]{2,1,0:T(8,128)(2,1)}, bf16[4,128,512]{2,1,0:T(8,128)(2,1)S(1)}, u32[]{:S(2)}) copy-start(bf16[4,128,512]{2,1,0:T(8,128)(2,1)S(1)} %pad_maximum_fusion.3.e0_ref) | copy-start | bytes 1572868
  234.2 8.5 %collective-permute-start.33 = (bf16[4,128,512]{2,1,0:T(8,128)(2,1)S(1)}, bf16[4,128,512]{2,1,0:T(8,128)(2,1)S(1)}, u32[]{:S(2)}, u32[]{:S(2)}) collective-permute-start(bf16[4,128,512]{2,1,0:T(8,128)(2,1)S(1)} %pad_maximum_fusion.3.e0_ref), channel_id=1, source_target_pairs={{0,16},{16,0},{1,17},{17,1},{2,18},{18,2},{3,19},{19,3},{4,20},{20... | collective-permute-start | bytes 1572872 | tf_op jit(solution)/shard_map/ppermute | solution.py:553
  238.2 6.0 %copy-start.15 = (bf16[4,128,512]{2,1,0:T(8,128)(2,1)}, bf16[4,128,512]{2,1,0:T(8,128)(2,1)S(1)}, u32[]{:S(2)}) copy-start(bf16[4,128,512]{2,1,0:T(8,128)(2,1)S(1)} %pad_maximum_fusion.4.e1_ref) | copy-start | bytes 1572868
  238.2 6.0 %collective-permute-start.34 = (bf16[4,128,512]{2,1,0:T(8,128)(2,1)S(1)}, bf16[4,128,512]{2,1,0:T(8,128)(2,1)S(1)}, u32[]{:S(2)}, u32[]{:S(2)}) collective-permute-start(bf16[4,128,512]{2,1,0:T(8,128)(2,1)S(1)} %pad_maximum_fusion.4.e1_ref), channel_id=1, source_target_pairs={{0,16},{16,0},{1,17},{17,1},{2,18},{18,2},{3,19},{19,3},{4,20},{20... | collective-permute-start | bytes 1572872 | tf_op jit(solution)/shard_map/ppermute | solution.py:553
  242.6 1.5 copy-start.17
  244.2 0.8 copy-start.18
